TPU v7x, 128 devices: a whole 4x4x4 slice. The times are simulated.
128 devices in a mesh: seq: 64 (over x, y_lo, z, core), expert: 2 (over y_hi).
Axes of the slice: x: 4, y: 4 (y_hi: 2, y_lo: 2; y = y_hi * 2 + y_lo), z: 4, core: 2. Of those that a mesh axis runs over, the one named last changes fastest.
Arguments:
- tokens: bfloat16 [8192, 2048], P('seq'), may hold values from -6 to 6
- attn_gain: bfloat16 [2048], P(('seq', 'expert')), may hold values from 0.5 to 1.5
- kv_weight: bfloat16 [2048, 4096], P(('seq', 'expert')), may hold values from -0.125 to 0.125
- attn_router: bfloat16 [2048, 8], P(('seq', 'expert')), may hold values from -0.09375 to 0.09375
- query_weight: bfloat16 [2048, 16384], P(None, ('seq', 'expert')), may hold values from -0.125 to 0.125
- output_weight: bfloat16 [16384, 2048], P(('seq', 'expert')), may hold values from -1.5 to 1.5
- mlp_gain: bfloat16 [2048], P(('seq', 'expert')), may hold values from 0.5 to 1.5
- mlp_router: bfloat16 [2048, 8], P(('seq', 'expert')), may hold values from -0.09375 to 0.09375
- gate_weight: bfloat16 [2048, 45056], P(None, ('seq', 'expert')), may hold values from -0.125 to 0.125
- up_weight: bfloat16 [2048, 45056], P(None, ('seq', 'expert')), may hold values from -0.125 to 0.125
- down_weight: bfloat16 [45056, 2048], P(('seq', 'expert')), may hold values from -0.15625 to 0.15625
- attn_experts: int32 [8192, 2], P('seq'), may hold values from 0 to 7, all different within a row; in each aligned block of 64 rows (0 to 63, 64 to 127, ...) at most 18 rows name the same one
- mlp_experts: int32 [8192, 2], P('seq'), may hold values from 0 to 7, all different within a row
- priority: int32 [64, 128], P('seq'), may hold values from 0 to 127, each once within a row
- cotangent: bfloat16 [8192, 2048], P('seq'), may hold values from -6 to 6
Outputs:
- mixed: bfloat16 [8192, 2048], P('seq')
- tokens_grad: bfloat16 [8192, 2048], P('seq')
- attn_gain_grad: float32 [2048], P(('seq', 'expert'))
- kv_grad: float32 [2048, 4096], P(('seq', 'expert'))
- attn_router_grad: float32 [2048, 8], P(('seq', 'expert'))
- query_grad: float32 [2048, 16384], P(None, ('seq', 'expert'))
- output_grad: float32 [16384, 2048], P(('seq', 'expert'))
- mlp_gain_grad: float32 [2048], P(('seq', 'expert'))
- mlp_router_grad: float32 [2048, 8], P(('seq', 'expert'))
- gate_grad: float32 [2048, 45056], P(None, ('seq', 'expert'))
- up_grad: float32 [2048, 45056], P(None, ('seq', 'expert'))
- down_grad: float32 [45056, 2048], P(('seq', 'expert'))
Inputs may be any that keep to these rules, and one draw needn't show every extreme that they name: `attn_experts`: each row names 2 different experts; in each aligned block of 64 rows no expert is named by more than 18 rows, and in some block one is named by exactly 18. `mlp_experts`: each row names 2 different experts. `priority`: each row holds every value of 0 to 127 once.
All inputs are finite; a program needn't handle non-finite values.
Results may differ from a plain program's by a relative error of at most 0.019.
Values may be sent and summed in bfloat16 or wider, within the bound.
No kernel may reach another device: no remote copies, remote signals or barrier semaphores. Data moves between devices by JAX's collectives and lax.ppermute only.
A program may use at most 320 MiB of HBM per device.

v0:
```python
import math

import jax
import jax.numpy as jnp
from jax import lax
from jax.sharding import PartitionSpec as P

KV_HEADS = 16
HEAD = 128
EXPERTS = 8
TOPK = 2
PIECES = 8
BLOCK = 256


epsilon = 1e-06
masked_score = -1e30


def rope_tables(positions, head_size):
    half_size = head_size // 2
    frequency = jnp.exp(
        jnp.arange(half_size, dtype=jnp.float32) * (-2.0 * math.log(10000.0) / head_size)
    )
    angles = positions.astype(jnp.float32)[:, None] * frequency[None, :]
    return (jnp.cos(angles)[:, None, :], jnp.sin(angles)[:, None, :])


def rotate(values, cosines, sines):
    half_size = values.shape[-1] // 2
    first = values[..., :half_size]
    second = values[..., half_size:]
    return jnp.concatenate(
        [first * cosines - second * sines, second * cosines + first * sines], axis=-1
    )


def rotate_back(grads, cosines, sines):
    half_size = grads.shape[-1] // 2
    first = grads[..., :half_size]
    second = grads[..., half_size:]
    return jnp.concatenate(
        [first * cosines + second * sines, second * cosines - first * sines], axis=-1
    )


def slot_table(expert_ids, ranks, slot_cap):
    block_rows = expert_ids.shape[0]
    expert_range = jnp.arange(EXPERTS, dtype=jnp.int32)
    member = jnp.sum(
        (expert_ids[:, :, None] == expert_range[None, None, :]).astype(jnp.int32), axis=1
    )
    earlier = (ranks[:, None] < ranks[None, :]).astype(jnp.int32)
    places = jnp.sum(earlier[:, :, None] * member[:, None, :], axis=0)
    kept = member * (places < slot_cap).astype(jnp.int32)
    slot_range = jnp.arange(slot_cap, dtype=jnp.int32)
    landing = kept[:, :, None] * (places[:, :, None] == slot_range[None, None, :]).astype(jnp.int32)
    row_range = jnp.arange(block_rows, dtype=jnp.int32)
    slot_token = jnp.sum(landing * row_range[:, None, None], axis=0)
    slot_valid = jnp.sum(landing, axis=0)
    return (places, kept, slot_token, slot_valid)


def pair_index(expert_ids, places, kept, slot_cap):
    chosen_place = jnp.take_along_axis(places, expert_ids, axis=1)
    chosen_kept = jnp.take_along_axis(kept, expert_ids, axis=1)
    return (
        expert_ids * slot_cap + jnp.minimum(chosen_place, slot_cap - 1),
        chosen_kept.astype(jnp.float32),
    )


def pair_gates(logits, expert_ids):
    return jax.nn.softmax(jnp.take_along_axis(logits, expert_ids, axis=1), axis=-1)


def expert_onehot(expert_ids):
    expert_range = jnp.arange(EXPERTS, dtype=jnp.int32)
    return (expert_ids[:, :, None] == expert_range[None, None, :]).astype(jnp.float32)


def gates_back(gates, gate_grads, expert_ids):
    inner = jnp.sum(gates * gate_grads, axis=1, keepdims=True)
    chosen_grads = gates * (gate_grads - inner)
    return jnp.sum(chosen_grads[:, :, None] * expert_onehot(expert_ids), axis=1)


def slot_gates(gates, pair_kept, expert_ids, slot_token, slot_valid):
    per_expert = jnp.sum((gates * pair_kept)[:, :, None] * expert_onehot(expert_ids), axis=1)
    return jnp.take_along_axis(per_expert.T, slot_token, axis=1) * slot_valid.astype(jnp.float32)


def pick_slots(values, slot_token, slot_valid):
    return jnp.where(slot_valid[:, :, None] > 0, values[slot_token], jnp.zeros((), values.dtype))


def fan_out(slot_values, group_size):
    experts_here, slot_cap, width = slot_values.shape
    spread_out = jnp.broadcast_to(slot_values[:, None], (experts_here, group_size, slot_cap, width))
    return spread_out.reshape(experts_here * group_size, slot_cap, width)


def fold_group(received, group_size):
    count, slot_cap, width = received.shape
    return jnp.sum(received.reshape(count // group_size, group_size, slot_cap, width), axis=1)


def norm_back(normed_grad, gain, normed, inverse):
    scaled = normed_grad * gain
    gain_grad = jnp.sum(normed_grad * normed, axis=0)
    input_grad = inverse * (scaled - normed * jnp.mean(scaled * normed, axis=-1, keepdims=True))
    return (input_grad, gain_grad)


def shards(
    tokens,
    attn_gain,
    kv_weight,
    attn_router,
    query_weight,
    output_weight,
    mlp_gain,
    mlp_router,
    gate_weight,
    up_weight,
    down_weight,
    attn_experts,
    mlp_experts,
    priority,
    cotangent,
):
    devices = lax.axis_size(("seq", "expert"))
    halves = lax.axis_size("expert")
    device_index = lax.axis_index(("seq", "expert"))
    half_index = lax.axis_index("expert")
    seq_tokens, width = tokens.shape
    own_rows = seq_tokens // halves
    group_size = devices // EXPERTS
    head_cols = query_weight.shape[1]
    local_heads = head_cols // HEAD
    key_cols = KV_HEADS * HEAD
    all_tokens = own_rows * devices
    seq_length = seq_tokens * PIECES
    sequences = all_tokens // seq_length
    slot_cap = (9 * TOPK * own_rows + 8 * EXPERTS - 1) // (8 * EXPERTS)
    slot_rows = devices * slot_cap
    seq_rows = slot_rows // sequences
    my_expert = device_index // group_size
    scale = 1.0 / math.sqrt(HEAD)

    def slot_sums(partial_value):
        return fold_group(
            lax.all_to_all(
                partial_value, ("seq", "expert"), split_axis=0, concat_axis=0, tiled=True
            ),
            group_size,
        )

    start_row = half_index * own_rows
    own_input = lax.dynamic_slice_in_dim(tokens, start_row, own_rows, 0).astype(jnp.float32)
    own_cotangent = lax.dynamic_slice_in_dim(cotangent, start_row, own_rows, 0).astype(jnp.float32)
    own_attn = lax.dynamic_slice_in_dim(attn_experts, start_row, own_rows, 0)
    own_mlp = lax.dynamic_slice_in_dim(mlp_experts, start_row, own_rows, 0)
    own_rank = lax.dynamic_slice_in_dim(priority[0], start_row, own_rows, 0)
    token_order = jnp.arange(own_rows, dtype=jnp.int32)

    def dense_weights():
        return (
            lax.all_gather(attn_gain, ("seq", "expert"), axis=0, tiled=True),
            lax.all_gather(kv_weight, ("seq", "expert"), axis=0, tiled=True),
            lax.all_gather(attn_router, ("seq", "expert"), axis=0, tiled=True),
            lax.all_gather(mlp_gain, ("seq", "expert"), axis=0, tiled=True),
            lax.all_gather(mlp_router, ("seq", "expert"), axis=0, tiled=True),
        )

    gain_one, kv_full, router_one, gain_two, router_two = dense_weights()
    routes_all = lax.all_gather(attn_experts, "seq", axis=0, tiled=True)
    inverse_one = lax.rsqrt(jnp.mean(own_input * own_input, axis=-1, keepdims=True) + epsilon)
    normed_one = own_input * inverse_one
    attn_input = (normed_one * gain_one.astype(jnp.float32)).astype(jnp.bfloat16)
    attn_logits = jnp.dot(attn_input, router_one, preferred_element_type=jnp.float32)
    key_value = jnp.dot(attn_input, kv_full, preferred_element_type=jnp.float32)
    own_positions = (device_index * own_rows + token_order) % seq_length
    own_cos, own_sin = rope_tables(own_positions, HEAD)
    own_keys = (
        rotate(key_value[:, :key_cols].reshape(own_rows, KV_HEADS, HEAD), own_cos, own_sin)
        .reshape(own_rows, key_cols)
        .astype(jnp.bfloat16)
    )
    own_values = key_value[:, key_cols:].astype(jnp.bfloat16)

    def spread(values):
        shaped = values.reshape(own_rows, 1, group_size, head_cols)
        return jnp.broadcast_to(shaped, (own_rows, EXPERTS, group_size, head_cols)).reshape(
            own_rows, devices, head_cols
        )

    head_keys, head_values = (
        lax.all_to_all(
            spread(own_keys), ("seq", "expert"), split_axis=1, concat_axis=0, tiled=True
        ),
        lax.all_to_all(
            spread(own_values), ("seq", "expert"), split_axis=1, concat_axis=0, tiled=True
        ),
    )
    seq_keys = head_keys.reshape(sequences, seq_length, local_heads, HEAD)
    seq_values = head_values.reshape(sequences, seq_length, local_heads, HEAD)
    attn_places, attn_kept, attn_token, attn_valid = slot_table(own_attn, token_order, slot_cap)
    mlp_places, mlp_kept, mlp_token, mlp_valid = slot_table(own_mlp, own_rank, slot_cap)
    block_routes = routes_all.reshape(devices, own_rows, TOPK)
    dest_tables = jax.vmap(lambda block_ids: slot_table(block_ids, token_order, slot_cap)[2])(
        block_routes
    )
    dest_token = jnp.take(dest_tables, my_expert, axis=1)
    attn_rows = lax.all_to_all(
        fan_out(pick_slots(attn_input, attn_token, attn_valid), group_size),
        ("seq", "expert"),
        split_axis=0,
        concat_axis=0,
        tiled=True,
    ).reshape(slot_rows, width)
    queries = jnp.dot(attn_rows, query_weight, preferred_element_type=jnp.float32)
    slot_positions = (
        (jnp.arange(devices, dtype=jnp.int32)[:, None] * own_rows + dest_token) % seq_length
    ).reshape(slot_rows)
    slot_cos, slot_sin = rope_tables(slot_positions, HEAD)
    rotated = rotate(queries.reshape(slot_rows, local_heads, HEAD), slot_cos, slot_sin).astype(
        jnp.bfloat16
    )
    seq_queries = rotated.reshape(sequences, seq_rows, local_heads, HEAD)
    query_blocks = (slot_positions // BLOCK).reshape(sequences, seq_rows)
    key_blocks = jnp.arange(seq_length, dtype=jnp.int32) // BLOCK

    def seq_scores(query_part, key_part, block_part):
        scores = (
            jnp.einsum("rhd,khd->hrk", query_part, key_part, preferred_element_type=jnp.float32)
            * scale
        )
        allowed = key_blocks[None, :] <= block_part[:, None]
        return jnp.where(allowed[None], scores, masked_score)

    def attend_forward(inputs):
        query_part, key_part, value_part, block_part = inputs
        scores = seq_scores(query_part, key_part, block_part)
        largest = jnp.max(scores, axis=-1, keepdims=True)
        weights = jnp.exp(scores - largest)
        totals = jnp.sum(weights, axis=-1, keepdims=True)
        probs = weights / totals
        mixed_part = jnp.einsum(
            "hrk,khd->rhd",
            probs.astype(jnp.bfloat16),
            value_part,
            preferred_element_type=jnp.float32,
        )
        return (mixed_part.astype(jnp.bfloat16), largest + jnp.log(totals))

    attn_mixed, log_totals = lax.map(
        attend_forward, (seq_queries, seq_keys, seq_values, query_blocks)
    )
    mixed_rows = attn_mixed.reshape(slot_rows, head_cols)
    attn_partial = jnp.dot(mixed_rows, output_weight, preferred_element_type=jnp.float32).reshape(
        devices, slot_cap, width
    )
    attn_slots = slot_sums(attn_partial)
    attn_gates = pair_gates(attn_logits, own_attn)
    attn_index, attn_pair_kept = pair_index(own_attn, attn_places, attn_kept, slot_cap)
    attn_picked = attn_slots.reshape(EXPERTS * slot_cap, width)[attn_index]
    hidden_state = own_input + jnp.sum(
        attn_picked * (attn_gates * attn_pair_kept)[:, :, None], axis=1
    )
    inverse_two = lax.rsqrt(jnp.mean(hidden_state * hidden_state, axis=-1, keepdims=True) + epsilon)
    normed_two = hidden_state * inverse_two
    mlp_input = (normed_two * gain_two.astype(jnp.float32)).astype(jnp.bfloat16)
    mlp_logits = jnp.dot(mlp_input, router_two, preferred_element_type=jnp.float32)
    mlp_rows = lax.all_to_all(
        fan_out(pick_slots(mlp_input, mlp_token, mlp_valid), group_size),
        ("seq", "expert"),
        split_axis=0,
        concat_axis=0,
        tiled=True,
    ).reshape(slot_rows, width)
    gate_pre = jnp.dot(mlp_rows, gate_weight, preferred_element_type=jnp.float32)
    up_pre = jnp.dot(mlp_rows, up_weight, preferred_element_type=jnp.float32)
    activated = jax.nn.silu(gate_pre)
    inner_rows = (activated * up_pre).astype(jnp.bfloat16)
    mlp_partial = jnp.dot(inner_rows, down_weight, preferred_element_type=jnp.float32).reshape(
        devices, slot_cap, width
    )
    mlp_slots = slot_sums(mlp_partial)
    mlp_gates = pair_gates(mlp_logits, own_mlp)
    mlp_index, mlp_pair_kept = pair_index(own_mlp, mlp_places, mlp_kept, slot_cap)
    mlp_picked = mlp_slots.reshape(EXPERTS * slot_cap, width)[mlp_index]
    own_output = hidden_state + jnp.sum(
        mlp_picked * (mlp_gates * mlp_pair_kept)[:, :, None], axis=1
    )
    gain_one, kv_full, router_one, gain_two, router_two = dense_weights()
    mlp_gate_grad = jnp.sum(mlp_picked * own_cotangent[:, None, :], axis=-1) * mlp_pair_kept
    mlp_logit_grad = gates_back(mlp_gates, mlp_gate_grad, own_mlp)
    mlp_slot_grad = (
        own_cotangent[mlp_token]
        * slot_gates(mlp_gates, mlp_pair_kept, own_mlp, mlp_token, mlp_valid)[:, :, None]
    ).astype(jnp.bfloat16)
    down_rows = lax.all_to_all(
        fan_out(mlp_slot_grad, group_size),
        ("seq", "expert"),
        split_axis=0,
        concat_axis=0,
        tiled=True,
    ).reshape(slot_rows, width)
    inner_grad = jnp.einsum("rd,fd->rf", down_rows, down_weight, preferred_element_type=jnp.float32)
    down_grad = jnp.einsum("rf,rd->fd", inner_rows, down_rows, preferred_element_type=jnp.float32)
    sigmoid_gate = jax.nn.sigmoid(gate_pre)
    gate_pre_grad = (
        inner_grad * up_pre * sigmoid_gate * (1.0 + gate_pre * (1.0 - sigmoid_gate))
    ).astype(jnp.bfloat16)
    up_pre_grad = (inner_grad * activated).astype(jnp.bfloat16)
    gate_grad = jnp.einsum("rd,rf->df", mlp_rows, gate_pre_grad, preferred_element_type=jnp.float32)
    up_grad = jnp.einsum("rd,rf->df", mlp_rows, up_pre_grad, preferred_element_type=jnp.float32)
    row_grad = jnp.einsum(
        "rf,df->rd", gate_pre_grad, gate_weight, preferred_element_type=jnp.float32
    ) + jnp.einsum("rf,df->rd", up_pre_grad, up_weight, preferred_element_type=jnp.float32)
    mlp_row_grad = slot_sums(row_grad.reshape(devices, slot_cap, width))
    mlp_input_grad = jnp.sum(
        mlp_row_grad.reshape(EXPERTS * slot_cap, width)[mlp_index] * mlp_pair_kept[:, :, None],
        axis=1,
    )
    mlp_input_grad = mlp_input_grad + jnp.dot(
        mlp_logit_grad, router_two.astype(jnp.float32).T, precision=lax.Precision.HIGHEST
    )
    mlp_router_own = jnp.dot(
        mlp_input.astype(jnp.float32).T, mlp_logit_grad, precision=lax.Precision.HIGHEST
    )
    hidden_grad, gain_two_own = norm_back(
        mlp_input_grad, gain_two.astype(jnp.float32), normed_two, inverse_two
    )
    hidden_grad = hidden_grad + own_cotangent
    attn_gate_grad = jnp.sum(attn_picked * hidden_grad[:, None, :], axis=-1) * attn_pair_kept
    attn_logit_grad = gates_back(attn_gates, attn_gate_grad, own_attn)
    attn_slot_grad = (
        hidden_grad[attn_token]
        * slot_gates(attn_gates, attn_pair_kept, own_attn, attn_token, attn_valid)[:, :, None]
    ).astype(jnp.bfloat16)
    out_rows = lax.all_to_all(
        fan_out(attn_slot_grad, group_size),
        ("seq", "expert"),
        split_axis=0,
        concat_axis=0,
        tiled=True,
    ).reshape(slot_rows, width)
    output_grad = jnp.einsum("rw,rd->wd", mixed_rows, out_rows, preferred_element_type=jnp.float32)
    mixed_grad = jnp.einsum(
        "rd,wd->rw", out_rows, output_weight, preferred_element_type=jnp.float32
    ).astype(jnp.bfloat16)
    seq_mixed_grad = mixed_grad.reshape(sequences, seq_rows, local_heads, HEAD)

    def attend_backward(inputs):
        query_part, key_part, value_part, block_part, log_part, grad_part = inputs
        probs = jnp.exp(seq_scores(query_part, key_part, block_part) - log_part)
        prob_grad = jnp.einsum(
            "rhd,khd->hrk", grad_part, value_part, preferred_element_type=jnp.float32
        )
        inner = jnp.sum(probs * prob_grad, axis=-1, keepdims=True)
        score_grad = (probs * (prob_grad - inner)).astype(jnp.bfloat16)
        value_grad = jnp.einsum(
            "hrk,rhd->khd",
            probs.astype(jnp.bfloat16),
            grad_part,
            preferred_element_type=jnp.float32,
        )
        key_grad = (
            jnp.einsum("hrk,rhd->khd", score_grad, query_part, preferred_element_type=jnp.float32)
            * scale
        )
        query_part_grad = (
            jnp.einsum("hrk,khd->rhd", score_grad, key_part, preferred_element_type=jnp.float32)
            * scale
        )
        return (query_part_grad, key_grad, value_grad)

    seq_query_grad, seq_key_grad, seq_value_grad = lax.map(
        attend_backward,
        (seq_queries, seq_keys, seq_values, query_blocks, log_totals, seq_mixed_grad),
    )
    query_rot_grad = (
        rotate_back(seq_query_grad.reshape(slot_rows, local_heads, HEAD), slot_cos, slot_sin)
        .reshape(slot_rows, head_cols)
        .astype(jnp.bfloat16)
    )
    query_grad = jnp.einsum(
        "rd,rw->dw", attn_rows, query_rot_grad, preferred_element_type=jnp.float32
    )
    query_row_grad = jnp.einsum(
        "rw,dw->rd", query_rot_grad, query_weight, preferred_element_type=jnp.float32
    )
    attn_row_grad = slot_sums(query_row_grad.reshape(devices, slot_cap, width))
    key_back, value_back = (
        lax.all_to_all(
            seq_key_grad.reshape(devices, own_rows, 1, head_cols).astype(jnp.bfloat16),
            ("seq", "expert"),
            split_axis=0,
            concat_axis=2,
            tiled=True,
        ).astype(jnp.float32),
        lax.all_to_all(
            seq_value_grad.reshape(devices, own_rows, 1, head_cols).astype(jnp.bfloat16),
            ("seq", "expert"),
            split_axis=0,
            concat_axis=2,
            tiled=True,
        ).astype(jnp.float32),
    )
    own_key_grad = jnp.sum(key_back.reshape(own_rows, EXPERTS, group_size, head_cols), axis=1)
    own_value_grad = jnp.sum(
        value_back.reshape(own_rows, EXPERTS, group_size, head_cols), axis=1
    ).reshape(own_rows, key_cols)
    kv_own_grad = jnp.concatenate(
        [rotate_back(own_key_grad, own_cos, own_sin).reshape(own_rows, key_cols), own_value_grad],
        axis=1,
    ).astype(jnp.bfloat16)
    attn_input_grad = jnp.sum(
        attn_row_grad.reshape(EXPERTS * slot_cap, width)[attn_index] * attn_pair_kept[:, :, None],
        axis=1,
    )
    attn_input_grad = attn_input_grad + jnp.einsum(
        "rc,dc->rd", kv_own_grad, kv_full, preferred_element_type=jnp.float32
    )
    attn_input_grad = attn_input_grad + jnp.dot(
        attn_logit_grad, router_one.astype(jnp.float32).T, precision=lax.Precision.HIGHEST
    )
    kv_own_weight = jnp.einsum(
        "rd,rc->dc", attn_input, kv_own_grad, preferred_element_type=jnp.float32
    )
    attn_router_own = jnp.dot(
        attn_input.astype(jnp.float32).T, attn_logit_grad, precision=lax.Precision.HIGHEST
    )
    input_grad, gain_one_own = norm_back(
        attn_input_grad, gain_one.astype(jnp.float32), normed_one, inverse_one
    )
    input_grad = input_grad + hidden_grad
    gain_one_grad, kv_grad, attn_router_grad, gain_two_grad, mlp_router_grad = (
        lax.psum_scatter(gain_one_own, ("seq", "expert"), scatter_dimension=0, tiled=True),
        lax.psum_scatter(kv_own_weight, ("seq", "expert"), scatter_dimension=0, tiled=True),
        lax.psum_scatter(attn_router_own, ("seq", "expert"), scatter_dimension=0, tiled=True),
        lax.psum_scatter(gain_two_own, ("seq", "expert"), scatter_dimension=0, tiled=True),
        lax.psum_scatter(mlp_router_own, ("seq", "expert"), scatter_dimension=0, tiled=True),
    )
    mixed_full, input_full = (
        lax.all_gather(own_output.astype(jnp.bfloat16), "expert", axis=0, tiled=True),
        lax.all_gather(input_grad.astype(jnp.bfloat16), "expert", axis=0, tiled=True),
    )
    return (
        mixed_full,
        input_full,
        gain_one_grad,
        kv_grad,
        attn_router_grad,
        query_grad,
        output_grad,
        gain_two_grad,
        mlp_router_grad,
        gate_grad,
        up_grad,
        down_grad,
    )


def solution(mesh):
    return jax.shard_map(
        shards,
        mesh=mesh,
        in_specs=(
            P("seq", None),
            P(("seq", "expert")),
            P(("seq", "expert"), None),
            P(("seq", "expert"), None),
            P(None, ("seq", "expert")),
            P(("seq", "expert"), None),
            P(("seq", "expert")),
            P(("seq", "expert"), None),
            P(None, ("seq", "expert")),
            P(None, ("seq", "expert")),
            P(("seq", "expert"), None),
            P("seq", None),
            P("seq", None),
            P("seq", None),
            P("seq", None),
        ),
        out_specs=(
            P("seq", None),
            P("seq", None),
            P(("seq", "expert")),
            P(("seq", "expert"), None),
            P(("seq", "expert"), None),
            P(None, ("seq", "expert")),
            P(("seq", "expert"), None),
            P(("seq", "expert")),
            P(("seq", "expert"), None),
            P(None, ("seq", "expert")),
            P(None, ("seq", "expert")),
            P(("seq", "expert"), None),
        ),
        check_vma=False,
    )
```

profile of v0, /device:TPU:1, one launch (start us, length us, event | category | flops | bytes accessed | tf_op | source)
XLA Modules:
  0.0 5571.8 jit_solution(1010828622336865888)
XLA Ops:
  16.0 68.9 %all-reduce.5 = (bf16[2048]{0:T(1024)(128)(2,1)S(1)}, bf16[2048]{0:T(1024)(128)(2,1)S(1)}) all-reduce(bf16[2048]{0:T(1024)(128)(2,1)S(1)} %dynamic-update-slice.1, bf16[2048]{0:T(1024)(128)(2,1)S(1)} %dynamic-update-slice.2), channel_id=1, replica_groups=mesh['seq'=64,'expert'=2] {'seq','expert'}, use_global_device_ids=true, to_apply=%add | all-reduce | flops 4096 | bytes 16384
  100.5 361.4 %all-gather.4.cloned.1.call-done = bf16[2048,4096]{1,0:T(8,128)(2,1)} async-done(((bf16[16,4096]{1,0:T(8,128)(2,1)}), bf16[2048,4096]{1,0:T(8,128)(2,1)}) %all-gather.4.cloned.1.call-update) | async-done | bytes 16777232 | tf_op jit(solution)/shard_map/all_gather | solution.py:170
  461.9 8.8 fusion.118
  473.5 13.0 all-to-all-start.2
  486.5 96.2 %all_gather.31 = s32[8192,2]{0,1:T(2,128)S(1)} all-gather(s32[128,2]{0,1:T(2,128)S(1)} %copy-done.77), channel_id=1, replica_groups=mesh['seq'=64,'expert'=2] {'seq'}, dimensions={0}, use_global_device_ids=true | all-gather | bytes 66560 | tf_op jit(solution)/shard_map/all_gather | solution.py:177
  598.5 14.1 reshape.754
  627.1 30.4 while.29
  661.4 29.4 copy.457
  690.7 8.5 all-to-all-start.3
  703.6 649.9 %all-gather = bf16[128,16,8]{1,2,0:T(8,128)(2,1)S(1)} all-gather(bf16[1,16,8]{1,2,0:T(8,128)(2,1)S(1)} %bitcast.294), channel_id=1, replica_groups=mesh['seq'=64,'expert'=2] {'seq','expert'}, dimensions={0}, use_global_device_ids=true | all-gather | bytes 33024 | tf_op jit(solution)/shard_map/all_gather | solution.py:171
  1356.8 10.9 bitcast_reduce_fusion.3
  1383.2 154.0 %all_to_all.88 = bf16[128,18,2048]{2,1,0:T(8,128)(2,1)} all-to-all(bf16[128,18,2048]{2,1,0:T(8,128)(2,1)} %bitcast.278), channel_id=1, replica_groups=mesh['seq'=64,'expert'=2] {'seq','expert'}, dimensions={0} | all-to-all | bytes 18874368 | tf_op jit(solution)/shard_map/all_to_all | solution.py:275
  1537.2 14.1 reshape.762
  1551.3 7.6 fusion.120
  1565.7 9.1 fusion.121
  1574.8 19.7 reshape.763
  1594.5 7.8 all-to-all-start.5
  1603.6 652.9 %all-gather.1 = bf16[128,16,8]{1,2,0:T(8,128)(2,1)S(1)} all-gather(bf16[1,16,8]{1,2,0:T(8,128)(2,1)S(1)} %bitcast.295), channel_id=1, replica_groups=mesh['seq'=64,'expert'=2] {'seq','expert'}, dimensions={0}, use_global_device_ids=true | all-gather | bytes 33024 | tf_op jit(solution)/shard_map/all_gather | solution.py:173
  2263.7 10.9 bitcast_reduce_fusion.2
  2286.7 7.2 broadcast_in_dim.105
  2293.9 154.1 %all_to_all.89 = bf16[128,18,2048]{2,1,0:T(8,128)(2,1)} all-to-all(bf16[128,18,2048]{2,1,0:T(8,128)(2,1)} %bitcast.279), channel_id=1, replica_groups=mesh['seq'=64,'expert'=2] {'seq','expert'}, dimensions={0} | all-to-all | bytes 18874368 | tf_op jit(solution)/shard_map/all_to_all | solution.py:303
  2448.0 14.1 reshape.767
  2462.1 11.8 multiply_convert_fusion.1
  2474.0 9.1 fusion.123
  2483.1 12.8 convolution_add_fusion
  2495.9 19.7 reshape.768
  2515.6 8.4 all-to-all-start.7
  2524.3 385.8 %all-to-all-done.7 = f32[128,18,2048]{2,1,0:T(8,128)} async-done(((f32[128,18,2048]{2,1,0:T(8,128)}), f32[128,18,2048]{2,1,0:T(8,128)}, u32[]{:S(2)}, u32[]{:S(2)}) %all-to-all-start.7) | async-done | bytes 18874400 | tf_op jit(solution)/shard_map/all_to_all | solution.py:153
  2910.1 9.8 bitcast_reduce_fusion.1
  2938.8 20.4 all-to-all-start.8
  2959.3 183.4 %all-to-all-done.8 = bf16[128,18,2048]{2,1,0:T(8,128)(2,1)} async-done(((bf16[128,18,2048]{2,1,0:T(8,128)(2,1)}), bf16[128,18,2048]{2,1,0:T(8,128)(2,1)}, u32[]{:S(2)}, u32[]{:S(2)}) %all-to-all-start.8) | async-done | bytes 9437216 | tf_op jit(solution)/shard_map/all_to_all | solution.py:343
  3142.6 14.1 reshape.772
  3156.7 7.1 convolution_convert_fusion.1
  3163.8 80.3 %while.30 = (s32[]{:T(128)}, f32[8,288,1,128]{3,1,2,0:T(8,128)}, bf16[8,1024,1,128]{3,1,0,2:T(8,128)(2,1)}, bf16[8,1024,1,128]{3,1,0,2:T(8,128)(2,1)}, bf16[8,10...) while((s32[]{:T(128)}, f32[8,288,1,128]{3,1,2,0:T(8,128)}, ...), condition=%wide.region_35.39_spmd.clone, body=%wide.region_33.38_spmd.clone.sunk | while | flops 380743392 | bytes 12719733 | solution.py:380
  3244.1 37.2 all_to_all.90
  3295.9 20.4 all-to-all-done.11
  3318.3 13.5 fusion.124
  3342.6 29.0 copy.498
  3377.9 756.3 %reduce-scatter.12.cloned.1.call-done = f32[16,8]{1,0:T(8,128)} async-done(((f32[2048,8]{1,0:T(8,128)}), f32[16,8]{1,0:T(8,128)}) %reduce-scatter.12.cloned.1.call-update) | async-done | bytes 528
  4135.6 9.4 fusion.128
  4145.0 8.9 fusion.129
  4159.1 7.9 all_gather.35
  4167.0 607.9 %reduce-scatter.10.cloned.1.call-done = f32[16,8]{1,0:T(8,128)} async-done(((f32[2048,8]{1,0:T(8,128)}), f32[16,8]{1,0:T(8,128)}) %reduce-scatter.10.cloned.1.call-update) | async-done | bytes 528
  4782.4 7.5 fusion.72
  4789.9 10.1 bitcast_reduce_fusion
  4803.9 11.1 convolution_add_fusion.2
  4815.7 736.8 %all-reduce.4 = (f32[2048]{0:T(1024)S(1)}, f32[2048]{0:T(1024)S(1)}) all-reduce(f32[2048]{0:T(1024)S(1)} %get-tuple-element.319, f32[2048]{0:T(1024)S(1)} %copy-done.66), channel_id=2, replica_groups=mesh['seq'=64,'expert'=2] {'seq','expert'}, use_global_device_ids=true, to_apply=%region_45.49.clone | all-reduce | flops 4096 | bytes 32768
  5553.9 9.6 all_gather.36
  (552 shorter events, 294.6 us)
Async XLA Ops:
  7.2 1558.5 %copy-start = (bf16[352,2048]{1,0:T(8,128)(2,1)S(1)}, bf16[352,2048]{1,0:T(8,128)(2,1)}, u32[]{:S(2)}) copy-start(bf16[352,2048]{1,0:T(8,128)(2,1)} %param.35) | copy-start | bytes 4325380
  7.2 454.7 %all-gather.4.cloned.1.call-start = ((), (), s32[]{:S(2)}) async-start(), calls=%async_computation.15 | async-start | bytes 16908288 | tf_op jit(solution)/shard_map/all_gather | solution.py:170
  12.6 1343.0 %copy-start.60 = (s32[64,2]{0,1:T(2,128)}, s32[64,2]{0,1:T(2,128)S(1)}, u32[]{:S(2)}) copy-start(s32[64,2]{0,1:T(2,128)S(1)} %get-tuple-element.384) | copy-start | bytes 1540
  13.5 72.5 %copy-start.55 = (s32[8,18]{0,1:T(8,128)}, s32[8,18]{0,1:T(8,128)S(1)}, u32[]{:S(2)}) copy-start(s32[8,18]{0,1:T(8,128)S(1)} %get-tuple-element.326) | copy-start | bytes 1732
  13.5 74.9 %copy-start.53 = (s32[8,18]{0,1:T(8,128)}, s32[8,18]{0,1:T(8,128)S(1)}, u32[]{:S(2)}) copy-start(s32[8,18]{0,1:T(8,128)S(1)} %get-tuple-element.325) | copy-start | bytes 1732
  87.2 1266.7 %copy-start.6 = (bf16[64,2048]{1,0:T(8,128)(2,1)}, bf16[64,2048]{1,0:T(8,128)(2,1)S(1)}, u32[]{:S(2)}) copy-start(bf16[64,2048]{1,0:T(8,128)(2,1)S(1)} %fusion.80) | copy-start | bytes 786436
  94.7 376.9 %all-to-all-start.1 = ((bf16[128,18,2048]{2,1,0:T(8,128)(2,1)}), bf16[128,18,2048]{2,1,0:T(8,128)(2,1)}, u32[]{:S(2)}, u32[]{:S(2)}) async-start(bf16[128,18,2048]{2,1,0:T(8,128)(2,1)} %bitcast.276), calls=%async_computation.1 | async-start | bytes 25165824 | tf_op jit(solution)/shard_map/all_to_all | solution.py:215
  100.3 519.2 %copy-start.75 = (f32[64]{0:T(128)}, f32[64]{0:T(128)S(1)}, u32[]{:S(2)}) copy-start(f32[64]{0:T(128)S(1)} %multiply_exponential_fusion) | copy-start | bytes 772
  100.5 370.5 %copy-start.43 = (f32[64,64]{1,0:T(8,128)}, f32[64,64]{1,0:T(8,128)S(1)}, u32[]{:S(2)}) copy-start(f32[64,64]{1,0:T(8,128)S(1)} %get-tuple-element.411) | copy-start | bytes 49156
  100.5 370.5 %copy-start.45 = (f32[64,64]{1,0:T(8,128)}, f32[64,64]{1,0:T(8,128)S(1)}, u32[]{:S(2)}) copy-start(f32[64,64]{1,0:T(8,128)S(1)} %get-tuple-element.412) | copy-start | bytes 49156
  473.5 13.1 copy-start.77
  473.5 116.1 %all-to-all-start.2 = ((bf16[64,128,128]{2,0,1:T(8,128)(2,1)}), bf16[64,128,128]{2,0,1:T(8,128)(2,1)}, u32[]{:S(2)}, u32[]{:S(2)}) async-start(bf16[64,128,128]{2,0,1:T(8,128)(2,1)} %bitcast.283), calls=%async_computation.2 | async-start | bytes 4194304 | tf_op jit(solution)/shard_map/all_to_all | solution.py:199
  591.4 35.7 all-to-all-start
  598.5 21.1 copy-start.51
  598.5 14.1 copy-start.28
  690.7 666.1 %all-to-all-start.3 = ((f32[128,18,2048]{2,1,0:T(8,128)}), f32[128,18,2048]{2,1,0:T(8,128)}, u32[]{:S(2)}, u32[]{:S(2)}) async-start(f32[128,18,2048]{2,1,0:T(8,128)} %copy.457), calls=%async_computation.3 | async-start | bytes 50331648 | tf_op jit(solution)/shard_map/all_to_all | solution.py:153
  1356.7 18.2 copy-start.49
  1356.8 12.5 copy-start.33
  1375.8 886.1 %copy-start.8 = (bf16[64,2048]{1,0:T(8,128)(2,1)}, bf16[64,2048]{1,0:T(8,128)(2,1)S(1)}, u32[]{:S(2)}) copy-start(bf16[64,2048]{1,0:T(8,128)(2,1)S(1)} %multiply_convert_fusion.6) | copy-start | bytes 786436
  1594.5 669.2 %all-to-all-start.5 = ((f32[128,18,2048]{2,1,0:T(8,128)}), f32[128,18,2048]{2,1,0:T(8,128)}, u32[]{:S(2)}, u32[]{:S(2)}) async-start(f32[128,18,2048]{2,1,0:T(8,128)} %reshape.763), calls=%async_computation.5 | async-start | bytes 50331648 | tf_op jit(solution)/shard_map/all_to_all | solution.py:153
  1602.3 654.7 %copy-start.63 = (s32[8,18,1]{0,1,2:T(8,128)S(1)}, s32[8,18,1]{0,1,2:T(8,128)}, u32[]{:S(2)}) copy-start(s32[8,18,1]{0,1,2:T(8,128)} %get-tuple-element.409) | copy-start | bytes 1732
  1602.4 654.9 %copy-start.37 = (bf16[128,2048]{1,0:T(8,128)(2,1)S(1)}, bf16[128,2048]{1,0:T(8,128)(2,1)}, u32[]{:S(2)}) copy-start(bf16[128,2048]{1,0:T(8,128)(2,1)} %param.39) | copy-start | bytes 1572868
  2462.1 11.9 copy-start.30
  2473.9 9.2 copy-start.24
  2473.9 9.2 copy-start.19
  2474.0 9.2 copy-start.32
  2515.6 394.5 %all-to-all-start.7 = ((f32[128,18,2048]{2,1,0:T(8,128)}), f32[128,18,2048]{2,1,0:T(8,128)}, u32[]{:S(2)}, u32[]{:S(2)}) async-start(f32[128,18,2048]{2,1,0:T(8,128)} %reshape.768), calls=%async_computation.7 | async-start | bytes 50331648 | tf_op jit(solution)/shard_map/all_to_all | solution.py:153
  2938.8 203.8 %all-to-all-start.8 = ((bf16[128,18,2048]{2,1,0:T(8,128)(2,1)}), bf16[128,18,2048]{2,1,0:T(8,128)(2,1)}, u32[]{:S(2)}, u32[]{:S(2)}) async-start(bf16[128,18,2048]{2,1,0:T(8,128)(2,1)} %bitcast.277), calls=%async_computation.8 | async-start | bytes 25165824 | tf_op jit(solution)/shard_map/all_to_all | solution.py:343
  2959.2 197.4 %copy-start.36 = (bf16[128,2048]{1,0:T(8,128)(2,1)S(1)}, bf16[128,2048]{1,0:T(8,128)(2,1)}, u32[]{:S(2)}) copy-start(bf16[128,2048]{1,0:T(8,128)(2,1)} %param.30) | copy-start | bytes 1572868
  3281.3 34.9 all-to-all-start.11
  3286.9 847.3 %reduce-scatter.12.cloned.1.call-start = ((), (), s32[]{:S(2)}) async-start(), calls=%async_computation.18 | async-start | bytes 1056768
  3288.6 1486.3 %reduce-scatter.10.cloned.1.call-start = ((), (), s32[]{:S(2)}) async-start(), calls=%async_computation.17 | async-start | bytes 1056768
  3290.4 2273.1 %reduce-scatter.8.cloned.1.call-start = ((), (), s32[]{:S(2)}) async-start(), calls=%async_computation.16 | async-start | bytes 33816576 | tf_op jit(solution)/shard_map/reduce_scatter | solution.py:442
  3371.6 1418.3 %all-to-all-start.9 = ((f32[128,18,2048]{2,1,0:T(8,128)}), f32[128,18,2048]{2,1,0:T(8,128)}, u32[]{:S(2)}, u32[]{:S(2)}) async-start(f32[128,18,2048]{2,1,0:T(8,128)} %copy.498), calls=%async_computation.9 | async-start | bytes 50331648 | tf_op jit(solution)/shard_map/all_to_all | solution.py:153
  4135.6 9.4 copy-start.25
  4135.6 18.3 slice-start
  4135.6 18.3 slice-start.1
  4145.0 8.9 slice-start.2
  4145.0 8.9 copy-start.20
  4154.0 622.3 %copy-start.18 = (bf16[8,288,1,128]{3,1,2,0:T(8,128)(2,1)S(1)}, bf16[8,288,1,128]{3,1,2,0:T(8,128)(2,1)}, u32[]{:S(2)}) copy-start(bf16[8,288,1,128]{3,1,2,0:T(8,128)(2,1)} %copy-done.17) | copy-start | bytes 1769476
  4803.8 11.2 copy-start.22
  4803.8 11.2 copy-start.40
  4803.8 11.2 copy-start.48
  4803.8 11.2 copy-start.72
  4803.8 11.8 copy-start.66
  4803.9 749.8 %copy-start.5 = (f32[64,2048]{1,0:T(8,128)S(1)}, f32[64,2048]{1,0:T(8,128)}, u32[]{:S(2)}) copy-start(f32[64,2048]{1,0:T(8,128)} %copy-done.4) | copy-start | bytes 1572868
  4815.0 748.4 %copy-start.26 = (bf16[128,2048]{1,0:T(8,128)(2,1)S(1)}, bf16[128,2048]{1,0:T(8,128)(2,1)}, u32[]{:S(2)}) copy-start(bf16[128,2048]{1,0:T(8,128)(2,1)} %all_gather.35) | copy-start | bytes 1572868
  5553.7 11.4 copy-start.1
  (49 other events, 131.5 us)
Sparse Core Ops, SparseCore 0:
  9.7 452.1 all-gather.3
  3290.7 843.5 reduce-scatter.11
  4137.3 637.6 reduce-scatter.9
  4777.8 736.5 reduce-scatter.7
where the time goes:
time: 5590 us; the launch traced here: 5570 us
  blocking collectives  2570 us (46%)
  waiting for transfers between devices  2320 us (42%)
  local copies, waits for them, and re-layouts  268 us (5%)
  matrix products  232 us (4%)
  other arithmetic  87.6 us (2%)
  starting transfers between devices  82.1 us (1%)
    unnamed x6, waiting for transfers between devices  1360 us
    unnamed x2, blocking collectives  806 us
    all_gather x1, blocking collectives, dense_weights(): lax.all_gather(mlp_router, ('seq', 'expert'), axis=0, tiled=True)  653 us
    all_gather x1, blocking collectives, dense_weights(): lax.all_gather(attn_router, ('seq', 'expert'), axis=0, tiled=True)  650 us
    all_to_all x4, waiting for transfers between devices, slot_sums(): lax.all_to_all(partial_value, ('seq', 'expert'), split_axis=0, concat_axi...  386 us
    all_gather x1, waiting for transfers between devices, dense_weights(): lax.all_gather(kv_weight, ('seq', 'expert'), axis=0, tiled=True)  361 us
    all_to_all x1, waiting for transfers between devices, shards(): lax.all_to_all(fan_out(attn_slot_grad, group_size), ('seq', 'expert'), sp...  183 us
    all_to_all x1, blocking collectives, shards(): lax.all_to_all(fan_out(mlp_slot_grad, group_size), ('seq', 'expert'), spl...  154 us
  transfers between devices with their start and end apart: 13, of which 7 were waited for; matrix products, arithmetic and copies ran while one was open for 4% of the time, Pallas kernels for 0%

commit v1 on v0

--- a/solution.py
+++ b/solution.py
@@ -164,17 +164,30 @@
     own_rank = lax.dynamic_slice_in_dim(priority[0], start_row, own_rows, 0)
     token_order = jnp.arange(own_rows, dtype=jnp.int32)
 
-    def dense_weights():
-        return (
-            lax.all_gather(attn_gain, ("seq", "expert"), axis=0, tiled=True),
-            lax.all_gather(kv_weight, ("seq", "expert"), axis=0, tiled=True),
-            lax.all_gather(attn_router, ("seq", "expert"), axis=0, tiled=True),
-            lax.all_gather(mlp_gain, ("seq", "expert"), axis=0, tiled=True),
-            lax.all_gather(mlp_router, ("seq", "expert"), axis=0, tiled=True),
-        )
-
-    gain_one, kv_full, router_one, gain_two, router_two = dense_weights()
-    routes_all = lax.all_gather(attn_experts, "seq", axis=0, tiled=True)
+    kv_rows, kv_width = kv_weight.shape
+    id_cols = own_rows * TOPK // kv_rows
+    extras = jnp.concatenate(
+        [
+            attn_gain[:, None],
+            mlp_gain[:, None],
+            attn_router,
+            mlp_router,
+            own_attn.reshape(kv_rows, id_cols).astype(jnp.bfloat16),
+        ],
+        axis=1,
+    )
+    extra_cols = extras.shape[1]
+    extra_pad = -(-extra_cols // 128) * 128
+    packed = jnp.concatenate(
+        [kv_weight, jnp.pad(extras, ((0, 0), (0, extra_pad - extra_cols)))], axis=1
+    )
+    gathered = lax.all_gather(packed, ("seq", "expert"), axis=0, tiled=True)
+    kv_full = gathered[:, :kv_width]
+    gain_one = gathered[:, kv_width]
+    gain_two = gathered[:, kv_width + 1]
+    router_one = gathered[:, kv_width + 2 : kv_width + 2 + EXPERTS]
+    router_two = gathered[:, kv_width + 2 + EXPERTS : kv_width + 2 + 2 * EXPERTS]
+    routes_all = gathered[:, kv_width + 2 + 2 * EXPERTS : kv_width + extra_cols].astype(jnp.int32)
     inverse_one = lax.rsqrt(jnp.mean(own_input * own_input, axis=-1, keepdims=True) + epsilon)
     normed_one = own_input * inverse_one
     attn_input = (normed_one * gain_one.astype(jnp.float32)).astype(jnp.bfloat16)
@@ -293,7 +306,6 @@
     own_output = hidden_state + jnp.sum(
         mlp_picked * (mlp_gates * mlp_pair_kept)[:, :, None], axis=1
     )
-    gain_one, kv_full, router_one, gain_two, router_two = dense_weights()
     mlp_gate_grad = jnp.sum(mlp_picked * own_cotangent[:, None, :], axis=-1) * mlp_pair_kept
     mlp_logit_grad = gates_back(mlp_gates, mlp_gate_grad, own_mlp)
     mlp_slot_grad = (
@@ -437,13 +449,22 @@
         attn_input_grad, gain_one.astype(jnp.float32), normed_one, inverse_one
     )
     input_grad = input_grad + hidden_grad
-    gain_one_grad, kv_grad, attn_router_grad, gain_two_grad, mlp_router_grad = (
-        lax.psum_scatter(gain_one_own, ("seq", "expert"), scatter_dimension=0, tiled=True),
-        lax.psum_scatter(kv_own_weight, ("seq", "expert"), scatter_dimension=0, tiled=True),
-        lax.psum_scatter(attn_router_own, ("seq", "expert"), scatter_dimension=0, tiled=True),
-        lax.psum_scatter(gain_two_own, ("seq", "expert"), scatter_dimension=0, tiled=True),
-        lax.psum_scatter(mlp_router_own, ("seq", "expert"), scatter_dimension=0, tiled=True),
-    )
+    grad_extras = jnp.concatenate(
+        [gain_one_own[:, None], gain_two_own[:, None], attn_router_own, mlp_router_own], axis=1
+    )
+    packed_grad = jnp.concatenate(
+        [
+            kv_own_weight,
+            jnp.pad(grad_extras, ((0, 0), (0, extra_pad - grad_extras.shape[1]))),
+        ],
+        axis=1,
+    )
+    scattered = lax.psum_scatter(packed_grad, ("seq", "expert"), scatter_dimension=0, tiled=True)
+    kv_grad = scattered[:, :kv_width]
+    gain_one_grad = scattered[:, kv_width]
+    gain_two_grad = scattered[:, kv_width + 1]
+    attn_router_grad = scattered[:, kv_width + 2 : kv_width + 2 + EXPERTS]
+    mlp_router_grad = scattered[:, kv_width + 2 + EXPERTS : kv_width + 2 + 2 * EXPERTS]
     mixed_full, input_full = (
         lax.all_gather(own_output.astype(jnp.bfloat16), "expert", axis=0, tiled=True),
         lax.all_gather(input_grad.astype(jnp.bfloat16), "expert", axis=0, tiled=True),

time: 5590 us -> 4080 us (0.73)
  blocking collectives: 2570 us -> 401 us
  waiting for transfers between devices: 2320 us -> 2950 us
    all_gather x3 -> x0, blocking collectives: 1400 us -> none  [the longest x1 653 us: dense_weights(): lax.all_gather(mlp_router, ('seq', 'expert'), axis=0, tiled=True)]
    unnamed x6 -> x2, waiting for transfers between devices: 1360 us -> 0.03 us
    all_to_all x4, waiting for transfers between devices: 386 us -> 1530 us  [slot_sums(): lax.all_to_all(partial_value, ('seq', 'expert'), split_axis=0, concat_axi...]
    unnamed x2 -> x0, blocking collectives: 806 us -> none
    reduce_scatter x1, waiting for transfers between devices: 0.01 us -> 713 us  [shards(): lax.psum_scatter(packed_grad, ('seq', 'expert'), scatter_dimension=0, til...]
    all_to_all x1, waiting for transfers between devices: 0.01 us -> 168 us  [shards(): lax.all_to_all(fan_out(pick_slots(attn_input, attn_token, attn_valid), gr...]
  transfers between devices with their start and end apart: 13 -> 11, of which waited for: 7 -> 10; matrix products, arithmetic and copies ran while one was open for 4% -> 4% of each run, Pallas kernels for 0% -> 0%
where the time goes in v1:
time: 4080 us; the launch traced here: 4060 us
  waiting for transfers between devices  2950 us (72%)
  blocking collectives  401 us (10%)
  local copies, waits for them, and re-layouts  282 us (7%)
  matrix products  212 us (5%)
  other arithmetic  114 us (3%)
  starting transfers between devices  84.3 us (2%)
    all_to_all x4, waiting for transfers between devices, slot_sums(): lax.all_to_all(partial_value, ('seq', 'expert'), split_axis=0, concat_axi...  1530 us
    reduce_scatter x1, waiting for transfers between devices, shards(): lax.psum_scatter(packed_grad, ('seq', 'expert'), scatter_dimension=0, til...  713 us
    all_gather x1, waiting for transfers between devices, shards(): gathered = lax.all_gather(packed, ('seq', 'expert'), axis=0, tiled=True)  332 us
    all_to_all x1, waiting for transfers between devices, shards(): lax.all_to_all(fan_out(attn_slot_grad, group_size), ('seq', 'expert'), sp...  183 us
    all_to_all x1, waiting for transfers between devices, shards(): lax.all_to_all(fan_out(pick_slots(attn_input, attn_token, attn_valid), gr...  168 us
    all_to_all x1, blocking collectives, shards(): lax.all_to_all(fan_out(pick_slots(mlp_input, mlp_token, mlp_valid), group...  168 us
    all_to_all x1, blocking collectives, shards(): lax.all_to_all(fan_out(mlp_slot_grad, group_size), ('seq', 'expert'), spl...  165 us
  transfers between devices with their start and end apart: 11, of which 10 were waited for; matrix products, arithmetic and copies ran while one was open for 4% of the time, Pallas kernels for 0%

profile of v1, /device:TPU:1, one launch (start us, length us, event | category | flops | bytes accessed | tf_op | source)
XLA Modules:
  0.0 4061.2 jit_solution(4993596616049152835)
XLA Ops:
  18.2 332.5 %all-gather.2.cloned.1.call-done = bf16[2048,4224]{1,0:T(8,128)(2,1)} async-done(((bf16[16,4224]{1,0:T(8,128)(2,1)}), bf16[2048,4224]{1,0:T(8,128)(2,1)}) %all-gather.2.cloned.1.call-update) | async-done | bytes 17301520 | tf_op jit(solution)/shard_map/all_gather | solution.py:184
  352.6 7.5 fusion.53
  363.5 9.0 all-to-all-start.2
  376.9 24.9 all-to-all-done.2
  429.3 168.0 %all-to-all-done.1 = bf16[128,18,2048]{2,1,0:T(8,128)(2,1)} async-done(((bf16[128,18,2048]{2,1,0:T(8,128)(2,1)}), bf16[128,18,2048]{2,1,0:T(8,128)(2,1)}, u32[]{:S(2)}, u32[]{:S(2)}) %all-to-all-start.1) | async-done | bytes 9437216 | tf_op jit(solution)/shard_map/all_to_all | solution.py:228
  599.1 7.9 all-to-all-start
  607.4 14.2 reshape.768
  621.6 6.9 convolution_bitcast_fusion.1
  636.4 29.9 while.29
  671.4 29.2 copy.506
  700.6 8.6 all-to-all-start.3
  714.3 391.4 %all-to-all-done.3 = f32[128,18,2048]{2,1,0:T(8,128)} async-done(((f32[128,18,2048]{2,1,0:T(8,128)}), f32[128,18,2048]{2,1,0:T(8,128)}, u32[]{:S(2)}, u32[]{:S(2)}) %all-to-all-start.3) | async-done | bytes 18874400 | tf_op jit(solution)/shard_map/all_to_all | solution.py:153
  1105.7 10.9 bitcast_reduce_fusion.3
  1132.2 167.6 %all_to_all.88 = bf16[128,18,2048]{2,1,0:T(8,128)(2,1)} all-to-all(bf16[128,18,2048]{2,1,0:T(8,128)(2,1)} %bitcast.270), channel_id=1, replica_groups=mesh['seq'=64,'expert'=2] {'seq','expert'}, dimensions={0} | all-to-all | bytes 18874368 | tf_op jit(solution)/shard_map/all_to_all | solution.py:288
  1299.9 14.2 reshape.776
  1314.0 7.6 fusion.134
  1328.4 9.0 fusion.135
  1337.4 19.8 reshape.777
  1357.2 8.2 all-to-all-start.5
  1374.8 376.6 %all-to-all-done.5 = f32[128,18,2048]{2,1,0:T(8,128)} async-done(((f32[128,18,2048]{2,1,0:T(8,128)}), f32[128,18,2048]{2,1,0:T(8,128)}, u32[]{:S(2)}, u32[]{:S(2)}) %all-to-all-start.5) | async-done | bytes 18874400 | tf_op jit(solution)/shard_map/all_to_all | solution.py:153
  1751.4 10.9 bitcast_reduce_fusion.2
  1774.4 7.4 broadcast_in_dim.115
  1781.7 164.6 %all_to_all.89 = bf16[128,18,2048]{2,1,0:T(8,128)(2,1)} all-to-all(bf16[128,18,2048]{2,1,0:T(8,128)(2,1)} %bitcast.271), channel_id=1, replica_groups=mesh['seq'=64,'expert'=2] {'seq','expert'}, dimensions={0} | all-to-all | bytes 18874368 | tf_op jit(solution)/shard_map/all_to_all | solution.py:315
  1946.3 14.1 reshape.781
  1960.4 11.9 multiply_convert_fusion.1
  1972.3 9.2 fusion.136
  1981.5 12.9 convolution_add_fusion
  1994.3 19.8 reshape.782
  2014.2 8.2 all-to-all-start.7
  2022.7 385.8 %all-to-all-done.7 = f32[128,18,2048]{2,1,0:T(8,128)} async-done(((f32[128,18,2048]{2,1,0:T(8,128)}), f32[128,18,2048]{2,1,0:T(8,128)}, u32[]{:S(2)}, u32[]{:S(2)}) %all-to-all-start.7) | async-done | bytes 18874400 | tf_op jit(solution)/shard_map/all_to_all | solution.py:153
  2408.4 9.8 bitcast_reduce_fusion.1
  2438.8 20.7 all-to-all-start.8
  2459.5 183.4 %all-to-all-done.8 = bf16[128,18,2048]{2,1,0:T(8,128)(2,1)} async-done(((bf16[128,18,2048]{2,1,0:T(8,128)(2,1)}), bf16[128,18,2048]{2,1,0:T(8,128)(2,1)}, u32[]{:S(2)}, u32[]{:S(2)}) %all-to-all-start.8) | async-done | bytes 9437216 | tf_op jit(solution)/shard_map/all_to_all | solution.py:355
  2642.8 14.1 reshape.786
  2663.2 68.0 %while.30 = (s32[]{:T(128)}, f32[8,288,1,128]{3,1,2,0:T(8,128)S(1)}, bf16[8,1024,1,128]{3,1,0,2:T(8,128)(2,1)}, bf16[8,1024,1,128]{3,1,0,2:T(8,128)(2,1)}, bf16[...) while((s32[]{:T(128)}, ...), condition=%wide.region_35.39_spmd.clone, body=%wide.region_33.38_spmd.clone.sunk | while | flops 380743392 | bytes 12718217 | solution.py:392
  2731.2 37.2 all_to_all.90
  2788.2 28.9 copy.545
  2817.2 10.2 all-to-all-start.9
  2838.1 13.2 fusion.137
  2851.3 372.6 %all-to-all-done.9 = f32[128,18,2048]{2,1,0:T(8,128)} async-done(((f32[128,18,2048]{2,1,0:T(8,128)}), f32[128,18,2048]{2,1,0:T(8,128)}, u32[]{:S(2)}, u32[]{:S(2)}) %all-to-all-start.9) | async-done | bytes 18874400 | tf_op jit(solution)/shard_map/all_to_all | solution.py:153
  3223.9 9.8 bitcast_reduce_fusion
  3237.7 8.8 fusion.56
  3249.0 23.0 select_maximum_fusion
  3272.1 9.4 fusion.141
  3281.5 8.9 fusion.143
  3295.6 16.1 all_gather.10
  3318.1 15.5 all_gather.11
  3333.6 713.4 %reduce-scatter.2.cloned.1.call-done = f32[16,4224]{1,0:T(8,128)} async-done(((f32[2048,4224]{1,0:T(8,128)}), f32[16,4224]{1,0:T(8,128)}) %reduce-scatter.2.cloned.1.call-update) | async-done | bytes 270352 | tf_op jit(solution)/shard_map/reduce_scatter | solution.py:462
  (579 shorter events, 290.7 us)
Async XLA Ops:
  7.2 1321.2 %copy-start = (bf16[352,2048]{1,0:T(8,128)(2,1)S(1)}, bf16[352,2048]{1,0:T(8,128)(2,1)}, u32[]{:S(2)}) copy-start(bf16[352,2048]{1,0:T(8,128)(2,1)} %param.35) | copy-start | bytes 4325380
  7.2 343.5 %all-gather.2.cloned.1.call-start = ((), (), s32[]{:S(2)}) async-start(), calls=%async_computation.13 | async-start | bytes 17436672 | tf_op jit(solution)/shard_map/all_gather | solution.py:184
  8.8 704.8 %copy-start.70 = (s32[64,2]{0,1:T(2,128)}, s32[64,2]{0,1:T(2,128)S(1)}, u32[]{:S(2)}) copy-start(s32[64,2]{0,1:T(2,128)S(1)} %get-tuple-element.492) | copy-start | bytes 1540
  17.9 610.6 %copy-start.85 = (f32[64]{0:T(128)}, f32[64]{0:T(128)S(1)}, u32[]{:S(2)}) copy-start(f32[64]{0:T(128)S(1)} %multiply_exponential_fusion) | copy-start | bytes 772
  18.0 342.1 %copy-start.83 = (f32[64]{0:T(128)}, f32[64]{0:T(128)S(1)}, u32[]{:S(2)}) copy-start(f32[64]{0:T(128)S(1)} %add_rsqrt_fusion.1) | copy-start | bytes 772
  18.2 342.9 %copy-start.50 = (f32[64,64]{1,0:T(8,128)}, f32[64,64]{1,0:T(8,128)S(1)}, u32[]{:S(2)}) copy-start(f32[64,64]{1,0:T(8,128)S(1)} %get-tuple-element.523) | copy-start | bytes 49156
  18.2 342.9 %copy-start.52 = (f32[64,64]{1,0:T(8,128)}, f32[64,64]{1,0:T(8,128)S(1)}, u32[]{:S(2)}) copy-start(f32[64,64]{1,0:T(8,128)S(1)} %get-tuple-element.524) | copy-start | bytes 49156
  352.5 771.3 %copy-start.57 = (f32[2048]{0:T(1024)}, f32[2048]{0:T(1024)S(1)}, u32[]{:S(2)}) copy-start(f32[2048]{0:T(1024)S(1)} %get-tuple-element.425) | copy-start | bytes 24580
  352.6 358.1 %copy-start.6 = (bf16[64,2048]{1,0:T(8,128)(2,1)}, bf16[64,2048]{1,0:T(8,128)(2,1)S(1)}, u32[]{:S(2)}) copy-start(bf16[64,2048]{1,0:T(8,128)(2,1)S(1)} %fusion.87) | copy-start | bytes 786436
  363.5 38.3 all-to-all-start.2
  408.0 189.3 %all-to-all-start.1 = ((bf16[128,18,2048]{2,1,0:T(8,128)(2,1)}), bf16[128,18,2048]{2,1,0:T(8,128)(2,1)}, u32[]{:S(2)}, u32[]{:S(2)}) async-start(bf16[128,18,2048]{2,1,0:T(8,128)(2,1)} %bitcast.268), calls=%async_computation.1 | async-start | bytes 25165824 | tf_op jit(solution)/shard_map/all_to_all | solution.py:228
  599.1 37.3 all-to-all-start
  607.4 21.1 copy-start.61
  607.4 14.2 copy-start.33
  700.6 405.1 %all-to-all-start.3 = ((f32[128,18,2048]{2,1,0:T(8,128)}), f32[128,18,2048]{2,1,0:T(8,128)}, u32[]{:S(2)}, u32[]{:S(2)}) async-start(f32[128,18,2048]{2,1,0:T(8,128)} %copy.506), calls=%async_computation.3 | async-start | bytes 50331648 | tf_op jit(solution)/shard_map/all_to_all | solution.py:153
  710.7 407.5 %copy-start.38 = (s32[1024]{0:T(1024)}, s32[1024]{0:T(1024)S(1)}, u32[]{:S(2)}) copy-start(s32[1024]{0:T(1024)S(1)} %pad_clamp_fusion.2) | copy-start | bytes 12292
  714.2 402.4 %copy-start.81 = (f32[64,2]{0,1:T(2,128)}, f32[64,2]{0,1:T(2,128)S(1)}, u32[]{:S(2)}) copy-start(f32[64,2]{0,1:T(2,128)S(1)} %get-tuple-element.488) | copy-start | bytes 1540
  1124.7 247.1 %copy-start.8 = (bf16[64,2048]{1,0:T(8,128)(2,1)}, bf16[64,2048]{1,0:T(8,128)(2,1)S(1)}, u32[]{:S(2)}) copy-start(bf16[64,2048]{1,0:T(8,128)(2,1)S(1)} %multiply_convert_fusion.6) | copy-start | bytes 786436
  1299.9 14.2 copy-start.34
  1357.2 394.2 %all-to-all-start.5 = ((f32[128,18,2048]{2,1,0:T(8,128)}), f32[128,18,2048]{2,1,0:T(8,128)}, u32[]{:S(2)}, u32[]{:S(2)}) async-start(f32[128,18,2048]{2,1,0:T(8,128)} %reshape.777), calls=%async_computation.5 | async-start | bytes 50331648 | tf_op jit(solution)/shard_map/all_to_all | solution.py:153
  1960.4 11.9 copy-start.35
  1972.2 9.2 copy-start.30
  1972.2 9.2 copy-start.23
  1972.2 9.2 copy-start.37
  2014.2 394.3 %all-to-all-start.7 = ((f32[128,18,2048]{2,1,0:T(8,128)}), f32[128,18,2048]{2,1,0:T(8,128)}, u32[]{:S(2)}, u32[]{:S(2)}) async-start(f32[128,18,2048]{2,1,0:T(8,128)} %reshape.782), calls=%async_computation.7 | async-start | bytes 50331648 | tf_op jit(solution)/shard_map/all_to_all | solution.py:153
  2438.8 204.1 %all-to-all-start.8 = ((bf16[128,18,2048]{2,1,0:T(8,128)(2,1)}), bf16[128,18,2048]{2,1,0:T(8,128)(2,1)}, u32[]{:S(2)}, u32[]{:S(2)}) async-start(bf16[128,18,2048]{2,1,0:T(8,128)(2,1)} %bitcast.269), calls=%async_computation.8 | async-start | bytes 25165824 | tf_op jit(solution)/shard_map/all_to_all | solution.py:355
  2459.5 197.4 %copy-start.47 = (bf16[128,2048]{1,0:T(8,128)(2,1)S(1)}, bf16[128,2048]{1,0:T(8,128)(2,1)}, u32[]{:S(2)}) copy-start(bf16[128,2048]{1,0:T(8,128)(2,1)} %param.30) | copy-start | bytes 1572868
  2731.2 37.2 copy-start.18
  2768.4 48.7 %all-to-all-start.10 = ((bf16[128,64,1,128]{3,1,2,0:T(8,128)(2,1)}), bf16[128,64,1,128]{3,1,2,0:T(8,128)(2,1)S(1)}, u32[]{:S(2)}, u32[]{:S(2)}) async-start(bf16[128,64,1,128]{3,1,2,0:T(8,128)(2,1)} %bitcast.284), calls=%async_computation.10 | async-start | bytes 4194304 | tf_op jit(solution)/shard_map/all_to_all | solution.py:409
  2817.2 11.2 copy-start.9
  2817.2 11.4 copy-start.7
  2817.2 406.7 %all-to-all-start.9 = ((f32[128,18,2048]{2,1,0:T(8,128)}), f32[128,18,2048]{2,1,0:T(8,128)}, u32[]{:S(2)}, u32[]{:S(2)}) async-start(f32[128,18,2048]{2,1,0:T(8,128)} %copy.545), calls=%async_computation.9 | async-start | bytes 50331648 | tf_op jit(solution)/shard_map/all_to_all | solution.py:153
  2827.3 1219.7 %reduce-scatter.2.cloned.1.call-start = ((), (), s32[]{:S(2)}) async-start(), calls=%async_computation.14 | async-start | bytes 34873344 | tf_op jit(solution)/shard_map/reduce_scatter | solution.py:462
  3237.6 8.8 copy-start.27
  3237.7 10.9 copy-start.54
  3237.7 10.9 copy-start.78
  3272.0 9.4 copy-start.24
  3272.1 18.4 slice-start.6
  3272.1 18.4 slice-start.7
  3281.5 8.9 slice-start.8
  3281.5 8.9 copy-start.31
  3281.5 30.2 slice-start
  3281.5 30.2 slice-start.1
  3290.5 21.2 slice-start.2
  3290.5 21.2 copy-start.22
  3290.5 23.7 slice-start.3
  3290.5 23.7 slice-start.4
  3317.9 736.0 %copy-start.1 = (bf16[352,2048]{1,0:T(8,128)(2,1)S(1)}, bf16[352,2048]{1,0:T(8,128)(2,1)}, u32[]{:S(2)}) copy-start(bf16[352,2048]{1,0:T(8,128)(2,1)} %param.35) | copy-start | bytes 4325380
  (63 other events, 200.7 us)
Sparse Core Ops, SparseCore 0:
  17.9 332.7 all-gather.1
  3272.2 774.8 reduce-scatter.1

commit v2 on v1

--- a/solution.py
+++ b/solution.py
@@ -151,8 +151,12 @@
     def slot_sums(partial_value):
         return fold_group(
             lax.all_to_all(
-                partial_value, ("seq", "expert"), split_axis=0, concat_axis=0, tiled=True
-            ),
+                partial_value.astype(jnp.bfloat16),
+                ("seq", "expert"),
+                split_axis=0,
+                concat_axis=0,
+                tiled=True,
+            ).astype(jnp.float32),
             group_size,
         )
 

time: 4080 us -> 3160 us (0.77)
  waiting for transfers between devices: 2950 us -> 2100 us
    all_to_all x4, waiting for transfers between devices: 1530 us -> 691 us  [slot_sums(): lax.all_to_all(partial_value.astype(jnp.bfloat16), ('seq', 'expert'), spl...]
    convert_element_type x0 -> x4, local copies, waits for them, and re-layouts: none -> 69.7 us  [slot_sums(): partial_value.astype(jnp.bfloat16)]
  transfers between devices with their start and end apart: 11 -> 11, of which waited for: 10 -> 10; matrix products, arithmetic and copies ran while one was open for 4% -> 5% of each run, Pallas kernels for 0% -> 0%
where the time goes in v2:
time: 3160 us; the launch traced here: 3140 us
  waiting for transfers between devices  2100 us (66%)
  blocking collectives  373 us (12%)
  local copies, waits for them, and re-layouts  250 us (8%)
  matrix products  210 us (7%)
  other arithmetic  106 us (3%)
  starting transfers between devices  82.6 us (3%)
    reduce_scatter x1, waiting for transfers between devices, shards(): lax.psum_scatter(packed_grad, ('seq', 'expert'), scatter_dimension=0, til...  696 us
    all_to_all x4, waiting for transfers between devices, slot_sums(): lax.all_to_all(partial_value.astype(jnp.bfloat16), ('seq', 'expert'), spl...  691 us
    all_gather x1, waiting for transfers between devices, shards(): gathered = lax.all_gather(packed, ('seq', 'expert'), axis=0, tiled=True)  332 us
    all_to_all x1, waiting for transfers between devices, shards(): lax.all_to_all(fan_out(attn_slot_grad, group_size), ('seq', 'expert'), sp...  183 us
    all_to_all x1, waiting for transfers between devices, shards(): lax.all_to_all(fan_out(pick_slots(attn_input, attn_token, attn_valid), gr...  168 us
    all_to_all x1, blocking collectives, shards(): lax.all_to_all(fan_out(pick_slots(mlp_input, mlp_token, mlp_valid), group...  153 us
    all_to_all x1, blocking collectives, shards(): lax.all_to_all(fan_out(mlp_slot_grad, group_size), ('seq', 'expert'), spl...  152 us
    convert_element_type x4, local copies, waits for them, and re-layouts, slot_sums(): partial_value.astype(jnp.bfloat16)  69.7 us
  transfers between devices with their start and end apart: 11, of which 10 were waited for; matrix products, arithmetic and copies ran while one was open for 5% of the time, Pallas kernels for 0%

profile of v2, /device:TPU:1, one launch (start us, length us, event | category | flops | bytes accessed | tf_op | source)
XLA Modules:
  0.0 3136.1 jit_solution(5325084763687967587)
XLA Ops:
  18.2 332.5 %all-gather.2.cloned.1.call-done = bf16[2048,4224]{1,0:T(8,128)(2,1)} async-done(((bf16[16,4224]{1,0:T(8,128)(2,1)}), bf16[2048,4224]{1,0:T(8,128)(2,1)}) %all-gather.2.cloned.1.call-update) | async-done | bytes 17301520 | tf_op jit(solution)/shard_map/all_gather | solution.py:188
  352.6 7.5 fusion.53
  363.5 9.0 all-to-all-start.2
  376.9 24.9 all-to-all-done.2
  407.9 16.7 all-to-all-start.1
  440.0 168.0 %all-to-all-done.1 = bf16[128,18,2048]{2,1,0:T(8,128)(2,1)} async-done(((bf16[128,18,2048]{2,1,0:T(8,128)(2,1)}), bf16[128,18,2048]{2,1,0:T(8,128)(2,1)}, u32[]{:S(2)}, u32[]{:S(2)}) %all-to-all-start.1) | async-done | bytes 9437216 | tf_op jit(solution)/shard_map/all_to_all | solution.py:232
  609.8 7.9 all-to-all-start
  618.2 14.1 reshape.778
  647.1 29.9 while.29
  682.1 21.0 copy.506
  703.1 8.9 all-to-all-start.3
  717.2 178.2 %all-to-all-done.3 = bf16[128,18,2048]{2,1,0:T(8,128)(2,1)} async-done(((bf16[128,18,2048]{2,1,0:T(8,128)(2,1)}), bf16[128,18,2048]{2,1,0:T(8,128)(2,1)}, u32[]{:S(2)}, u32[]{:S(2)}) %all-to-all-start.3) | async-done | bytes 9437216 | tf_op jit(solution)/shard_map/all_to_all | solution.py:153
  895.4 8.8 convert_reduce_fusion.3
  919.8 152.6 %all_to_all.88 = bf16[128,18,2048]{2,1,0:T(8,128)(2,1)} all-to-all(bf16[128,18,2048]{2,1,0:T(8,128)(2,1)} %bitcast.274), channel_id=1, replica_groups=mesh['seq'=64,'expert'=2] {'seq','expert'}, dimensions={0} | all-to-all | bytes 18874368 | tf_op jit(solution)/shard_map/all_to_all | solution.py:292
  1072.3 14.2 reshape.787
  1086.6 7.8 fusion.132
  1100.0 7.5 convolution_convert_fusion.1
  1107.6 13.9 convert_element_type.302
  1121.4 8.1 all-to-all-start.5
  1136.7 176.3 %all-to-all-done.5 = bf16[128,18,2048]{2,1,0:T(8,128)(2,1)} async-done(((bf16[128,18,2048]{2,1,0:T(8,128)(2,1)}), bf16[128,18,2048]{2,1,0:T(8,128)(2,1)}, u32[]{:S(2)}, u32[]{:S(2)}) %all-to-all-start.5) | async-done | bytes 9437216 | tf_op jit(solution)/shard_map/all_to_all | solution.py:153
  1313.0 8.8 convert_reduce_fusion.2
  1333.8 7.2 broadcast_in_dim.115
  1341.0 152.4 %all_to_all.89 = bf16[128,18,2048]{2,1,0:T(8,128)(2,1)} all-to-all(bf16[128,18,2048]{2,1,0:T(8,128)(2,1)} %bitcast.275), channel_id=1, replica_groups=mesh['seq'=64,'expert'=2] {'seq','expert'}, dimensions={0} | all-to-all | bytes 18874368 | tf_op jit(solution)/shard_map/all_to_all | solution.py:319
  1493.4 14.1 reshape.792
  1507.5 11.9 multiply_convert_fusion.1
  1519.4 9.2 fusion.133
  1528.6 11.3 add_convert_fusion
  1539.9 13.9 convert_element_type.311
  1553.7 8.4 all-to-all-start.7
  1562.4 183.1 %all-to-all-done.7 = bf16[128,18,2048]{2,1,0:T(8,128)(2,1)} async-done(((bf16[128,18,2048]{2,1,0:T(8,128)(2,1)}), bf16[128,18,2048]{2,1,0:T(8,128)(2,1)}, u32[]{:S(2)}, u32[]{:S(2)}) %all-to-all-start.7) | async-done | bytes 9437216 | tf_op jit(solution)/shard_map/all_to_all | solution.py:153
  1745.5 7.6 convert_reduce_fusion.1
  1773.6 8.2 all-to-all-start.8
  1781.8 183.4 %all-to-all-done.8 = bf16[128,18,2048]{2,1,0:T(8,128)(2,1)} async-done(((bf16[128,18,2048]{2,1,0:T(8,128)(2,1)}), bf16[128,18,2048]{2,1,0:T(8,128)(2,1)}, u32[]{:S(2)}, u32[]{:S(2)}) %all-to-all-start.8) | async-done | bytes 9437216 | tf_op jit(solution)/shard_map/all_to_all | solution.py:359
  1965.2 14.1 reshape.797
  1985.6 68.0 %while.30 = (s32[]{:T(128)}, f32[8,288,1,128]{3,1,2,0:T(8,128)S(1)}, bf16[8,1024,1,128]{3,1,0,2:T(8,128)(2,1)}, bf16[8,1024,1,128]{3,1,0,2:T(8,128)(2,1)}, bf16[...) while((s32[]{:T(128)}, ...), condition=%wide.region_35.39_spmd.clone, body=%wide.region_33.38_spmd.clone.sunk | while | flops 380743392 | bytes 12718217 | solution.py:396
  2053.5 37.3 %all_to_all.90 = bf16[128,64,1,128]{3,1,2,0:T(8,128)(2,1)} all-to-all(bf16[128,64,1,128]{3,1,2,0:T(8,128)(2,1)} %bitcast.287), channel_id=1, replica_groups=mesh['seq'=64,'expert'=2] {'seq','expert'}, dimensions={0} | all-to-all | bytes 4194304 | tf_op jit(solution)/shard_map/all_to_all | solution.py:420
  2110.5 21.0 copy.545
  2131.5 10.2 all-to-all-start.9
  2152.3 13.5 fusion.134
  2165.8 153.8 %all-to-all-done.9 = bf16[128,18,2048]{2,1,0:T(8,128)(2,1)} async-done(((bf16[128,18,2048]{2,1,0:T(8,128)(2,1)}), bf16[128,18,2048]{2,1,0:T(8,128)(2,1)}, u32[]{:S(2)}, u32[]{:S(2)}) %all-to-all-start.9) | async-done | bytes 9437216 | tf_op jit(solution)/shard_map/all_to_all | solution.py:153
  2319.6 7.6 convert_reduce_fusion
  2331.2 8.8 fusion.56
  2342.5 22.8 select_maximum_fusion
  2365.4 9.4 fusion.138
  2374.8 9.0 fusion.140
  2389.0 15.3 all_gather.10
  2410.7 15.1 all_gather.11
  2425.8 696.4 %reduce-scatter.2.cloned.1.call-done = f32[16,4224]{1,0:T(8,128)} async-done(((f32[2048,4224]{1,0:T(8,128)}), f32[16,4224]{1,0:T(8,128)}) %reduce-scatter.2.cloned.1.call-update) | async-done | bytes 270352 | tf_op jit(solution)/shard_map/reduce_scatter | solution.py:466
  (575 shorter events, 288.0 us)
Async XLA Ops:
  7.2 1092.9 %copy-start = (bf16[352,2048]{1,0:T(8,128)(2,1)S(1)}, bf16[352,2048]{1,0:T(8,128)(2,1)}, u32[]{:S(2)}) copy-start(bf16[352,2048]{1,0:T(8,128)(2,1)} %param.35) | copy-start | bytes 4325380
  7.2 343.5 %all-gather.2.cloned.1.call-start = ((), (), s32[]{:S(2)}) async-start(), calls=%async_computation.13 | async-start | bytes 17436672 | tf_op jit(solution)/shard_map/all_gather | solution.py:188
  8.8 707.7 %copy-start.67 = (s32[64,2]{0,1:T(2,128)}, s32[64,2]{0,1:T(2,128)S(1)}, u32[]{:S(2)}) copy-start(s32[64,2]{0,1:T(2,128)S(1)} %get-tuple-element.492) | copy-start | bytes 1540
  17.9 621.3 %copy-start.82 = (f32[64]{0:T(128)}, f32[64]{0:T(128)S(1)}, u32[]{:S(2)}) copy-start(f32[64]{0:T(128)S(1)} %multiply_exponential_fusion) | copy-start | bytes 772
  18.0 342.1 %copy-start.80 = (f32[64]{0:T(128)}, f32[64]{0:T(128)S(1)}, u32[]{:S(2)}) copy-start(f32[64]{0:T(128)S(1)} %add_rsqrt_fusion.1) | copy-start | bytes 772
  18.2 342.9 %copy-start.47 = (f32[64,64]{1,0:T(8,128)}, f32[64,64]{1,0:T(8,128)S(1)}, u32[]{:S(2)}) copy-start(f32[64,64]{1,0:T(8,128)S(1)} %get-tuple-element.523) | copy-start | bytes 49156
  18.2 342.9 %copy-start.49 = (f32[64,64]{1,0:T(8,128)}, f32[64,64]{1,0:T(8,128)S(1)}, u32[]{:S(2)}) copy-start(f32[64,64]{1,0:T(8,128)S(1)} %get-tuple-element.524) | copy-start | bytes 49156
  352.5 559.0 %copy-start.54 = (f32[2048]{0:T(1024)}, f32[2048]{0:T(1024)S(1)}, u32[]{:S(2)}) copy-start(f32[2048]{0:T(1024)S(1)} %get-tuple-element.425) | copy-start | bytes 24580
  352.6 361.0 %copy-start.4 = (bf16[64,2048]{1,0:T(8,128)(2,1)}, bf16[64,2048]{1,0:T(8,128)(2,1)S(1)}, u32[]{:S(2)}) copy-start(bf16[64,2048]{1,0:T(8,128)(2,1)S(1)} %fusion.85) | copy-start | bytes 786436
  363.5 38.3 %all-to-all-start.2 = ((bf16[64,128,128]{2,0,1:T(8,128)(2,1)}), bf16[64,128,128]{2,0,1:T(8,128)(2,1)}, u32[]{:S(2)}, u32[]{:S(2)}) async-start(bf16[64,128,128]{2,0,1:T(8,128)(2,1)} %bitcast.280), calls=%async_computation.2 | async-start | bytes 4194304 | tf_op jit(solution)/shard_map/all_to_all | solution.py:216
  407.9 200.1 %all-to-all-start.1 = ((bf16[128,18,2048]{2,1,0:T(8,128)(2,1)}), bf16[128,18,2048]{2,1,0:T(8,128)(2,1)}, u32[]{:S(2)}, u32[]{:S(2)}) async-start(bf16[128,18,2048]{2,1,0:T(8,128)(2,1)} %bitcast.272), calls=%async_computation.1 | async-start | bytes 25165824 | tf_op jit(solution)/shard_map/all_to_all | solution.py:232
  609.8 37.3 %all-to-all-start = ((bf16[64,128,128]{2,0,1:T(8,128)(2,1)}), bf16[64,128,128]{2,0,1:T(8,128)(2,1)}, u32[]{:S(2)}, u32[]{:S(2)}) async-start(bf16[64,128,128]{2,0,1:T(8,128)(2,1)} %bitcast.281), calls=%async_computation | async-start | bytes 4194304 | tf_op jit(solution)/shard_map/all_to_all | solution.py:219
  618.1 21.1 copy-start.58
  618.2 14.1 copy-start.30
  703.1 192.3 %all-to-all-start.3 = ((bf16[128,18,2048]{2,1,0:T(8,128)(2,1)}), bf16[128,18,2048]{2,1,0:T(8,128)(2,1)}, u32[]{:S(2)}, u32[]{:S(2)}) async-start(bf16[128,18,2048]{2,1,0:T(8,128)(2,1)} %copy.506), calls=%async_computation.3 | async-start | bytes 25165824 | tf_op jit(solution)/shard_map/all_to_all | solution.py:153
  713.6 192.2 %copy-start.35 = (s32[1024]{0:T(1024)}, s32[1024]{0:T(1024)S(1)}, u32[]{:S(2)}) copy-start(s32[1024]{0:T(1024)S(1)} %pad_clamp_fusion.2) | copy-start | bytes 12292
  717.1 187.1 %copy-start.78 = (f32[64,2]{0,1:T(2,128)}, f32[64,2]{0,1:T(2,128)S(1)}, u32[]{:S(2)}) copy-start(f32[64,2]{0,1:T(2,128)S(1)} %get-tuple-element.488) | copy-start | bytes 1540
  912.3 221.4 %copy-start.6 = (bf16[64,2048]{1,0:T(8,128)(2,1)}, bf16[64,2048]{1,0:T(8,128)(2,1)S(1)}, u32[]{:S(2)}) copy-start(bf16[64,2048]{1,0:T(8,128)(2,1)S(1)} %multiply_convert_fusion.6) | copy-start | bytes 786436
  1072.3 14.2 copy-start.31
  1121.4 191.5 %all-to-all-start.5 = ((bf16[128,18,2048]{2,1,0:T(8,128)(2,1)}), bf16[128,18,2048]{2,1,0:T(8,128)(2,1)}, u32[]{:S(2)}, u32[]{:S(2)}) async-start(bf16[128,18,2048]{2,1,0:T(8,128)(2,1)} %convert_element_type.302), calls=%async_computation.5 | async-start | bytes 25165824 | tf_op jit(solution)/shard_map/all_to_all | solution.py:153
  1507.5 11.9 copy-start.32
  1519.4 9.2 copy-start.27
  1519.4 9.2 copy-start.21
  1519.4 9.2 copy-start.34
  1553.7 191.8 %all-to-all-start.7 = ((bf16[128,18,2048]{2,1,0:T(8,128)(2,1)}), bf16[128,18,2048]{2,1,0:T(8,128)(2,1)}, u32[]{:S(2)}, u32[]{:S(2)}) async-start(bf16[128,18,2048]{2,1,0:T(8,128)(2,1)} %convert_element_type.311), calls=%async_computation.7 | async-start | bytes 25165824 | tf_op jit(solution)/shard_map/all_to_all | solution.py:153
  1773.6 191.6 %all-to-all-start.8 = ((bf16[128,18,2048]{2,1,0:T(8,128)(2,1)}), bf16[128,18,2048]{2,1,0:T(8,128)(2,1)}, u32[]{:S(2)}, u32[]{:S(2)}) async-start(bf16[128,18,2048]{2,1,0:T(8,128)(2,1)} %bitcast.273), calls=%async_computation.8 | async-start | bytes 25165824 | tf_op jit(solution)/shard_map/all_to_all | solution.py:359
  1781.8 197.4 %copy-start.44 = (bf16[128,2048]{1,0:T(8,128)(2,1)S(1)}, bf16[128,2048]{1,0:T(8,128)(2,1)}, u32[]{:S(2)}) copy-start(bf16[128,2048]{1,0:T(8,128)(2,1)} %param.30) | copy-start | bytes 1572868
  2053.5 37.3 %copy-start.16 = (f32[8,288,1,128]{3,1,2,0:T(8,128)}, f32[8,288,1,128]{3,1,2,0:T(8,128)S(1)}, u32[]{:S(2)}) copy-start(f32[8,288,1,128]{3,1,2,0:T(8,128)S(1)} %get-tuple-element.119) | copy-start | bytes 3538948
  2090.8 40.7 %all-to-all-start.10 = ((bf16[128,64,1,128]{3,1,2,0:T(8,128)(2,1)}), bf16[128,64,1,128]{3,1,2,0:T(8,128)(2,1)S(1)}, u32[]{:S(2)}, u32[]{:S(2)}) async-start(bf16[128,64,1,128]{3,1,2,0:T(8,128)(2,1)} %bitcast.288), calls=%async_computation.10 | async-start | bytes 4194304 | tf_op jit(solution)/shard_map/all_to_all | solution.py:413
  2131.5 10.9 copy-start.7
  2131.5 11.2 copy-start.5
  2131.5 188.0 %all-to-all-start.9 = ((bf16[128,18,2048]{2,1,0:T(8,128)(2,1)}), bf16[128,18,2048]{2,1,0:T(8,128)(2,1)}, u32[]{:S(2)}, u32[]{:S(2)}) async-start(bf16[128,18,2048]{2,1,0:T(8,128)(2,1)} %copy.545), calls=%async_computation.9 | async-start | bytes 25165824 | tf_op jit(solution)/shard_map/all_to_all | solution.py:153
  2141.7 980.5 %reduce-scatter.2.cloned.1.call-start = ((), (), s32[]{:S(2)}) async-start(), calls=%async_computation.14 | async-start | bytes 34873344 | tf_op jit(solution)/shard_map/reduce_scatter | solution.py:466
  2331.2 8.8 copy-start.25
  2331.2 10.9 copy-start.51
  2331.2 10.9 copy-start.75
  2365.4 9.4 copy-start.22
  2365.4 18.4 slice-start.6
  2365.4 18.4 slice-start.7
  2374.8 9.0 slice-start.8
  2374.8 9.0 copy-start.28
  2374.8 29.5 slice-start
  2374.8 29.5 slice-start.1
  2383.8 20.5 slice-start.2
  2383.9 20.5 copy-start.20
  2383.9 22.9 slice-start.3
  2383.9 22.9 slice-start.4
  2410.5 718.6 %copy-start.1 = (bf16[352,2048]{1,0:T(8,128)(2,1)S(1)}, bf16[352,2048]{1,0:T(8,128)(2,1)}, u32[]{:S(2)}) copy-start(bf16[352,2048]{1,0:T(8,128)(2,1)} %param.35) | copy-start | bytes 4325380
  (61 other events, 198.5 us)
Sparse Core Ops, SparseCore 0:
  17.9 332.7 all-gather.1
  2365.5 756.6 reduce-scatter.1

commit v3 on v2

--- a/solution.py
+++ b/solution.py
@@ -5,6 +5,9 @@
 from jax import lax
 from jax.sharding import PartitionSpec as P
 
+ALL_AXES = ("grp", "sub", "expert")
+SEQ_AXES = ("grp", "sub")
+GROUP_AXES = ("sub", "expert")
 KV_HEADS = 16
 HEAD = 128
 EXPERTS = 8
@@ -129,9 +132,9 @@
     priority,
     cotangent,
 ):
-    devices = lax.axis_size(("seq", "expert"))
+    devices = lax.axis_size(ALL_AXES)
     halves = lax.axis_size("expert")
-    device_index = lax.axis_index(("seq", "expert"))
+    device_index = lax.axis_index(ALL_AXES)
     half_index = lax.axis_index("expert")
     seq_tokens, width = tokens.shape
     own_rows = seq_tokens // halves
@@ -152,7 +155,7 @@
         return fold_group(
             lax.all_to_all(
                 partial_value.astype(jnp.bfloat16),
-                ("seq", "expert"),
+                ALL_AXES,
                 split_axis=0,
                 concat_axis=0,
                 tiled=True,
@@ -185,7 +188,7 @@
     packed = jnp.concatenate(
         [kv_weight, jnp.pad(extras, ((0, 0), (0, extra_pad - extra_cols)))], axis=1
     )
-    gathered = lax.all_gather(packed, ("seq", "expert"), axis=0, tiled=True)
+    gathered = lax.all_gather(packed, ALL_AXES, axis=0, tiled=True)
     kv_full = gathered[:, :kv_width]
     gain_one = gathered[:, kv_width]
     gain_two = gathered[:, kv_width + 1]
@@ -196,6 +199,7 @@
     normed_one = own_input * inverse_one
     attn_input = (normed_one * gain_one.astype(jnp.float32)).astype(jnp.bfloat16)
     attn_logits = jnp.dot(attn_input, router_one, preferred_element_type=jnp.float32)
+    seq_input = lax.all_gather(attn_input, GROUP_AXES, axis=0, tiled=True)
     key_value = jnp.dot(attn_input, kv_full, preferred_element_type=jnp.float32)
     own_positions = (device_index * own_rows + token_order) % seq_length
     own_cos, own_sin = rope_tables(own_positions, HEAD)
@@ -214,10 +218,10 @@
 
     head_keys, head_values = (
         lax.all_to_all(
-            spread(own_keys), ("seq", "expert"), split_axis=1, concat_axis=0, tiled=True
+            spread(own_keys), ALL_AXES, split_axis=1, concat_axis=0, tiled=True
         ),
         lax.all_to_all(
-            spread(own_values), ("seq", "expert"), split_axis=1, concat_axis=0, tiled=True
+            spread(own_values), ALL_AXES, split_axis=1, concat_axis=0, tiled=True
         ),
     )
     seq_keys = head_keys.reshape(sequences, seq_length, local_heads, HEAD)
@@ -231,7 +235,7 @@
     dest_token = jnp.take(dest_tables, my_expert, axis=1)
     attn_rows = lax.all_to_all(
         fan_out(pick_slots(attn_input, attn_token, attn_valid), group_size),
-        ("seq", "expert"),
+        ALL_AXES,
         split_axis=0,
         concat_axis=0,
         tiled=True,
@@ -291,7 +295,7 @@
     mlp_logits = jnp.dot(mlp_input, router_two, preferred_element_type=jnp.float32)
     mlp_rows = lax.all_to_all(
         fan_out(pick_slots(mlp_input, mlp_token, mlp_valid), group_size),
-        ("seq", "expert"),
+        ALL_AXES,
         split_axis=0,
         concat_axis=0,
         tiled=True,
@@ -318,7 +322,7 @@
     ).astype(jnp.bfloat16)
     down_rows = lax.all_to_all(
         fan_out(mlp_slot_grad, group_size),
-        ("seq", "expert"),
+        ALL_AXES,
         split_axis=0,
         concat_axis=0,
         tiled=True,
@@ -358,7 +362,7 @@
     ).astype(jnp.bfloat16)
     out_rows = lax.all_to_all(
         fan_out(attn_slot_grad, group_size),
-        ("seq", "expert"),
+        ALL_AXES,
         split_axis=0,
         concat_axis=0,
         tiled=True,
@@ -412,14 +416,14 @@
     key_back, value_back = (
         lax.all_to_all(
             seq_key_grad.reshape(devices, own_rows, 1, head_cols).astype(jnp.bfloat16),
-            ("seq", "expert"),
+            ALL_AXES,
             split_axis=0,
             concat_axis=2,
             tiled=True,
         ).astype(jnp.float32),
         lax.all_to_all(
             seq_value_grad.reshape(devices, own_rows, 1, head_cols).astype(jnp.bfloat16),
-            ("seq", "expert"),
+            ALL_AXES,
             split_axis=0,
             concat_axis=2,
             tiled=True,
@@ -443,8 +447,16 @@
     attn_input_grad = attn_input_grad + jnp.dot(
         attn_logit_grad, router_one.astype(jnp.float32).T, precision=lax.Precision.HIGHEST
     )
-    kv_own_weight = jnp.einsum(
-        "rd,rc->dc", attn_input, kv_own_grad, preferred_element_type=jnp.float32
+    col_block = kv_width // group_size
+    kv_col_grad = lax.all_to_all(
+        kv_own_grad.reshape(own_rows, group_size, col_block),
+        GROUP_AXES,
+        split_axis=1,
+        concat_axis=0,
+        tiled=True,
+    ).reshape(own_rows * group_size, col_block)
+    kv_col_weight = jnp.einsum(
+        "rd,rc->dc", seq_input, kv_col_grad, preferred_element_type=jnp.float32
     )
     attn_router_own = jnp.dot(
         attn_input.astype(jnp.float32).T, attn_logit_grad, precision=lax.Precision.HIGHEST
@@ -458,17 +470,25 @@
     )
     packed_grad = jnp.concatenate(
         [
-            kv_own_weight,
+            kv_col_weight,
             jnp.pad(grad_extras, ((0, 0), (0, extra_pad - grad_extras.shape[1]))),
         ],
         axis=1,
     )
-    scattered = lax.psum_scatter(packed_grad, ("seq", "expert"), scatter_dimension=0, tiled=True)
-    kv_grad = scattered[:, :kv_width]
-    gain_one_grad = scattered[:, kv_width]
-    gain_two_grad = scattered[:, kv_width + 1]
-    attn_router_grad = scattered[:, kv_width + 2 : kv_width + 2 + EXPERTS]
-    mlp_router_grad = scattered[:, kv_width + 2 + EXPERTS : kv_width + 2 + 2 * EXPERTS]
+    group_sum = lax.psum_scatter(packed_grad, "grp", scatter_dimension=0, tiled=True)
+    dealt = lax.all_to_all(
+        group_sum.reshape(group_size, kv_rows, col_block + extra_pad),
+        GROUP_AXES,
+        split_axis=0,
+        concat_axis=0,
+        tiled=True,
+    )
+    kv_grad = jnp.moveaxis(dealt[:, :, :col_block], 0, 1).reshape(kv_rows, kv_width)
+    extra_grad = jnp.sum(dealt[:, :, col_block:], axis=0)
+    gain_one_grad = extra_grad[:, 0]
+    gain_two_grad = extra_grad[:, 1]
+    attn_router_grad = extra_grad[:, 2 : 2 + EXPERTS]
+    mlp_router_grad = extra_grad[:, 2 + EXPERTS : 2 + 2 * EXPERTS]
     mixed_full, input_full = (
         lax.all_gather(own_output.astype(jnp.bfloat16), "expert", axis=0, tiled=True),
         lax.all_gather(input_grad.astype(jnp.bfloat16), "expert", axis=0, tiled=True),
@@ -490,39 +510,43 @@
 
 
 def solution(mesh):
+    seq_size, halves = mesh.devices.shape
+    grouped = jax.sharding.Mesh(
+        mesh.devices.reshape(EXPERTS, seq_size // EXPERTS, halves), ALL_AXES
+    )
     return jax.shard_map(
         shards,
-        mesh=mesh,
+        mesh=grouped,
         in_specs=(
-            P("seq", None),
-            P(("seq", "expert")),
-            P(("seq", "expert"), None),
-            P(("seq", "expert"), None),
-            P(None, ("seq", "expert")),
-            P(("seq", "expert"), None),
-            P(("seq", "expert")),
-            P(("seq", "expert"), None),
-            P(None, ("seq", "expert")),
-            P(None, ("seq", "expert")),
-            P(("seq", "expert"), None),
-            P("seq", None),
-            P("seq", None),
-            P("seq", None),
-            P("seq", None),
+            P(SEQ_AXES, None),
+            P(ALL_AXES),
+            P(ALL_AXES, None),
+            P(ALL_AXES, None),
+            P(None, ALL_AXES),
+            P(ALL_AXES, None),
+            P(ALL_AXES),
+            P(ALL_AXES, None),
+            P(None, ALL_AXES),
+            P(None, ALL_AXES),
+            P(ALL_AXES, None),
+            P(SEQ_AXES, None),
+            P(SEQ_AXES, None),
+            P(SEQ_AXES, None),
+            P(SEQ_AXES, None),
         ),
         out_specs=(
-            P("seq", None),
-            P("seq", None),
-            P(("seq", "expert")),
-            P(("seq", "expert"), None),
-            P(("seq", "expert"), None),
-            P(None, ("seq", "expert")),
-            P(("seq", "expert"), None),
-            P(("seq", "expert")),
-            P(("seq", "expert"), None),
-            P(None, ("seq", "expert")),
-            P(None, ("seq", "expert")),
-            P(("seq", "expert"), None),
+            P(SEQ_AXES, None),
+            P(SEQ_AXES, None),
+            P(ALL_AXES),
+            P(ALL_AXES, None),
+            P(ALL_AXES, None),
+            P(None, ALL_AXES),
+            P(ALL_AXES, None),
+            P(ALL_AXES),
+            P(ALL_AXES, None),
+            P(None, ALL_AXES),
+            P(None, ALL_AXES),
+            P(ALL_AXES, None),
         ),
         check_vma=False,
     )

time: 3160 us -> 2510 us (0.79)
  waiting for transfers between devices: 2100 us -> 1460 us
    reduce_scatter x1, waiting for transfers between devices: 696 us -> 25 us  [shards(): lax.psum_scatter(packed_grad, 'grp', scatter_dimension=0, tiled=True)]
    all_gather x1 -> x2, waiting for transfers between devices: 332 us -> 518 us  [the longest x1 332 us: shards(): gathered = lax.all_gather(packed, ALL_AXES, axis=0, tiled=True)]
    all_to_all x8 -> x10, waiting for transfers between devices: 901 us -> 756 us  [the longest x4 529 us: slot_sums(): lax.all_to_all(partial_value.astype(jnp.bfloat16), ALL_AXES, split_axis=0...]
    all_to_all x8 -> x10, starting transfers between devices: 65.9 us -> 76.2 us  [the longest x4 33.8 us: slot_sums(): lax.all_to_all(partial_value.astype(jnp.bfloat16), ALL_AXES, split_axis=0...]
  transfers between devices with their start and end apart: 11 -> 14, of which waited for: 10 -> 11; matrix products, arithmetic and copies ran while one was open for 5% -> 5% of each run, Pallas kernels for 0% -> 0%
where the time goes in v3:
time: 2510 us; the launch traced here: 2490 us
  waiting for transfers between devices  1460 us (58%)
  blocking collectives  376 us (15%)
  local copies, waits for them, and re-layouts  257 us (10%)
  matrix products  213 us (8%)
  other arithmetic  86.4 us (3%)
  starting transfers between devices  82 us (3%)
    all_to_all x4, waiting for transfers between devices, slot_sums(): lax.all_to_all(partial_value.astype(jnp.bfloat16), ALL_AXES, split_axis=0...  529 us
    all_gather x1, waiting for transfers between devices, shards(): gathered = lax.all_gather(packed, ALL_AXES, axis=0, tiled=True)  332 us
    all_gather x1, waiting for transfers between devices, shards(): seq_input = lax.all_gather(attn_input, GROUP_AXES, axis=0, tiled=True)  186 us
    all_to_all x1, waiting for transfers between devices, shards(): lax.all_to_all(fan_out(attn_slot_grad, group_size), ALL_AXES, split_axis=...  183 us
    all_to_all x1, waiting for transfers between devices, shards(): lax.all_to_all(fan_out(pick_slots(attn_input, attn_token, attn_valid), gr...  162 us
    all_to_all x1, blocking collectives, shards(): lax.all_to_all(fan_out(mlp_slot_grad, group_size), ALL_AXES, split_axis=0...  152 us
    all_to_all x1, blocking collectives, shards(): lax.all_to_all(fan_out(pick_slots(mlp_input, mlp_token, mlp_valid), group...  151 us
    convert_element_type x4, local copies, waits for them, and re-layouts, slot_sums(): partial_value.astype(jnp.bfloat16)  69.7 us
  transfers between devices with their start and end apart: 14, of which 11 were waited for; matrix products, arithmetic and copies ran while one was open for 5% of the time, Pallas kernels for 0%

profile of v3, /device:TPU:1, one launch (start us, length us, event | category | flops | bytes accessed | tf_op | source)
XLA Modules:
  0.0 2493.9 jit_solution(2889299862343514329)
XLA Ops:
  15.0 332.5 %all-gather.3.cloned.1.call-done = bf16[2048,4224]{1,0:T(8,128)(2,1)} async-done(((bf16[16,4224]{1,0:T(8,128)(2,1)}), bf16[2048,4224]{1,0:T(8,128)(2,1)}) %all-gather.3.cloned.1.call-update) | async-done | bytes 17301520 | tf_op jit(solution)/shard_map/all_gather | solution.py:191
  349.4 7.5 fusion.53
  360.3 9.0 all-to-all-start.2
  372.1 26.4 %all-to-all-done.2 = bf16[64,128,128]{2,0,1:T(8,128)(2,1)} async-done(((bf16[64,128,128]{2,0,1:T(8,128)(2,1)}), bf16[64,128,128]{2,0,1:T(8,128)(2,1)}, u32[]{:S(2)}, u32[]{:S(2)}) %all-to-all-start.2) | async-done | bytes 2097184 | tf_op jit(solution)/shard_map/all_to_all | solution.py:220
  425.7 162.5 %all-to-all-done.1 = bf16[128,18,2048]{2,1,0:T(8,128)(2,1)} async-done(((bf16[128,18,2048]{2,1,0:T(8,128)(2,1)}), bf16[128,18,2048]{2,1,0:T(8,128)(2,1)}, u32[]{:S(2)}, u32[]{:S(2)}) %all-to-all-start.1) | async-done | bytes 9437216 | tf_op jit(solution)/shard_map/all_to_all | solution.py:236
  596.6 14.1 reshape.795
  610.7 6.9 convolution_bitcast_fusion.1
  625.7 30.1 %while.29 = (s32[]{:T(128)}, bf16[8,288,1,128]{3,1,2,0:T(8,128)(2,1)S(1)}, f32[8,1,288,1]{2,3,1,0:T(1,128)}, bf16[8,1024,1,128]{3,1,2,0:T(8,128)(2,1)}, s32[8,28...) while((s32[]{:T(128)}, ...), condition=%wide.region_11.12_spmd.clone, body=%wide.region_8.11_spmd.clone.sunk | while | flops 153693920 | bytes 4239577 | solution.py:278
  660.9 21.0 copy.559
  681.9 8.6 all-to-all-start.3
  696.5 171.9 %all-to-all-done.3 = bf16[128,18,2048]{2,1,0:T(8,128)(2,1)} async-done(((bf16[128,18,2048]{2,1,0:T(8,128)(2,1)}), bf16[128,18,2048]{2,1,0:T(8,128)(2,1)}, u32[]{:S(2)}, u32[]{:S(2)}) %all-to-all-start.3) | async-done | bytes 9437216 | tf_op jit(solution)/shard_map/all_to_all | solution.py:156
  868.4 8.8 convert_reduce_fusion.3
  894.8 150.7 %all_to_all.108 = bf16[128,18,2048]{2,1,0:T(8,128)(2,1)} all-to-all(bf16[128,18,2048]{2,1,0:T(8,128)(2,1)} %bitcast.283), channel_id=1, replica_groups=mesh['grp'=8,'sub'=8,'expert'=2] {'grp','sub','expert'}, dimensions={0} | all-to-all | bytes 18874368 | tf_op jit(solution)/shard_map/all_to_all | solution.py:296
  1045.5 14.1 reshape.804
  1059.7 7.4 fusion.136
  1072.9 7.5 convolution_convert_fusion.1
  1080.4 13.9 convert_element_type.303
  1094.2 8.4 all-to-all-start.5
  1112.0 174.0 %all-to-all-done.5 = bf16[128,18,2048]{2,1,0:T(8,128)(2,1)} async-done(((bf16[128,18,2048]{2,1,0:T(8,128)(2,1)}), bf16[128,18,2048]{2,1,0:T(8,128)(2,1)}, u32[]{:S(2)}, u32[]{:S(2)}) %all-to-all-start.5) | async-done | bytes 9437216 | tf_op jit(solution)/shard_map/all_to_all | solution.py:156
  1286.0 8.8 convert_reduce_fusion.2
  1306.8 7.3 broadcast_in_dim.115
  1314.1 152.3 %all_to_all.109 = bf16[128,18,2048]{2,1,0:T(8,128)(2,1)} all-to-all(bf16[128,18,2048]{2,1,0:T(8,128)(2,1)} %bitcast.284), channel_id=1, replica_groups=mesh['grp'=8,'sub'=8,'expert'=2] {'grp','sub','expert'}, dimensions={0} | all-to-all | bytes 18874368 | tf_op jit(solution)/shard_map/all_to_all | solution.py:323
  1466.5 14.1 reshape.809
  1480.6 11.9 multiply_convert_fusion.1
  1492.5 9.1 fusion.137
  1501.6 11.2 add_convert_fusion
  1512.8 13.9 convert_element_type.312
  1526.7 8.2 all-to-all-start.7
  1535.1 183.1 %all-to-all-done.7 = bf16[128,18,2048]{2,1,0:T(8,128)(2,1)} async-done(((bf16[128,18,2048]{2,1,0:T(8,128)(2,1)}), bf16[128,18,2048]{2,1,0:T(8,128)(2,1)}, u32[]{:S(2)}, u32[]{:S(2)}) %all-to-all-start.7) | async-done | bytes 9437216 | tf_op jit(solution)/shard_map/all_to_all | solution.py:156
  1718.2 7.6 convert_reduce_fusion.1
  1746.4 8.3 all-to-all-start.8
  1754.7 183.4 %all-to-all-done.8 = bf16[128,18,2048]{2,1,0:T(8,128)(2,1)} async-done(((bf16[128,18,2048]{2,1,0:T(8,128)(2,1)}), bf16[128,18,2048]{2,1,0:T(8,128)(2,1)}, u32[]{:S(2)}, u32[]{:S(2)}) %all-to-all-start.8) | async-done | bytes 9437216 | tf_op jit(solution)/shard_map/all_to_all | solution.py:363
  1938.1 14.1 reshape.814
  1952.2 6.3 convolution_convert_fusion.4
  1958.5 88.2 %while.30 = (s32[]{:T(128)}, f32[8,288,1,128]{3,1,2,0:T(8,128)}, bf16[8,1024,1,128]{3,1,0,2:T(8,128)(2,1)}, bf16[8,1024,1,128]{3,1,0,2:T(8,128)(2,1)}, bf16[8,10...) while((s32[]{:T(128)}, f32[8,288,1,128]{3,1,2,0:T(8,128)}, ...), condition=%wide.region_35.39_spmd.clone, body=%wide.region_33.38_spmd.clone.sunk | while | flops 380743392 | bytes 22157028 | solution.py:400
  2046.7 37.3 %all_to_all.110 = bf16[128,64,1,128]{3,1,2,0:T(8,128)(2,1)} all-to-all(bf16[128,64,1,128]{3,1,2,0:T(8,128)(2,1)} %bitcast.295), channel_id=1, replica_groups=mesh['grp'=8,'sub'=8,'expert'=2] {'grp','sub','expert'}, dimensions={0} | all-to-all | bytes 4194304 | tf_op jit(solution)/shard_map/all_to_all | solution.py:417
  2103.1 15.8 all-to-all-done.11
  2131.2 21.0 copy.598
  2152.2 8.7 all-to-all-start.9
  2164.6 185.9 %all-gather.5.cloned.1.call-done = bf16[1024,2048]{1,0:T(8,128)(2,1)} async-done(((bf16[64,2048]{1,0:T(8,128)(2,1)}), bf16[1024,2048]{1,0:T(8,128)(2,1)}) %all-gather.5.cloned.1.call-update) | async-done | bytes 4194320 | tf_op jit(solution)/shard_map/all_gather | solution.py:202
  2355.5 7.6 convert_reduce_fusion
  2367.2 9.0 fusion.56
  2380.5 9.4 fusion.142
  2389.9 8.9 fusion.143
  2404.0 21.9 all_gather.13
  2432.0 25.0 %reduce-scatter.2.cloned.1.call-done = f32[256,384]{0,1:T(8,128)} async-done(((f32[2048,384]{0,1:T(8,128)}), f32[256,384]{0,1:T(8,128)}) %reduce-scatter.2.cloned.1.call-update) | async-done | bytes 393232 | tf_op jit(solution)/shard_map/reduce_scatter | solution.py:478
  2458.9 8.2 all-to-all-start.13
  2467.3 13.5 all_gather.14
  (656 shorter events, 320.1 us)
Async XLA Ops:
  7.2 1065.7 %copy-start = (bf16[352,2048]{1,0:T(8,128)(2,1)S(1)}, bf16[352,2048]{1,0:T(8,128)(2,1)}, u32[]{:S(2)}) copy-start(bf16[352,2048]{1,0:T(8,128)(2,1)} %param.35) | copy-start | bytes 4325380
  7.2 340.3 %all-gather.3.cloned.1.call-start = ((), (), s32[]{:S(2)}) async-start(), calls=%async_computation.15 | async-start | bytes 17436672 | tf_op jit(solution)/shard_map/all_gather | solution.py:191
  10.8 685.1 %copy-start.67 = (s32[64,2]{0,1:T(2,128)}, s32[64,2]{0,1:T(2,128)S(1)}, u32[]{:S(2)}) copy-start(s32[64,2]{0,1:T(2,128)S(1)} %get-tuple-element.485) | copy-start | bytes 1540
  14.7 602.9 %copy-start.81 = (f32[64]{0:T(128)}, f32[64]{0:T(128)S(1)}, u32[]{:S(2)}) copy-start(f32[64]{0:T(128)S(1)} %multiply_exponential_fusion) | copy-start | bytes 772
  14.7 342.2 %copy-start.79 = (f32[64]{0:T(128)}, f32[64]{0:T(128)S(1)}, u32[]{:S(2)}) copy-start(f32[64]{0:T(128)S(1)} %add_rsqrt_fusion.1) | copy-start | bytes 772
  14.9 343.0 %copy-start.48 = (f32[64,64]{1,0:T(8,128)}, f32[64,64]{1,0:T(8,128)S(1)}, u32[]{:S(2)}) copy-start(f32[64,64]{1,0:T(8,128)S(1)} %get-tuple-element.516) | copy-start | bytes 49156
  15.0 342.9 %copy-start.50 = (f32[64,64]{1,0:T(8,128)}, f32[64,64]{1,0:T(8,128)S(1)}, u32[]{:S(2)}) copy-start(f32[64,64]{1,0:T(8,128)S(1)} %get-tuple-element.517) | copy-start | bytes 49156
  349.3 535.1 %copy-start.56 = (f32[2048]{0:T(1024)}, f32[2048]{0:T(1024)S(1)}, u32[]{:S(2)}) copy-start(f32[2048]{0:T(1024)S(1)} %get-tuple-element.418) | copy-start | bytes 24580
  349.4 343.5 %copy-start.2 = (bf16[64,2048]{1,0:T(8,128)(2,1)}, bf16[64,2048]{1,0:T(8,128)(2,1)S(1)}, u32[]{:S(2)}) copy-start(bf16[64,2048]{1,0:T(8,128)(2,1)S(1)} %fusion.85) | copy-start | bytes 786436
  360.3 38.3 %all-to-all-start.2 = ((bf16[64,128,128]{2,0,1:T(8,128)(2,1)}), bf16[64,128,128]{2,0,1:T(8,128)(2,1)}, u32[]{:S(2)}, u32[]{:S(2)}) async-start(bf16[64,128,128]{2,0,1:T(8,128)(2,1)} %bitcast.289), calls=%async_computation.2 | async-start | bytes 4194304 | tf_op jit(solution)/shard_map/all_to_all | solution.py:220
  404.8 183.4 %all-to-all-start.1 = ((bf16[128,18,2048]{2,1,0:T(8,128)(2,1)}), bf16[128,18,2048]{2,1,0:T(8,128)(2,1)}, u32[]{:S(2)}, u32[]{:S(2)}) async-start(bf16[128,18,2048]{2,1,0:T(8,128)(2,1)} %bitcast.281), calls=%async_computation.1 | async-start | bytes 25165824 | tf_op jit(solution)/shard_map/all_to_all | solution.py:236
  590.0 35.6 %all-to-all-start = ((bf16[64,128,128]{2,0,1:T(8,128)(2,1)}), bf16[64,128,128]{2,0,1:T(8,128)(2,1)}, u32[]{:S(2)}, u32[]{:S(2)}) async-start(bf16[64,128,128]{2,0,1:T(8,128)(2,1)} %bitcast.288), calls=%async_computation | async-start | bytes 4194304 | tf_op jit(solution)/shard_map/all_to_all | solution.py:223
  596.5 21.1 copy-start.60
  596.6 14.1 copy-start.29
  681.9 186.4 %all-to-all-start.3 = ((bf16[128,18,2048]{2,1,0:T(8,128)(2,1)}), bf16[128,18,2048]{2,1,0:T(8,128)(2,1)}, u32[]{:S(2)}, u32[]{:S(2)}) async-start(bf16[128,18,2048]{2,1,0:T(8,128)(2,1)} %copy.559), calls=%async_computation.3 | async-start | bytes 25165824 | tf_op jit(solution)/shard_map/all_to_all | solution.py:156
  692.9 185.8 %copy-start.35 = (s32[1024]{0:T(1024)}, s32[1024]{0:T(1024)S(1)}, u32[]{:S(2)}) copy-start(s32[1024]{0:T(1024)S(1)} %pad_clamp_fusion.2) | copy-start | bytes 12292
  696.4 180.7 %copy-start.77 = (f32[64,2]{0,1:T(2,128)}, f32[64,2]{0,1:T(2,128)S(1)}, u32[]{:S(2)}) copy-start(f32[64,2]{0,1:T(2,128)S(1)} %get-tuple-element.481) | copy-start | bytes 1540
  885.3 223.7 %copy-start.4 = (bf16[64,2048]{1,0:T(8,128)(2,1)}, bf16[64,2048]{1,0:T(8,128)(2,1)S(1)}, u32[]{:S(2)}) copy-start(bf16[64,2048]{1,0:T(8,128)(2,1)S(1)} %multiply_convert_fusion.6) | copy-start | bytes 786436
  1045.5 14.1 copy-start.31
  1094.2 191.8 %all-to-all-start.5 = ((bf16[128,18,2048]{2,1,0:T(8,128)(2,1)}), bf16[128,18,2048]{2,1,0:T(8,128)(2,1)}, u32[]{:S(2)}, u32[]{:S(2)}) async-start(bf16[128,18,2048]{2,1,0:T(8,128)(2,1)} %convert_element_type.303), calls=%async_computation.5 | async-start | bytes 25165824 | tf_op jit(solution)/shard_map/all_to_all | solution.py:156
  1480.6 11.9 copy-start.32
  1492.4 9.2 copy-start.25
  1492.4 9.2 copy-start.19
  1492.5 9.2 copy-start.34
  1526.7 191.6 %all-to-all-start.7 = ((bf16[128,18,2048]{2,1,0:T(8,128)(2,1)}), bf16[128,18,2048]{2,1,0:T(8,128)(2,1)}, u32[]{:S(2)}, u32[]{:S(2)}) async-start(bf16[128,18,2048]{2,1,0:T(8,128)(2,1)} %convert_element_type.312), calls=%async_computation.7 | async-start | bytes 25165824 | tf_op jit(solution)/shard_map/all_to_all | solution.py:156
  1746.4 191.7 %all-to-all-start.8 = ((bf16[128,18,2048]{2,1,0:T(8,128)(2,1)}), bf16[128,18,2048]{2,1,0:T(8,128)(2,1)}, u32[]{:S(2)}, u32[]{:S(2)}) async-start(bf16[128,18,2048]{2,1,0:T(8,128)(2,1)} %bitcast.282), calls=%async_computation.8 | async-start | bytes 25165824 | tf_op jit(solution)/shard_map/all_to_all | solution.py:363
  1754.7 197.5 %copy-start.45 = (bf16[128,2048]{1,0:T(8,128)(2,1)S(1)}, bf16[128,2048]{1,0:T(8,128)(2,1)}, u32[]{:S(2)}) copy-start(bf16[128,2048]{1,0:T(8,128)(2,1)} %param.30) | copy-start | bytes 1572868
  2084.0 34.9 %all-to-all-start.11 = ((bf16[128,64,1,128]{3,1,2,0:T(8,128)(2,1)}), bf16[128,64,1,128]{3,1,2,0:T(8,128)(2,1)}, u32[]{:S(2)}, u32[]{:S(2)}) async-start(bf16[128,64,1,128]{3,1,2,0:T(8,128)(2,1)} %bitcast.296), calls=%async_computation.11 | async-start | bytes 4194304 | tf_op jit(solution)/shard_map/all_to_all | solution.py:424
  2095.5 31.9 %copy-start.37 = (bf16[2304,1,64]{0,2,1:T(8,128)(2,1)}, bf16[2304,1,64]{0,2,1:T(8,128)(2,1)S(1)}, u32[]{:S(2)}) copy-start(bf16[2304,1,64]{0,2,1:T(8,128)(2,1)S(1)} %get-tuple-element.494) | copy-start | bytes 884740
  2095.5 31.9 %copy-start.39 = (bf16[2304,1,64]{0,2,1:T(8,128)(2,1)}, bf16[2304,1,64]{0,2,1:T(8,128)(2,1)S(1)}, u32[]{:S(2)}) copy-start(bf16[2304,1,64]{0,2,1:T(8,128)(2,1)S(1)} %get-tuple-element.495) | copy-start | bytes 884740
  2122.2 30.1 %all-to-all-start.12 = ((bf16[64,16,256]{2,0,1:T(8,128)(2,1)}), bf16[64,16,256]{2,0,1:T(8,128)(2,1)}, u32[]{:S(2)}, u32[]{:S(2)}) async-start(bf16[64,16,256]{2,0,1:T(8,128)(2,1)} %copy.611), calls=%async_computation.12 | async-start | bytes 1048576 | tf_op jit(solution)/shard_map/all_to_all | solution.py:451
  2152.2 10.4 copy-start.5
  2152.2 10.6 copy-start.3
  2152.2 203.2 %all-to-all-start.9 = ((bf16[128,18,2048]{2,1,0:T(8,128)(2,1)}), bf16[128,18,2048]{2,1,0:T(8,128)(2,1)}, u32[]{:S(2)}, u32[]{:S(2)}) async-start(bf16[128,18,2048]{2,1,0:T(8,128)(2,1)} %copy.598), calls=%async_computation.9 | async-start | bytes 25165824 | tf_op jit(solution)/shard_map/all_to_all | solution.py:156
  2160.9 189.7 %all-gather.5.cloned.1.call-start = ((), (), s32[]{:S(2)}) async-start(), calls=%async_computation.16 | async-start | bytes 4456448 | tf_op jit(solution)/shard_map/all_gather | solution.py:202
  2161.7 295.4 %reduce-scatter.2.cloned.1.call-start = ((), (), s32[]{:S(2)}) async-start(), calls=%async_computation.17 | async-start | bytes 3538944 | tf_op jit(solution)/shard_map/reduce_scatter | solution.py:478
  2367.1 11.3 copy-start.74
  2380.5 9.4 copy-start.26
  2380.5 18.4 slice-start.6
  2380.5 18.4 slice-start.7
  2389.9 36.0 %slice-start = ((s8[9437184]{0:T(1024)(128)(4,1)}), s8[4194304]{0:T(1024)(128)(4,1)S(1)}, s32[]{:S(2)}) async-start(s8[9437184]{0:T(1024)(128)(4,1)} %bitcast.277), calls=%async_computation.18 | async-start | bytes 8388608
  2389.9 36.0 %slice-start.1 = ((s8[9437184]{0:T(1024)(128)(4,1)}), s8[4194304]{0:T(1024)(128)(4,1)S(1)}, s32[]{:S(2)}) async-start(s8[9437184]{0:T(1024)(128)(4,1)} %bitcast.277), calls=%async_computation.19 | async-start | bytes 8388608
  2398.9 27.0 %slice-start.2 = ((s8[9437184]{0:T(1024)(128)(4,1)}), s8[1048576]{0:T(1024)(128)(4,1)S(1)}, s32[]{:S(2)}) async-start(s8[9437184]{0:T(1024)(128)(4,1)} %bitcast.277), calls=%async_computation.20 | async-start | bytes 2097152
  2398.9 27.0 %copy-start.18 = (bf16[8,288,1,128]{3,1,2,0:T(8,128)(2,1)S(1)}, bf16[8,288,1,128]{3,1,2,0:T(8,128)(2,1)}, u32[]{:S(2)}) copy-start(bf16[8,288,1,128]{3,1,2,0:T(8,128)(2,1)} %copy-done.17) | copy-start | bytes 1769476
  2398.9 29.4 %slice-start.3 = ((s8[9437184]{0:T(1024)(128)(4,1)}), s8[4194304]{0:T(1024)(128)(4,1)S(1)}, s32[]{:S(2)}) async-start(s8[9437184]{0:T(1024)(128)(4,1)} %bitcast.279), calls=%async_computation.21 | async-start | bytes 8388608
  2398.9 29.4 %slice-start.4 = ((s8[9437184]{0:T(1024)(128)(4,1)}), s8[4194304]{0:T(1024)(128)(4,1)S(1)}, s32[]{:S(2)}) async-start(s8[9437184]{0:T(1024)(128)(4,1)} %bitcast.279), calls=%async_computation.22 | async-start | bytes 8388608
  2458.9 21.9 all-to-all-start.13
  2467.1 20.0 copy-start.1
  (96 other events, 293.4 us)
Sparse Core Ops, SparseCore 0:
  14.6 332.7 all-gather.2
  2164.3 186.2 all-gather.4
  2380.6 76.4 reduce-scatter.1

commit v4 on v3

--- a/solution.py
+++ b/solution.py
@@ -149,19 +149,32 @@
     slot_rows = devices * slot_cap
     seq_rows = slot_rows // sequences
     my_expert = device_index // group_size
+    groups = lax.axis_size("grp")
+    head_index = device_index % group_size
+
+    def dispatch(slot_values):
+        by_group = lax.all_to_all(slot_values, "grp", split_axis=0, concat_axis=0, tiled=True)
+        return lax.all_gather(by_group, GROUP_AXES, axis=0, tiled=True).reshape(slot_rows, width)
+
+    def combine(partial_value):
+        parts = lax.all_to_all(
+            partial_value.astype(jnp.bfloat16).reshape(group_size, groups * slot_cap, width),
+            GROUP_AXES,
+            split_axis=0,
+            concat_axis=0,
+            tiled=True,
+        )
+        summed = jnp.sum(parts.astype(jnp.float32), axis=0).reshape(groups, slot_cap, width)
+        return lax.all_to_all(summed, "grp", split_axis=0, concat_axis=0, tiled=True)
+
+    def to_gj(rows):
+        shaped = rows.reshape((group_size, groups, slot_cap) + rows.shape[1:])
+        return jnp.swapaxes(shaped, 0, 1).reshape(rows.shape)
+
+    def to_jg(rows):
+        shaped = rows.reshape((groups, group_size, slot_cap) + rows.shape[1:])
+        return jnp.swapaxes(shaped, 0, 1).reshape(rows.shape)
     scale = 1.0 / math.sqrt(HEAD)
-
-    def slot_sums(partial_value):
-        return fold_group(
-            lax.all_to_all(
-                partial_value.astype(jnp.bfloat16),
-                ALL_AXES,
-                split_axis=0,
-                concat_axis=0,
-                tiled=True,
-            ).astype(jnp.float32),
-            group_size,
-        )
 
     start_row = half_index * own_rows
     own_input = lax.dynamic_slice_in_dim(tokens, start_row, own_rows, 0).astype(jnp.float32)
@@ -188,7 +201,12 @@
     packed = jnp.concatenate(
         [kv_weight, jnp.pad(extras, ((0, 0), (0, extra_pad - extra_cols)))], axis=1
     )
-    gathered = lax.all_gather(packed, ALL_AXES, axis=0, tiled=True)
+    gathered = lax.all_gather(
+        lax.all_gather(packed, "grp", axis=0, tiled=True), GROUP_AXES, axis=0, tiled=True
+    )
+    gathered = jnp.swapaxes(
+        gathered.reshape(group_size, groups, kv_rows, extra_pad + kv_width), 0, 1
+    ).reshape(devices * kv_rows, extra_pad + kv_width)
     kv_full = gathered[:, :kv_width]
     gain_one = gathered[:, kv_width]
     gain_two = gathered[:, kv_width + 1]
@@ -200,32 +218,29 @@
     attn_input = (normed_one * gain_one.astype(jnp.float32)).astype(jnp.bfloat16)
     attn_logits = jnp.dot(attn_input, router_one, preferred_element_type=jnp.float32)
     seq_input = lax.all_gather(attn_input, GROUP_AXES, axis=0, tiled=True)
-    key_value = jnp.dot(attn_input, kv_full, preferred_element_type=jnp.float32)
     own_positions = (device_index * own_rows + token_order) % seq_length
     own_cos, own_sin = rope_tables(own_positions, HEAD)
-    own_keys = (
-        rotate(key_value[:, :key_cols].reshape(own_rows, KV_HEADS, HEAD), own_cos, own_sin)
-        .reshape(own_rows, key_cols)
-        .astype(jnp.bfloat16)
-    )
-    own_values = key_value[:, key_cols:].astype(jnp.bfloat16)
-
-    def spread(values):
-        shaped = values.reshape(own_rows, 1, group_size, head_cols)
-        return jnp.broadcast_to(shaped, (own_rows, EXPERTS, group_size, head_cols)).reshape(
-            own_rows, devices, head_cols
-        )
-
-    head_keys, head_values = (
-        lax.all_to_all(
-            spread(own_keys), ALL_AXES, split_axis=1, concat_axis=0, tiled=True
-        ),
-        lax.all_to_all(
-            spread(own_values), ALL_AXES, split_axis=1, concat_axis=0, tiled=True
-        ),
-    )
-    seq_keys = head_keys.reshape(sequences, seq_length, local_heads, HEAD)
-    seq_values = head_values.reshape(sequences, seq_length, local_heads, HEAD)
+    head_kv = jnp.concatenate(
+        [
+            lax.dynamic_slice_in_dim(kv_full, head_index * head_cols, head_cols, axis=1),
+            lax.dynamic_slice_in_dim(kv_full, key_cols + head_index * head_cols, head_cols, axis=1),
+        ],
+        axis=1,
+    )
+    seq_kv = jnp.dot(seq_input, head_kv, preferred_element_type=jnp.float32)
+    seq_cos, seq_sin = rope_tables(jnp.arange(seq_length, dtype=jnp.int32), HEAD)
+    seq_pair = jnp.concatenate(
+        [
+            rotate(seq_kv[:, :head_cols].reshape(seq_length, local_heads, HEAD), seq_cos, seq_sin)
+            .reshape(seq_length, head_cols)
+            .astype(jnp.bfloat16),
+            seq_kv[:, head_cols:].astype(jnp.bfloat16),
+        ],
+        axis=1,
+    )
+    all_pairs = lax.all_gather(seq_pair, "grp", axis=0, tiled=True)
+    seq_keys = all_pairs[:, :head_cols].reshape(sequences, seq_length, local_heads, HEAD)
+    seq_values = all_pairs[:, head_cols:].reshape(sequences, seq_length, local_heads, HEAD)
     attn_places, attn_kept, attn_token, attn_valid = slot_table(own_attn, token_order, slot_cap)
     mlp_places, mlp_kept, mlp_token, mlp_valid = slot_table(own_mlp, own_rank, slot_cap)
     block_routes = routes_all.reshape(devices, own_rows, TOPK)
@@ -233,14 +248,8 @@
         block_routes
     )
     dest_token = jnp.take(dest_tables, my_expert, axis=1)
-    attn_rows = lax.all_to_all(
-        fan_out(pick_slots(attn_input, attn_token, attn_valid), group_size),
-        ALL_AXES,
-        split_axis=0,
-        concat_axis=0,
-        tiled=True,
-    ).reshape(slot_rows, width)
-    queries = jnp.dot(attn_rows, query_weight, preferred_element_type=jnp.float32)
+    attn_rows = dispatch(pick_slots(attn_input, attn_token, attn_valid))
+    queries = to_gj(jnp.dot(attn_rows, query_weight, preferred_element_type=jnp.float32))
     slot_positions = (
         (jnp.arange(devices, dtype=jnp.int32)[:, None] * own_rows + dest_token) % seq_length
     ).reshape(slot_rows)
@@ -278,11 +287,9 @@
     attn_mixed, log_totals = lax.map(
         attend_forward, (seq_queries, seq_keys, seq_values, query_blocks)
     )
-    mixed_rows = attn_mixed.reshape(slot_rows, head_cols)
-    attn_partial = jnp.dot(mixed_rows, output_weight, preferred_element_type=jnp.float32).reshape(
-        devices, slot_cap, width
-    )
-    attn_slots = slot_sums(attn_partial)
+    mixed_rows = to_jg(attn_mixed.reshape(slot_rows, head_cols))
+    attn_partial = jnp.dot(mixed_rows, output_weight, preferred_element_type=jnp.float32)
+    attn_slots = combine(attn_partial)
     attn_gates = pair_gates(attn_logits, own_attn)
     attn_index, attn_pair_kept = pair_index(own_attn, attn_places, attn_kept, slot_cap)
     attn_picked = attn_slots.reshape(EXPERTS * slot_cap, width)[attn_index]
@@ -293,21 +300,13 @@
     normed_two = hidden_state * inverse_two
     mlp_input = (normed_two * gain_two.astype(jnp.float32)).astype(jnp.bfloat16)
     mlp_logits = jnp.dot(mlp_input, router_two, preferred_element_type=jnp.float32)
-    mlp_rows = lax.all_to_all(
-        fan_out(pick_slots(mlp_input, mlp_token, mlp_valid), group_size),
-        ALL_AXES,
-        split_axis=0,
-        concat_axis=0,
-        tiled=True,
-    ).reshape(slot_rows, width)
+    mlp_rows = dispatch(pick_slots(mlp_input, mlp_token, mlp_valid))
     gate_pre = jnp.dot(mlp_rows, gate_weight, preferred_element_type=jnp.float32)
     up_pre = jnp.dot(mlp_rows, up_weight, preferred_element_type=jnp.float32)
     activated = jax.nn.silu(gate_pre)
     inner_rows = (activated * up_pre).astype(jnp.bfloat16)
-    mlp_partial = jnp.dot(inner_rows, down_weight, preferred_element_type=jnp.float32).reshape(
-        devices, slot_cap, width
-    )
-    mlp_slots = slot_sums(mlp_partial)
+    mlp_partial = jnp.dot(inner_rows, down_weight, preferred_element_type=jnp.float32)
+    mlp_slots = combine(mlp_partial)
     mlp_gates = pair_gates(mlp_logits, own_mlp)
     mlp_index, mlp_pair_kept = pair_index(own_mlp, mlp_places, mlp_kept, slot_cap)
     mlp_picked = mlp_slots.reshape(EXPERTS * slot_cap, width)[mlp_index]
@@ -320,13 +319,7 @@
         own_cotangent[mlp_token]
         * slot_gates(mlp_gates, mlp_pair_kept, own_mlp, mlp_token, mlp_valid)[:, :, None]
     ).astype(jnp.bfloat16)
-    down_rows = lax.all_to_all(
-        fan_out(mlp_slot_grad, group_size),
-        ALL_AXES,
-        split_axis=0,
-        concat_axis=0,
-        tiled=True,
-    ).reshape(slot_rows, width)
+    down_rows = dispatch(mlp_slot_grad)
     inner_grad = jnp.einsum("rd,fd->rf", down_rows, down_weight, preferred_element_type=jnp.float32)
     down_grad = jnp.einsum("rf,rd->fd", inner_rows, down_rows, preferred_element_type=jnp.float32)
     sigmoid_gate = jax.nn.sigmoid(gate_pre)
@@ -339,7 +332,7 @@
     row_grad = jnp.einsum(
         "rf,df->rd", gate_pre_grad, gate_weight, preferred_element_type=jnp.float32
     ) + jnp.einsum("rf,df->rd", up_pre_grad, up_weight, preferred_element_type=jnp.float32)
-    mlp_row_grad = slot_sums(row_grad.reshape(devices, slot_cap, width))
+    mlp_row_grad = combine(row_grad)
     mlp_input_grad = jnp.sum(
         mlp_row_grad.reshape(EXPERTS * slot_cap, width)[mlp_index] * mlp_pair_kept[:, :, None],
         axis=1,
@@ -360,18 +353,12 @@
         hidden_grad[attn_token]
         * slot_gates(attn_gates, attn_pair_kept, own_attn, attn_token, attn_valid)[:, :, None]
     ).astype(jnp.bfloat16)
-    out_rows = lax.all_to_all(
-        fan_out(attn_slot_grad, group_size),
-        ALL_AXES,
-        split_axis=0,
-        concat_axis=0,
-        tiled=True,
-    ).reshape(slot_rows, width)
+    out_rows = dispatch(attn_slot_grad)
     output_grad = jnp.einsum("rw,rd->wd", mixed_rows, out_rows, preferred_element_type=jnp.float32)
     mixed_grad = jnp.einsum(
         "rd,wd->rw", out_rows, output_weight, preferred_element_type=jnp.float32
     ).astype(jnp.bfloat16)
-    seq_mixed_grad = mixed_grad.reshape(sequences, seq_rows, local_heads, HEAD)
+    seq_mixed_grad = to_gj(mixed_grad).reshape(sequences, seq_rows, local_heads, HEAD)
 
     def attend_backward(inputs):
         query_part, key_part, value_part, block_part, log_part, grad_part = inputs
@@ -401,7 +388,7 @@
         attend_backward,
         (seq_queries, seq_keys, seq_values, query_blocks, log_totals, seq_mixed_grad),
     )
-    query_rot_grad = (
+    query_rot_grad = to_jg(
         rotate_back(seq_query_grad.reshape(slot_rows, local_heads, HEAD), slot_cos, slot_sin)
         .reshape(slot_rows, head_cols)
         .astype(jnp.bfloat16)
@@ -412,7 +399,7 @@
     query_row_grad = jnp.einsum(
         "rw,dw->rd", query_rot_grad, query_weight, preferred_element_type=jnp.float32
     )
-    attn_row_grad = slot_sums(query_row_grad.reshape(devices, slot_cap, width))
+    attn_row_grad = combine(query_row_grad)
     key_back, value_back = (
         lax.all_to_all(
             seq_key_grad.reshape(devices, own_rows, 1, head_cols).astype(jnp.bfloat16),

time: 2510 us -> 1840 us (0.73)
  waiting for transfers between devices: 1460 us -> 965 us
  blocking collectives: 376 us -> 244 us
  starting transfers between devices: 82 us -> 51.9 us
    all_to_all x9 -> x8, waiting for transfers between devices: 919 us -> 398 us  [the longest x3 302 us: combine(): lax.all_to_all(partial_value.astype(jnp.bfloat16).reshape(group_size, gro...]
    all_gather x1 -> x7, waiting for transfers between devices: 332 us -> 514 us  [the longest x4 304 us: dispatch(): lax.all_gather(by_group, GROUP_AXES, axis=0, tiled=True)]
    all_gather x1, waiting for transfers between devices: 186 us -> 44.5 us  [shards(): seq_input = lax.all_gather(attn_input, GROUP_AXES, axis=0, tiled=True)]
    all_to_all x3 -> x6, blocking collectives: 340 us -> 208 us  [the longest x1 110 us: combine(): lax.all_to_all(partial_value.astype(jnp.bfloat16).reshape(group_size, gro...]
    convert_element_type x5 -> x1, local copies, waits for them, and re-layouts: 69.9 us -> 0.17 us  [shards(): query_rot_grad = to_jg(rotate_back(seq_query_grad.reshape(slot_rows, loca...]
    all_gather x0 -> x4, local copies, waits for them, and re-layouts: none -> 53.1 us  [dispatch(): lax.all_gather(by_group, GROUP_AXES, axis=0, tiled=True)]
    broadcast_in_dim x7 -> x0, local copies, waits for them, and re-layouts: 30.7 us -> none  [the longest x4 25.9 us: fan_out(): jnp.broadcast_to(slot_values[:, None], (experts_here, group_size, slot_ca...]
    all_to_all x9 -> x8, starting transfers between devices: 68.3 us -> 38.6 us  [the longest x4 17.9 us: combine(): lax.all_to_all(summed, 'grp', split_axis=0, concat_axis=0, tiled=True)]
  transfers between devices with their start and end apart: 14 -> 19, of which waited for: 11 -> 18; matrix products, arithmetic and copies ran while one was open for 5% -> 7% of each run, Pallas kernels for 0% -> 0%
where the time goes in v4:
time: 1840 us; the launch traced here: 1830 us
  waiting for transfers between devices  965 us (52%)
  local copies, waits for them, and re-layouts  267 us (15%)
  blocking collectives  244 us (13%)
  matrix products  207 us (11%)
  other arithmetic  79.1 us (4%)
  starting transfers between devices  51.9 us (3%)
    all_gather x4, waiting for transfers between devices, dispatch(): lax.all_gather(by_group, GROUP_AXES, axis=0, tiled=True)  304 us
    all_to_all x3, waiting for transfers between devices, combine(): lax.all_to_all(partial_value.astype(jnp.bfloat16).reshape(group_size, gro...  302 us
    all_gather x1, waiting for transfers between devices, shards(): lax.all_gather(lax.all_gather(packed, 'grp', axis=0, tiled=True), GROUP_A...  119 us
    all_to_all x1, blocking collectives, combine(): lax.all_to_all(partial_value.astype(jnp.bfloat16).reshape(group_size, gro...  110 us
    all_to_all x4, waiting for transfers between devices, combine(): lax.all_to_all(summed, 'grp', split_axis=0, concat_axis=0, tiled=True)  78.6 us
    all_to_all x4, blocking collectives, dispatch(): lax.all_to_all(slot_values, 'grp', split_axis=0, concat_axis=0, tiled=True)  62.8 us
    reshape x4, local copies, waits for them, and re-layouts, dispatch(): lax.all_gather(by_group, GROUP_AXES, axis=0, tiled=True)  56.5 us
    all_gather x4, local copies, waits for them, and re-layouts, dispatch(): lax.all_gather(by_group, GROUP_AXES, axis=0, tiled=True)  53.1 us
  transfers between devices with their start and end apart: 19, of which 18 were waited for; matrix products, arithmetic and copies ran while one was open for 7% of the time, Pallas kernels for 0%

profile of v4, /device:TPU:1, one launch (start us, length us, event | category | flops | bytes accessed | tf_op | source)
XLA Modules:
  0.0 1830.9 jit_solution(9693969943914504780)
XLA Ops:
  17.8 37.3 %all-gather.9.cloned.1.call-done = bf16[128,4224]{1,0:T(8,128)(2,1)} async-done(((bf16[16,4224]{1,0:T(8,128)(2,1)}), bf16[128,4224]{1,0:T(8,128)(2,1)}) %all-gather.9.cloned.1.call-update) | async-done | bytes 1081360 | tf_op jit(solution)/shard_map/all_gather | solution.py:205
  55.4 119.1 %all-gather.11.cloned.1.call-done = bf16[2048,4224]{1,0:T(8,128)(2,1)} async-done(((bf16[128,4224]{1,0:T(8,128)(2,1)}), bf16[2048,4224]{1,0:T(8,128)(2,1)}) %all-gather.11.cloned.1.call-update) | async-done | bytes 17301520 | tf_op jit(solution)/shard_map/all_gather | solution.py:204
  174.5 8.1 copy.566
  182.6 6.0 copy-done.4
  190.1 8.3 slice.139
  198.7 44.5 %all-gather.13.cloned.1.call-done = bf16[1024,2048]{1,0:T(8,128)(2,1)} async-done(((bf16[64,2048]{1,0:T(8,128)(2,1)}), bf16[1024,2048]{1,0:T(8,128)(2,1)}) %all-gather.13.cloned.1.call-update) | async-done | bytes 4194320 | tf_op jit(solution)/shard_map/all_gather | solution.py:220
  253.8 21.7 %all_to_all.98 = bf16[8,18,2048]{2,1,0:T(8,128)(2,1)S(1)} all-to-all(bf16[8,18,2048]{2,1,0:T(8,128)(2,1)S(1)} %broadcast_select_fusion.1), channel_id=1, replica_groups=mesh['grp'=8,'sub'=8,'expert'=2] {'grp'}, dimensions={0} | all-to-all | bytes 1179648 | tf_op jit(solution)/shard_map/all_to_all | solution.py:156
  291.4 53.0 %all-gather.15.cloned.1.call-done = bf16[8192,256]{0,1:T(8,128)(2,1)} async-done(((bf16[1024,256]{0,1:T(8,128)(2,1)}), bf16[8192,256]{0,1:T(8,128)(2,1)}) %all-gather.15.cloned.1.call-update) | async-done | bytes 4194320 | tf_op jit(solution)/shard_map/all_gather | solution.py:241
  357.2 69.8 %all-gather.17.cloned.1.call-done = bf16[128,18,2048]{2,0,1:T(8,128)(2,1)} async-done(((bf16[8,18,2048]{2,0,1:T(8,128)(2,1)}), bf16[128,18,2048]{2,0,1:T(8,128)(2,1)}) %all-gather.17.cloned.1.call-update) | async-done | bytes 9437200 | tf_op jit(solution)/shard_map/all_gather | solution.py:157
  427.0 11.8 copy.573
  460.1 35.0 %while.29 = (s32[]{:T(128)}, bf16[8,288,1,128]{3,1,2,0:T(8,128)(2,1)}, f32[8,1,288,1]{2,3,1,0:T(1,128)}, bf16[8,1024,1,128]{3,1,2,0:T(8,128)(2,1)}, s32[8,288]{1...) while((s32[]{:T(128)}, ...), condition=%wide.region_11.12_spmd.clone, body=%wide.region_8.11_spmd.clone.sunk | while | flops 153693920 | bytes 4236389 | solution.py:287
  509.6 105.2 %all-to-all-done.1 = bf16[16,144,2048]{2,1,0:T(8,128)(2,1)} async-done(((bf16[16,144,2048]{2,1,0:T(8,128)(2,1)}), bf16[16,144,2048]{2,1,0:T(8,128)(2,1)}, u32[]{:S(2)}, u32[]{:S(2)}) %all-to-all-start.1) | async-done | bytes 9437216 | tf_op jit(solution)/shard_map/all_to_all | solution.py:160
  631.5 17.7 all-to-all-done.2
  660.5 13.7 all_to_all.99
  675.3 79.5 %all-gather.19.cloned.1.call-done = bf16[128,18,2048]{2,0,1:T(8,128)(2,1)} async-done(((bf16[8,18,2048]{2,0,1:T(8,128)(2,1)}), bf16[128,18,2048]{2,0,1:T(8,128)(2,1)}) %all-gather.19.cloned.1.call-update) | async-done | bytes 9437200 | tf_op jit(solution)/shard_map/all_gather | solution.py:157
  754.8 13.8 copy.595
  768.6 14.2 reshape.829
  782.7 7.5 fusion.135
  795.8 7.5 convolution_convert_fusion.2
  810.2 104.3 %all-to-all-done.4 = bf16[16,144,2048]{2,1,0:T(8,128)(2,1)} async-done(((bf16[16,144,2048]{2,1,0:T(8,128)(2,1)}), bf16[16,144,2048]{2,1,0:T(8,128)(2,1)}, u32[]{:S(2)}, u32[]{:S(2)}) %all-to-all-start.4) | async-done | bytes 9437216 | tf_op jit(solution)/shard_map/all_to_all | solution.py:160
  914.5 5.9 convert_reduce_fusion.2
  931.6 17.5 all-to-all-done.5
  960.3 13.6 all_to_all.100
  975.1 79.3 %all-gather.21.cloned.1.call-done = bf16[128,18,2048]{2,0,1:T(8,128)(2,1)} async-done(((bf16[8,18,2048]{2,0,1:T(8,128)(2,1)}), bf16[128,18,2048]{2,0,1:T(8,128)(2,1)}) %all-gather.21.cloned.1.call-update) | async-done | bytes 9437200 | tf_op jit(solution)/shard_map/all_gather | solution.py:157
  1054.4 13.8 copy.609
  1068.2 14.0 reshape.833
  1082.2 11.8 multiply_convert_fusion.1
  1094.1 9.2 fusion.136
  1103.3 9.1 add_convert_fusion
  1112.4 110.0 %all_to_all.101 = bf16[16,144,2048]{2,1,0:T(8,128)(2,1)} all-to-all(bf16[16,144,2048]{2,1,0:T(8,128)(2,1)S(1)} %bitcast.261), channel_id=1, replica_groups=mesh['grp'=8,'sub'=8,'expert'=2] {'sub','expert'}, dimensions={0} | all-to-all | bytes 18874368 | tf_op jit(solution)/shard_map/all_to_all | solution.py:160
  1234.8 23.8 %all-to-all-done.8 = f32[8,18,2048]{2,1,0:T(8,128)S(1)} async-done(((f32[8,18,2048]{2,1,0:T(8,128)}), f32[8,18,2048]{2,1,0:T(8,128)S(1)}, u32[]{:S(2)}, u32[]{:S(2)}) %all-to-all-start.8) | async-done | bytes 1179680 | tf_op jit(solution)/shard_map/all_to_all | solution.py:168
  1275.0 13.9 all_to_all.102
  1290.1 75.9 %all-gather.23.cloned.1.call-done = bf16[128,18,2048]{2,0,1:T(8,128)(2,1)} async-done(((bf16[8,18,2048]{2,0,1:T(8,128)(2,1)}), bf16[128,18,2048]{2,0,1:T(8,128)(2,1)}) %all-gather.23.cloned.1.call-update) | async-done | bytes 9437200 | tf_op jit(solution)/shard_map/all_gather | solution.py:157
  1366.0 13.8 copy.617
  1379.8 14.2 reshape.837
  1393.9 6.3 convolution_convert_fusion.4
  1401.4 75.4 %while.30 = (s32[]{:T(128)}, f32[8,288,1,128]{3,1,2,0:T(8,128)S(1)}, bf16[8,1024,1,128]{3,1,0,2:T(8,128)(2,1)}, bf16[8,1024,1,128]{3,1,0,2:T(8,128)(2,1)}, bf16[...) while((s32[]{:T(128)}, ...), condition=%wide.region_35.39_spmd.clone, body=%wide.region_33.38_spmd.clone.sunk | while | flops 380743392 | bytes 12718217 | solution.py:387
  1476.8 35.3 %all_to_all.103 = bf16[128,64,1,128]{3,1,2,0:T(8,128)(2,1)} all-to-all(bf16[128,64,1,128]{3,1,2,0:T(8,128)(2,1)} %bitcast.280), channel_id=1, replica_groups=mesh['grp'=8,'sub'=8,'expert'=2] {'grp','sub','expert'}, dimensions={0} | all-to-all | bytes 4194304 | tf_op jit(solution)/shard_map/all_to_all | solution.py:411
  1530.1 16.9 all-to-all-done.12
  1565.4 92.8 %all-to-all-done.10 = bf16[16,144,2048]{2,1,0:T(8,128)(2,1)} async-done(((bf16[16,144,2048]{2,1,0:T(8,128)(2,1)}), bf16[16,144,2048]{2,1,0:T(8,128)(2,1)}, u32[]{:S(2)}, u32[]{:S(2)}) %all-to-all-start.10) | async-done | bytes 9437216 | tf_op jit(solution)/shard_map/all_to_all | solution.py:160
  1682.9 19.6 %all-to-all-done.11 = f32[8,18,2048]{2,1,0:T(8,128)} async-done(((f32[8,18,2048]{2,1,0:T(8,128)}), f32[8,18,2048]{2,1,0:T(8,128)}, u32[]{:S(2)}, u32[]{:S(2)}) %all-to-all-start.11) | async-done | bytes 1179680 | tf_op jit(solution)/shard_map/all_to_all | solution.py:168
  1707.4 9.2 convolution_add_fusion.2
  1720.9 14.1 reshape.849
  1735.0 9.5 fusion.142
  1744.5 9.0 fusion.144
  1758.7 22.6 %all_gather.36 = bf16[128,2048]{1,0:T(8,128)(2,1)} all-gather(bf16[64,2048]{1,0:T(8,128)(2,1)S(1)} %copy-done.33), channel_id=1, replica_groups=mesh['grp'=8,'sub'=8,'expert'=2] {'expert'}, dimensions={0}, use_global_device_ids=true | all-gather | bytes 786432 | tf_op jit(solution)/shard_map/all_gather | solution.py:480
  1795.1 8.0 all-to-all-start.15
  1803.3 13.5 all_gather.39
  (598 shorter events, 389.3 us)
Async XLA Ops:
  7.2 788.7 %copy-start = (bf16[352,2048]{1,0:T(8,128)(2,1)S(1)}, bf16[352,2048]{1,0:T(8,128)(2,1)}, u32[]{:S(2)}) copy-start(bf16[352,2048]{1,0:T(8,128)(2,1)} %param.35) | copy-start | bytes 4325380
  7.2 47.9 %all-gather.9.cloned.1.call-start = ((), (), s32[]{:S(2)}) async-start(), calls=%async_computation.17 | async-start | bytes 1216512 | tf_op jit(solution)/shard_map/all_gather | solution.py:205
  8.8 621.9 %copy-start.53 = (s32[64,2]{0,1:T(2,128)}, s32[64,2]{0,1:T(2,128)S(1)}, u32[]{:S(2)}) copy-start(s32[64,2]{0,1:T(2,128)S(1)} %get-tuple-element.492) | copy-start | bytes 1540
  14.9 40.3 %copy-start.21 = (bf16[128,2048]{1,0:T(8,128)(2,1)S(1)}, bf16[128,2048]{1,0:T(8,128)(2,1)}, u32[]{:S(2)}) copy-start(bf16[128,2048]{1,0:T(8,128)(2,1)} %param.25) | copy-start | bytes 1572868
  17.8 156.7 %all-gather.11.cloned.1.call-start = ((), (), s32[]{:S(2)}) async-start(), calls=%async_computation.18 | async-start | bytes 18382848 | tf_op jit(solution)/shard_map/all_gather | solution.py:204
  55.1 188.1 %all-gather.13.cloned.1.call-start = ((), (), s32[]{:S(2)}) async-start(), calls=%async_computation.19 | async-start | bytes 4456448 | tf_op jit(solution)/shard_map/all_gather | solution.py:220
  55.4 133.8 %copy-start.67 = (f32[64]{0:T(128)}, f32[64]{0:T(128)S(1)}, u32[]{:S(2)}) copy-start(f32[64]{0:T(128)S(1)} %add_rsqrt_fusion.1) | copy-start | bytes 772
  189.1 9.3 copy-start.42
  190.0 154.4 %all-gather.15.cloned.1.call-start = ((), (), s32[]{:S(2)}) async-start(), calls=%async_computation.20 | async-start | bytes 4718592 | tf_op jit(solution)/shard_map/all_gather | solution.py:241
  190.1 261.5 %copy-start.65 = (f32[64]{0:T(128)}, f32[64]{0:T(128)S(1)}, u32[]{:S(2)}) copy-start(f32[64]{0:T(128)S(1)} %multiply_exponential_fusion) | copy-start | bytes 772
  248.8 178.1 %all-gather.17.cloned.1.call-start = ((), (), s32[]{:S(2)}) async-start(), calls=%async_computation.21 | async-start | bytes 10027008 | tf_op jit(solution)/shard_map/all_gather | solution.py:157
  291.3 160.3 %copy-start.46 = (f32[2304]{0:T(1024)}, f32[2304]{0:T(1024)S(1)}, u32[]{:S(2)}) copy-start(f32[2304]{0:T(1024)S(1)} %fusion.110) | copy-start | bytes 27652
  357.2 81.6 %copy-start.36 = (bf16[2048,128]{1,0:T(8,128)(2,1)S(1)}, bf16[2048,128]{1,0:T(8,128)(2,1)}, u32[]{:S(2)}) copy-start(bf16[2048,128]{1,0:T(8,128)(2,1)} %param.29) | copy-start | bytes 1572868
  503.9 110.8 %all-to-all-start.1 = ((bf16[16,144,2048]{2,1,0:T(8,128)(2,1)}), bf16[16,144,2048]{2,1,0:T(8,128)(2,1)}, u32[]{:S(2)}, u32[]{:S(2)}) async-start(bf16[16,144,2048]{2,1,0:T(8,128)(2,1)} %bitcast.263), calls=%async_computation.1 | async-start | bytes 18874368 | tf_op jit(solution)/shard_map/all_to_all | solution.py:160
  621.9 27.2 %all-to-all-start.2 = ((f32[8,18,2048]{2,1,0:T(8,128)}), f32[8,18,2048]{2,1,0:T(8,128)}, u32[]{:S(2)}, u32[]{:S(2)}) async-start(f32[8,18,2048]{2,1,0:T(8,128)} %reshape.827), calls=%async_computation.2 | async-start | bytes 3145728 | tf_op jit(solution)/shard_map/all_to_all | solution.py:168
  626.2 128.6 %all-gather.19.cloned.1.call-start = ((), (), s32[]{:S(2)}) async-start(), calls=%async_computation.22 | async-start | bytes 10027008 | tf_op jit(solution)/shard_map/all_gather | solution.py:157
  627.8 22.9 %copy-start.31 = (s32[1024]{0:T(1024)}, s32[1024]{0:T(1024)S(1)}, u32[]{:S(2)}) copy-start(s32[1024]{0:T(1024)S(1)} %pad_clamp_fusion.2) | copy-start | bytes 12292
  631.4 21.3 %copy-start.63 = (f32[64,2]{0,1:T(2,128)}, f32[64,2]{0,1:T(2,128)S(1)}, u32[]{:S(2)}) copy-start(f32[64,2]{0,1:T(2,128)S(1)} %get-tuple-element.488) | copy-start | bytes 1540
  768.5 14.2 copy-start.27
  803.3 111.2 %all-to-all-start.4 = ((bf16[16,144,2048]{2,1,0:T(8,128)(2,1)}), bf16[16,144,2048]{2,1,0:T(8,128)(2,1)}, u32[]{:S(2)}, u32[]{:S(2)}) async-start(bf16[16,144,2048]{2,1,0:T(8,128)(2,1)} %bitcast.268), calls=%async_computation.4 | async-start | bytes 18874368 | tf_op jit(solution)/shard_map/all_to_all | solution.py:160
  921.7 27.4 %all-to-all-start.5 = ((f32[8,18,2048]{2,1,0:T(8,128)}), f32[8,18,2048]{2,1,0:T(8,128)}, u32[]{:S(2)}, u32[]{:S(2)}) async-start(f32[8,18,2048]{2,1,0:T(8,128)} %reshape.831), calls=%async_computation.5 | async-start | bytes 3145728 | tf_op jit(solution)/shard_map/all_to_all | solution.py:168
  926.2 128.2 %all-gather.21.cloned.1.call-start = ((), (), s32[]{:S(2)}) async-start(), calls=%async_computation.23 | async-start | bytes 10027008 | tf_op jit(solution)/shard_map/all_gather | solution.py:157
  1082.2 11.9 copy-start.28
  1229.6 29.0 %all-to-all-start.8 = ((f32[8,18,2048]{2,1,0:T(8,128)}), f32[8,18,2048]{2,1,0:T(8,128)S(1)}, u32[]{:S(2)}, u32[]{:S(2)}) async-start(f32[8,18,2048]{2,1,0:T(8,128)} %reshape.835), calls=%async_computation.8 | async-start | bytes 3145728 | tf_op jit(solution)/shard_map/all_to_all | solution.py:168
  1234.5 131.6 %all-gather.23.cloned.1.call-start = ((), (), s32[]{:S(2)}) async-start(), calls=%async_computation.24 | async-start | bytes 10027008 | tf_op jit(solution)/shard_map/all_gather | solution.py:157
  1379.8 14.2 copy-start.35
  1512.1 34.9 %all-to-all-start.12 = ((bf16[128,64,1,128]{3,1,2,0:T(8,128)(2,1)}), bf16[128,64,1,128]{3,1,2,0:T(8,128)(2,1)}, u32[]{:S(2)}, u32[]{:S(2)}) async-start(bf16[128,64,1,128]{3,1,2,0:T(8,128)(2,1)} %bitcast.281), calls=%async_computation.12 | async-start | bytes 4194304 | tf_op jit(solution)/shard_map/all_to_all | solution.py:404
  1547.0 111.2 %all-to-all-start.10 = ((bf16[16,144,2048]{2,1,0:T(8,128)(2,1)}), bf16[16,144,2048]{2,1,0:T(8,128)(2,1)}, u32[]{:S(2)}, u32[]{:S(2)}) async-start(bf16[16,144,2048]{2,1,0:T(8,128)(2,1)} %bitcast.262), calls=%async_computation.10 | async-start | bytes 18874368 | tf_op jit(solution)/shard_map/all_to_all | solution.py:160
  1658.2 15.4 all-to-all-start.14
  1673.6 28.9 %all-to-all-start.11 = ((f32[8,18,2048]{2,1,0:T(8,128)}), f32[8,18,2048]{2,1,0:T(8,128)}, u32[]{:S(2)}, u32[]{:S(2)}) async-start(f32[8,18,2048]{2,1,0:T(8,128)} %reshape.842), calls=%async_computation.11 | async-start | bytes 3145728 | tf_op jit(solution)/shard_map/all_to_all | solution.py:168
  1677.9 115.3 %reduce-scatter.2.cloned.1.call-start = ((), (), s32[]{:S(2)}) async-start(), calls=%async_computation.25 | async-start | bytes 3538944 | tf_op jit(solution)/shard_map/reduce_scatter | solution.py:465
  1682.9 21.1 %copy-start.32 = (s32[1024]{0:T(1024)S(1)}, s32[1024]{0:T(1024)}, u32[]{:S(2)}) copy-start(s32[1024]{0:T(1024)} %copy-done.31) | copy-start | bytes 12292
  1707.3 9.2 copy-start.22
  1707.3 9.2 copy-start.43
  1707.4 11.5 copy-start.40
  1707.4 11.4 copy-start.41
  1707.4 11.4 copy-start.60
  1735.0 9.5 copy-start.18
  1735.0 18.5 %slice-start.3 = ((s8[9437184]{0:T(1024)(128)(4,1)}), s8[4194304]{0:T(1024)(128)(4,1)S(1)}, s32[]{:S(2)}) async-start(s8[9437184]{0:T(1024)(128)(4,1)} %bitcast.269), calls=%async_computation.29 | async-start | bytes 8388608
  1735.0 18.5 %slice-start.4 = ((s8[9437184]{0:T(1024)(128)(4,1)}), s8[4194304]{0:T(1024)(128)(4,1)S(1)}, s32[]{:S(2)}) async-start(s8[9437184]{0:T(1024)(128)(4,1)} %bitcast.269), calls=%async_computation.30 | async-start | bytes 8388608
  1744.5 36.8 %slice-start = ((s8[9437184]{0:T(1024)(128)(4,1)}), s8[4194304]{0:T(1024)(128)(4,1)S(1)}, s32[]{:S(2)}) async-start(s8[9437184]{0:T(1024)(128)(4,1)} %bitcast.259), calls=%async_computation.26 | async-start | bytes 8388608
  1744.5 36.8 %slice-start.1 = ((s8[9437184]{0:T(1024)(128)(4,1)}), s8[4194304]{0:T(1024)(128)(4,1)S(1)}, s32[]{:S(2)}) async-start(s8[9437184]{0:T(1024)(128)(4,1)} %bitcast.259), calls=%async_computation.27 | async-start | bytes 8388608
  1753.6 27.7 %slice-start.2 = ((s8[9437184]{0:T(1024)(128)(4,1)}), s8[1048576]{0:T(1024)(128)(4,1)S(1)}, s32[]{:S(2)}) async-start(s8[9437184]{0:T(1024)(128)(4,1)} %bitcast.259), calls=%async_computation.28 | async-start | bytes 2097152
  1753.6 27.7 %copy-start.9 = (bf16[2304,128]{1,0:T(8,128)(2,1)S(1)}, bf16[2304,128]{1,0:T(8,128)(2,1)}, u32[]{:S(2)}) copy-start(bf16[2304,128]{1,0:T(8,128)(2,1)} %copy-done.8) | copy-start | bytes 1769476
  1753.6 30.1 %slice-start.6 = ((s8[9437184]{0:T(1024)(128)(4,1)}), s8[1048576]{0:T(1024)(128)(4,1)S(1)}, s32[]{:S(2)}) async-start(s8[9437184]{0:T(1024)(128)(4,1)} %bitcast.271), calls=%async_computation.32 | async-start | bytes 2097152
  1753.6 30.1 %slice-start.7 = ((s8[9437184]{0:T(1024)(128)(4,1)}), s8[4194304]{0:T(1024)(128)(4,1)S(1)}, s32[]{:S(2)}) async-start(s8[9437184]{0:T(1024)(128)(4,1)} %bitcast.271), calls=%async_computation.33 | async-start | bytes 8388608
  1795.1 21.7 %all-to-all-start.15 = ((f32[16,16,384]{2,1,0:T(8,128)}), f32[16,16,384]{2,1,0:T(8,128)}, u32[]{:S(2)}, u32[]{:S(2)}) async-start(f32[16,16,384]{2,1,0:T(8,128)} %bitcast.49), calls=%async_computation.16 | async-start | bytes 786432 | tf_op jit(solution)/shard_map/all_to_all | solution.py:466
  1803.1 21.1 %copy-start.1 = (bf16[352,2048]{1,0:T(8,128)(2,1)S(1)}, bf16[352,2048]{1,0:T(8,128)(2,1)}, u32[]{:S(2)}) copy-start(bf16[352,2048]{1,0:T(8,128)(2,1)} %param.35) | copy-start | bytes 4325380
  (52 other events, 212.0 us)
Sparse Core Ops, SparseCore 0:
  17.9 37.1 all-gather.8
  57.6 116.8 all-gather.10
  190.1 53.0 all-gather.12
  248.9 95.4 all-gather.14
  347.4 79.5 all-gather.16
  675.4 79.2 all-gather.18
  975.2 79.1 all-gather.20
  1290.2 75.7 all-gather.22
  1721.0 72.1 reduce-scatter.1

commit v5 on v4

--- a/solution.py
+++ b/solution.py
@@ -154,7 +154,9 @@
 
     def dispatch(slot_values):
         by_group = lax.all_to_all(slot_values, "grp", split_axis=0, concat_axis=0, tiled=True)
-        return lax.all_gather(by_group, GROUP_AXES, axis=0, tiled=True).reshape(slot_rows, width)
+        return lax.all_gather(
+            by_group.reshape(groups * slot_cap, width), GROUP_AXES, axis=0, tiled=True
+        )
 
     def combine(partial_value):
         parts = lax.all_to_all(
@@ -476,10 +478,15 @@
     gain_two_grad = extra_grad[:, 1]
     attn_router_grad = extra_grad[:, 2 : 2 + EXPERTS]
     mlp_router_grad = extra_grad[:, 2 + EXPERTS : 2 + 2 * EXPERTS]
-    mixed_full, input_full = (
-        lax.all_gather(own_output.astype(jnp.bfloat16), "expert", axis=0, tiled=True),
-        lax.all_gather(input_grad.astype(jnp.bfloat16), "expert", axis=0, tiled=True),
-    )
+    both_full = lax.all_gather(
+        jnp.concatenate(
+            [own_output.astype(jnp.bfloat16), input_grad.astype(jnp.bfloat16)], axis=1
+        ),
+        "expert",
+        axis=0,
+        tiled=True,
+    )
+    mixed_full, input_full = both_full[:, :width], both_full[:, width:]
     return (
         mixed_full,
         input_full,

time: 1840 us -> 1750 us (0.951)
  local copies, waits for them, and re-layouts: 267 us -> 149 us
  waiting for transfers between devices: 965 us -> 1010 us
  blocking collectives: 244 us -> 208 us
  matrix products: 207 us -> 226 us
    all_gather x4 -> x0, local copies, waits for them, and re-layouts: 53.1 us -> none  [dispatch(): lax.all_gather(by_group, GROUP_AXES, axis=0, tiled=True)]
    reshape x4, local copies, waits for them, and re-layouts: 56.5 us -> 3.98 us  [dispatch(): by_group.reshape(groups * slot_cap, width)]
    all_gather x2 -> x0, blocking collectives: 36.1 us -> none  [the longest x1 22.6 us: shards(): lax.all_gather(own_output.astype(jnp.bfloat16), 'expert', axis=0, tiled=T...]
    reduce_scatter x1, waiting for transfers between devices: 5.75 us -> 27.6 us  [shards(): lax.psum_scatter(packed_grad, 'grp', scatter_dimension=0, tiled=True)]
    all_gather x4 -> x5, waiting for transfers between devices: 304 us -> 324 us  [the longest x4 304 us: dispatch(): lax.all_gather(by_group.reshape(groups * slot_cap, width), GROUP_AXES, ax...]
  transfers between devices with their start and end apart: 19 -> 20, of which waited for: 18 -> 19; matrix products, arithmetic and copies ran while one was open for 7% -> 8% of each run, Pallas kernels for 0% -> 0%
where the time goes in v5:
time: 1750 us; the launch traced here: 1740 us
  waiting for transfers between devices  1010 us (58%)
  matrix products  226 us (13%)
  blocking collectives  208 us (12%)
  local copies, waits for them, and re-layouts  149 us (9%)
  other arithmetic  77 us (4%)
  starting transfers between devices  52.3 us (3%)
    all_to_all x3, waiting for transfers between devices, combine(): lax.all_to_all(partial_value.astype(jnp.bfloat16).reshape(group_size, gro...  304 us
    all_gather x4, waiting for transfers between devices, dispatch(): lax.all_gather(by_group.reshape(groups * slot_cap, width), GROUP_AXES, ax...  304 us
    all_gather x1, waiting for transfers between devices, shards(): lax.all_gather(lax.all_gather(packed, 'grp', axis=0, tiled=True), GROUP_A...  119 us
    all_to_all x1, blocking collectives, combine(): lax.all_to_all(partial_value.astype(jnp.bfloat16).reshape(group_size, gro...  110 us
    all_to_all x4, waiting for transfers between devices, combine(): lax.all_to_all(summed, 'grp', split_axis=0, concat_axis=0, tiled=True)  77.4 us
    all_to_all x4, blocking collectives, dispatch(): lax.all_to_all(slot_values, 'grp', split_axis=0, concat_axis=0, tiled=True)  63.3 us
    all_gather x1, waiting for transfers between devices, shards(): all_pairs = lax.all_gather(seq_pair, 'grp', axis=0, tiled=True)  53.9 us
    all_gather x1, waiting for transfers between devices, shards(): seq_input = lax.all_gather(attn_input, GROUP_AXES, axis=0, tiled=True)  44.5 us
  transfers between devices with their start and end apart: 20, of which 19 were waited for; matrix products, arithmetic and copies ran while one was open for 8% of the time, Pallas kernels for 0%

profile of v5, /device:TPU:1, one launch (start us, length us, event | category | flops | bytes accessed | tf_op | source)
XLA Modules:
  0.0 1736.1 jit_solution(9840756600424994361)
XLA Ops:
  14.0 37.3 %all-gather.10.cloned.1.call-done = bf16[128,4224]{1,0:T(8,128)(2,1)} async-done(((bf16[16,4224]{1,0:T(8,128)(2,1)}), bf16[128,4224]{1,0:T(8,128)(2,1)}) %all-gather.10.cloned.1.call-update) | async-done | bytes 1081360 | tf_op jit(solution)/shard_map/all_gather | solution.py:207
  51.5 119.1 %all-gather.12.cloned.1.call-done = bf16[2048,4224]{1,0:T(8,128)(2,1)} async-done(((bf16[128,4224]{1,0:T(8,128)(2,1)}), bf16[2048,4224]{1,0:T(8,128)(2,1)}) %all-gather.12.cloned.1.call-update) | async-done | bytes 17301520 | tf_op jit(solution)/shard_map/all_gather | solution.py:206
  170.7 8.1 copy.512
  178.8 5.9 copy-done.4
  186.3 8.3 slice.147
  194.8 44.5 %all-gather.14.cloned.1.call-done = bf16[1024,2048]{1,0:T(8,128)(2,1)} async-done(((bf16[64,2048]{1,0:T(8,128)(2,1)}), bf16[1024,2048]{1,0:T(8,128)(2,1)}) %all-gather.14.cloned.1.call-update) | async-done | bytes 4194320 | tf_op jit(solution)/shard_map/all_gather | solution.py:222
  247.9 22.8 %all_to_all.98 = bf16[8,18,2048]{2,1,0:T(8,128)(2,1)S(1)} all-to-all(bf16[8,18,2048]{2,1,0:T(8,128)(2,1)S(1)} %broadcast_select_fusion.1), channel_id=1, replica_groups=mesh['grp'=8,'sub'=8,'expert'=2] {'grp'}, dimensions={0} | all-to-all | bytes 1179648 | tf_op jit(solution)/shard_map/all_to_all | solution.py:156
  286.6 53.9 %all-gather.16.cloned.1.call-done = bf16[8192,256]{0,1:T(8,128)(2,1)} async-done(((bf16[1024,256]{0,1:T(8,128)(2,1)}), bf16[8192,256]{0,1:T(8,128)(2,1)}) %all-gather.16.cloned.1.call-update) | async-done | bytes 4194320 | tf_op jit(solution)/shard_map/all_gather | solution.py:243
  353.4 69.1 %all-gather.18.cloned.1.call-done = bf16[2304,2048]{1,0:T(8,128)(2,1)} async-done(((bf16[144,2048]{1,0:T(8,128)(2,1)}), bf16[2304,2048]{1,0:T(8,128)(2,1)}) %all-gather.18.cloned.1.call-update) | async-done | bytes 9437200 | tf_op jit(solution)/shard_map/all_gather | solution.py:157
  422.5 7.3 fusion.135
  445.0 35.3 %while.29 = (s32[]{:T(128)}, bf16[8,288,1,128]{3,1,2,0:T(8,128)(2,1)}, f32[8,1,288,1]{2,3,1,0:T(1,128)}, bf16[8,1024,1,128]{3,1,2,0:T(8,128)(2,1)}, s32[8,288]{1...) while((s32[]{:T(128)}, ...), condition=%wide.region_11.12_spmd.clone, body=%wide.region_8.11_spmd.clone.sunk | while | flops 153693920 | bytes 4236889 | solution.py:289
  481.9 6.5 convolution_convert_fusion.3
  494.2 105.1 %all-to-all-done.1 = bf16[16,144,2048]{2,1,0:T(8,128)(2,1)} async-done(((bf16[16,144,2048]{2,1,0:T(8,128)(2,1)}), bf16[16,144,2048]{2,1,0:T(8,128)(2,1)}, u32[]{:S(2)}, u32[]{:S(2)}) %all-to-all-start.1) | async-done | bytes 9437216 | tf_op jit(solution)/shard_map/all_to_all | solution.py:162
  599.2 5.9 convert_reduce_fusion.3
  615.3 18.4 %all-to-all-done.2 = f32[8,18,2048]{2,1,0:T(8,128)} async-done(((f32[8,18,2048]{2,1,0:T(8,128)}), f32[8,18,2048]{2,1,0:T(8,128)}, u32[]{:S(2)}, u32[]{:S(2)}) %all-to-all-start.2) | async-done | bytes 1179680 | tf_op jit(solution)/shard_map/all_to_all | solution.py:170
  645.1 13.4 all_to_all.99
  659.6 79.4 %all-gather.20.cloned.1.call-done = bf16[2304,2048]{1,0:T(8,128)(2,1)} async-done(((bf16[144,2048]{1,0:T(8,128)(2,1)}), bf16[2304,2048]{1,0:T(8,128)(2,1)}) %all-gather.20.cloned.1.call-update) | async-done | bytes 9437200 | tf_op jit(solution)/shard_map/all_gather | solution.py:157
  739.0 7.5 fusion.136
  752.0 7.5 convolution_convert_fusion.2
  765.9 104.4 %all-to-all-done.4 = bf16[16,144,2048]{2,1,0:T(8,128)(2,1)} async-done(((bf16[16,144,2048]{2,1,0:T(8,128)(2,1)}), bf16[16,144,2048]{2,1,0:T(8,128)(2,1)}, u32[]{:S(2)}, u32[]{:S(2)}) %all-to-all-start.4) | async-done | bytes 9437216 | tf_op jit(solution)/shard_map/all_to_all | solution.py:162
  870.3 5.9 convert_reduce_fusion.2
  887.8 17.0 all-to-all-done.5
  916.0 13.2 all_to_all.100
  930.3 79.4 %all-gather.22.cloned.1.call-done = bf16[2304,2048]{1,0:T(8,128)(2,1)} async-done(((bf16[144,2048]{1,0:T(8,128)(2,1)}), bf16[2304,2048]{1,0:T(8,128)(2,1)}) %all-gather.22.cloned.1.call-update) | async-done | bytes 9437200 | tf_op jit(solution)/shard_map/all_gather | solution.py:157
  1009.7 11.8 multiply_convert_fusion.1
  1021.6 9.1 fusion.137
  1030.8 9.1 add_convert_fusion
  1039.8 109.5 %all_to_all.101 = bf16[16,144,2048]{2,1,0:T(8,128)(2,1)} all-to-all(bf16[16,144,2048]{2,1,0:T(8,128)(2,1)S(1)} %bitcast.253), channel_id=1, replica_groups=mesh['grp'=8,'sub'=8,'expert'=2] {'sub','expert'}, dimensions={0} | all-to-all | bytes 18874368 | tf_op jit(solution)/shard_map/all_to_all | solution.py:162
  1149.4 5.9 convert_reduce_fusion.1
  1161.9 23.7 %all-to-all-done.8 = f32[8,18,2048]{2,1,0:T(8,128)S(1)} async-done(((f32[8,18,2048]{2,1,0:T(8,128)}), f32[8,18,2048]{2,1,0:T(8,128)S(1)}, u32[]{:S(2)}, u32[]{:S(2)}) %all-to-all-start.8) | async-done | bytes 1179680 | tf_op jit(solution)/shard_map/all_to_all | solution.py:170
  1201.6 13.8 all_to_all.102
  1216.5 75.9 %all-gather.24.cloned.1.call-done = bf16[2304,2048]{1,0:T(8,128)(2,1)} async-done(((bf16[144,2048]{1,0:T(8,128)(2,1)}), bf16[2304,2048]{1,0:T(8,128)(2,1)}) %all-gather.24.cloned.1.call-update) | async-done | bytes 9437200 | tf_op jit(solution)/shard_map/all_gather | solution.py:157
  1292.4 6.3 convolution_convert_fusion.4
  1299.8 81.1 %while.30 = (s32[]{:T(128)}, f32[8,288,1,128]{3,1,2,0:T(8,128)}, bf16[8,1024,1,128]{3,1,0,2:T(8,128)(2,1)}, bf16[8,1024,1,128]{3,1,0,2:T(8,128)(2,1)}, bf16[8,10...) while((s32[]{:T(128)}, f32[8,288,1,128]{3,1,2,0:T(8,128)}, ...), condition=%wide.region_35.39_spmd.clone, body=%wide.region_33.38_spmd.clone.sunk | while | flops 380743392 | bytes 12719733 | solution.py:389
  1381.0 35.3 %all_to_all.103 = bf16[128,64,1,128]{3,1,2,0:T(8,128)(2,1)} all-to-all(bf16[128,64,1,128]{3,1,2,0:T(8,128)(2,1)} %bitcast.267), channel_id=1, replica_groups=mesh['grp'=8,'sub'=8,'expert'=2] {'grp','sub','expert'}, dimensions={0} | all-to-all | bytes 4194304 | tf_op jit(solution)/shard_map/all_to_all | solution.py:406
  1429.2 6.0 convolution_convert_fusion.1
  1435.2 16.0 all-to-all-done.13
  1467.6 94.6 %all-to-all-done.10 = bf16[16,144,2048]{2,1,0:T(8,128)(2,1)} async-done(((bf16[16,144,2048]{2,1,0:T(8,128)(2,1)}), bf16[16,144,2048]{2,1,0:T(8,128)(2,1)}, u32[]{:S(2)}, u32[]{:S(2)}) %all-to-all-start.10) | async-done | bytes 9437216 | tf_op jit(solution)/shard_map/all_to_all | solution.py:162
  1567.1 5.9 convert_reduce_fusion
  1588.3 18.4 %all-to-all-done.11 = f32[8,18,2048]{2,1,0:T(8,128)} async-done(((f32[8,18,2048]{2,1,0:T(8,128)}), f32[8,18,2048]{2,1,0:T(8,128)}, u32[]{:S(2)}, u32[]{:S(2)}) %all-to-all-start.11) | async-done | bytes 1179680 | tf_op jit(solution)/shard_map/all_to_all | solution.py:170
  1613.6 9.6 convolution_add_fusion.2
  1627.9 9.4 fusion.143
  1637.3 9.1 fusion.144
  1652.6 6.1 fusion.142
  1658.7 7.4 fusion.141
  1666.1 27.6 %reduce-scatter.2.cloned.1.call-done = f32[256,384]{0,1:T(8,128)} async-done(((f32[2048,384]{0,1:T(8,128)}), f32[256,384]{0,1:T(8,128)}) %reduce-scatter.2.cloned.1.call-update) | async-done | bytes 393232 | tf_op jit(solution)/shard_map/reduce_scatter | solution.py:467
  1695.7 8.3 all-to-all-start.15
  1704.0 20.0 %all-gather.26.cloned.1.call-done = bf16[128,4096]{1,0:T(8,128)(2,1)} async-done(((bf16[64,4096]{1,0:T(8,128)(2,1)}), bf16[128,4096]{1,0:T(8,128)(2,1)}) %all-gather.26.cloned.1.call-update) | async-done | bytes 1048592 | tf_op jit(solution)/shard_map/all_gather | solution.py:481
  (558 shorter events, 340.7 us)
Async XLA Ops:
  7.2 744.8 %copy-start = (bf16[352,2048]{1,0:T(8,128)(2,1)S(1)}, bf16[352,2048]{1,0:T(8,128)(2,1)}, u32[]{:S(2)}) copy-start(bf16[352,2048]{1,0:T(8,128)(2,1)} %param.35) | copy-start | bytes 4325380
  7.2 44.1 %all-gather.10.cloned.1.call-start = ((), (), s32[]{:S(2)}) async-start(), calls=%async_computation.17 | async-start | bytes 1216512 | tf_op jit(solution)/shard_map/all_gather | solution.py:207
  11.3 40.1 %copy-start.17 = (bf16[128,2048]{1,0:T(8,128)(2,1)S(1)}, bf16[128,2048]{1,0:T(8,128)(2,1)}, u32[]{:S(2)}) copy-start(bf16[128,2048]{1,0:T(8,128)(2,1)} %param.25) | copy-start | bytes 1572868
  13.9 156.7 %all-gather.12.cloned.1.call-start = ((), (), s32[]{:S(2)}) async-start(), calls=%async_computation.18 | async-start | bytes 18382848 | tf_op jit(solution)/shard_map/all_gather | solution.py:206
  51.3 188.0 %all-gather.14.cloned.1.call-start = ((), (), s32[]{:S(2)}) async-start(), calls=%async_computation.19 | async-start | bytes 4456448 | tf_op jit(solution)/shard_map/all_gather | solution.py:222
  51.5 133.7 %copy-start.52 = (f32[64]{0:T(128)}, f32[64]{0:T(128)S(1)}, u32[]{:S(2)}) copy-start(f32[64]{0:T(128)S(1)} %add_rsqrt_fusion.1) | copy-start | bytes 772
  185.3 9.3 copy-start.35
  186.1 154.4 %all-gather.16.cloned.1.call-start = ((), (), s32[]{:S(2)}) async-start(), calls=%async_computation.20 | async-start | bytes 4718592 | tf_op jit(solution)/shard_map/all_gather | solution.py:243
  186.2 252.3 %copy-start.50 = (f32[64]{0:T(128)}, f32[64]{0:T(128)S(1)}, u32[]{:S(2)}) copy-start(f32[64]{0:T(128)S(1)} %multiply_exponential_fusion) | copy-start | bytes 772
  245.0 177.6 %all-gather.18.cloned.1.call-start = ((), (), s32[]{:S(2)}) async-start(), calls=%async_computation.21 | async-start | bytes 10027008 | tf_op jit(solution)/shard_map/all_gather | solution.py:157
  286.6 152.0 %copy-start.38 = (f32[2304]{0:T(1024)}, f32[2304]{0:T(1024)S(1)}, u32[]{:S(2)}) copy-start(f32[2304]{0:T(1024)S(1)} %fusion.109) | copy-start | bytes 27652
  349.3 73.3 %copy-start.31 = (bf16[2048,128]{1,0:T(8,128)(2,1)S(1)}, bf16[2048,128]{1,0:T(8,128)(2,1)}, u32[]{:S(2)}) copy-start(bf16[2048,128]{1,0:T(8,128)(2,1)} %param.29) | copy-start | bytes 1572868
  480.2 8.2 copy-start.44
  481.9 6.5 copy-start.5
  488.4 110.8 %all-to-all-start.1 = ((bf16[16,144,2048]{2,1,0:T(8,128)(2,1)}), bf16[16,144,2048]{2,1,0:T(8,128)(2,1)}, u32[]{:S(2)}, u32[]{:S(2)}) async-start(bf16[16,144,2048]{2,1,0:T(8,128)(2,1)} %bitcast.255), calls=%async_computation.1 | async-start | bytes 18874368 | tf_op jit(solution)/shard_map/all_to_all | solution.py:162
  606.5 27.2 %all-to-all-start.2 = ((f32[8,18,2048]{2,1,0:T(8,128)}), f32[8,18,2048]{2,1,0:T(8,128)}, u32[]{:S(2)}, u32[]{:S(2)}) async-start(f32[8,18,2048]{2,1,0:T(8,128)} %reshape.829), calls=%async_computation.2 | async-start | bytes 3145728 | tf_op jit(solution)/shard_map/all_to_all | solution.py:170
  610.8 128.3 %all-gather.20.cloned.1.call-start = ((), (), s32[]{:S(2)}) async-start(), calls=%async_computation.22 | async-start | bytes 10027008 | tf_op jit(solution)/shard_map/all_gather | solution.py:157
  610.8 24.5 %copy-start.27 = (s32[1024]{0:T(1024)}, s32[1024]{0:T(1024)S(1)}, u32[]{:S(2)}) copy-start(s32[1024]{0:T(1024)S(1)} %pad_clamp_fusion.2) | copy-start | bytes 12292
  659.6 86.9 %copy-start.25 = (bf16[2048,352]{0,1:T(8,128)(2,1)S(1)}, bf16[2048,352]{0,1:T(8,128)(2,1)}, u32[]{:S(2)}) copy-start(bf16[2048,352]{0,1:T(8,128)(2,1)} %param.34) | copy-start | bytes 4325380
  739.0 7.5 copy-start.59
  752.0 7.5 copy-start.61
  759.5 110.8 %all-to-all-start.4 = ((bf16[16,144,2048]{2,1,0:T(8,128)(2,1)}), bf16[16,144,2048]{2,1,0:T(8,128)(2,1)}, u32[]{:S(2)}, u32[]{:S(2)}) async-start(bf16[16,144,2048]{2,1,0:T(8,128)(2,1)} %bitcast.259), calls=%async_computation.4 | async-start | bytes 18874368 | tf_op jit(solution)/shard_map/all_to_all | solution.py:162
  877.5 27.4 %all-to-all-start.5 = ((f32[8,18,2048]{2,1,0:T(8,128)}), f32[8,18,2048]{2,1,0:T(8,128)}, u32[]{:S(2)}, u32[]{:S(2)}) async-start(f32[8,18,2048]{2,1,0:T(8,128)} %reshape.833), calls=%async_computation.5 | async-start | bytes 3145728 | tf_op jit(solution)/shard_map/all_to_all | solution.py:170
  881.9 127.8 %all-gather.22.cloned.1.call-start = ((), (), s32[]{:S(2)}) async-start(), calls=%async_computation.23 | async-start | bytes 10027008 | tf_op jit(solution)/shard_map/all_gather | solution.py:157
  1009.7 11.9 copy-start.24
  1021.6 9.2 copy-start.20
  1021.6 9.2 copy-start.15
  1021.6 9.2 copy-start.26
  1156.6 29.1 %all-to-all-start.8 = ((f32[8,18,2048]{2,1,0:T(8,128)}), f32[8,18,2048]{2,1,0:T(8,128)S(1)}, u32[]{:S(2)}, u32[]{:S(2)}) async-start(f32[8,18,2048]{2,1,0:T(8,128)} %reshape.837), calls=%async_computation.8 | async-start | bytes 3145728 | tf_op jit(solution)/shard_map/all_to_all | solution.py:170
  1161.5 130.9 %all-gather.24.cloned.1.call-start = ((), (), s32[]{:S(2)}) async-start(), calls=%async_computation.24 | async-start | bytes 10027008 | tf_op jit(solution)/shard_map/all_gather | solution.py:157
  1201.6 90.8 %copy-start.30 = (bf16[128,2048]{1,0:T(8,128)(2,1)S(1)}, bf16[128,2048]{1,0:T(8,128)(2,1)}, u32[]{:S(2)}) copy-start(bf16[128,2048]{1,0:T(8,128)(2,1)} %param.30) | copy-start | bytes 1572868
  1416.3 34.9 %all-to-all-start.13 = ((bf16[128,64,1,128]{3,1,2,0:T(8,128)(2,1)}), bf16[128,64,1,128]{3,1,2,0:T(8,128)(2,1)}, u32[]{:S(2)}, u32[]{:S(2)}) async-start(bf16[128,64,1,128]{3,1,2,0:T(8,128)(2,1)} %bitcast.268), calls=%async_computation.13 | async-start | bytes 4194304 | tf_op jit(solution)/shard_map/all_to_all | solution.py:413
  1451.2 110.9 %all-to-all-start.10 = ((bf16[16,144,2048]{2,1,0:T(8,128)(2,1)}), bf16[16,144,2048]{2,1,0:T(8,128)(2,1)}, u32[]{:S(2)}, u32[]{:S(2)}) async-start(bf16[16,144,2048]{2,1,0:T(8,128)(2,1)} %bitcast.254), calls=%async_computation.10 | async-start | bytes 18874368 | tf_op jit(solution)/shard_map/all_to_all | solution.py:162
  1562.2 15.5 all-to-all-start.14
  1577.7 28.9 %all-to-all-start.11 = ((f32[8,18,2048]{2,1,0:T(8,128)}), f32[8,18,2048]{2,1,0:T(8,128)}, u32[]{:S(2)}, u32[]{:S(2)}) async-start(f32[8,18,2048]{2,1,0:T(8,128)} %reshape.844), calls=%async_computation.11 | async-start | bytes 3145728 | tf_op jit(solution)/shard_map/all_to_all | solution.py:170
  1582.0 111.7 %reduce-scatter.2.cloned.1.call-start = ((), (), s32[]{:S(2)}) async-start(), calls=%async_computation.26 | async-start | bytes 3538944 | tf_op jit(solution)/shard_map/reduce_scatter | solution.py:467
  1588.3 19.9 %copy-start.28 = (s32[1024]{0:T(1024)S(1)}, s32[1024]{0:T(1024)}, u32[]{:S(2)}) copy-start(s32[1024]{0:T(1024)} %copy-done.27) | copy-start | bytes 12292
  1613.6 9.6 copy-start.19
  1613.6 9.6 copy-start.36
  1613.6 9.6 copy-start.53
  1627.6 96.4 %all-gather.26.cloned.1.call-start = ((), (), s32[]{:S(2)}) async-start(), calls=%async_computation.25 | async-start | bytes 1572864 | tf_op jit(solution)/shard_map/all_gather | solution.py:481
  1627.8 9.4 copy-start.21
  1627.8 18.5 %slice-start = ((s8[9437184]{0:T(1024)(128)(4,1)}), s8[4194304]{0:T(1024)(128)(4,1)S(1)}, s32[]{:S(2)}) async-start(s8[9437184]{0:T(1024)(128)(4,1)} %bitcast.274), calls=%async_computation.27 | async-start | bytes 8388608
  1627.8 18.5 %slice-start.1 = ((s8[9437184]{0:T(1024)(128)(4,1)}), s8[4194304]{0:T(1024)(128)(4,1)S(1)}, s32[]{:S(2)}) async-start(s8[9437184]{0:T(1024)(128)(4,1)} %bitcast.274), calls=%async_computation.28 | async-start | bytes 8388608
  1637.3 9.1 copy-start.16
  1637.3 9.1 slice-start.2
  1693.7 35.4 %copy-start.1 = (bf16[352,2048]{1,0:T(8,128)(2,1)S(1)}, bf16[352,2048]{1,0:T(8,128)(2,1)}, u32[]{:S(2)}) copy-start(bf16[352,2048]{1,0:T(8,128)(2,1)} %param.35) | copy-start | bytes 4325380
  1695.7 30.5 %all-to-all-start.15 = ((f32[16,16,384]{2,1,0:T(8,128)}), f32[16,16,384]{2,1,0:T(8,128)S(1)}, u32[]{:S(2)}, u32[]{:S(2)}) async-start(f32[16,16,384]{2,1,0:T(8,128)} %bitcast.46), calls=%async_computation.16 | async-start | bytes 786432 | tf_op jit(solution)/shard_map/all_to_all | solution.py:468
  (37 other events, 110.6 us)
Sparse Core Ops, SparseCore 0:
  14.0 37.1 all-gather.9
  53.8 116.8 all-gather.11
  186.3 53.0 all-gather.13
  245.1 95.4 all-gather.15
  343.4 79.0 all-gather.17
  659.7 79.2 all-gather.19
  930.4 79.2 all-gather.21
  1216.6 75.7 all-gather.23
  1627.7 65.9 reduce-scatter.1
  1695.8 28.1 all-gather.25

commit v6 on v5

--- a/solution.py
+++ b/solution.py
@@ -1,8 +1,10 @@
+import functools
 import math
 
 import jax
 import jax.numpy as jnp
 from jax import lax
+from jax.experimental import pallas as pl
 from jax.sharding import PartitionSpec as P
 
 ALL_AXES = ("grp", "sub", "expert")
@@ -18,6 +20,71 @@
 
 epsilon = 1e-06
 masked_score = -1e30
+
+
+def _scores(q, k, qb, scale):
+    s = lax.dot_general(q, k, (((1,), (1,)), ((), ())), preferred_element_type=jnp.float32) * scale
+    kblock = lax.broadcasted_iota(jnp.int32, s.shape, 1) // BLOCK
+    return jnp.where(kblock <= qb, s, masked_score)
+
+def _fwd_kernel(scale, q_ref, k_ref, v_ref, qb_ref, o_ref, lse_ref):
+    s = _scores(q_ref[...], k_ref[...], qb_ref[...], scale)
+    largest = jnp.max(s, axis=-1, keepdims=True)
+    weights = jnp.exp(s - largest)
+    totals = jnp.sum(weights, axis=-1, keepdims=True)
+    probs = weights / totals
+    o_ref[...] = jnp.dot(probs.astype(jnp.bfloat16), v_ref[...],
+                         preferred_element_type=jnp.float32).astype(o_ref.dtype)
+    lse_ref[...] = largest + jnp.log(totals)
+
+def _bwd_kernel(scale, q_ref, k_ref, v_ref, qb_ref, lse_ref, do_ref, dq_ref, dk_ref, dv_ref):
+    q = q_ref[...]; k = k_ref[...]; v = v_ref[...]; do = do_ref[...]
+    probs = jnp.exp(_scores(q, k, qb_ref[...], scale) - lse_ref[...])
+    dp = lax.dot_general(do, v, (((1,), (1,)), ((), ())), preferred_element_type=jnp.float32)
+    inner = jnp.sum(probs * dp, axis=-1, keepdims=True)
+    ds = (probs * (dp - inner)).astype(jnp.bfloat16)
+    dv_ref[...] = lax.dot_general(probs.astype(jnp.bfloat16), do, (((0,), (0,)), ((), ())),
+                                  preferred_element_type=jnp.float32)
+    dk_ref[...] = lax.dot_general(ds, q, (((0,), (0,)), ((), ())),
+                                  preferred_element_type=jnp.float32) * scale
+    dq_ref[...] = jnp.dot(ds, k, preferred_element_type=jnp.float32) * scale
+
+def attn_fwd(q, k, v, qb):
+    n, rows, d = q.shape; keys = k.shape[1]
+    scale = 1.0 / math.sqrt(d)
+    rspec = pl.BlockSpec((None, rows, d), lambda i: (i, 0, 0))
+    kspec = pl.BlockSpec((None, keys, d), lambda i: (i, 0, 0))
+    cspec = pl.BlockSpec((None, rows, 1), lambda i: (i, 0, 0))
+    return pl.pallas_call(
+        functools.partial(_fwd_kernel, scale),
+        grid=(n,),
+        in_specs=[rspec, kspec, kspec, cspec],
+        out_specs=[rspec, cspec],
+        out_shape=[jax.ShapeDtypeStruct((n, rows, d), jnp.bfloat16),
+                   jax.ShapeDtypeStruct((n, rows, 1), jnp.float32)],
+        cost_estimate=pl.CostEstimate(flops=4 * n * rows * keys * d,
+                                      transcendentals=n * rows * keys,
+                                      bytes_accessed=2 * n * (2 * rows * d + 2 * keys * d)),
+    )(q, k, v, qb)
+
+def attn_bwd(q, k, v, qb, lse, do):
+    n, rows, d = q.shape; keys = k.shape[1]
+    scale = 1.0 / math.sqrt(d)
+    rspec = pl.BlockSpec((None, rows, d), lambda i: (i, 0, 0))
+    kspec = pl.BlockSpec((None, keys, d), lambda i: (i, 0, 0))
+    cspec = pl.BlockSpec((None, rows, 1), lambda i: (i, 0, 0))
+    return pl.pallas_call(
+        functools.partial(_bwd_kernel, scale),
+        grid=(n,),
+        in_specs=[rspec, kspec, kspec, cspec, cspec, rspec],
+        out_specs=[rspec, kspec, kspec],
+        out_shape=[jax.ShapeDtypeStruct((n, rows, d), jnp.float32),
+                   jax.ShapeDtypeStruct((n, keys, d), jnp.float32),
+                   jax.ShapeDtypeStruct((n, keys, d), jnp.float32)],
+        cost_estimate=pl.CostEstimate(flops=10 * n * rows * keys * d,
+                                      transcendentals=n * rows * keys,
+                                      bytes_accessed=2 * n * (3 * rows * d + 2 * keys * d) + 8 * n * (rows * d + 2 * keys * d)),
+    )(q, k, v, qb, lse, do)
 
 
 def rope_tables(positions, head_size):
@@ -263,31 +330,11 @@
     query_blocks = (slot_positions // BLOCK).reshape(sequences, seq_rows)
     key_blocks = jnp.arange(seq_length, dtype=jnp.int32) // BLOCK
 
-    def seq_scores(query_part, key_part, block_part):
-        scores = (
-            jnp.einsum("rhd,khd->hrk", query_part, key_part, preferred_element_type=jnp.float32)
-            * scale
-        )
-        allowed = key_blocks[None, :] <= block_part[:, None]
-        return jnp.where(allowed[None], scores, masked_score)
-
-    def attend_forward(inputs):
-        query_part, key_part, value_part, block_part = inputs
-        scores = seq_scores(query_part, key_part, block_part)
-        largest = jnp.max(scores, axis=-1, keepdims=True)
-        weights = jnp.exp(scores - largest)
-        totals = jnp.sum(weights, axis=-1, keepdims=True)
-        probs = weights / totals
-        mixed_part = jnp.einsum(
-            "hrk,khd->rhd",
-            probs.astype(jnp.bfloat16),
-            value_part,
-            preferred_element_type=jnp.float32,
-        )
-        return (mixed_part.astype(jnp.bfloat16), largest + jnp.log(totals))
-
-    attn_mixed, log_totals = lax.map(
-        attend_forward, (seq_queries, seq_keys, seq_values, query_blocks)
+    attn_mixed, log_totals = attn_fwd(
+        seq_queries.reshape(sequences, seq_rows, HEAD),
+        seq_keys.reshape(sequences, seq_length, HEAD),
+        seq_values.reshape(sequences, seq_length, HEAD),
+        query_blocks[:, :, None],
     )
     mixed_rows = to_jg(attn_mixed.reshape(slot_rows, head_cols))
     attn_partial = jnp.dot(mixed_rows, output_weight, preferred_element_type=jnp.float32)
@@ -362,33 +409,13 @@
     ).astype(jnp.bfloat16)
     seq_mixed_grad = to_gj(mixed_grad).reshape(sequences, seq_rows, local_heads, HEAD)
 
-    def attend_backward(inputs):
-        query_part, key_part, value_part, block_part, log_part, grad_part = inputs
-        probs = jnp.exp(seq_scores(query_part, key_part, block_part) - log_part)
-        prob_grad = jnp.einsum(
-            "rhd,khd->hrk", grad_part, value_part, preferred_element_type=jnp.float32
-        )
-        inner = jnp.sum(probs * prob_grad, axis=-1, keepdims=True)
-        score_grad = (probs * (prob_grad - inner)).astype(jnp.bfloat16)
-        value_grad = jnp.einsum(
-            "hrk,rhd->khd",
-            probs.astype(jnp.bfloat16),
-            grad_part,
-            preferred_element_type=jnp.float32,
-        )
-        key_grad = (
-            jnp.einsum("hrk,rhd->khd", score_grad, query_part, preferred_element_type=jnp.float32)
-            * scale
-        )
-        query_part_grad = (
-            jnp.einsum("hrk,khd->rhd", score_grad, key_part, preferred_element_type=jnp.float32)
-            * scale
-        )
-        return (query_part_grad, key_grad, value_grad)
-
-    seq_query_grad, seq_key_grad, seq_value_grad = lax.map(
-        attend_backward,
-        (seq_queries, seq_keys, seq_values, query_blocks, log_totals, seq_mixed_grad),
+    seq_query_grad, seq_key_grad, seq_value_grad = attn_bwd(
+        seq_queries.reshape(sequences, seq_rows, HEAD),
+        seq_keys.reshape(sequences, seq_length, HEAD),
+        seq_values.reshape(sequences, seq_length, HEAD),
+        query_blocks[:, :, None],
+        log_totals,
+        seq_mixed_grad.reshape(sequences, seq_rows, HEAD),
     )
     query_rot_grad = to_jg(
         rotate_back(seq_query_grad.reshape(slot_rows, local_heads, HEAD), slot_cos, slot_sin)

time: 1750 us -> 1650 us (0.943)
  matrix products: 226 us -> 139 us
  blocking collectives: 208 us -> 173 us
  local copies, waits for them, and re-layouts: 149 us -> 119 us
  Pallas kernels: 0 us -> 24.6 us
  waiting for transfers between devices: 1010 us -> 1030 us
    dot_general x56 -> x0, matrix products: 85.3 us -> none  [the longest x16 24.2 us: seq_scores(): jnp.einsum('rhd,khd->hrk', query_part, key_part, preferred_element_type=j...]
    all_to_all x1 -> x0, blocking collectives: 35.3 us -> none  [shards(): lax.all_to_all(seq_key_grad.reshape(devices, own_rows, 1, head_cols).asty...]
    all_to_all x0 -> x1, waiting for transfers between devices: none -> 25.5 us  [shards(): lax.all_to_all(seq_key_grad.reshape(devices, own_rows, 1, head_cols).asty...]
    pallas_call x0 -> x2, Pallas kernels: none -> 24.6 us  [the longest x1 13.7 us: attn_bwd(): pl.pallas_call(functools.partial(_bwd_kernel, scale), grid=(n,), in_specs...]
  transfers between devices with their start and end apart: 20 -> 21, of which waited for: 19 -> 20; matrix products, arithmetic and copies ran while one was open for 8% -> 9% of each run, Pallas kernels for 0% -> 0%
where the time goes in v6:
time: 1650 us
  waiting for transfers between devices  1030 us (62%)
  blocking collectives  173 us (10%)
  matrix products  139 us (8%)
  local copies, waits for them, and re-layouts  119 us (7%)
  other arithmetic  89.6 us (5%)
  starting transfers between devices  58.2 us (4%)
  Pallas kernels  24.6 us (1%)
    all_gather x4, waiting for transfers between devices, dispatch(): lax.all_gather(by_group.reshape(groups * slot_cap, width), GROUP_AXES, ax...  304 us
    all_to_all x3, waiting for transfers between devices, combine(): lax.all_to_all(partial_value.astype(jnp.bfloat16).reshape(group_size, gro...  303 us
    all_gather x1, waiting for transfers between devices, shards(): lax.all_gather(lax.all_gather(packed, 'grp', axis=0, tiled=True), GROUP_A...  119 us
    all_to_all x1, blocking collectives, combine(): lax.all_to_all(partial_value.astype(jnp.bfloat16).reshape(group_size, gro...  110 us
    all_to_all x4, waiting for transfers between devices, combine(): lax.all_to_all(summed, 'grp', split_axis=0, concat_axis=0, tiled=True)  77.9 us
    all_to_all x4, blocking collectives, dispatch(): lax.all_to_all(slot_values, 'grp', split_axis=0, concat_axis=0, tiled=True)  63.7 us
    all_gather x1, waiting for transfers between devices, shards(): all_pairs = lax.all_gather(seq_pair, 'grp', axis=0, tiled=True)  46.8 us
    all_gather x1, waiting for transfers between devices, shards(): seq_input = lax.all_gather(attn_input, GROUP_AXES, axis=0, tiled=True)  44.5 us
  transfers between devices with their start and end apart: 21, of which 20 were waited for; matrix products, arithmetic and copies ran while one was open for 9% of the time, Pallas kernels for 0%

profile of v6, /device:TPU:1, one launch (start us, length us, event | category | flops | bytes accessed | tf_op | source)
XLA Modules:
  0.0 1646.3 jit_solution(16639604555737943397)
XLA Ops:
  17.2 37.3 %all-gather.10.cloned.1.call-done = bf16[128,4224]{1,0:T(8,128)(2,1)} async-done(((bf16[16,4224]{1,0:T(8,128)(2,1)}), bf16[128,4224]{1,0:T(8,128)(2,1)}) %all-gather.10.cloned.1.call-update) | async-done | bytes 1081360 | tf_op jit(solution)/shard_map/all_gather | solution.py:274
  54.8 119.1 %all-gather.12.cloned.1.call-done = bf16[2048,4224]{1,0:T(8,128)(2,1)} async-done(((bf16[128,4224]{1,0:T(8,128)(2,1)}), bf16[2048,4224]{1,0:T(8,128)(2,1)}) %all-gather.12.cloned.1.call-update) | async-done | bytes 17301520 | tf_op jit(solution)/shard_map/all_gather | solution.py:273
  173.9 8.1 copy.460
  182.1 5.9 copy-done.4
  189.5 8.3 slice.150
  198.1 44.5 %all-gather.16.cloned.1.call-done = bf16[1024,2048]{1,0:T(8,128)(2,1)} async-done(((bf16[64,2048]{1,0:T(8,128)(2,1)}), bf16[1024,2048]{1,0:T(8,128)(2,1)}) %all-gather.16.cloned.1.call-update) | async-done | bytes 4194320 | tf_op jit(solution)/shard_map/all_gather | solution.py:289
  251.2 22.8 %all_to_all.98 = bf16[8,18,2048]{2,1,0:T(8,128)(2,1)S(1)} all-to-all(bf16[8,18,2048]{2,1,0:T(8,128)(2,1)S(1)} %broadcast_select_fusion.1), channel_id=1, replica_groups=mesh['grp'=8,'sub'=8,'expert'=2] {'grp'}, dimensions={0} | all-to-all | bytes 1179648 | tf_op jit(solution)/shard_map/all_to_all | solution.py:223
  297.0 46.8 %all-gather.18.cloned.1.call-done = bf16[8192,256]{0,1:T(8,128)(2,1)} async-done(((bf16[1024,256]{0,1:T(8,128)(2,1)}), bf16[8192,256]{0,1:T(8,128)(2,1)}) %all-gather.18.cloned.1.call-update) | async-done | bytes 4194320 | tf_op jit(solution)/shard_map/all_gather | solution.py:310
  356.7 69.1 %all-gather.14.cloned.1.call-done = bf16[2304,2048]{1,0:T(8,128)(2,1)} async-done(((bf16[144,2048]{1,0:T(8,128)(2,1)}), bf16[2304,2048]{1,0:T(8,128)(2,1)}) %all-gather.14.cloned.1.call-update) | async-done | bytes 9437200 | tf_op jit(solution)/shard_map/all_gather | solution.py:224
  425.8 7.3 fusion.81
  443.7 10.8 shard_map.238
  456.2 6.3 convolution_convert_fusion.2
  468.2 105.2 %all-to-all-done.1 = bf16[16,144,2048]{2,1,0:T(8,128)(2,1)} async-done(((bf16[16,144,2048]{2,1,0:T(8,128)(2,1)}), bf16[16,144,2048]{2,1,0:T(8,128)(2,1)}, u32[]{:S(2)}, u32[]{:S(2)}) %all-to-all-start.1) | async-done | bytes 9437216 | tf_op jit(solution)/shard_map/all_to_all | solution.py:229
  573.3 5.9 convert_reduce_fusion.3
  590.1 17.8 %all-to-all-done.2 = f32[8,18,2048]{2,1,0:T(8,128)} async-done(((f32[8,18,2048]{2,1,0:T(8,128)}), f32[8,18,2048]{2,1,0:T(8,128)}, u32[]{:S(2)}, u32[]{:S(2)}) %all-to-all-start.2) | async-done | bytes 1179680 | tf_op jit(solution)/shard_map/all_to_all | solution.py:237
  617.2 13.9 all_to_all.99
  632.2 79.2 %all-gather.20.cloned.1.call-done = bf16[2304,2048]{1,0:T(8,128)(2,1)} async-done(((bf16[144,2048]{1,0:T(8,128)(2,1)}), bf16[2304,2048]{1,0:T(8,128)(2,1)}) %all-gather.20.cloned.1.call-update) | async-done | bytes 9437200 | tf_op jit(solution)/shard_map/all_gather | solution.py:224
  711.4 7.6 fusion.82
  724.6 7.5 convolution_convert_fusion.1
  738.5 104.4 %all-to-all-done.4 = bf16[16,144,2048]{2,1,0:T(8,128)(2,1)} async-done(((bf16[16,144,2048]{2,1,0:T(8,128)(2,1)}), bf16[16,144,2048]{2,1,0:T(8,128)(2,1)}, u32[]{:S(2)}, u32[]{:S(2)}) %all-to-all-start.4) | async-done | bytes 9437216 | tf_op jit(solution)/shard_map/all_to_all | solution.py:229
  842.9 5.9 convert_reduce_fusion.2
  860.2 17.2 %all-to-all-done.5 = f32[8,18,2048]{2,1,0:T(8,128)} async-done(((f32[8,18,2048]{2,1,0:T(8,128)}), f32[8,18,2048]{2,1,0:T(8,128)}, u32[]{:S(2)}, u32[]{:S(2)}) %all-to-all-start.5) | async-done | bytes 1179680 | tf_op jit(solution)/shard_map/all_to_all | solution.py:237
  889.2 13.2 all_to_all.100
  903.4 79.5 %all-gather.22.cloned.1.call-done = bf16[2304,2048]{1,0:T(8,128)(2,1)} async-done(((bf16[144,2048]{1,0:T(8,128)(2,1)}), bf16[2304,2048]{1,0:T(8,128)(2,1)}) %all-gather.22.cloned.1.call-update) | async-done | bytes 9437200 | tf_op jit(solution)/shard_map/all_gather | solution.py:224
  982.9 11.9 multiply_convert_fusion
  994.8 9.2 fusion.83
  1004.0 9.1 add_convert_fusion
  1013.1 109.5 %all_to_all.101 = bf16[16,144,2048]{2,1,0:T(8,128)(2,1)} all-to-all(bf16[16,144,2048]{2,1,0:T(8,128)(2,1)S(1)} %bitcast.154), channel_id=1, replica_groups=mesh['grp'=8,'sub'=8,'expert'=2] {'sub','expert'}, dimensions={0} | all-to-all | bytes 18874368 | tf_op jit(solution)/shard_map/all_to_all | solution.py:229
  1122.6 5.9 convert_reduce_fusion.1
  1135.4 23.4 %all-to-all-done.8 = f32[8,18,2048]{2,1,0:T(8,128)S(1)} async-done(((f32[8,18,2048]{2,1,0:T(8,128)}), f32[8,18,2048]{2,1,0:T(8,128)S(1)}, u32[]{:S(2)}, u32[]{:S(2)}) %all-to-all-start.8) | async-done | bytes 1179680 | tf_op jit(solution)/shard_map/all_to_all | solution.py:237
  1175.6 13.8 all_to_all.102
  1190.5 75.9 %all-gather.24.cloned.1.call-done = bf16[2304,2048]{1,0:T(8,128)(2,1)} async-done(((bf16[144,2048]{1,0:T(8,128)(2,1)}), bf16[2304,2048]{1,0:T(8,128)(2,1)}) %all-gather.24.cloned.1.call-update) | async-done | bytes 9437200 | tf_op jit(solution)/shard_map/all_gather | solution.py:224
  1266.4 6.3 convolution_convert_fusion.3
  1273.9 13.7 shard_map.239
  1291.5 6.0 all-to-all-start.12
  1301.3 25.5 %all-to-all-done.12 = bf16[128,64,1,128]{3,1,2,0:T(8,128)(2,1)} async-done(((bf16[128,64,1,128]{3,1,2,0:T(8,128)(2,1)}), bf16[128,64,1,128]{3,1,2,0:T(8,128)(2,1)}, u32[]{:S(2)}, u32[]{:S(2)}) %all-to-all-start.12) | async-done | bytes 2097184 | tf_op jit(solution)/shard_map/all_to_all | solution.py:433
  1344.4 17.3 %all-to-all-done.13 = bf16[128,64,1,128]{3,1,2,0:T(8,128)(2,1)} async-done(((bf16[128,64,1,128]{3,1,2,0:T(8,128)(2,1)}), bf16[128,64,1,128]{3,1,2,0:T(8,128)(2,1)}, u32[]{:S(2)}, u32[]{:S(2)}) %all-to-all-start.13) | async-done | bytes 2097184 | tf_op jit(solution)/shard_map/all_to_all | solution.py:440
  1378.8 93.9 %all-to-all-done.10 = bf16[16,144,2048]{2,1,0:T(8,128)(2,1)} async-done(((bf16[16,144,2048]{2,1,0:T(8,128)(2,1)}), bf16[16,144,2048]{2,1,0:T(8,128)(2,1)}, u32[]{:S(2)}, u32[]{:S(2)}) %all-to-all-start.10) | async-done | bytes 9437216 | tf_op jit(solution)/shard_map/all_to_all | solution.py:229
  1477.6 5.9 convert_reduce_fusion
  1497.6 19.5 %all-to-all-done.11 = f32[8,18,2048]{2,1,0:T(8,128)} async-done(((f32[8,18,2048]{2,1,0:T(8,128)}), f32[8,18,2048]{2,1,0:T(8,128)}, u32[]{:S(2)}, u32[]{:S(2)}) %all-to-all-start.11) | async-done | bytes 1179680 | tf_op jit(solution)/shard_map/all_to_all | solution.py:237
  1524.0 8.8 convolution_add_fusion.2
  1538.1 9.4 fusion.89
  1547.5 9.0 fusion.91
  1562.8 6.2 fusion.88
  1569.0 7.4 fusion.87
  1576.3 27.6 %reduce-scatter.2.cloned.1.call-done = f32[256,384]{0,1:T(8,128)} async-done(((f32[2048,384]{0,1:T(8,128)}), f32[256,384]{0,1:T(8,128)}) %reduce-scatter.2.cloned.1.call-update) | async-done | bytes 393232 | tf_op jit(solution)/shard_map/reduce_scatter | solution.py:494
  1605.8 8.3 all-to-all-start.15
  1614.1 20.0 %all-gather.26.cloned.1.call-done = bf16[128,4096]{1,0:T(8,128)(2,1)} async-done(((bf16[64,4096]{1,0:T(8,128)(2,1)}), bf16[128,4096]{1,0:T(8,128)(2,1)}) %all-gather.26.cloned.1.call-update) | async-done | bytes 1048592 | tf_op jit(solution)/shard_map/all_gather | solution.py:508
  (398 shorter events, 243.4 us)
Async XLA Ops:
  7.2 717.4 %copy-start = (bf16[352,2048]{1,0:T(8,128)(2,1)S(1)}, bf16[352,2048]{1,0:T(8,128)(2,1)}, u32[]{:S(2)}) copy-start(bf16[352,2048]{1,0:T(8,128)(2,1)} %param.31) | copy-start | bytes 4325380
  7.2 47.3 %all-gather.10.cloned.1.call-start = ((), (), s32[]{:S(2)}) async-start(), calls=%async_computation.17 | async-start | bytes 1216512 | tf_op jit(solution)/shard_map/all_gather | solution.py:274
  15.9 38.7 %copy-start.17 = (bf16[128,2048]{1,0:T(8,128)(2,1)S(1)}, bf16[128,2048]{1,0:T(8,128)(2,1)}, u32[]{:S(2)}) copy-start(bf16[128,2048]{1,0:T(8,128)(2,1)} %param.21) | copy-start | bytes 1572868
  17.2 156.7 %all-gather.12.cloned.1.call-start = ((), (), s32[]{:S(2)}) async-start(), calls=%async_computation.18 | async-start | bytes 18382848 | tf_op jit(solution)/shard_map/all_gather | solution.py:273
  54.5 188.1 %all-gather.16.cloned.1.call-start = ((), (), s32[]{:S(2)}) async-start(), calls=%async_computation.20 | async-start | bytes 4456448 | tf_op jit(solution)/shard_map/all_gather | solution.py:289
  54.8 133.8 %copy-start.57 = (f32[64]{0:T(128)}, f32[64]{0:T(128)S(1)}, u32[]{:S(2)}) copy-start(f32[64]{0:T(128)S(1)} %add_rsqrt_fusion.1) | copy-start | bytes 772
  188.5 9.3 copy-start.36
  189.4 154.4 %all-gather.18.cloned.1.call-start = ((), (), s32[]{:S(2)}) async-start(), calls=%async_computation.21 | async-start | bytes 4718592 | tf_op jit(solution)/shard_map/all_gather | solution.py:310
  189.5 247.6 %copy-start.55 = (f32[64]{0:T(128)}, f32[64]{0:T(128)S(1)}, u32[]{:S(2)}) copy-start(f32[64]{0:T(128)S(1)} %multiply_exponential_fusion) | copy-start | bytes 772
  248.2 177.5 %all-gather.14.cloned.1.call-start = ((), (), s32[]{:S(2)}) async-start(), calls=%async_computation.19 | async-start | bytes 10027008 | tf_op jit(solution)/shard_map/all_gather | solution.py:224
  293.6 143.5 %copy-start.40 = (f32[2304]{0:T(1024)}, f32[2304]{0:T(1024)S(1)}, u32[]{:S(2)}) copy-start(f32[2304]{0:T(1024)S(1)} %fusion.59) | copy-start | bytes 27652
  352.5 73.2 %copy-start.32 = (bf16[2048,128]{1,0:T(8,128)(2,1)S(1)}, bf16[2048,128]{1,0:T(8,128)(2,1)}, u32[]{:S(2)}) copy-start(bf16[2048,128]{1,0:T(8,128)(2,1)} %param.25) | copy-start | bytes 1572868
  462.5 110.8 %all-to-all-start.1 = ((bf16[16,144,2048]{2,1,0:T(8,128)(2,1)}), bf16[16,144,2048]{2,1,0:T(8,128)(2,1)}, u32[]{:S(2)}, u32[]{:S(2)}) async-start(bf16[16,144,2048]{2,1,0:T(8,128)(2,1)} %bitcast.156), calls=%async_computation.1 | async-start | bytes 18874368 | tf_op jit(solution)/shard_map/all_to_all | solution.py:229
  580.6 27.3 %all-to-all-start.2 = ((f32[8,18,2048]{2,1,0:T(8,128)}), f32[8,18,2048]{2,1,0:T(8,128)}, u32[]{:S(2)}, u32[]{:S(2)}) async-start(f32[8,18,2048]{2,1,0:T(8,128)} %reshape.773), calls=%async_computation.2 | async-start | bytes 3145728 | tf_op jit(solution)/shard_map/all_to_all | solution.py:237
  584.9 126.5 %all-gather.20.cloned.1.call-start = ((), (), s32[]{:S(2)}) async-start(), calls=%async_computation.22 | async-start | bytes 10027008 | tf_op jit(solution)/shard_map/all_gather | solution.py:224
  586.5 22.9 %copy-start.29 = (s32[1024]{0:T(1024)}, s32[1024]{0:T(1024)S(1)}, u32[]{:S(2)}) copy-start(s32[1024]{0:T(1024)S(1)} %pad_clamp_fusion.2) | copy-start | bytes 12292
  590.0 21.3 %copy-start.53 = (f32[64,2]{0,1:T(2,128)}, f32[64,2]{0,1:T(2,128)S(1)}, u32[]{:S(2)}) copy-start(f32[64,2]{0,1:T(2,128)S(1)} %get-tuple-element.149) | copy-start | bytes 1540
  632.1 86.8 %copy-start.27 = (bf16[2048,352]{0,1:T(8,128)(2,1)S(1)}, bf16[2048,352]{0,1:T(8,128)(2,1)}, u32[]{:S(2)}) copy-start(bf16[2048,352]{0,1:T(8,128)(2,1)} %param.30) | copy-start | bytes 4325380
  711.4 7.6 copy-start.61
  732.1 110.8 %all-to-all-start.4 = ((bf16[16,144,2048]{2,1,0:T(8,128)(2,1)}), bf16[16,144,2048]{2,1,0:T(8,128)(2,1)}, u32[]{:S(2)}, u32[]{:S(2)}) async-start(bf16[16,144,2048]{2,1,0:T(8,128)(2,1)} %bitcast.159), calls=%async_computation.4 | async-start | bytes 18874368 | tf_op jit(solution)/shard_map/all_to_all | solution.py:229
  850.1 27.4 %all-to-all-start.5 = ((f32[8,18,2048]{2,1,0:T(8,128)}), f32[8,18,2048]{2,1,0:T(8,128)}, u32[]{:S(2)}, u32[]{:S(2)}) async-start(f32[8,18,2048]{2,1,0:T(8,128)} %reshape.777), calls=%async_computation.5 | async-start | bytes 3145728 | tf_op jit(solution)/shard_map/all_to_all | solution.py:237
  854.5 128.4 %all-gather.22.cloned.1.call-start = ((), (), s32[]{:S(2)}) async-start(), calls=%async_computation.23 | async-start | bytes 10027008 | tf_op jit(solution)/shard_map/all_gather | solution.py:224
  982.9 11.9 copy-start.26
  994.8 9.2 copy-start.21
  994.8 9.2 copy-start.13
  994.8 9.2 copy-start.28
  1129.8 29.0 %all-to-all-start.8 = ((f32[8,18,2048]{2,1,0:T(8,128)}), f32[8,18,2048]{2,1,0:T(8,128)S(1)}, u32[]{:S(2)}, u32[]{:S(2)}) async-start(f32[8,18,2048]{2,1,0:T(8,128)} %reshape.781), calls=%async_computation.8 | async-start | bytes 3145728 | tf_op jit(solution)/shard_map/all_to_all | solution.py:237
  1134.7 131.7 %all-gather.24.cloned.1.call-start = ((), (), s32[]{:S(2)}) async-start(), calls=%async_computation.24 | async-start | bytes 10027008 | tf_op jit(solution)/shard_map/all_gather | solution.py:224
  1175.6 90.8 %copy-start.31 = (bf16[128,2048]{1,0:T(8,128)(2,1)S(1)}, bf16[128,2048]{1,0:T(8,128)(2,1)}, u32[]{:S(2)}) copy-start(bf16[128,2048]{1,0:T(8,128)(2,1)} %param.26) | copy-start | bytes 1572868
  1291.5 35.3 %all-to-all-start.12 = ((bf16[128,64,1,128]{3,1,2,0:T(8,128)(2,1)}), bf16[128,64,1,128]{3,1,2,0:T(8,128)(2,1)}, u32[]{:S(2)}, u32[]{:S(2)}) async-start(bf16[128,64,1,128]{3,1,2,0:T(8,128)(2,1)} %bitcast.165), calls=%async_computation.12 | async-start | bytes 4194304 | tf_op jit(solution)/shard_map/all_to_all | solution.py:433
  1326.8 34.9 %all-to-all-start.13 = ((bf16[128,64,1,128]{3,1,2,0:T(8,128)(2,1)}), bf16[128,64,1,128]{3,1,2,0:T(8,128)(2,1)}, u32[]{:S(2)}, u32[]{:S(2)}) async-start(bf16[128,64,1,128]{3,1,2,0:T(8,128)(2,1)} %bitcast.164), calls=%async_computation.13 | async-start | bytes 4194304 | tf_op jit(solution)/shard_map/all_to_all | solution.py:440
  1361.7 110.9 %all-to-all-start.10 = ((bf16[16,144,2048]{2,1,0:T(8,128)(2,1)}), bf16[16,144,2048]{2,1,0:T(8,128)(2,1)}, u32[]{:S(2)}, u32[]{:S(2)}) async-start(bf16[16,144,2048]{2,1,0:T(8,128)(2,1)} %bitcast.155), calls=%async_computation.10 | async-start | bytes 18874368 | tf_op jit(solution)/shard_map/all_to_all | solution.py:229
  1472.7 15.5 all-to-all-start.14
  1488.2 28.9 %all-to-all-start.11 = ((f32[8,18,2048]{2,1,0:T(8,128)}), f32[8,18,2048]{2,1,0:T(8,128)}, u32[]{:S(2)}, u32[]{:S(2)}) async-start(f32[8,18,2048]{2,1,0:T(8,128)} %reshape.788), calls=%async_computation.11 | async-start | bytes 3145728 | tf_op jit(solution)/shard_map/all_to_all | solution.py:237
  1492.5 111.5 %reduce-scatter.2.cloned.1.call-start = ((), (), s32[]{:S(2)}) async-start(), calls=%async_computation.26 | async-start | bytes 3538944 | tf_op jit(solution)/shard_map/reduce_scatter | solution.py:494
  1497.6 21.0 %copy-start.30 = (s32[1024]{0:T(1024)S(1)}, s32[1024]{0:T(1024)}, u32[]{:S(2)}) copy-start(s32[1024]{0:T(1024)} %copy-done.29) | copy-start | bytes 12292
  1523.9 8.8 copy-start.19
  1524.0 8.8 copy-start.37
  1524.0 8.8 copy-start.58
  1524.0 11.8 copy-start.50
  1537.8 9.7 copy-start.14
  1537.9 96.3 %all-gather.26.cloned.1.call-start = ((), (), s32[]{:S(2)}) async-start(), calls=%async_computation.25 | async-start | bytes 1572864 | tf_op jit(solution)/shard_map/all_gather | solution.py:508
  1538.1 18.4 %slice-start = ((s8[9437184]{0:T(1024)(128)(4,1)}), s8[4194304]{0:T(1024)(128)(4,1)S(1)}, s32[]{:S(2)}) async-start(s8[9437184]{0:T(1024)(128)(4,1)} %bitcast.179), calls=%async_computation.27 | async-start | bytes 8388608
  1538.1 18.4 %slice-start.1 = ((s8[9437184]{0:T(1024)(128)(4,1)}), s8[4194304]{0:T(1024)(128)(4,1)S(1)}, s32[]{:S(2)}) async-start(s8[9437184]{0:T(1024)(128)(4,1)} %bitcast.179), calls=%async_computation.28 | async-start | bytes 8388608
  1547.5 9.0 copy-start.22
  1547.5 9.0 slice-start.2
  1605.8 30.6 %all-to-all-start.15 = ((f32[16,16,384]{2,1,0:T(8,128)}), f32[16,16,384]{2,1,0:T(8,128)S(1)}, u32[]{:S(2)}, u32[]{:S(2)}) async-start(f32[16,16,384]{2,1,0:T(8,128)} %bitcast.50), calls=%async_computation.16 | async-start | bytes 786432 | tf_op jit(solution)/shard_map/all_to_all | solution.py:495
  1614.1 25.1 %copy-start.1 = (bf16[352,2048]{1,0:T(8,128)(2,1)S(1)}, bf16[352,2048]{1,0:T(8,128)(2,1)}, u32[]{:S(2)}) copy-start(bf16[352,2048]{1,0:T(8,128)(2,1)} %param.31) | copy-start | bytes 4325380
  (40 other events, 140.0 us)
Sparse Core Ops, SparseCore 0:
  17.3 37.1 all-gather.9
  57.0 116.8 all-gather.11
  189.5 53.0 all-gather.15
  248.4 95.4 all-gather.17
  346.7 78.9 all-gather.13
  632.3 79.0 all-gather.19
  903.6 79.3 all-gather.21
  1190.6 75.7 all-gather.23
  1538.0 65.9 reduce-scatter.1
  1606.0 28.0 all-gather.25

commit v7 on v6

--- a/solution.py
+++ b/solution.py
@@ -236,6 +236,21 @@
         summed = jnp.sum(parts.astype(jnp.float32), axis=0).reshape(groups, slot_cap, width)
         return lax.all_to_all(summed, "grp", split_axis=0, concat_axis=0, tiled=True)
 
+    def to_rows(per_head):
+        parts = lax.all_to_all(
+            per_head.reshape(group_size, groups * slot_cap, head_cols),
+            GROUP_AXES,
+            split_axis=0,
+            concat_axis=0,
+            tiled=True,
+        )
+        return jnp.swapaxes(parts, 0, 1).reshape(groups * slot_cap, group_size * head_cols)
+
+    def to_owners(row_values):
+        return lax.all_to_all(
+            row_values.reshape(groups, slot_cap, width), "grp", split_axis=0, concat_axis=0, tiled=True
+        )
+
     def to_gj(rows):
         shaped = rows.reshape((group_size, groups, slot_cap) + rows.shape[1:])
         return jnp.swapaxes(shaped, 0, 1).reshape(rows.shape)
@@ -337,8 +352,10 @@
         query_blocks[:, :, None],
     )
     mixed_rows = to_jg(attn_mixed.reshape(slot_rows, head_cols))
-    attn_partial = jnp.dot(mixed_rows, output_weight, preferred_element_type=jnp.float32)
-    attn_slots = combine(attn_partial)
+    output_stack = lax.all_gather(output_weight, GROUP_AXES, axis=0, tiled=True)
+    attn_slots = to_owners(
+        jnp.dot(to_rows(mixed_rows), output_stack, preferred_element_type=jnp.float32)
+    )
     attn_gates = pair_gates(attn_logits, own_attn)
     attn_index, attn_pair_kept = pair_index(own_attn, attn_places, attn_kept, slot_cap)
     attn_picked = attn_slots.reshape(EXPERTS * slot_cap, width)[attn_index]
@@ -425,10 +442,12 @@
     query_grad = jnp.einsum(
         "rd,rw->dw", attn_rows, query_rot_grad, preferred_element_type=jnp.float32
     )
-    query_row_grad = jnp.einsum(
-        "rw,dw->rd", query_rot_grad, query_weight, preferred_element_type=jnp.float32
-    )
-    attn_row_grad = combine(query_row_grad)
+    query_stack = lax.all_gather(query_weight, GROUP_AXES, axis=1, tiled=True)
+    attn_row_grad = to_owners(
+        jnp.einsum(
+            "rw,dw->rd", to_rows(query_rot_grad), query_stack, preferred_element_type=jnp.float32
+        )
+    )
     key_back, value_back = (
         lax.all_to_all(
             seq_key_grad.reshape(devices, own_rows, 1, head_cols).astype(jnp.bfloat16),

time: 1650 us -> 1530 us (0.927)
  waiting for transfers between devices: 1030 us -> 892 us
  blocking collectives: 173 us -> 190 us
    all_to_all x3 -> x1, waiting for transfers between devices: 303 us -> 104 us  [combine(): lax.all_to_all(partial_value.astype(jnp.bfloat16).reshape(group_size, gro...]
    all_gather x0 -> x2, waiting for transfers between devices: none -> 57.5 us  [the longest x1 31.2 us: shards(): query_stack = lax.all_gather(query_weight, GROUP_AXES, axis=1, tiled=True)]
    all_to_all x0 -> x3, waiting for transfers between devices: none -> 54.8 us  [the longest x2 39.1 us: to_owners(): lax.all_to_all(row_values.reshape(groups, slot_cap, width), 'grp', split_...]
    all_to_all x4 -> x2, waiting for transfers between devices: 77.9 us -> 40.7 us  [combine(): lax.all_to_all(summed, 'grp', split_axis=0, concat_axis=0, tiled=True)]
    all_to_all x0 -> x1, blocking collectives: none -> 17.7 us  [to_rows(): lax.all_to_all(per_head.reshape(group_size, groups * slot_cap, head_cols)...]
  transfers between devices with their start and end apart: 21 -> 22, of which waited for: 20 -> 20; matrix products, arithmetic and copies ran while one was open for 9% -> 12% of each run, Pallas kernels for 0% -> 2%
where the time goes in v7:
time: 1530 us; the launch traced here: 1520 us
  waiting for transfers between devices  892 us (58%)
  blocking collectives  190 us (12%)
  matrix products  140 us (9%)
  local copies, waits for them, and re-layouts  121 us (8%)
  other arithmetic  80.5 us (5%)
  starting transfers between devices  53.8 us (4%)
  Pallas kernels  24.6 us (2%)
  between operations  16.3 us (1%)
    all_gather x4, waiting for transfers between devices, dispatch(): lax.all_gather(by_group.reshape(groups * slot_cap, width), GROUP_AXES, ax...  300 us
    all_gather x1, waiting for transfers between devices, shards(): lax.all_gather(lax.all_gather(packed, 'grp', axis=0, tiled=True), GROUP_A...  119 us
    all_to_all x1, blocking collectives, combine(): lax.all_to_all(partial_value.astype(jnp.bfloat16).reshape(group_size, gro...  110 us
    all_to_all x1, waiting for transfers between devices, combine(): lax.all_to_all(partial_value.astype(jnp.bfloat16).reshape(group_size, gro...  104 us
    all_to_all x4, blocking collectives, dispatch(): lax.all_to_all(slot_values, 'grp', split_axis=0, concat_axis=0, tiled=True)  63.1 us
    all_gather x1, waiting for transfers between devices, shards(): all_pairs = lax.all_gather(seq_pair, 'grp', axis=0, tiled=True)  46.6 us
    all_gather x1, waiting for transfers between devices, shards(): seq_input = lax.all_gather(attn_input, GROUP_AXES, axis=0, tiled=True)  44.5 us
    all_to_all x2, waiting for transfers between devices, combine(): lax.all_to_all(summed, 'grp', split_axis=0, concat_axis=0, tiled=True)  40.7 us
  transfers between devices with their start and end apart: 22, of which 20 were waited for; matrix products, arithmetic and copies ran while one was open for 12% of the time, Pallas kernels for 2%

profile of v7, /device:TPU:1, one launch (start us, length us, event | category | flops | bytes accessed | tf_op | source)
XLA Modules:
  0.0 1519.3 jit_solution(12751809194098670773)
XLA Ops:
  17.2 37.3 %all-gather.12.cloned.1.call-done = bf16[128,4224]{1,0:T(8,128)(2,1)} async-done(((bf16[16,4224]{1,0:T(8,128)(2,1)}), bf16[128,4224]{1,0:T(8,128)(2,1)}) %all-gather.12.cloned.1.call-update) | async-done | bytes 1081360 | tf_op jit(solution)/shard_map/all_gather | solution.py:289
  54.8 119.1 %all-gather.14.cloned.1.call-done = bf16[2048,4224]{1,0:T(8,128)(2,1)} async-done(((bf16[128,4224]{1,0:T(8,128)(2,1)}), bf16[2048,4224]{1,0:T(8,128)(2,1)}) %all-gather.14.cloned.1.call-update) | async-done | bytes 17301520 | tf_op jit(solution)/shard_map/all_gather | solution.py:288
  173.9 8.1 copy.500
  182.1 6.0 copy-done.4
  189.6 8.3 slice.150
  198.2 44.5 %all-gather.18.cloned.1.call-done = bf16[1024,2048]{1,0:T(8,128)(2,1)} async-done(((bf16[64,2048]{1,0:T(8,128)(2,1)}), bf16[1024,2048]{1,0:T(8,128)(2,1)}) %all-gather.18.cloned.1.call-update) | async-done | bytes 4194320 | tf_op jit(solution)/shard_map/all_gather | solution.py:304
  251.3 22.5 %all_to_all.98 = bf16[8,18,2048]{2,1,0:T(8,128)(2,1)S(1)} all-to-all(bf16[8,18,2048]{2,1,0:T(8,128)(2,1)S(1)} %broadcast_select_fusion.1), channel_id=1, replica_groups=mesh['grp'=8,'sub'=8,'expert'=2] {'grp'}, dimensions={0} | all-to-all | bytes 1179648 | tf_op jit(solution)/shard_map/all_to_all | solution.py:223
  297.3 46.6 %all-gather.20.cloned.1.call-done = bf16[8192,256]{0,1:T(8,128)(2,1)} async-done(((bf16[1024,256]{0,1:T(8,128)(2,1)}), bf16[8192,256]{0,1:T(8,128)(2,1)}) %all-gather.20.cloned.1.call-update) | async-done | bytes 4194320 | tf_op jit(solution)/shard_map/all_gather | solution.py:325
  356.7 68.9 %all-gather.16.cloned.1.call-done = bf16[2304,2048]{1,0:T(8,128)(2,1)} async-done(((bf16[144,2048]{1,0:T(8,128)(2,1)}), bf16[2304,2048]{1,0:T(8,128)(2,1)}) %all-gather.16.cloned.1.call-update) | async-done | bytes 9437200 | tf_op jit(solution)/shard_map/all_gather | solution.py:224
  425.7 7.3 fusion.85
  443.6 10.8 shard_map.238
  462.7 15.8 %all-to-all-done.1 = bf16[16,144,128]{2,1,0:T(8,128)(2,1)S(1)} async-done(((bf16[16,144,128]{2,1,0:T(8,128)(2,1)}), bf16[16,144,128]{2,1,0:T(8,128)(2,1)S(1)}, u32[]{:S(2)}, u32[]{:S(2)}) %all-to-all-start.1) | async-done | bytes 589856 | tf_op jit(solution)/shard_map/all_to_all | solution.py:240
  478.9 26.3 %all-gather.22.cloned.1.call-done = bf16[2048,2048]{1,0:T(8,128)(2,1)} async-done(((bf16[128,2048]{1,0:T(8,128)(2,1)}), bf16[2048,2048]{1,0:T(8,128)(2,1)}) %all-gather.22.cloned.1.call-update) | async-done | bytes 8388624 | tf_op jit(solution)/shard_map/all_gather | solution.py:355
  505.2 6.4 fusion.2
  520.5 19.3 %all-to-all-done.2 = f32[8,18,2048]{2,1,0:T(8,128)} async-done(((f32[8,18,2048]{2,1,0:T(8,128)}), f32[8,18,2048]{2,1,0:T(8,128)}, u32[]{:S(2)}, u32[]{:S(2)}) %all-to-all-start.2) | async-done | bytes 1179680 | tf_op jit(solution)/shard_map/all_to_all | solution.py:250
  549.2 13.7 all_to_all.99
  563.9 76.3 %all-gather.24.cloned.1.call-done = bf16[2304,2048]{1,0:T(8,128)(2,1)} async-done(((bf16[144,2048]{1,0:T(8,128)(2,1)}), bf16[2304,2048]{1,0:T(8,128)(2,1)}) %all-gather.24.cloned.1.call-update) | async-done | bytes 9437200 | tf_op jit(solution)/shard_map/all_gather | solution.py:224
  640.2 7.5 fusion.86
  653.3 7.5 convolution_convert_fusion
  667.2 104.4 %all-to-all-done.4 = bf16[16,144,2048]{2,1,0:T(8,128)(2,1)} async-done(((bf16[16,144,2048]{2,1,0:T(8,128)(2,1)}), bf16[16,144,2048]{2,1,0:T(8,128)(2,1)}, u32[]{:S(2)}, u32[]{:S(2)}) %all-to-all-start.4) | async-done | bytes 9437216 | tf_op jit(solution)/shard_map/all_to_all | solution.py:229
  789.0 17.2 %all-to-all-done.5 = f32[8,18,2048]{2,1,0:T(8,128)} async-done(((f32[8,18,2048]{2,1,0:T(8,128)}), f32[8,18,2048]{2,1,0:T(8,128)}, u32[]{:S(2)}, u32[]{:S(2)}) %all-to-all-start.5) | async-done | bytes 1179680 | tf_op jit(solution)/shard_map/all_to_all | solution.py:237
  817.3 13.2 all_to_all.100
  831.6 79.5 %all-gather.26.cloned.1.call-done = bf16[2304,2048]{1,0:T(8,128)(2,1)} async-done(((bf16[144,2048]{1,0:T(8,128)(2,1)}), bf16[2304,2048]{1,0:T(8,128)(2,1)}) %all-gather.26.cloned.1.call-update) | async-done | bytes 9437200 | tf_op jit(solution)/shard_map/all_gather | solution.py:224
  911.1 11.8 multiply_convert_fusion
  923.0 9.1 fusion.87
  932.1 9.1 add_convert_fusion
  941.2 109.6 %all_to_all.101 = bf16[16,144,2048]{2,1,0:T(8,128)(2,1)} all-to-all(bf16[16,144,2048]{2,1,0:T(8,128)(2,1)S(1)} %bitcast.160), channel_id=1, replica_groups=mesh['grp'=8,'sub'=8,'expert'=2] {'sub','expert'}, dimensions={0} | all-to-all | bytes 18874368 | tf_op jit(solution)/shard_map/all_to_all | solution.py:229
  1063.5 23.4 %all-to-all-done.8 = f32[8,18,2048]{2,1,0:T(8,128)S(1)} async-done(((f32[8,18,2048]{2,1,0:T(8,128)}), f32[8,18,2048]{2,1,0:T(8,128)S(1)}, u32[]{:S(2)}, u32[]{:S(2)}) %all-to-all-start.8) | async-done | bytes 1179680 | tf_op jit(solution)/shard_map/all_to_all | solution.py:237
  1103.9 13.7 all_to_all.102
  1119.2 75.4 %all-gather.28.cloned.1.call-done = bf16[2304,2048]{1,0:T(8,128)(2,1)} async-done(((bf16[144,2048]{1,0:T(8,128)(2,1)}), bf16[2304,2048]{1,0:T(8,128)(2,1)}) %all-gather.28.cloned.1.call-update) | async-done | bytes 9437200 | tf_op jit(solution)/shard_map/all_gather | solution.py:224
  1194.6 6.3 convolution_convert_fusion.1
  1202.0 13.8 shard_map.239
  1215.8 7.9 fusion.18
  1224.5 17.7 %all_to_all.103 = bf16[16,144,128]{2,1,0:T(8,128)(2,1)S(1)} all-to-all(bf16[16,144,128]{2,1,0:T(8,128)(2,1)S(1)} %copy.546), channel_id=1, replica_groups=mesh['grp'=8,'sub'=8,'expert'=2] {'sub','expert'}, dimensions={0} | all-to-all | bytes 1179648 | tf_op jit(solution)/shard_map/all_to_all | solution.py:240
  1242.7 31.2 %all-gather.30.cloned.1.call-done = bf16[2048,2048]{1,0:T(8,128)(2,1)} async-done(((bf16[2048,128]{1,0:T(8,128)(2,1)}), bf16[2048,2048]{1,0:T(8,128)(2,1)}) %all-gather.30.cloned.1.call-update) | async-done | bytes 8388624 | tf_op jit(solution)/shard_map/all_gather | solution.py:445
  1273.9 7.4 fusion
  1289.9 19.8 %all-to-all-done.11 = f32[8,18,2048]{2,1,0:T(8,128)} async-done(((f32[8,18,2048]{2,1,0:T(8,128)}), f32[8,18,2048]{2,1,0:T(8,128)}, u32[]{:S(2)}, u32[]{:S(2)}) %all-to-all-start.11) | async-done | bytes 1179680 | tf_op jit(solution)/shard_map/all_to_all | solution.py:250
  1319.5 25.6 %all-to-all-done.12 = bf16[128,64,1,128]{3,1,2,0:T(8,128)(2,1)} async-done(((bf16[128,64,1,128]{3,1,2,0:T(8,128)(2,1)}), bf16[128,64,1,128]{3,1,2,0:T(8,128)(2,1)}, u32[]{:S(2)}, u32[]{:S(2)}) %all-to-all-start.12) | async-done | bytes 2097184 | tf_op jit(solution)/shard_map/all_to_all | solution.py:452
  1345.1 6.0 all-to-all-start.13
  1367.4 12.8 all-to-all-done.13
  1389.2 8.8 convolution_add_fusion.2
  1408.0 9.4 fusion.93
  1417.4 8.9 fusion.95
  1435.1 6.1 fusion.92
  1441.2 7.4 fusion.91
  1448.6 28.1 %reduce-scatter.2.cloned.1.call-done = f32[256,384]{0,1:T(8,128)} async-done(((f32[2048,384]{0,1:T(8,128)}), f32[256,384]{0,1:T(8,128)}) %reduce-scatter.2.cloned.1.call-update) | async-done | bytes 393232 | tf_op jit(solution)/shard_map/reduce_scatter | solution.py:513
  1478.6 8.3 all-to-all-start.15
  1486.9 20.0 %all-gather.32.cloned.1.call-done = bf16[128,4096]{1,0:T(8,128)(2,1)} async-done(((bf16[64,4096]{1,0:T(8,128)(2,1)}), bf16[128,4096]{1,0:T(8,128)(2,1)}) %all-gather.32.cloned.1.call-update) | async-done | bytes 1048592 | tf_op jit(solution)/shard_map/all_gather | solution.py:527
  (385 shorter events, 239.0 us)
Async XLA Ops:
  7.2 646.1 %copy-start = (bf16[352,2048]{1,0:T(8,128)(2,1)S(1)}, bf16[352,2048]{1,0:T(8,128)(2,1)}, u32[]{:S(2)}) copy-start(bf16[352,2048]{1,0:T(8,128)(2,1)} %param.31) | copy-start | bytes 4325380
  7.2 47.3 %all-gather.12.cloned.1.call-start = ((), (), s32[]{:S(2)}) async-start(), calls=%async_computation.17 | async-start | bytes 1216512 | tf_op jit(solution)/shard_map/all_gather | solution.py:289
  15.9 38.7 %copy-start.14 = (bf16[128,2048]{1,0:T(8,128)(2,1)S(1)}, bf16[128,2048]{1,0:T(8,128)(2,1)}, u32[]{:S(2)}) copy-start(bf16[128,2048]{1,0:T(8,128)(2,1)} %param.21) | copy-start | bytes 1572868
  17.2 156.7 %all-gather.14.cloned.1.call-start = ((), (), s32[]{:S(2)}) async-start(), calls=%async_computation.18 | async-start | bytes 18382848 | tf_op jit(solution)/shard_map/all_gather | solution.py:288
  54.5 188.1 %all-gather.18.cloned.1.call-start = ((), (), s32[]{:S(2)}) async-start(), calls=%async_computation.20 | async-start | bytes 4456448 | tf_op jit(solution)/shard_map/all_gather | solution.py:304
  54.8 133.8 %copy-start.48 = (f32[64]{0:T(128)}, f32[64]{0:T(128)S(1)}, u32[]{:S(2)}) copy-start(f32[64]{0:T(128)S(1)} %add_rsqrt_fusion.1) | copy-start | bytes 772
  188.6 9.3 copy-start.34
  189.5 154.4 %all-gather.20.cloned.1.call-start = ((), (), s32[]{:S(2)}) async-start(), calls=%async_computation.21 | async-start | bytes 4718592 | tf_op jit(solution)/shard_map/all_gather | solution.py:325
  189.6 247.5 %copy-start.46 = (f32[64]{0:T(128)}, f32[64]{0:T(128)S(1)}, u32[]{:S(2)}) copy-start(f32[64]{0:T(128)S(1)} %multiply_exponential_fusion) | copy-start | bytes 772
  248.3 177.4 %all-gather.16.cloned.1.call-start = ((), (), s32[]{:S(2)}) async-start(), calls=%async_computation.19 | async-start | bytes 10027008 | tf_op jit(solution)/shard_map/all_gather | solution.py:224
  274.8 230.4 %all-gather.22.cloned.1.call-start = ((), (), s32[]{:S(2)}) async-start(), calls=%async_computation.22 | async-start | bytes 8912896 | tf_op jit(solution)/shard_map/all_gather | solution.py:355
  293.9 143.1 %copy-start.37 = (f32[2304]{0:T(1024)}, f32[2304]{0:T(1024)S(1)}, u32[]{:S(2)}) copy-start(f32[2304]{0:T(1024)S(1)} %fusion.63) | copy-start | bytes 27652
  352.6 73.1 %copy-start.30 = (bf16[2048,128]{1,0:T(8,128)(2,1)S(1)}, bf16[2048,128]{1,0:T(8,128)(2,1)}, u32[]{:S(2)}) copy-start(bf16[2048,128]{1,0:T(8,128)(2,1)} %param.25) | copy-start | bytes 1572868
  457.6 20.8 %all-to-all-start.1 = ((bf16[16,144,128]{2,1,0:T(8,128)(2,1)}), bf16[16,144,128]{2,1,0:T(8,128)(2,1)S(1)}, u32[]{:S(2)}, u32[]{:S(2)}) async-start(bf16[16,144,128]{2,1,0:T(8,128)(2,1)} %copy.512), calls=%async_computation.1 | async-start | bytes 1179648 | tf_op jit(solution)/shard_map/all_to_all | solution.py:240
  511.5 28.2 %all-to-all-start.2 = ((f32[8,18,2048]{2,1,0:T(8,128)}), f32[8,18,2048]{2,1,0:T(8,128)}, u32[]{:S(2)}, u32[]{:S(2)}) async-start(f32[8,18,2048]{2,1,0:T(8,128)} %fusion.2), calls=%async_computation.2 | async-start | bytes 3145728 | tf_op jit(solution)/shard_map/all_to_all | solution.py:250
  515.8 124.4 %all-gather.24.cloned.1.call-start = ((), (), s32[]{:S(2)}) async-start(), calls=%async_computation.23 | async-start | bytes 10027008 | tf_op jit(solution)/shard_map/all_gather | solution.py:224
  517.5 23.9 %copy-start.25 = (s32[1024]{0:T(1024)}, s32[1024]{0:T(1024)S(1)}, u32[]{:S(2)}) copy-start(s32[1024]{0:T(1024)S(1)} %pad_clamp_fusion.2) | copy-start | bytes 12292
  563.9 83.8 %copy-start.23 = (bf16[2048,352]{0,1:T(8,128)(2,1)S(1)}, bf16[2048,352]{0,1:T(8,128)(2,1)}, u32[]{:S(2)}) copy-start(bf16[2048,352]{0,1:T(8,128)(2,1)} %param.30) | copy-start | bytes 4325380
  653.3 7.5 copy-start.52
  660.8 110.8 %all-to-all-start.4 = ((bf16[16,144,2048]{2,1,0:T(8,128)(2,1)}), bf16[16,144,2048]{2,1,0:T(8,128)(2,1)}, u32[]{:S(2)}, u32[]{:S(2)}) async-start(bf16[16,144,2048]{2,1,0:T(8,128)(2,1)} %bitcast.163), calls=%async_computation.4 | async-start | bytes 18874368 | tf_op jit(solution)/shard_map/all_to_all | solution.py:229
  778.9 27.4 %all-to-all-start.5 = ((f32[8,18,2048]{2,1,0:T(8,128)}), f32[8,18,2048]{2,1,0:T(8,128)}, u32[]{:S(2)}, u32[]{:S(2)}) async-start(f32[8,18,2048]{2,1,0:T(8,128)} %reshape.770), calls=%async_computation.5 | async-start | bytes 3145728 | tf_op jit(solution)/shard_map/all_to_all | solution.py:237
  783.3 127.8 %all-gather.26.cloned.1.call-start = ((), (), s32[]{:S(2)}) async-start(), calls=%async_computation.24 | async-start | bytes 10027008 | tf_op jit(solution)/shard_map/all_gather | solution.py:224
  911.1 11.9 copy-start.22
  922.9 9.2 copy-start.18
  923.0 9.2 copy-start.12
  923.0 9.1 copy-start.24
  1058.0 29.0 %all-to-all-start.8 = ((f32[8,18,2048]{2,1,0:T(8,128)}), f32[8,18,2048]{2,1,0:T(8,128)S(1)}, u32[]{:S(2)}, u32[]{:S(2)}) async-start(f32[8,18,2048]{2,1,0:T(8,128)} %reshape.774), calls=%async_computation.8 | async-start | bytes 3145728 | tf_op jit(solution)/shard_map/all_to_all | solution.py:237
  1062.8 131.7 %all-gather.28.cloned.1.call-start = ((), (), s32[]{:S(2)}) async-start(), calls=%async_computation.25 | async-start | bytes 10027008 | tf_op jit(solution)/shard_map/all_gather | solution.py:224
  1117.6 77.0 %copy-start.29 = (bf16[128,2048]{1,0:T(8,128)(2,1)S(1)}, bf16[128,2048]{1,0:T(8,128)(2,1)}, u32[]{:S(2)}) copy-start(bf16[128,2048]{1,0:T(8,128)(2,1)} %param.26) | copy-start | bytes 1572868
  1118.6 155.3 %all-gather.30.cloned.1.call-start = ((), (), s32[]{:S(2)}) async-start(), calls=%async_computation.26 | async-start | bytes 8912896 | tf_op jit(solution)/shard_map/all_gather | solution.py:445
  1202.0 13.8 copy-start.38
  1202.0 13.8 copy-start.47
  1281.3 28.5 %all-to-all-start.11 = ((f32[8,18,2048]{2,1,0:T(8,128)}), f32[8,18,2048]{2,1,0:T(8,128)}, u32[]{:S(2)}, u32[]{:S(2)}) async-start(f32[8,18,2048]{2,1,0:T(8,128)} %fusion), calls=%async_computation.11 | async-start | bytes 3145728 | tf_op jit(solution)/shard_map/all_to_all | solution.py:250
  1309.7 35.4 %all-to-all-start.12 = ((bf16[128,64,1,128]{3,1,2,0:T(8,128)(2,1)}), bf16[128,64,1,128]{3,1,2,0:T(8,128)(2,1)}, u32[]{:S(2)}, u32[]{:S(2)}) async-start(bf16[128,64,1,128]{3,1,2,0:T(8,128)(2,1)} %bitcast.169), calls=%async_computation.12 | async-start | bytes 4194304 | tf_op jit(solution)/shard_map/all_to_all | solution.py:452
  1345.1 35.1 %all-to-all-start.13 = ((bf16[128,64,1,128]{3,1,2,0:T(8,128)(2,1)}), bf16[128,64,1,128]{3,1,2,0:T(8,128)(2,1)}, u32[]{:S(2)}, u32[]{:S(2)}) async-start(bf16[128,64,1,128]{3,1,2,0:T(8,128)(2,1)} %bitcast.168), calls=%async_computation.13 | async-start | bytes 4194304 | tf_op jit(solution)/shard_map/all_to_all | solution.py:459
  1384.5 16.5 %all-to-all-start.14 = ((bf16[64,16,256]{2,0,1:T(8,128)(2,1)}), bf16[64,16,256]{2,0,1:T(8,128)(2,1)}, u32[]{:S(2)}, u32[]{:S(2)}) async-start(bf16[64,16,256]{2,0,1:T(8,128)(2,1)} %copy.556), calls=%async_computation.14 | async-start | bytes 1048576 | tf_op jit(solution)/shard_map/all_to_all | solution.py:486
  1389.1 8.9 copy-start.16
  1389.1 8.9 copy-start.35
  1389.1 8.9 copy-start.49
  1389.1 87.5 %reduce-scatter.2.cloned.1.call-start = ((), (), s32[]{:S(2)}) async-start(), calls=%async_computation.28 | async-start | bytes 3538944 | tf_op jit(solution)/shard_map/reduce_scatter | solution.py:513
  1406.5 100.3 %all-gather.32.cloned.1.call-start = ((), (), s32[]{:S(2)}) async-start(), calls=%async_computation.27 | async-start | bytes 1572864 | tf_op jit(solution)/shard_map/all_gather | solution.py:527
  1407.9 9.4 copy-start.13
  1407.9 18.4 %slice-start = ((s8[9437184]{0:T(1024)(128)(4,1)}), s8[4194304]{0:T(1024)(128)(4,1)S(1)}, s32[]{:S(2)}) async-start(s8[9437184]{0:T(1024)(128)(4,1)} %bitcast.189), calls=%async_computation.29 | async-start | bytes 8388608
  1408.0 18.3 %slice-start.1 = ((s8[9437184]{0:T(1024)(128)(4,1)}), s8[4194304]{0:T(1024)(128)(4,1)S(1)}, s32[]{:S(2)}) async-start(s8[9437184]{0:T(1024)(128)(4,1)} %bitcast.189), calls=%async_computation.30 | async-start | bytes 8388608
  1417.4 8.9 copy-start.19
  1417.4 8.9 slice-start.2
  1478.6 30.5 %all-to-all-start.15 = ((f32[16,16,384]{2,1,0:T(8,128)}), f32[16,16,384]{2,1,0:T(8,128)S(1)}, u32[]{:S(2)}, u32[]{:S(2)}) async-start(f32[16,16,384]{2,1,0:T(8,128)} %bitcast.54), calls=%async_computation.16 | async-start | bytes 786432 | tf_op jit(solution)/shard_map/all_to_all | solution.py:514
  1486.9 25.1 %copy-start.1 = (bf16[352,2048]{1,0:T(8,128)(2,1)S(1)}, bf16[352,2048]{1,0:T(8,128)(2,1)}, u32[]{:S(2)}) copy-start(bf16[352,2048]{1,0:T(8,128)(2,1)} %param.31) | copy-start | bytes 4325380
  (30 other events, 97.0 us)
Sparse Core Ops, SparseCore 0:
  17.3 37.1 all-gather.11
  57.0 116.8 all-gather.13
  189.6 53.0 all-gather.17
  248.4 95.4 all-gather.19
  346.8 78.8 all-gather.15
  428.0 77.1 all-gather.21
  564.0 76.1 all-gather.23
  831.7 79.3 all-gather.25
  1118.7 75.8 all-gather.27
  1196.7 77.1 all-gather.29
  1406.6 69.9 reduce-scatter.1
  1478.7 28.0 all-gather.31

commit v8 on v7

--- a/solution.py
+++ b/solution.py
@@ -322,7 +322,13 @@
         ],
         axis=1,
     )
-    all_pairs = lax.all_gather(seq_pair, "grp", axis=0, tiled=True)
+    all_pairs = lax.all_to_all(
+        jnp.broadcast_to(seq_pair[None], (groups,) + seq_pair.shape),
+        "grp",
+        split_axis=0,
+        concat_axis=0,
+        tiled=True,
+    ).reshape(groups * seq_length, 2 * head_cols)
     seq_keys = all_pairs[:, :head_cols].reshape(sequences, seq_length, local_heads, HEAD)
     seq_values = all_pairs[:, head_cols:].reshape(sequences, seq_length, local_heads, HEAD)
     attn_places, attn_kept, attn_token, attn_valid = slot_table(own_attn, token_order, slot_cap)
@@ -366,26 +372,43 @@
     normed_two = hidden_state * inverse_two
     mlp_input = (normed_two * gain_two.astype(jnp.float32)).astype(jnp.bfloat16)
     mlp_logits = jnp.dot(mlp_input, router_two, preferred_element_type=jnp.float32)
-    mlp_rows = dispatch(pick_slots(mlp_input, mlp_token, mlp_valid))
+    mlp_gates = pair_gates(mlp_logits, own_mlp)
+    mlp_index, mlp_pair_kept = pair_index(own_mlp, mlp_places, mlp_kept, slot_cap)
+    mlp_slot_grad = (
+        own_cotangent[mlp_token]
+        * slot_gates(mlp_gates, mlp_pair_kept, own_mlp, mlp_token, mlp_valid)[:, :, None]
+    ).astype(jnp.bfloat16)
+    mlp_by_group = lax.all_to_all(
+        jnp.concatenate([pick_slots(mlp_input, mlp_token, mlp_valid), mlp_slot_grad], axis=1),
+        "grp",
+        split_axis=0,
+        concat_axis=0,
+        tiled=True,
+    )
+    mlp_rows = lax.all_gather(
+        mlp_by_group[:, :slot_cap].reshape(groups * slot_cap, width),
+        GROUP_AXES,
+        axis=0,
+        tiled=True,
+    )
+    down_rows = lax.all_gather(
+        mlp_by_group[:, slot_cap:].reshape(groups * slot_cap, width),
+        GROUP_AXES,
+        axis=0,
+        tiled=True,
+    )
     gate_pre = jnp.dot(mlp_rows, gate_weight, preferred_element_type=jnp.float32)
     up_pre = jnp.dot(mlp_rows, up_weight, preferred_element_type=jnp.float32)
     activated = jax.nn.silu(gate_pre)
     inner_rows = (activated * up_pre).astype(jnp.bfloat16)
     mlp_partial = jnp.dot(inner_rows, down_weight, preferred_element_type=jnp.float32)
     mlp_slots = combine(mlp_partial)
-    mlp_gates = pair_gates(mlp_logits, own_mlp)
-    mlp_index, mlp_pair_kept = pair_index(own_mlp, mlp_places, mlp_kept, slot_cap)
     mlp_picked = mlp_slots.reshape(EXPERTS * slot_cap, width)[mlp_index]
     own_output = hidden_state + jnp.sum(
         mlp_picked * (mlp_gates * mlp_pair_kept)[:, :, None], axis=1
     )
     mlp_gate_grad = jnp.sum(mlp_picked * own_cotangent[:, None, :], axis=-1) * mlp_pair_kept
     mlp_logit_grad = gates_back(mlp_gates, mlp_gate_grad, own_mlp)
-    mlp_slot_grad = (
-        own_cotangent[mlp_token]
-        * slot_gates(mlp_gates, mlp_pair_kept, own_mlp, mlp_token, mlp_valid)[:, :, None]
-    ).astype(jnp.bfloat16)
-    down_rows = dispatch(mlp_slot_grad)
     inner_grad = jnp.einsum("rd,fd->rf", down_rows, down_weight, preferred_element_type=jnp.float32)
     down_grad = jnp.einsum("rf,rd->fd", inner_rows, down_rows, preferred_element_type=jnp.float32)
     sigmoid_gate = jax.nn.sigmoid(gate_pre)

time: 1530 us -> 1430 us (0.935)
  blocking collectives: 190 us -> 65 us
    all_gather x4 -> x2, waiting for transfers between devices: 300 us -> 123 us  [dispatch(): lax.all_gather(by_group.reshape(groups * slot_cap, width), GROUP_AXES, ax...]
    all_gather x1 -> x2, waiting for transfers between devices: 46.6 us -> 143 us  [the longest x1 73.8 us: shards(): lax.all_gather(mlp_by_group[:, :slot_cap].reshape(groups * slot_cap, widt...]
    all_to_all x1, blocking collectives: 110 us -> 19.2 us  [shards(): lax.all_to_all(jnp.concatenate([pick_slots(mlp_input, mlp_token, mlp_vali...]
    all_to_all x1 -> x2, waiting for transfers between devices: 104 us -> 183 us  [combine(): lax.all_to_all(partial_value.astype(jnp.bfloat16).reshape(group_size, gro...]
    all_to_all x0 -> x1, waiting for transfers between devices: none -> 37.4 us  [shards(): lax.all_to_all(jnp.broadcast_to(seq_pair[None], (groups,) + seq_pair.shap...]
    all_to_all x4 -> x2, blocking collectives: 63.1 us -> 28.2 us  [dispatch(): lax.all_to_all(slot_values, 'grp', split_axis=0, concat_axis=0, tiled=True)]
  transfers between devices with their start and end apart: 22 -> 23, of which waited for: 20 -> 21; matrix products, arithmetic and copies ran while one was open for 12% -> 17% of each run, Pallas kernels for 2% -> 2%
where the time goes in v8:
time: 1430 us; the launch traced here: 1420 us
  waiting for transfers between devices  892 us (62%)
  matrix products  144 us (10%)
  local copies, waits for them, and re-layouts  135 us (9%)
  other arithmetic  81.7 us (6%)
  blocking collectives  65 us (5%)
  starting transfers between devices  63.5 us (4%)
  Pallas kernels  24.6 us (2%)
  between operations  15.8 us (1%)
    all_to_all x2, waiting for transfers between devices, combine(): lax.all_to_all(partial_value.astype(jnp.bfloat16).reshape(group_size, gro...  183 us
    all_gather x2, waiting for transfers between devices, dispatch(): lax.all_gather(by_group.reshape(groups * slot_cap, width), GROUP_AXES, ax...  123 us
    all_gather x1, waiting for transfers between devices, shards(): lax.all_gather(lax.all_gather(packed, 'grp', axis=0, tiled=True), GROUP_A...  119 us
    all_gather x1, waiting for transfers between devices, shards(): lax.all_gather(mlp_by_group[:, :slot_cap].reshape(groups * slot_cap, widt...  73.8 us
    all_gather x1, waiting for transfers between devices, shards(): lax.all_gather(mlp_by_group[:, slot_cap:].reshape(groups * slot_cap, widt...  69 us
    all_to_all x1, waiting for transfers between devices, shards(): lax.all_to_all(jnp.broadcast_to(seq_pair[None], (groups,) + seq_pair.shap...  37.4 us
    all_gather x1, waiting for transfers between devices, shards(): lax.all_gather(packed, 'grp', axis=0, tiled=True)  37.3 us
    all_to_all x2, waiting for transfers between devices, to_owners(): lax.all_to_all(row_values.reshape(groups, slot_cap, width), 'grp', split_...  33 us
  transfers between devices with their start and end apart: 23, of which 21 were waited for; matrix products, arithmetic and copies ran while one was open for 17% of the time, Pallas kernels for 2%

profile of v8, /device:TPU:1, one launch (start us, length us, event | category | flops | bytes accessed | tf_op | source)
XLA Modules:
  0.0 1421.2 jit_solution(16367807882572894516)
XLA Ops:
  17.8 37.3 %all-gather.11.cloned.1.call-done = bf16[128,4224]{1,0:T(8,128)(2,1)} async-done(((bf16[16,4224]{1,0:T(8,128)(2,1)}), bf16[128,4224]{1,0:T(8,128)(2,1)}) %all-gather.11.cloned.1.call-update) | async-done | bytes 1081360 | tf_op jit(solution)/shard_map/all_gather | solution.py:289
  55.3 119.1 %all-gather.13.cloned.1.call-done = bf16[2048,4224]{1,0:T(8,128)(2,1)} async-done(((bf16[128,4224]{1,0:T(8,128)(2,1)}), bf16[2048,4224]{1,0:T(8,128)(2,1)}) %all-gather.13.cloned.1.call-update) | async-done | bytes 17301520 | tf_op jit(solution)/shard_map/all_gather | solution.py:288
  174.5 8.1 copy.491
  192.4 15.8 %all_to_all.98 = bf16[8,18,2048]{2,1,0:T(8,128)(2,1)S(1)} all-to-all(bf16[8,18,2048]{2,1,0:T(8,128)(2,1)S(1)} %broadcast_select_fusion.1), channel_id=1, replica_groups=mesh['grp'=8,'sub'=8,'expert'=2] {'grp'}, dimensions={0} | all-to-all | bytes 1179648 | tf_op jit(solution)/shard_map/all_to_all | solution.py:223
  209.8 8.2 slice.158
  218.3 30.7 %all-gather.17.cloned.1.call-done = bf16[1024,2048]{1,0:T(8,128)(2,1)} async-done(((bf16[64,2048]{1,0:T(8,128)(2,1)}), bf16[1024,2048]{1,0:T(8,128)(2,1)}) %all-gather.17.cloned.1.call-update) | async-done | bytes 4194320 | tf_op jit(solution)/shard_map/all_gather | solution.py:304
  283.1 37.4 %all-to-all-done.1 = bf16[8,1024,256]{2,1,0:T(8,128)(2,1)} async-done(((bf16[8,1024,256]{2,1,0:T(8,128)(2,1)}), bf16[8,1024,256]{2,1,0:T(8,128)(2,1)}, u32[]{:S(2)}, u32[]{:S(2)}) %all-to-all-start.1) | async-done | bytes 4194336 | tf_op jit(solution)/shard_map/all_to_all | solution.py:325
  325.0 41.9 %all-gather.15.cloned.1.call-done = bf16[2304,2048]{1,0:T(8,128)(2,1)} async-done(((bf16[144,2048]{1,0:T(8,128)(2,1)}), bf16[2304,2048]{1,0:T(8,128)(2,1)}) %all-gather.15.cloned.1.call-update) | async-done | bytes 9437200 | tf_op jit(solution)/shard_map/all_gather | solution.py:224
  366.9 7.3 fusion.86
  384.9 10.8 shard_map.238
  404.9 14.8 %all-to-all-done.2 = bf16[16,144,128]{2,1,0:T(8,128)(2,1)S(1)} async-done(((bf16[16,144,128]{2,1,0:T(8,128)(2,1)}), bf16[16,144,128]{2,1,0:T(8,128)(2,1)S(1)}, u32[]{:S(2)}, u32[]{:S(2)}) %all-to-all-start.2) | async-done | bytes 589856 | tf_op jit(solution)/shard_map/all_to_all | solution.py:240
  422.1 24.3 %all-gather.19.cloned.1.call-done = bf16[2048,2048]{1,0:T(8,128)(2,1)} async-done(((bf16[128,2048]{1,0:T(8,128)(2,1)}), bf16[2048,2048]{1,0:T(8,128)(2,1)}) %all-gather.19.cloned.1.call-update) | async-done | bytes 8388624 | tf_op jit(solution)/shard_map/all_gather | solution.py:361
  446.4 6.4 fusion.2
  467.8 13.3 all-to-all-done.3
  504.8 19.2 %all_to_all.99 = bf16[8,36,2048]{2,1,0:T(8,128)(2,1)S(1)} all-to-all(bf16[8,36,2048]{2,1,0:T(8,128)(2,1)S(1)} %pad_maximum_fusion.1), channel_id=1, replica_groups=mesh['grp'=8,'sub'=8,'expert'=2] {'grp'}, dimensions={0} | all-to-all | bytes 2359296 | tf_op jit(solution)/shard_map/all_to_all | solution.py:381
  530.0 73.8 %all-gather.21.cloned.1.call-done = bf16[2304,2048]{1,0:T(8,128)(2,1)} async-done(((bf16[144,2048]{1,0:T(8,128)(2,1)}), bf16[2304,2048]{1,0:T(8,128)(2,1)}) %all-gather.21.cloned.1.call-update) | async-done | bytes 9437200 | tf_op jit(solution)/shard_map/all_gather | solution.py:388
  603.8 9.3 fusion.87
  613.1 69.0 %all-gather.23.cloned.1.call-done = bf16[2304,2048]{1,0:T(8,128)(2,1)} async-done(((bf16[144,2048]{1,0:T(8,128)(2,1)}), bf16[2304,2048]{1,0:T(8,128)(2,1)}) %all-gather.23.cloned.1.call-update) | async-done | bytes 9437200 | tf_op jit(solution)/shard_map/all_gather | solution.py:394
  682.1 7.1 fusion.88
  689.9 8.6 multiply_convert_fusion.2
  698.5 7.5 convolution_convert_fusion
  711.2 10.7 fusion.89
  722.0 11.2 add_convert_fusion
  733.2 83.9 %all-to-all-done.5 = bf16[16,144,2048]{2,1,0:T(8,128)(2,1)} async-done(((bf16[16,144,2048]{2,1,0:T(8,128)(2,1)}), bf16[16,144,2048]{2,1,0:T(8,128)(2,1)}, u32[]{:S(2)}, u32[]{:S(2)}) %all-to-all-start.5) | async-done | bytes 9437216 | tf_op jit(solution)/shard_map/all_to_all | solution.py:229
  829.8 98.8 %all-to-all-done.7 = bf16[16,144,2048]{2,1,0:T(8,128)(2,1)} async-done(((bf16[16,144,2048]{2,1,0:T(8,128)(2,1)}), bf16[16,144,2048]{2,1,0:T(8,128)(2,1)}, u32[]{:S(2)}, u32[]{:S(2)}) %all-to-all-start.7) | async-done | bytes 9437216 | tf_op jit(solution)/shard_map/all_to_all | solution.py:229
  940.1 15.8 %all-to-all-done.6 = f32[8,18,2048]{2,1,0:T(8,128)} async-done(((f32[8,18,2048]{2,1,0:T(8,128)}), f32[8,18,2048]{2,1,0:T(8,128)}, u32[]{:S(2)}, u32[]{:S(2)}) %all-to-all-start.6) | async-done | bytes 1179680 | tf_op jit(solution)/shard_map/all_to_all | solution.py:237
  969.6 12.6 all-to-all-done.8
  1001.0 12.5 all_to_all.100
  1015.3 80.7 %all-gather.25.cloned.1.call-done = bf16[2304,2048]{1,0:T(8,128)(2,1)} async-done(((bf16[144,2048]{1,0:T(8,128)(2,1)}), bf16[2304,2048]{1,0:T(8,128)(2,1)}) %all-gather.25.cloned.1.call-update) | async-done | bytes 9437200 | tf_op jit(solution)/shard_map/all_gather | solution.py:224
  1096.0 6.3 convolution_convert_fusion.1
  1103.4 13.8 shard_map.239
  1117.2 7.9 fusion.18
  1125.9 17.6 %all_to_all.101 = bf16[16,144,128]{2,1,0:T(8,128)(2,1)S(1)} all-to-all(bf16[16,144,128]{2,1,0:T(8,128)(2,1)S(1)} %copy.536), channel_id=1, replica_groups=mesh['grp'=8,'sub'=8,'expert'=2] {'sub','expert'}, dimensions={0} | all-to-all | bytes 1179648 | tf_op jit(solution)/shard_map/all_to_all | solution.py:240
  1144.0 31.3 %all-gather.27.cloned.1.call-done = bf16[2048,2048]{1,0:T(8,128)(2,1)} async-done(((bf16[2048,128]{1,0:T(8,128)(2,1)}), bf16[2048,2048]{1,0:T(8,128)(2,1)}) %all-gather.27.cloned.1.call-update) | async-done | bytes 8388624 | tf_op jit(solution)/shard_map/all_gather | solution.py:468
  1175.3 7.4 fusion
  1191.4 19.7 %all-to-all-done.11 = f32[8,18,2048]{2,1,0:T(8,128)S(1)} async-done(((f32[8,18,2048]{2,1,0:T(8,128)}), f32[8,18,2048]{2,1,0:T(8,128)S(1)}, u32[]{:S(2)}, u32[]{:S(2)}) %all-to-all-start.11) | async-done | bytes 1179680 | tf_op jit(solution)/shard_map/all_to_all | solution.py:250
  1212.2 5.9 all-to-all-start.12
  1221.9 25.6 %all-to-all-done.12 = bf16[128,64,1,128]{3,1,2,0:T(8,128)(2,1)} async-done(((bf16[128,64,1,128]{3,1,2,0:T(8,128)(2,1)}), bf16[128,64,1,128]{3,1,2,0:T(8,128)(2,1)}, u32[]{:S(2)}, u32[]{:S(2)}) %all-to-all-start.12) | async-done | bytes 2097184 | tf_op jit(solution)/shard_map/all_to_all | solution.py:475
  1247.6 6.0 all-to-all-start.13
  1268.5 14.2 %all-to-all-done.13 = bf16[128,64,1,128]{3,1,2,0:T(8,128)(2,1)} async-done(((bf16[128,64,1,128]{3,1,2,0:T(8,128)(2,1)}), bf16[128,64,1,128]{3,1,2,0:T(8,128)(2,1)}, u32[]{:S(2)}, u32[]{:S(2)}) %all-to-all-start.13) | async-done | bytes 2097184 | tf_op jit(solution)/shard_map/all_to_all | solution.py:482
  1291.7 8.8 convolution_add_fusion.2
  1312.2 9.4 fusion.95
  1321.6 9.0 fusion.96
  1339.4 6.1 fusion.94
  1345.5 7.4 fusion.93
  1352.9 26.0 %reduce-scatter.2.cloned.1.call-done = f32[256,384]{0,1:T(8,128)} async-done(((f32[2048,384]{0,1:T(8,128)}), f32[256,384]{0,1:T(8,128)}) %reduce-scatter.2.cloned.1.call-update) | async-done | bytes 393232 | tf_op jit(solution)/shard_map/reduce_scatter | solution.py:536
  1380.8 8.3 all-to-all-start.15
  1389.1 20.0 %all-gather.29.cloned.1.call-done = bf16[128,4096]{1,0:T(8,128)(2,1)} async-done(((bf16[64,4096]{1,0:T(8,128)(2,1)}), bf16[128,4096]{1,0:T(8,128)(2,1)}) %all-gather.29.cloned.1.call-update) | async-done | bytes 1048592 | tf_op jit(solution)/shard_map/all_gather | solution.py:550
  (369 shorter events, 258.5 us)
Async XLA Ops:
  7.2 682.1 %copy-start = (bf16[2048,352]{0,1:T(8,128)(2,1)S(1)}, bf16[2048,352]{0,1:T(8,128)(2,1)}, u32[]{:S(2)}) copy-start(bf16[2048,352]{0,1:T(8,128)(2,1)} %param.30) | copy-start | bytes 4325380
  7.2 47.9 %all-gather.11.cloned.1.call-start = ((), (), s32[]{:S(2)}) async-start(), calls=%async_computation.17 | async-start | bytes 1216512 | tf_op jit(solution)/shard_map/all_gather | solution.py:289
  15.9 39.2 %copy-start.10 = (bf16[128,2048]{1,0:T(8,128)(2,1)S(1)}, bf16[128,2048]{1,0:T(8,128)(2,1)}, u32[]{:S(2)}) copy-start(bf16[128,2048]{1,0:T(8,128)(2,1)} %param.21) | copy-start | bytes 1572868
  17.7 156.7 %all-gather.13.cloned.1.call-start = ((), (), s32[]{:S(2)}) async-start(), calls=%async_computation.18 | async-start | bytes 18382848 | tf_op jit(solution)/shard_map/all_gather | solution.py:288
  55.1 193.9 %all-gather.17.cloned.1.call-start = ((), (), s32[]{:S(2)}) async-start(), calls=%async_computation.20 | async-start | bytes 4456448 | tf_op jit(solution)/shard_map/all_gather | solution.py:304
  55.3 127.8 %copy-start.36 = (f32[64]{0:T(128)}, f32[64]{0:T(128)S(1)}, u32[]{:S(2)}) copy-start(f32[64]{0:T(128)S(1)} %add_rsqrt_fusion.1) | copy-start | bytes 772
  183.2 7.9 copy-start.21
  189.4 177.5 %all-gather.15.cloned.1.call-start = ((), (), s32[]{:S(2)}) async-start(), calls=%async_computation.19 | async-start | bytes 10027008 | tf_op jit(solution)/shard_map/all_gather | solution.py:224
  209.2 237.3 %all-gather.19.cloned.1.call-start = ((), (), s32[]{:S(2)}) async-start(), calls=%async_computation.21 | async-start | bytes 8912896 | tf_op jit(solution)/shard_map/all_gather | solution.py:361
  209.8 168.5 %copy-start.34 = (f32[64]{0:T(128)}, f32[64]{0:T(128)S(1)}, u32[]{:S(2)}) copy-start(f32[64]{0:T(128)S(1)} %multiply_exponential_fusion) | copy-start | bytes 772
  256.2 64.3 %all-to-all-start.1 = ((bf16[8,1024,256]{2,1,0:T(8,128)(2,1)}), bf16[8,1024,256]{2,1,0:T(8,128)(2,1)}, u32[]{:S(2)}, u32[]{:S(2)}) async-start(bf16[8,1024,256]{2,1,0:T(8,128)(2,1)} %broadcast_in_dim.53), calls=%async_computation.1 | async-start | bytes 8388608 | tf_op jit(solution)/shard_map/all_to_all | solution.py:325
  279.7 98.7 %copy-start.24 = (f32[2304]{0:T(1024)}, f32[2304]{0:T(1024)S(1)}, u32[]{:S(2)}) copy-start(f32[2304]{0:T(1024)S(1)} %fusion.63) | copy-start | bytes 27652
  320.5 46.5 %copy-start.18 = (bf16[2048,128]{1,0:T(8,128)(2,1)S(1)}, bf16[2048,128]{1,0:T(8,128)(2,1)}, u32[]{:S(2)}) copy-start(bf16[2048,128]{1,0:T(8,128)(2,1)} %param.25) | copy-start | bytes 1572868
  399.0 20.8 %all-to-all-start.2 = ((bf16[16,144,128]{2,1,0:T(8,128)(2,1)}), bf16[16,144,128]{2,1,0:T(8,128)(2,1)S(1)}, u32[]{:S(2)}, u32[]{:S(2)}) async-start(bf16[16,144,128]{2,1,0:T(8,128)(2,1)} %copy.502), calls=%async_computation.2 | async-start | bytes 1179648 | tf_op jit(solution)/shard_map/all_to_all | solution.py:240
  452.8 28.3 %all-to-all-start.3 = ((f32[8,18,2048]{2,1,0:T(8,128)}), f32[8,18,2048]{2,1,0:T(8,128)}, u32[]{:S(2)}, u32[]{:S(2)}) async-start(f32[8,18,2048]{2,1,0:T(8,128)} %fusion.2), calls=%async_computation.3 | async-start | bytes 3145728 | tf_op jit(solution)/shard_map/all_to_all | solution.py:250
  457.1 146.7 %all-gather.21.cloned.1.call-start = ((), (), s32[]{:S(2)}) async-start(), calls=%async_computation.22 | async-start | bytes 10027008 | tf_op jit(solution)/shard_map/all_gather | solution.py:388
  527.6 154.5 %all-gather.23.cloned.1.call-start = ((), (), s32[]{:S(2)}) async-start(), calls=%async_computation.23 | async-start | bytes 10027008 | tf_op jit(solution)/shard_map/all_gather | solution.py:394
  682.1 7.8 copy-start.42
  689.9 8.6 copy-start.41
  698.5 7.5 copy-start.43
  706.1 111.1 %all-to-all-start.5 = ((bf16[16,144,2048]{2,1,0:T(8,128)(2,1)}), bf16[16,144,2048]{2,1,0:T(8,128)(2,1)}, u32[]{:S(2)}, u32[]{:S(2)}) async-start(bf16[16,144,2048]{2,1,0:T(8,128)(2,1)} %bitcast.164), calls=%async_computation.5 | async-start | bytes 18874368 | tf_op jit(solution)/shard_map/all_to_all | solution.py:229
  711.2 10.8 copy-start.8
  817.2 111.5 %all-to-all-start.7 = ((bf16[16,144,2048]{2,1,0:T(8,128)(2,1)}), bf16[16,144,2048]{2,1,0:T(8,128)(2,1)}, u32[]{:S(2)}, u32[]{:S(2)}) async-start(bf16[16,144,2048]{2,1,0:T(8,128)(2,1)} %bitcast.161), calls=%async_computation.7 | async-start | bytes 18874368 | tf_op jit(solution)/shard_map/all_to_all | solution.py:229
  928.6 27.3 %all-to-all-start.6 = ((f32[8,18,2048]{2,1,0:T(8,128)}), f32[8,18,2048]{2,1,0:T(8,128)}, u32[]{:S(2)}, u32[]{:S(2)}) async-start(f32[8,18,2048]{2,1,0:T(8,128)} %reshape.775), calls=%async_computation.6 | async-start | bytes 3145728 | tf_op jit(solution)/shard_map/all_to_all | solution.py:237
  940.1 20.5 %copy-start.30 = (s32[8,18,1]{0,1,2:T(8,128)S(1)}, s32[8,18,1]{0,1,2:T(8,128)}, u32[]{:S(2)}) copy-start(s32[8,18,1]{0,1,2:T(8,128)} %get-tuple-element.172) | copy-start | bytes 1732
  940.1 20.7 %copy-start.38 = (s32[64,2]{0,1:T(2,128)S(1)}, s32[64,2]{0,1:T(2,128)}, u32[]{:S(2)}) copy-start(s32[64,2]{0,1:T(2,128)} %get-tuple-element.184) | copy-start | bytes 1540
  955.9 26.4 %all-to-all-start.8 = ((f32[8,18,2048]{2,1,0:T(8,128)}), f32[8,18,2048]{2,1,0:T(8,128)}, u32[]{:S(2)}, u32[]{:S(2)}) async-start(f32[8,18,2048]{2,1,0:T(8,128)} %reshape.779), calls=%async_computation.8 | async-start | bytes 3145728 | tf_op jit(solution)/shard_map/all_to_all | solution.py:237
  960.2 135.8 %all-gather.25.cloned.1.call-start = ((), (), s32[]{:S(2)}) async-start(), calls=%async_computation.24 | async-start | bytes 10027008 | tf_op jit(solution)/shard_map/all_gather | solution.py:224
  1013.5 82.5 %copy-start.17 = (bf16[128,2048]{1,0:T(8,128)(2,1)S(1)}, bf16[128,2048]{1,0:T(8,128)(2,1)}, u32[]{:S(2)}) copy-start(bf16[128,2048]{1,0:T(8,128)(2,1)} %param.26) | copy-start | bytes 1572868
  1014.5 160.7 %all-gather.27.cloned.1.call-start = ((), (), s32[]{:S(2)}) async-start(), calls=%async_computation.25 | async-start | bytes 8912896 | tf_op jit(solution)/shard_map/all_gather | solution.py:468
  1103.4 13.8 copy-start.25
  1103.4 13.8 copy-start.35
  1182.7 28.4 %all-to-all-start.11 = ((f32[8,18,2048]{2,1,0:T(8,128)}), f32[8,18,2048]{2,1,0:T(8,128)S(1)}, u32[]{:S(2)}, u32[]{:S(2)}) async-start(f32[8,18,2048]{2,1,0:T(8,128)} %fusion), calls=%async_computation.11 | async-start | bytes 3145728 | tf_op jit(solution)/shard_map/all_to_all | solution.py:250
  1212.2 35.4 %all-to-all-start.12 = ((bf16[128,64,1,128]{3,1,2,0:T(8,128)(2,1)}), bf16[128,64,1,128]{3,1,2,0:T(8,128)(2,1)}, u32[]{:S(2)}, u32[]{:S(2)}) async-start(bf16[128,64,1,128]{3,1,2,0:T(8,128)(2,1)} %bitcast.166), calls=%async_computation.12 | async-start | bytes 4194304 | tf_op jit(solution)/shard_map/all_to_all | solution.py:475
  1247.6 35.1 %all-to-all-start.13 = ((bf16[128,64,1,128]{3,1,2,0:T(8,128)(2,1)}), bf16[128,64,1,128]{3,1,2,0:T(8,128)(2,1)}, u32[]{:S(2)}, u32[]{:S(2)}) async-start(bf16[128,64,1,128]{3,1,2,0:T(8,128)(2,1)} %bitcast.165), calls=%async_computation.13 | async-start | bytes 4194304 | tf_op jit(solution)/shard_map/all_to_all | solution.py:482
  1287.0 16.2 %all-to-all-start.14 = ((bf16[64,16,256]{2,0,1:T(8,128)(2,1)}), bf16[64,16,256]{2,0,1:T(8,128)(2,1)}, u32[]{:S(2)}, u32[]{:S(2)}) async-start(bf16[64,16,256]{2,0,1:T(8,128)(2,1)} %copy.546), calls=%async_computation.14 | async-start | bytes 1048576 | tf_op jit(solution)/shard_map/all_to_all | solution.py:509
  1291.6 8.9 copy-start.12
  1291.6 8.9 copy-start.22
  1291.6 8.9 copy-start.37
  1291.6 87.3 %reduce-scatter.2.cloned.1.call-start = ((), (), s32[]{:S(2)}) async-start(), calls=%async_computation.27 | async-start | bytes 3538944 | tf_op jit(solution)/shard_map/reduce_scatter | solution.py:536
  1308.7 100.3 %all-gather.29.cloned.1.call-start = ((), (), s32[]{:S(2)}) async-start(), calls=%async_computation.26 | async-start | bytes 1572864 | tf_op jit(solution)/shard_map/all_gather | solution.py:550
  1312.1 9.4 copy-start.14
  1312.1 18.4 %slice-start = ((s8[9437184]{0:T(1024)(128)(4,1)}), s8[4194304]{0:T(1024)(128)(4,1)S(1)}, s32[]{:S(2)}) async-start(s8[9437184]{0:T(1024)(128)(4,1)} %bitcast.190), calls=%async_computation.28 | async-start | bytes 8388608
  1312.1 18.4 %slice-start.1 = ((s8[9437184]{0:T(1024)(128)(4,1)}), s8[4194304]{0:T(1024)(128)(4,1)S(1)}, s32[]{:S(2)}) async-start(s8[9437184]{0:T(1024)(128)(4,1)} %bitcast.190), calls=%async_computation.29 | async-start | bytes 8388608
  1321.6 9.0 copy-start.9
  1321.6 9.0 slice-start.2
  1380.8 30.5 %all-to-all-start.15 = ((f32[16,16,384]{2,1,0:T(8,128)}), f32[16,16,384]{2,1,0:T(8,128)S(1)}, u32[]{:S(2)}, u32[]{:S(2)}) async-start(f32[16,16,384]{2,1,0:T(8,128)} %bitcast.55), calls=%async_computation.16 | async-start | bytes 786432 | tf_op jit(solution)/shard_map/all_to_all | solution.py:537
  1389.1 25.1 %copy-start.1 = (bf16[2048,352]{0,1:T(8,128)(2,1)S(1)}, bf16[2048,352]{0,1:T(8,128)(2,1)}, u32[]{:S(2)}) copy-start(bf16[2048,352]{0,1:T(8,128)(2,1)} %param.30) | copy-start | bytes 4325380
  (22 other events, 55.1 us)
Sparse Core Ops, SparseCore 0:
  17.8 37.1 all-gather.10
  57.6 116.8 all-gather.12
  189.5 59.4 all-gather.16
  251.9 114.9 all-gather.14
  369.3 77.1 all-gather.18
  527.7 76.0 all-gather.20
  606.9 75.2 all-gather.22
  1014.6 81.2 all-gather.24
  1098.2 77.0 all-gather.26
  1308.8 69.9 reduce-scatter.1
  1381.1 27.8 all-gather.28

commit v9 on v8

--- a/solution.py
+++ b/solution.py
@@ -217,7 +217,6 @@
     seq_rows = slot_rows // sequences
     my_expert = device_index // group_size
     groups = lax.axis_size("grp")
-    head_index = device_index % group_size
 
     def dispatch(slot_values):
         by_group = lax.all_to_all(slot_values, "grp", split_axis=0, concat_axis=0, tiled=True)
@@ -282,35 +281,38 @@
     )
     extra_cols = extras.shape[1]
     extra_pad = -(-extra_cols // 128) * 128
-    packed = jnp.concatenate(
-        [kv_weight, jnp.pad(extras, ((0, 0), (0, extra_pad - extra_cols)))], axis=1
+    pair_cols = 2 * head_cols
+    head_blocks = jnp.transpose(
+        kv_weight.reshape(kv_rows, 2, group_size, head_cols), (2, 0, 1, 3)
+    ).reshape(group_size, kv_rows, pair_cols)
+    padded_extras = jnp.pad(extras, ((0, 0), (0, extra_pad - extra_cols)))
+    dealt_rows = lax.all_to_all(
+        jnp.concatenate(
+            [
+                head_blocks,
+                jnp.broadcast_to(padded_extras[None], (group_size, kv_rows, extra_pad)),
+            ],
+            axis=2,
+        ),
+        GROUP_AXES,
+        split_axis=0,
+        concat_axis=0,
+        tiled=True,
     )
     gathered = lax.all_gather(
-        lax.all_gather(packed, "grp", axis=0, tiled=True), GROUP_AXES, axis=0, tiled=True
-    )
-    gathered = jnp.swapaxes(
-        gathered.reshape(group_size, groups, kv_rows, extra_pad + kv_width), 0, 1
-    ).reshape(devices * kv_rows, extra_pad + kv_width)
-    kv_full = gathered[:, :kv_width]
-    gain_one = gathered[:, kv_width]
-    gain_two = gathered[:, kv_width + 1]
-    router_one = gathered[:, kv_width + 2 : kv_width + 2 + EXPERTS]
-    router_two = gathered[:, kv_width + 2 + EXPERTS : kv_width + 2 + 2 * EXPERTS]
-    routes_all = gathered[:, kv_width + 2 + 2 * EXPERTS : kv_width + extra_cols].astype(jnp.int32)
+        dealt_rows.reshape(group_size * kv_rows, pair_cols + extra_pad), "grp", axis=0, tiled=True
+    )
+    head_kv = gathered[:, :pair_cols]
+    gain_one = gathered[:, pair_cols]
+    gain_two = gathered[:, pair_cols + 1]
+    router_one = gathered[:, pair_cols + 2 : pair_cols + 2 + EXPERTS]
+    router_two = gathered[:, pair_cols + 2 + EXPERTS : pair_cols + 2 + 2 * EXPERTS]
+    routes_all = gathered[:, pair_cols + 2 + 2 * EXPERTS : pair_cols + extra_cols].astype(jnp.int32)
     inverse_one = lax.rsqrt(jnp.mean(own_input * own_input, axis=-1, keepdims=True) + epsilon)
     normed_one = own_input * inverse_one
     attn_input = (normed_one * gain_one.astype(jnp.float32)).astype(jnp.bfloat16)
     attn_logits = jnp.dot(attn_input, router_one, preferred_element_type=jnp.float32)
     seq_input = lax.all_gather(attn_input, GROUP_AXES, axis=0, tiled=True)
-    own_positions = (device_index * own_rows + token_order) % seq_length
-    own_cos, own_sin = rope_tables(own_positions, HEAD)
-    head_kv = jnp.concatenate(
-        [
-            lax.dynamic_slice_in_dim(kv_full, head_index * head_cols, head_cols, axis=1),
-            lax.dynamic_slice_in_dim(kv_full, key_cols + head_index * head_cols, head_cols, axis=1),
-        ],
-        axis=1,
-    )
     seq_kv = jnp.dot(seq_input, head_kv, preferred_element_type=jnp.float32)
     seq_cos, seq_sin = rope_tables(jnp.arange(seq_length, dtype=jnp.int32), HEAD)
     seq_pair = jnp.concatenate(
@@ -471,50 +473,44 @@
             "rw,dw->rd", to_rows(query_rot_grad), query_stack, preferred_element_type=jnp.float32
         )
     )
-    key_back, value_back = (
-        lax.all_to_all(
-            seq_key_grad.reshape(devices, own_rows, 1, head_cols).astype(jnp.bfloat16),
-            ALL_AXES,
-            split_axis=0,
-            concat_axis=2,
-            tiled=True,
-        ).astype(jnp.float32),
-        lax.all_to_all(
-            seq_value_grad.reshape(devices, own_rows, 1, head_cols).astype(jnp.bfloat16),
-            ALL_AXES,
-            split_axis=0,
-            concat_axis=2,
-            tiled=True,
-        ).astype(jnp.float32),
-    )
-    own_key_grad = jnp.sum(key_back.reshape(own_rows, EXPERTS, group_size, head_cols), axis=1)
-    own_value_grad = jnp.sum(
-        value_back.reshape(own_rows, EXPERTS, group_size, head_cols), axis=1
-    ).reshape(own_rows, key_cols)
-    kv_own_grad = jnp.concatenate(
-        [rotate_back(own_key_grad, own_cos, own_sin).reshape(own_rows, key_cols), own_value_grad],
+    pair_back = lax.all_to_all(
+        jnp.concatenate([seq_key_grad, seq_value_grad], axis=2).astype(jnp.bfloat16),
+        "grp",
+        split_axis=0,
+        concat_axis=0,
+        tiled=True,
+    )
+    seq_pair_grad = jnp.sum(pair_back.astype(jnp.float32), axis=0)
+    kv_col_grad = jnp.concatenate(
+        [
+            rotate_back(
+                seq_pair_grad[:, :head_cols].reshape(seq_length, local_heads, HEAD),
+                seq_cos,
+                seq_sin,
+            ).reshape(seq_length, head_cols),
+            seq_pair_grad[:, head_cols:],
+        ],
         axis=1,
     ).astype(jnp.bfloat16)
+    kv_col_weight = jnp.einsum(
+        "rd,rc->dc", seq_input, kv_col_grad, preferred_element_type=jnp.float32
+    )
+    kv_input_parts = lax.all_to_all(
+        jnp.einsum("rc,dc->rd", kv_col_grad, head_kv, preferred_element_type=jnp.float32)
+        .astype(jnp.bfloat16)
+        .reshape(group_size, own_rows, width),
+        GROUP_AXES,
+        split_axis=0,
+        concat_axis=0,
+        tiled=True,
+    )
     attn_input_grad = jnp.sum(
         attn_row_grad.reshape(EXPERTS * slot_cap, width)[attn_index] * attn_pair_kept[:, :, None],
         axis=1,
     )
-    attn_input_grad = attn_input_grad + jnp.einsum(
-        "rc,dc->rd", kv_own_grad, kv_full, preferred_element_type=jnp.float32
-    )
+    attn_input_grad = attn_input_grad + jnp.sum(kv_input_parts.astype(jnp.float32), axis=0)
     attn_input_grad = attn_input_grad + jnp.dot(
         attn_logit_grad, router_one.astype(jnp.float32).T, precision=lax.Precision.HIGHEST
-    )
-    col_block = kv_width // group_size
-    kv_col_grad = lax.all_to_all(
-        kv_own_grad.reshape(own_rows, group_size, col_block),
-        GROUP_AXES,
-        split_axis=1,
-        concat_axis=0,
-        tiled=True,
-    ).reshape(own_rows * group_size, col_block)
-    kv_col_weight = jnp.einsum(
-        "rd,rc->dc", seq_input, kv_col_grad, preferred_element_type=jnp.float32
     )
     attn_router_own = jnp.dot(
         attn_input.astype(jnp.float32).T, attn_logit_grad, precision=lax.Precision.HIGHEST
@@ -535,14 +531,16 @@
     )
     group_sum = lax.psum_scatter(packed_grad, "grp", scatter_dimension=0, tiled=True)
     dealt = lax.all_to_all(
-        group_sum.reshape(group_size, kv_rows, col_block + extra_pad),
+        group_sum.reshape(group_size, kv_rows, pair_cols + extra_pad),
         GROUP_AXES,
         split_axis=0,
         concat_axis=0,
         tiled=True,
     )
-    kv_grad = jnp.moveaxis(dealt[:, :, :col_block], 0, 1).reshape(kv_rows, kv_width)
-    extra_grad = jnp.sum(dealt[:, :, col_block:], axis=0)
+    kv_grad = jnp.transpose(
+        dealt[:, :, :pair_cols].reshape(group_size, kv_rows, 2, head_cols), (1, 2, 0, 3)
+    ).reshape(kv_rows, kv_width)
+    extra_grad = jnp.sum(dealt[:, :, pair_cols:], axis=0)
     gain_one_grad = extra_grad[:, 0]
     gain_two_grad = extra_grad[:, 1]
     attn_router_grad = extra_grad[:, 2 : 2 + EXPERTS]

time: 1430 us -> 1330 us (0.930)
  waiting for transfers between devices: 892 us -> 833 us
  local copies, waits for them, and re-layouts: 135 us -> 111 us
    all_gather x2 -> x1, waiting for transfers between devices: 156 us -> 43.1 us  [shards(): lax.all_gather(dealt_rows.reshape(group_size * kv_rows, pair_cols + extra...]
    all_gather x1, waiting for transfers between devices: 31.3 us -> 72.3 us  [shards(): query_stack = lax.all_gather(query_weight, GROUP_AXES, axis=1, tiled=True)]
    all_to_all x4 -> x3, waiting for transfers between devices: 39.9 us -> 37.6 us  [the longest x1 37.6 us: shards(): lax.all_to_all(jnp.einsum('rc,dc->rd', kv_col_grad, head_kv, preferred_el...]
  transfers between devices with their start and end apart: 23 -> 22, of which waited for: 21 -> 20; matrix products, arithmetic and copies ran while one was open for 17% -> 17% of each run, Pallas kernels for 2% -> 2%
where the time goes in v9:
time: 1330 us; the launch traced here: 1320 us
  waiting for transfers between devices  833 us (63%)
  matrix products  136 us (10%)
  local copies, waits for them, and re-layouts  111 us (8%)
  other arithmetic  72.9 us (5%)
  blocking collectives  63.6 us (5%)
  starting transfers between devices  60.6 us (5%)
  Pallas kernels  24.6 us (2%)
  between operations  16.1 us (1%)
    all_to_all x2, waiting for transfers between devices, combine(): lax.all_to_all(partial_value.astype(jnp.bfloat16).reshape(group_size, gro...  183 us
    all_gather x2, waiting for transfers between devices, dispatch(): lax.all_gather(by_group.reshape(groups * slot_cap, width), GROUP_AXES, ax...  122 us
    all_gather x1, waiting for transfers between devices, shards(): lax.all_gather(mlp_by_group[:, :slot_cap].reshape(groups * slot_cap, widt...  73.8 us
    all_gather x1, waiting for transfers between devices, shards(): query_stack = lax.all_gather(query_weight, GROUP_AXES, axis=1, tiled=True)  72.3 us
    all_gather x1, waiting for transfers between devices, shards(): lax.all_gather(mlp_by_group[:, slot_cap:].reshape(groups * slot_cap, widt...  68.9 us
    all_gather x1, waiting for transfers between devices, shards(): seq_input = lax.all_gather(attn_input, GROUP_AXES, axis=0, tiled=True)  43.6 us
    all_gather x1, waiting for transfers between devices, shards(): lax.all_gather(dealt_rows.reshape(group_size * kv_rows, pair_cols + extra...  43.1 us
    all_to_all x1, waiting for transfers between devices, shards(): lax.all_to_all(jnp.einsum('rc,dc->rd', kv_col_grad, head_kv, preferred_el...  37.6 us
  transfers between devices with their start and end apart: 22, of which 20 were waited for; matrix products, arithmetic and copies ran while one was open for 17% of the time, Pallas kernels for 2%

profile of v9, /device:TPU:1, one launch (start us, length us, event | category | flops | bytes accessed | tf_op | source)
XLA Modules:
  0.0 1317.8 jit_solution(10336872903268347737)
XLA Ops:
  17.3 17.5 %all_to_all.80 = bf16[16,16,384]{2,1,0:T(8,128)(2,1)S(1)} all-to-all(bf16[16,16,384]{2,1,0:T(8,128)(2,1)S(1)} %pad_maximum_fusion.10), channel_id=1, replica_groups=mesh['grp'=8,'sub'=8,'expert'=2] {'sub','expert'}, dimensions={0} | all-to-all | bytes 393216 | tf_op jit(solution)/shard_map/all_to_all | solution.py:289
  35.9 43.1 %all-gather.10.cloned.1.call-done = bf16[2048,384]{0,1:T(8,128)(2,1)} async-done(((bf16[256,384]{0,1:T(8,128)(2,1)}), bf16[2048,384]{0,1:T(8,128)(2,1)}) %all-gather.10.cloned.1.call-update) | async-done | bytes 1572880 | tf_op jit(solution)/shard_map/all_gather | solution.py:302
  84.4 14.4 %all_to_all.81 = bf16[8,18,2048]{2,1,0:T(8,128)(2,1)S(1)} all-to-all(bf16[8,18,2048]{2,1,0:T(8,128)(2,1)S(1)} %broadcast_select_fusion.1), channel_id=1, replica_groups=mesh['grp'=8,'sub'=8,'expert'=2] {'grp'}, dimensions={0} | all-to-all | bytes 1179648 | tf_op jit(solution)/shard_map/all_to_all | solution.py:222
  100.4 43.6 %all-gather.14.cloned.1.call-done = bf16[1024,2048]{1,0:T(8,128)(2,1)} async-done(((bf16[64,2048]{1,0:T(8,128)(2,1)}), bf16[1024,2048]{1,0:T(8,128)(2,1)}) %all-gather.14.cloned.1.call-update) | async-done | bytes 4194320 | tf_op jit(solution)/shard_map/all_gather | solution.py:315
  166.8 5.6 multiply_reduce_fusion
  178.4 37.5 %all-to-all-done.2 = bf16[8,1024,256]{2,1,0:T(8,128)(2,1)} async-done(((bf16[8,1024,256]{2,1,0:T(8,128)(2,1)}), bf16[8,1024,256]{2,1,0:T(8,128)(2,1)}, u32[]{:S(2)}, u32[]{:S(2)}) %all-to-all-start.2) | async-done | bytes 4194336 | tf_op jit(solution)/shard_map/all_to_all | solution.py:327
  220.4 41.8 %all-gather.12.cloned.1.call-done = bf16[2304,2048]{1,0:T(8,128)(2,1)} async-done(((bf16[144,2048]{1,0:T(8,128)(2,1)}), bf16[2304,2048]{1,0:T(8,128)(2,1)}) %all-gather.12.cloned.1.call-update) | async-done | bytes 9437200 | tf_op jit(solution)/shard_map/all_gather | solution.py:223
  262.2 5.2 fusion.86
  272.9 5.4 fusion.14
  279.4 10.8 shard_map.238
  298.5 15.5 %all-to-all-done.3 = bf16[16,144,128]{2,1,0:T(8,128)(2,1)S(1)} async-done(((bf16[16,144,128]{2,1,0:T(8,128)(2,1)}), bf16[16,144,128]{2,1,0:T(8,128)(2,1)S(1)}, u32[]{:S(2)}, u32[]{:S(2)}) %all-to-all-start.3) | async-done | bytes 589856 | tf_op jit(solution)/shard_map/all_to_all | solution.py:239
  316.4 25.3 %all-gather.16.cloned.1.call-done = bf16[2048,2048]{1,0:T(8,128)(2,1)} async-done(((bf16[128,2048]{1,0:T(8,128)(2,1)}), bf16[2048,2048]{1,0:T(8,128)(2,1)}) %all-gather.16.cloned.1.call-update) | async-done | bytes 8388624 | tf_op jit(solution)/shard_map/all_gather | solution.py:363
  341.7 6.4 fusion.2
  360.2 16.2 %all-to-all-done.4 = f32[8,18,2048]{2,1,0:T(8,128)} async-done(((f32[8,18,2048]{2,1,0:T(8,128)}), f32[8,18,2048]{2,1,0:T(8,128)}, u32[]{:S(2)}, u32[]{:S(2)}) %all-to-all-start.4) | async-done | bytes 1179680 | tf_op jit(solution)/shard_map/all_to_all | solution.py:249
  395.4 19.2 %all_to_all.82 = bf16[8,36,2048]{2,1,0:T(8,128)(2,1)S(1)} all-to-all(bf16[8,36,2048]{2,1,0:T(8,128)(2,1)S(1)} %pad_maximum_fusion.2), channel_id=1, replica_groups=mesh['grp'=8,'sub'=8,'expert'=2] {'grp'}, dimensions={0} | all-to-all | bytes 2359296 | tf_op jit(solution)/shard_map/all_to_all | solution.py:383
  420.5 73.8 %all-gather.18.cloned.1.call-done = bf16[2304,2048]{1,0:T(8,128)(2,1)} async-done(((bf16[144,2048]{1,0:T(8,128)(2,1)}), bf16[2304,2048]{1,0:T(8,128)(2,1)}) %all-gather.18.cloned.1.call-update) | async-done | bytes 9437200 | tf_op jit(solution)/shard_map/all_gather | solution.py:390
  494.2 9.3 fusion.87
  503.5 68.9 %all-gather.20.cloned.1.call-done = bf16[2304,2048]{1,0:T(8,128)(2,1)} async-done(((bf16[144,2048]{1,0:T(8,128)(2,1)}), bf16[2304,2048]{1,0:T(8,128)(2,1)}) %all-gather.20.cloned.1.call-update) | async-done | bytes 9437200 | tf_op jit(solution)/shard_map/all_gather | solution.py:396
  572.4 7.1 fusion.88
  580.2 8.6 multiply_convert_fusion.2
  588.8 7.5 convolution_convert_fusion
  601.5 10.7 fusion.89
  612.2 11.2 add_convert_fusion
  623.4 84.0 %all-to-all-done.6 = bf16[16,144,2048]{2,1,0:T(8,128)(2,1)} async-done(((bf16[16,144,2048]{2,1,0:T(8,128)(2,1)}), bf16[16,144,2048]{2,1,0:T(8,128)(2,1)}, u32[]{:S(2)}, u32[]{:S(2)}) %all-to-all-start.6) | async-done | bytes 9437216 | tf_op jit(solution)/shard_map/all_to_all | solution.py:228
  707.4 5.5 all-to-all-start.8
  712.9 5.9 convert_reduce_fusion.1
  720.1 98.8 %all-to-all-done.8 = bf16[16,144,2048]{2,1,0:T(8,128)(2,1)} async-done(((bf16[16,144,2048]{2,1,0:T(8,128)(2,1)}), bf16[16,144,2048]{2,1,0:T(8,128)(2,1)}, u32[]{:S(2)}, u32[]{:S(2)}) %all-to-all-start.8) | async-done | bytes 9437216 | tf_op jit(solution)/shard_map/all_to_all | solution.py:228
  823.2 5.9 convert_reduce_fusion
  830.4 15.8 %all-to-all-done.7 = f32[8,18,2048]{2,1,0:T(8,128)} async-done(((f32[8,18,2048]{2,1,0:T(8,128)}), f32[8,18,2048]{2,1,0:T(8,128)}, u32[]{:S(2)}, u32[]{:S(2)}) %all-to-all-start.7) | async-done | bytes 1179680 | tf_op jit(solution)/shard_map/all_to_all | solution.py:236
  859.9 12.7 all-to-all-done.9
  889.2 12.5 all_to_all.83
  903.5 80.6 %all-gather.22.cloned.1.call-done = bf16[2304,2048]{1,0:T(8,128)(2,1)} async-done(((bf16[144,2048]{1,0:T(8,128)(2,1)}), bf16[2304,2048]{1,0:T(8,128)(2,1)}) %all-gather.22.cloned.1.call-update) | async-done | bytes 9437200 | tf_op jit(solution)/shard_map/all_gather | solution.py:223
  984.1 6.3 convolution_convert_fusion.2
  991.6 13.8 %shard_map.239 = (f32[8,288,128]{2,1,0:T(8,128)}, f32[8,1024,128]{2,1,0:T(8,128)}, f32[8,1024,128]{2,1,0:T(8,128)}) custom-call(bf16[8,288,128]{2,1,0:T(8,128)(2,1)} %pad_maximum_fusion.3.q_ref, bf16[8,1024,128]{2,1,0:T(8,128)(2,1)} %bitcast.137, bf16[8,1024,128]{2,1,0:T(8,128)(2,1)} %bitcast.135, s32[8,288,1]{2,1,0:T(8,128)} %add_select_fusion.qb_ref, ...), custom_call_target="tpu_custom_call" | custom-call | flops 3019898880 | bytes 25100288 | tf_op jit(solution)/shard_map/pallas_call | solution.py:76
  1005.4 7.9 fusion.18
  1024.8 8.0 all-to-all-done.11
  1037.9 72.3 %all-gather.24.cloned.1.call-done = bf16[2048,2048]{1,0:T(8,128)(2,1)} async-done(((bf16[2048,128]{1,0:T(8,128)(2,1)}), bf16[2048,2048]{1,0:T(8,128)(2,1)}) %all-gather.24.cloned.1.call-update) | async-done | bytes 8388624 | tf_op jit(solution)/shard_map/all_gather | solution.py:470
  1110.2 7.4 fusion
  1131.4 14.4 %all-to-all-done.12 = f32[8,18,2048]{2,1,0:T(8,128)} async-done(((f32[8,18,2048]{2,1,0:T(8,128)}), f32[8,18,2048]{2,1,0:T(8,128)}, u32[]{:S(2)}, u32[]{:S(2)}) %all-to-all-start.12) | async-done | bytes 1179680 | tf_op jit(solution)/shard_map/all_to_all | solution.py:249
  1145.8 5.7 all-to-all-start.14
  1163.8 37.6 %all-to-all-done.14 = bf16[16,64,2048]{2,1,0:T(8,128)(2,1)} async-done(((bf16[16,64,2048]{2,1,0:T(8,128)(2,1)}), bf16[16,64,2048]{2,1,0:T(8,128)(2,1)}, u32[]{:S(2)}, u32[]{:S(2)}) %all-to-all-start.14) | async-done | bytes 4194336 | tf_op jit(solution)/shard_map/all_to_all | solution.py:498
  1211.5 9.7 fusion.94
  1221.3 9.0 fusion.95
  1239.1 6.1 fusion.93
  1245.2 7.4 fusion.92
  1252.6 22.0 %reduce-scatter.2.cloned.1.call-done = f32[256,384]{0,1:T(8,128)} async-done(((f32[2048,384]{0,1:T(8,128)}), f32[256,384]{0,1:T(8,128)}) %reduce-scatter.2.cloned.1.call-update) | async-done | bytes 393232 | tf_op jit(solution)/shard_map/reduce_scatter | solution.py:532
  1276.5 8.3 all-to-all-start.15
  1284.8 20.0 %all-gather.26.cloned.1.call-done = bf16[128,4096]{1,0:T(8,128)(2,1)} async-done(((bf16[64,4096]{1,0:T(8,128)(2,1)}), bf16[128,4096]{1,0:T(8,128)(2,1)}) %all-gather.26.cloned.1.call-update) | async-done | bytes 1048592 | tf_op jit(solution)/shard_map/all_gather | solution.py:548
  (372 shorter events, 219.6 us)
Async XLA Ops:
  7.2 572.3 %copy-start = (bf16[2048,352]{0,1:T(8,128)(2,1)S(1)}, bf16[2048,352]{0,1:T(8,128)(2,1)}, u32[]{:S(2)}) copy-start(bf16[2048,352]{0,1:T(8,128)(2,1)} %param.30) | copy-start | bytes 4325380
  7.2 71.9 %all-gather.10.cloned.1.call-start = ((), (), s32[]{:S(2)}) async-start(), calls=%async_computation.17 | async-start | bytes 1769472 | tf_op jit(solution)/shard_map/all_gather | solution.py:302
  15.9 19.8 %copy-start.11 = (bf16[128,2048]{1,0:T(8,128)(2,1)S(1)}, bf16[128,2048]{1,0:T(8,128)(2,1)}, u32[]{:S(2)}) copy-start(bf16[128,2048]{1,0:T(8,128)(2,1)} %param.21) | copy-start | bytes 1572868
  35.7 108.4 %all-gather.14.cloned.1.call-start = ((), (), s32[]{:S(2)}) async-start(), calls=%async_computation.19 | async-start | bytes 4456448 | tf_op jit(solution)/shard_map/all_gather | solution.py:315
  35.9 48.1 %copy-start.40 = (f32[64]{0:T(128)}, f32[64]{0:T(128)S(1)}, u32[]{:S(2)}) copy-start(f32[64]{0:T(128)S(1)} %add_rsqrt_fusion.1) | copy-start | bytes 772
  81.4 180.8 %all-gather.12.cloned.1.call-start = ((), (), s32[]{:S(2)}) async-start(), calls=%async_computation.18 | async-start | bytes 10027008 | tf_op jit(solution)/shard_map/all_gather | solution.py:223
  99.8 241.9 %all-gather.16.cloned.1.call-start = ((), (), s32[]{:S(2)}) async-start(), calls=%async_computation.20 | async-start | bytes 8912896 | tf_op jit(solution)/shard_map/all_gather | solution.py:363
  100.4 172.5 %copy-start.38 = (f32[64]{0:T(128)}, f32[64]{0:T(128)S(1)}, u32[]{:S(2)}) copy-start(f32[64]{0:T(128)S(1)} %multiply_exponential_fusion) | copy-start | bytes 772
  100.4 47.5 %copy-start.34 = (f32[1024]{0:T(1024)}, f32[1024]{0:T(1024)S(1)}, u32[]{:S(2)}) copy-start(f32[1024]{0:T(1024)S(1)} %iota_convert_fusion) | copy-start | bytes 12292
  151.6 64.3 %all-to-all-start.2 = ((bf16[8,1024,256]{2,1,0:T(8,128)(2,1)}), bf16[8,1024,256]{2,1,0:T(8,128)(2,1)}, u32[]{:S(2)}, u32[]{:S(2)}) async-start(bf16[8,1024,256]{2,1,0:T(8,128)(2,1)} %broadcast_in_dim.56), calls=%async_computation.2 | async-start | bytes 8388608 | tf_op jit(solution)/shard_map/all_to_all | solution.py:327
  175.0 97.9 %copy-start.27 = (f32[2304]{0:T(1024)}, f32[2304]{0:T(1024)S(1)}, u32[]{:S(2)}) copy-start(f32[2304]{0:T(1024)S(1)} %fusion.66) | copy-start | bytes 27652
  215.9 46.3 %copy-start.21 = (bf16[2048,128]{1,0:T(8,128)(2,1)S(1)}, bf16[2048,128]{1,0:T(8,128)(2,1)}, u32[]{:S(2)}) copy-start(bf16[2048,128]{1,0:T(8,128)(2,1)} %param.25) | copy-start | bytes 1572868
  292.4 6.1 copy-start.22
  293.5 20.6 %all-to-all-start.3 = ((bf16[16,144,128]{2,1,0:T(8,128)(2,1)}), bf16[16,144,128]{2,1,0:T(8,128)(2,1)S(1)}, u32[]{:S(2)}, u32[]{:S(2)}) async-start(bf16[16,144,128]{2,1,0:T(8,128)(2,1)} %copy.493), calls=%async_computation.3 | async-start | bytes 1179648 | tf_op jit(solution)/shard_map/all_to_all | solution.py:239
  348.0 28.4 %all-to-all-start.4 = ((f32[8,18,2048]{2,1,0:T(8,128)}), f32[8,18,2048]{2,1,0:T(8,128)}, u32[]{:S(2)}, u32[]{:S(2)}) async-start(f32[8,18,2048]{2,1,0:T(8,128)} %fusion.2), calls=%async_computation.4 | async-start | bytes 3145728 | tf_op jit(solution)/shard_map/all_to_all | solution.py:249
  352.4 141.9 %all-gather.18.cloned.1.call-start = ((), (), s32[]{:S(2)}) async-start(), calls=%async_computation.21 | async-start | bytes 10027008 | tf_op jit(solution)/shard_map/all_gather | solution.py:390
  418.1 154.3 %all-gather.20.cloned.1.call-start = ((), (), s32[]{:S(2)}) async-start(), calls=%async_computation.22 | async-start | bytes 10027008 | tf_op jit(solution)/shard_map/all_gather | solution.py:396
  572.4 7.1 copy-start.43
  572.4 7.8 copy-start.45
  580.2 8.6 copy-start.44
  588.8 7.5 copy-start.46
  596.3 111.1 %all-to-all-start.6 = ((bf16[16,144,2048]{2,1,0:T(8,128)(2,1)}), bf16[16,144,2048]{2,1,0:T(8,128)(2,1)}, u32[]{:S(2)}, u32[]{:S(2)}) async-start(bf16[16,144,2048]{2,1,0:T(8,128)(2,1)} %bitcast.133), calls=%async_computation.6 | async-start | bytes 18874368 | tf_op jit(solution)/shard_map/all_to_all | solution.py:228
  601.5 10.7 copy-start.9
  707.4 111.5 %all-to-all-start.8 = ((bf16[16,144,2048]{2,1,0:T(8,128)(2,1)}), bf16[16,144,2048]{2,1,0:T(8,128)(2,1)}, u32[]{:S(2)}, u32[]{:S(2)}) async-start(bf16[16,144,2048]{2,1,0:T(8,128)(2,1)} %bitcast.131), calls=%async_computation.8 | async-start | bytes 18874368 | tf_op jit(solution)/shard_map/all_to_all | solution.py:228
  818.9 27.3 %all-to-all-start.7 = ((f32[8,18,2048]{2,1,0:T(8,128)}), f32[8,18,2048]{2,1,0:T(8,128)}, u32[]{:S(2)}, u32[]{:S(2)}) async-start(f32[8,18,2048]{2,1,0:T(8,128)} %reshape.665), calls=%async_computation.7 | async-start | bytes 3145728 | tf_op jit(solution)/shard_map/all_to_all | solution.py:236
  830.4 20.5 %copy-start.33 = (s32[8,18,1]{0,1,2:T(8,128)S(1)}, s32[8,18,1]{0,1,2:T(8,128)}, u32[]{:S(2)}) copy-start(s32[8,18,1]{0,1,2:T(8,128)} %get-tuple-element.170) | copy-start | bytes 1732
  830.4 20.7 %copy-start.42 = (s32[64,2]{0,1:T(2,128)S(1)}, s32[64,2]{0,1:T(2,128)}, u32[]{:S(2)}) copy-start(s32[64,2]{0,1:T(2,128)} %get-tuple-element.180) | copy-start | bytes 1540
  846.2 26.4 %all-to-all-start.9 = ((f32[8,18,2048]{2,1,0:T(8,128)}), f32[8,18,2048]{2,1,0:T(8,128)}, u32[]{:S(2)}, u32[]{:S(2)}) async-start(f32[8,18,2048]{2,1,0:T(8,128)} %reshape.669), calls=%async_computation.9 | async-start | bytes 3145728 | tf_op jit(solution)/shard_map/all_to_all | solution.py:236
  850.5 133.7 %all-gather.22.cloned.1.call-start = ((), (), s32[]{:S(2)}) async-start(), calls=%async_computation.23 | async-start | bytes 10027008 | tf_op jit(solution)/shard_map/all_gather | solution.py:223
  901.7 82.4 %copy-start.20 = (bf16[128,2048]{1,0:T(8,128)(2,1)S(1)}, bf16[128,2048]{1,0:T(8,128)(2,1)}, u32[]{:S(2)}) copy-start(bf16[128,2048]{1,0:T(8,128)(2,1)} %param.26) | copy-start | bytes 1572868
  902.7 207.4 %all-gather.24.cloned.1.call-start = ((), (), s32[]{:S(2)}) async-start(), calls=%async_computation.24 | async-start | bytes 8912896 | tf_op jit(solution)/shard_map/all_gather | solution.py:470
  991.6 13.8 %copy-start.28 = (f32[2304]{0:T(1024)S(1)}, f32[2304]{0:T(1024)}, u32[]{:S(2)}) copy-start(f32[2304]{0:T(1024)} %copy-done.27) | copy-start | bytes 27652
  991.6 13.8 %copy-start.39 = (f32[64]{0:T(128)S(1)}, f32[64]{0:T(128)}, u32[]{:S(2)}) copy-start(f32[64]{0:T(128)} %copy-done.38) | copy-start | bytes 772
  1014.9 17.9 %all-to-all-start.11 = ((bf16[16,144,128]{2,1,0:T(8,128)(2,1)}), bf16[16,144,128]{2,1,0:T(8,128)(2,1)S(1)}, u32[]{:S(2)}, u32[]{:S(2)}) async-start(bf16[16,144,128]{2,1,0:T(8,128)(2,1)} %copy.527), calls=%async_computation.11 | async-start | bytes 1179648 | tf_op jit(solution)/shard_map/all_to_all | solution.py:239
  1032.8 84.8 %all-to-all-start.13 = ((bf16[8,1024,256]{2,1,0:T(8,128)(2,1)}), bf16[8,1024,256]{2,1,0:T(8,128)(2,1)}, u32[]{:S(2)}, u32[]{:S(2)}) async-start(bf16[8,1024,256]{2,1,0:T(8,128)(2,1)} %pad_maximum_fusion), calls=%async_computation.13 | async-start | bytes 8388608 | tf_op jit(solution)/shard_map/all_to_all | solution.py:476
  1117.6 28.3 %all-to-all-start.12 = ((f32[8,18,2048]{2,1,0:T(8,128)}), f32[8,18,2048]{2,1,0:T(8,128)}, u32[]{:S(2)}, u32[]{:S(2)}) async-start(f32[8,18,2048]{2,1,0:T(8,128)} %fusion), calls=%async_computation.12 | async-start | bytes 3145728 | tf_op jit(solution)/shard_map/all_to_all | solution.py:249
  1145.8 55.6 %all-to-all-start.14 = ((bf16[16,64,2048]{2,1,0:T(8,128)(2,1)}), bf16[16,64,2048]{2,1,0:T(8,128)(2,1)}, u32[]{:S(2)}, u32[]{:S(2)}) async-start(bf16[16,64,2048]{2,1,0:T(8,128)(2,1)} %bitcast.132), calls=%async_computation.14 | async-start | bytes 8388608 | tf_op jit(solution)/shard_map/all_to_all | solution.py:498
  1151.5 123.1 %reduce-scatter.2.cloned.1.call-start = ((), (), s32[]{:S(2)}) async-start(), calls=%async_computation.26 | async-start | bytes 3538944 | tf_op jit(solution)/shard_map/reduce_scatter | solution.py:532
  1163.8 40.6 %copy-start.13 = (bf16[128,2048]{1,0:T(8,128)(2,1)S(1)}, bf16[128,2048]{1,0:T(8,128)(2,1)}, u32[]{:S(2)}) copy-start(bf16[128,2048]{1,0:T(8,128)(2,1)} %param.21) | copy-start | bytes 1572868
  1163.8 40.6 %copy-start.25 = (f32[2048,1]{0,1:T(1,128)S(1)}, f32[2048,1]{0,1:T(1,128)}, u32[]{:S(2)}) copy-start(f32[2048,1]{0,1:T(1,128)} %copy-done.24) | copy-start | bytes 24580
  1163.8 40.6 %copy-start.41 = (f32[64]{0:T(128)S(1)}, f32[64]{0:T(128)}, u32[]{:S(2)}) copy-start(f32[64]{0:T(128)} %copy-done.40) | copy-start | bytes 772
  1208.1 96.7 %all-gather.26.cloned.1.call-start = ((), (), s32[]{:S(2)}) async-start(), calls=%async_computation.25 | async-start | bytes 1572864 | tf_op jit(solution)/shard_map/all_gather | solution.py:548
  1211.5 9.8 copy-start.15
  1211.5 18.7 %slice-start = ((s8[9437184]{0:T(1024)(128)(4,1)}), s8[4194304]{0:T(1024)(128)(4,1)S(1)}, s32[]{:S(2)}) async-start(s8[9437184]{0:T(1024)(128)(4,1)} %bitcast.170), calls=%async_computation.27 | async-start | bytes 8388608
  1211.5 18.7 %slice-start.1 = ((s8[9437184]{0:T(1024)(128)(4,1)}), s8[4194304]{0:T(1024)(128)(4,1)S(1)}, s32[]{:S(2)}) async-start(s8[9437184]{0:T(1024)(128)(4,1)} %bitcast.170), calls=%async_computation.28 | async-start | bytes 8388608
  1221.3 9.0 copy-start.10
  1221.3 9.0 slice-start.2
  1276.5 30.7 %all-to-all-start.15 = ((f32[16,16,384]{2,1,0:T(8,128)}), f32[16,16,384]{2,1,0:T(8,128)S(1)}, u32[]{:S(2)}, u32[]{:S(2)}) async-start(f32[16,16,384]{2,1,0:T(8,128)} %bitcast.46), calls=%async_computation.16 | async-start | bytes 786432 | tf_op jit(solution)/shard_map/all_to_all | solution.py:533
  (24 other events, 51.7 us)
Sparse Core Ops, SparseCore 0:
  35.8 43.1 all-gather.9
  82.1 61.9 all-gather.13
  147.1 115.0 all-gather.11
  264.5 77.1 all-gather.15
  418.2 75.9 all-gather.17
  497.2 75.2 all-gather.19
  902.8 81.2 all-gather.21
  986.4 123.7 all-gather.23
  1208.2 66.3 reduce-scatter.1
  1276.7 28.0 all-gather.25

commit v10 on v9

--- a/solution.py
+++ b/solution.py
@@ -299,9 +299,16 @@
         concat_axis=0,
         tiled=True,
     )
-    gathered = lax.all_gather(
-        dealt_rows.reshape(group_size * kv_rows, pair_cols + extra_pad), "grp", axis=0, tiled=True
-    )
+    gathered = lax.all_to_all(
+        jnp.broadcast_to(
+            dealt_rows.reshape(1, group_size * kv_rows, pair_cols + extra_pad),
+            (groups, group_size * kv_rows, pair_cols + extra_pad),
+        ),
+        "grp",
+        split_axis=0,
+        concat_axis=0,
+        tiled=True,
+    ).reshape(devices * kv_rows, pair_cols + extra_pad)
     head_kv = gathered[:, :pair_cols]
     gain_one = gathered[:, pair_cols]
     gain_two = gathered[:, pair_cols + 1]
@@ -405,6 +412,8 @@
     inner_rows = (activated * up_pre).astype(jnp.bfloat16)
     mlp_partial = jnp.dot(inner_rows, down_weight, preferred_element_type=jnp.float32)
     mlp_slots = combine(mlp_partial)
+    query_stack = lax.all_gather(query_weight, GROUP_AXES, axis=1, tiled=True)
+    mlp_slots, query_stack = lax.optimization_barrier((mlp_slots, query_stack))
     mlp_picked = mlp_slots.reshape(EXPERTS * slot_cap, width)[mlp_index]
     own_output = hidden_state + jnp.sum(
         mlp_picked * (mlp_gates * mlp_pair_kept)[:, :, None], axis=1
@@ -467,7 +476,6 @@
     query_grad = jnp.einsum(
         "rd,rw->dw", attn_rows, query_rot_grad, preferred_element_type=jnp.float32
     )
-    query_stack = lax.all_gather(query_weight, GROUP_AXES, axis=1, tiled=True)
     attn_row_grad = to_owners(
         jnp.einsum(
             "rw,dw->rd", to_rows(query_rot_grad), query_stack, preferred_element_type=jnp.float32

time: 1330 us -> 1330 us (level)
  waiting for transfers between devices: 833 us -> 815 us
    all_gather x1, waiting for transfers between devices: 72.3 us -> 0.01 us  [shards(): query_stack = lax.all_gather(query_weight, GROUP_AXES, axis=1, tiled=True)]
    all_to_all x1, waiting for transfers between devices: 0.01 us -> 49.5 us  [shards(): lax.all_to_all(jnp.concatenate([seq_key_grad, seq_value_grad], axis=2).as...]
    all_gather x1 -> x0, waiting for transfers between devices: 43.1 us -> none  [shards(): lax.all_gather(dealt_rows.reshape(group_size * kv_rows, pair_cols + extra...]
    all_to_all x2, waiting for transfers between devices: 183 us -> 210 us  [combine(): lax.all_to_all(partial_value.astype(jnp.bfloat16).reshape(group_size, gro...]
    all_to_all x0 -> x1, waiting for transfers between devices: none -> 23.2 us  [shards(): lax.all_to_all(jnp.broadcast_to(dealt_rows.reshape(1, group_size * kv_row...]
  transfers between devices with their start and end apart: 22 -> 22, of which waited for: 20 -> 20; matrix products, arithmetic and copies ran while one was open for 17% -> 16% of each run, Pallas kernels for 2% -> 1%
where the time goes in v10:
time: 1330 us; the launch traced here: 1320 us
  waiting for transfers between devices  815 us (61%)
  matrix products  139 us (10%)
  local copies, waits for them, and re-layouts  115 us (9%)
  other arithmetic  78.5 us (6%)
  starting transfers between devices  65 us (5%)
  blocking collectives  63.5 us (5%)
  Pallas kernels  24.6 us (2%)
  between operations  15.8 us (1%)
    all_to_all x2, waiting for transfers between devices, combine(): lax.all_to_all(partial_value.astype(jnp.bfloat16).reshape(group_size, gro...  210 us
    all_gather x2, waiting for transfers between devices, dispatch(): lax.all_gather(by_group.reshape(groups * slot_cap, width), GROUP_AXES, ax...  123 us
    all_gather x1, waiting for transfers between devices, shards(): lax.all_gather(mlp_by_group[:, :slot_cap].reshape(groups * slot_cap, widt...  75.4 us
    all_gather x1, waiting for transfers between devices, shards(): lax.all_gather(mlp_by_group[:, slot_cap:].reshape(groups * slot_cap, widt...  68.8 us
    all_to_all x1, waiting for transfers between devices, shards(): lax.all_to_all(jnp.concatenate([seq_key_grad, seq_value_grad], axis=2).as...  49.5 us
    all_gather x1, waiting for transfers between devices, shards(): seq_input = lax.all_gather(attn_input, GROUP_AXES, axis=0, tiled=True)  39.5 us
    all_to_all x1, waiting for transfers between devices, shards(): lax.all_to_all(jnp.einsum('rc,dc->rd', kv_col_grad, head_kv, preferred_el...  37.6 us
    all_to_all x1, waiting for transfers between devices, shards(): lax.all_to_all(jnp.broadcast_to(seq_pair[None], (groups,) + seq_pair.shap...  37.4 us
  transfers between devices with their start and end apart: 22, of which 20 were waited for; matrix products, arithmetic and copies ran while one was open for 16% of the time, Pallas kernels for 1%

profile of v10, /device:TPU:1, one launch (start us, length us, event | category | flops | bytes accessed | tf_op | source)
XLA Modules:
  0.0 1316.2 jit_solution(5408936357408325766)
XLA Ops:
  17.3 17.5 %all_to_all.85 = bf16[16,16,384]{2,1,0:T(8,128)(2,1)S(1)} all-to-all(bf16[16,16,384]{2,1,0:T(8,128)(2,1)S(1)} %pad_maximum_fusion.10), channel_id=1, replica_groups=mesh['grp'=8,'sub'=8,'expert'=2] {'sub','expert'}, dimensions={0} | all-to-all | bytes 393216 | tf_op jit(solution)/shard_map/all_to_all | solution.py:289
  40.9 23.2 %all-to-all-done.1 = bf16[8,256,384]{1,2,0:T(8,128)(2,1)} async-done(((bf16[8,256,384]{1,2,0:T(8,128)(2,1)}), bf16[8,256,384]{1,2,0:T(8,128)(2,1)}, u32[]{:S(2)}, u32[]{:S(2)}) %all-to-all-start.1) | async-done | bytes 1572896 | tf_op jit(solution)/shard_map/all_to_all | solution.py:302
  73.4 13.5 %all_to_all.86 = bf16[8,18,2048]{2,1,0:T(8,128)(2,1)S(1)} all-to-all(bf16[8,18,2048]{2,1,0:T(8,128)(2,1)S(1)} %broadcast_select_fusion.1), channel_id=1, replica_groups=mesh['grp'=8,'sub'=8,'expert'=2] {'grp'}, dimensions={0} | all-to-all | bytes 1179648 | tf_op jit(solution)/shard_map/all_to_all | solution.py:222
  88.6 39.5 %all-gather.11.cloned.1.call-done = bf16[1024,2048]{1,0:T(8,128)(2,1)} async-done(((bf16[64,2048]{1,0:T(8,128)(2,1)}), bf16[1024,2048]{1,0:T(8,128)(2,1)}) %all-gather.11.cloned.1.call-update) | async-done | bytes 4194320 | tf_op jit(solution)/shard_map/all_gather | solution.py:322
  151.0 5.6 multiply_reduce_fusion
  162.6 37.4 %all-to-all-done.3 = bf16[8,1024,256]{2,1,0:T(8,128)(2,1)} async-done(((bf16[8,1024,256]{2,1,0:T(8,128)(2,1)}), bf16[8,1024,256]{2,1,0:T(8,128)(2,1)}, u32[]{:S(2)}, u32[]{:S(2)}) %all-to-all-start.3) | async-done | bytes 4194336 | tf_op jit(solution)/shard_map/all_to_all | solution.py:334
  204.4 41.8 %all-gather.9.cloned.1.call-done = bf16[2304,2048]{1,0:T(8,128)(2,1)} async-done(((bf16[144,2048]{1,0:T(8,128)(2,1)}), bf16[2304,2048]{1,0:T(8,128)(2,1)}) %all-gather.9.cloned.1.call-update) | async-done | bytes 9437200 | tf_op jit(solution)/shard_map/all_gather | solution.py:223
  246.2 5.4 fusion.86
  257.1 5.4 fusion.14
  263.7 10.8 shard_map.238
  282.8 15.6 %all-to-all-done.4 = bf16[16,144,128]{2,1,0:T(8,128)(2,1)S(1)} async-done(((bf16[16,144,128]{2,1,0:T(8,128)(2,1)}), bf16[16,144,128]{2,1,0:T(8,128)(2,1)S(1)}, u32[]{:S(2)}, u32[]{:S(2)}) %all-to-all-start.4) | async-done | bytes 589856 | tf_op jit(solution)/shard_map/all_to_all | solution.py:239
  300.8 25.1 %all-gather.13.cloned.1.call-done = bf16[2048,2048]{1,0:T(8,128)(2,1)} async-done(((bf16[128,2048]{1,0:T(8,128)(2,1)}), bf16[2048,2048]{1,0:T(8,128)(2,1)}) %all-gather.13.cloned.1.call-update) | async-done | bytes 8388624 | tf_op jit(solution)/shard_map/all_gather | solution.py:370
  325.9 6.3 fusion.2
  344.9 15.4 %all-to-all-done.5 = f32[8,18,2048]{2,1,0:T(8,128)} async-done(((f32[8,18,2048]{2,1,0:T(8,128)}), f32[8,18,2048]{2,1,0:T(8,128)}, u32[]{:S(2)}, u32[]{:S(2)}) %all-to-all-start.5) | async-done | bytes 1179680 | tf_op jit(solution)/shard_map/all_to_all | solution.py:249
  378.0 19.1 %all_to_all.87 = bf16[8,36,2048]{2,1,0:T(8,128)(2,1)S(1)} all-to-all(bf16[8,36,2048]{2,1,0:T(8,128)(2,1)S(1)} %pad_maximum_fusion.2), channel_id=1, replica_groups=mesh['grp'=8,'sub'=8,'expert'=2] {'grp'}, dimensions={0} | all-to-all | bytes 2359296 | tf_op jit(solution)/shard_map/all_to_all | solution.py:390
  401.6 75.4 %all-gather.15.cloned.1.call-done = bf16[2304,2048]{1,0:T(8,128)(2,1)} async-done(((bf16[144,2048]{1,0:T(8,128)(2,1)}), bf16[2304,2048]{1,0:T(8,128)(2,1)}) %all-gather.15.cloned.1.call-update) | async-done | bytes 9437200 | tf_op jit(solution)/shard_map/all_gather | solution.py:397
  477.0 9.4 fusion.87
  486.4 68.8 %all-gather.19.cloned.1.call-done = bf16[2304,2048]{1,0:T(8,128)(2,1)} async-done(((bf16[144,2048]{1,0:T(8,128)(2,1)}), bf16[2304,2048]{1,0:T(8,128)(2,1)}) %all-gather.19.cloned.1.call-update) | async-done | bytes 9437200 | tf_op jit(solution)/shard_map/all_gather | solution.py:403
  555.2 7.1 fusion.88
  563.0 8.6 multiply_convert_fusion.2
  571.6 7.5 convolution_convert_fusion
  584.5 10.9 fusion.89
  595.4 11.7 add_convert_fusion
  607.1 90.5 %all-to-all-done.7 = bf16[16,144,2048]{2,1,0:T(8,128)(2,1)} async-done(((bf16[16,144,2048]{2,1,0:T(8,128)(2,1)}), bf16[16,144,2048]{2,1,0:T(8,128)(2,1)}, u32[]{:S(2)}, u32[]{:S(2)}) %all-to-all-start.7) | async-done | bytes 9437216 | tf_op jit(solution)/shard_map/all_to_all | solution.py:228
  697.6 5.1 all-to-all-start.9
  702.7 6.1 convert_reduce_fusion.1
  710.1 119.2 %all-to-all-done.9 = bf16[16,144,2048]{2,1,0:T(8,128)(2,1)} async-done(((bf16[16,144,2048]{2,1,0:T(8,128)(2,1)}), bf16[16,144,2048]{2,1,0:T(8,128)(2,1)}, u32[]{:S(2)}, u32[]{:S(2)}) %all-to-all-start.9) | async-done | bytes 9437216 | tf_op jit(solution)/shard_map/all_to_all | solution.py:228
  833.6 5.9 convert_reduce_fusion
  840.8 16.1 %all-to-all-done.8 = f32[8,18,2048]{2,1,0:T(8,128)} async-done(((f32[8,18,2048]{2,1,0:T(8,128)}), f32[8,18,2048]{2,1,0:T(8,128)}, u32[]{:S(2)}, u32[]{:S(2)}) %all-to-all-start.8) | async-done | bytes 1179680 | tf_op jit(solution)/shard_map/all_to_all | solution.py:236
  868.5 15.1 %all-to-all-done.10 = f32[8,18,2048]{2,1,0:T(8,128)} async-done(((f32[8,18,2048]{2,1,0:T(8,128)}), f32[8,18,2048]{2,1,0:T(8,128)}, u32[]{:S(2)}, u32[]{:S(2)}) %all-to-all-start.10) | async-done | bytes 1179680 | tf_op jit(solution)/shard_map/all_to_all | solution.py:236
  905.4 13.4 %all_to_all.88 = bf16[8,18,2048]{2,1,0:T(8,128)(2,1)} all-to-all(bf16[8,18,2048]{2,1,0:T(8,128)(2,1)S(1)} %multiply_convert_fusion.3), channel_id=1, replica_groups=mesh['grp'=8,'sub'=8,'expert'=2] {'grp'}, dimensions={0} | all-to-all | bytes 1179648 | tf_op jit(solution)/shard_map/all_to_all | solution.py:222
  921.0 80.7 %all-gather.21.cloned.1.call-done = bf16[2304,2048]{1,0:T(8,128)(2,1)} async-done(((bf16[144,2048]{1,0:T(8,128)(2,1)}), bf16[2304,2048]{1,0:T(8,128)(2,1)}) %all-gather.21.cloned.1.call-update) | async-done | bytes 9437200 | tf_op jit(solution)/shard_map/all_gather | solution.py:223
  1001.8 7.1 convolution_convert_fusion.2
  1011.1 13.8 %shard_map.239 = (f32[8,288,128]{2,1,0:T(8,128)}, f32[8,1024,128]{2,1,0:T(8,128)}, f32[8,1024,128]{2,1,0:T(8,128)}) custom-call(bf16[8,288,128]{2,1,0:T(8,128)(2,1)} %pad_maximum_fusion.3.q_ref, bf16[8,1024,128]{2,1,0:T(8,128)(2,1)} %bitcast.144, bf16[8,1024,128]{2,1,0:T(8,128)(2,1)} %bitcast.142, s32[8,288,1]{2,1,0:T(8,128)} %add_select_fusion.qb_ref, ...), custom_call_target="tpu_custom_call" | custom-call | flops 3019898880 | bytes 25100288 | tf_op jit(solution)/shard_map/pallas_call | solution.py:76
  1024.9 7.9 fusion.18
  1058.5 7.6 fusion
  1066.2 49.5 %all-to-all-done.14 = bf16[8,1024,256]{2,1,0:T(8,128)(2,1)} async-done(((bf16[8,1024,256]{2,1,0:T(8,128)(2,1)}), bf16[8,1024,256]{2,1,0:T(8,128)(2,1)}, u32[]{:S(2)}, u32[]{:S(2)}) %all-to-all-start.14) | async-done | bytes 4194336 | tf_op jit(solution)/shard_map/all_to_all | solution.py:484
  1129.9 13.4 %all-to-all-done.13 = f32[8,18,2048]{2,1,0:T(8,128)} async-done(((f32[8,18,2048]{2,1,0:T(8,128)}), f32[8,18,2048]{2,1,0:T(8,128)}, u32[]{:S(2)}, u32[]{:S(2)}) %all-to-all-start.13) | async-done | bytes 1179680 | tf_op jit(solution)/shard_map/all_to_all | solution.py:249
  1143.3 6.0 all-to-all-start.15
  1161.5 37.6 %all-to-all-done.15 = bf16[16,64,2048]{2,1,0:T(8,128)(2,1)} async-done(((bf16[16,64,2048]{2,1,0:T(8,128)(2,1)}), bf16[16,64,2048]{2,1,0:T(8,128)(2,1)}, u32[]{:S(2)}, u32[]{:S(2)}) %all-to-all-start.15) | async-done | bytes 4194336 | tf_op jit(solution)/shard_map/all_to_all | solution.py:506
  1208.7 9.6 fusion.94
  1218.3 9.0 fusion.95
  1227.3 5.1 fusion.96
  1235.4 6.2 fusion.93
  1241.6 7.4 fusion.92
  1249.0 24.6 %reduce-scatter.2.cloned.1.call-done = f32[256,384]{0,1:T(8,128)} async-done(((f32[2048,384]{0,1:T(8,128)}), f32[256,384]{0,1:T(8,128)}) %reduce-scatter.2.cloned.1.call-update) | async-done | bytes 393232 | tf_op jit(solution)/shard_map/reduce_scatter | solution.py:540
  1275.5 8.1 all-to-all-start.16
  1283.6 20.0 %all-gather.23.cloned.1.call-done = bf16[128,4096]{1,0:T(8,128)(2,1)} async-done(((bf16[64,4096]{1,0:T(8,128)(2,1)}), bf16[128,4096]{1,0:T(8,128)(2,1)}) %all-gather.23.cloned.1.call-update) | async-done | bytes 1048592 | tf_op jit(solution)/shard_map/all_gather | solution.py:556
  (388 shorter events, 234.4 us)
Async XLA Ops:
  7.2 555.1 %copy-start = (bf16[2048,352]{0,1:T(8,128)(2,1)S(1)}, bf16[2048,352]{0,1:T(8,128)(2,1)}, u32[]{:S(2)}) copy-start(bf16[2048,352]{0,1:T(8,128)(2,1)} %param.30) | copy-start | bytes 4325380
  36.2 27.9 %all-to-all-start.1 = ((bf16[8,256,384]{1,2,0:T(8,128)(2,1)}), bf16[8,256,384]{1,2,0:T(8,128)(2,1)}, u32[]{:S(2)}, u32[]{:S(2)}) async-start(bf16[8,256,384]{1,2,0:T(8,128)(2,1)} %broadcast_in_dim.57), calls=%async_computation.1 | async-start | bytes 3145728 | tf_op jit(solution)/shard_map/all_to_all | solution.py:302
  40.6 87.5 %all-gather.11.cloned.1.call-start = ((), (), s32[]{:S(2)}) async-start(), calls=%async_computation.19 | async-start | bytes 4456448 | tf_op jit(solution)/shard_map/all_gather | solution.py:322
  40.9 25.7 %copy-start.48 = (f32[64]{0:T(128)}, f32[64]{0:T(128)S(1)}, u32[]{:S(2)}) copy-start(f32[64]{0:T(128)S(1)} %add_rsqrt_fusion.1) | copy-start | bytes 772
  68.4 177.8 %all-gather.9.cloned.1.call-start = ((), (), s32[]{:S(2)}) async-start(), calls=%async_computation.18 | async-start | bytes 10027008 | tf_op jit(solution)/shard_map/all_gather | solution.py:223
  87.8 238.0 %all-gather.13.cloned.1.call-start = ((), (), s32[]{:S(2)}) async-start(), calls=%async_computation.20 | async-start | bytes 8912896 | tf_op jit(solution)/shard_map/all_gather | solution.py:370
  88.6 168.5 %copy-start.46 = (f32[64]{0:T(128)}, f32[64]{0:T(128)S(1)}, u32[]{:S(2)}) copy-start(f32[64]{0:T(128)S(1)} %multiply_exponential_fusion) | copy-start | bytes 772
  88.6 43.4 %copy-start.42 = (f32[1024]{0:T(1024)}, f32[1024]{0:T(1024)S(1)}, u32[]{:S(2)}) copy-start(f32[1024]{0:T(1024)S(1)} %iota_convert_fusion) | copy-start | bytes 12292
  135.7 64.3 %all-to-all-start.3 = ((bf16[8,1024,256]{2,1,0:T(8,128)(2,1)}), bf16[8,1024,256]{2,1,0:T(8,128)(2,1)}, u32[]{:S(2)}, u32[]{:S(2)}) async-start(bf16[8,1024,256]{2,1,0:T(8,128)(2,1)} %broadcast_in_dim.66), calls=%async_computation.3 | async-start | bytes 8388608 | tf_op jit(solution)/shard_map/all_to_all | solution.py:334
  159.2 97.9 %copy-start.35 = (f32[2304]{0:T(1024)}, f32[2304]{0:T(1024)S(1)}, u32[]{:S(2)}) copy-start(f32[2304]{0:T(1024)S(1)} %fusion.66) | copy-start | bytes 27652
  276.7 6.1 copy-start.30
  277.8 20.6 %all-to-all-start.4 = ((bf16[16,144,128]{2,1,0:T(8,128)(2,1)}), bf16[16,144,128]{2,1,0:T(8,128)(2,1)S(1)}, u32[]{:S(2)}, u32[]{:S(2)}) async-start(bf16[16,144,128]{2,1,0:T(8,128)(2,1)} %copy.493), calls=%async_computation.4 | async-start | bytes 1179648 | tf_op jit(solution)/shard_map/all_to_all | solution.py:239
  332.2 28.2 %all-to-all-start.5 = ((f32[8,18,2048]{2,1,0:T(8,128)}), f32[8,18,2048]{2,1,0:T(8,128)}, u32[]{:S(2)}, u32[]{:S(2)}) async-start(f32[8,18,2048]{2,1,0:T(8,128)} %fusion.2), calls=%async_computation.5 | async-start | bytes 3145728 | tf_op jit(solution)/shard_map/all_to_all | solution.py:249
  336.5 140.5 %all-gather.15.cloned.1.call-start = ((), (), s32[]{:S(2)}) async-start(), calls=%async_computation.21 | async-start | bytes 10027008 | tf_op jit(solution)/shard_map/all_gather | solution.py:397
  400.4 154.8 %all-gather.19.cloned.1.call-start = ((), (), s32[]{:S(2)}) async-start(), calls=%async_computation.23 | async-start | bytes 10027008 | tf_op jit(solution)/shard_map/all_gather | solution.py:403
  555.2 7.1 copy-start.51
  555.2 7.8 copy-start.53
  562.9 8.6 copy-start.52
  571.6 7.5 copy-start.54
  579.1 118.5 %all-to-all-start.7 = ((bf16[16,144,2048]{2,1,0:T(8,128)(2,1)}), bf16[16,144,2048]{2,1,0:T(8,128)(2,1)}, u32[]{:S(2)}, u32[]{:S(2)}) async-start(bf16[16,144,2048]{2,1,0:T(8,128)(2,1)} %bitcast.140), calls=%async_computation.7 | async-start | bytes 18874368 | tf_op jit(solution)/shard_map/all_to_all | solution.py:228
  583.9 278.4 %all-gather.17.cloned.1.call-start = ((), (), s32[]{:S(2)}) async-start(), calls=%async_computation.22 | async-start | bytes 8912896 | tf_op jit(solution)/shard_map/all_gather | solution.py:415
  584.5 10.9 copy-start.15
  697.6 131.6 %all-to-all-start.9 = ((bf16[16,144,2048]{2,1,0:T(8,128)(2,1)}), bf16[16,144,2048]{2,1,0:T(8,128)(2,1)}, u32[]{:S(2)}, u32[]{:S(2)}) async-start(bf16[16,144,2048]{2,1,0:T(8,128)(2,1)} %bitcast.130), calls=%async_computation.9 | async-start | bytes 18874368 | tf_op jit(solution)/shard_map/all_to_all | solution.py:228
  829.2 27.6 %all-to-all-start.8 = ((f32[8,18,2048]{2,1,0:T(8,128)}), f32[8,18,2048]{2,1,0:T(8,128)}, u32[]{:S(2)}, u32[]{:S(2)}) async-start(f32[8,18,2048]{2,1,0:T(8,128)} %reshape.667), calls=%async_computation.8 | async-start | bytes 3145728 | tf_op jit(solution)/shard_map/all_to_all | solution.py:236
  840.8 20.9 %copy-start.41 = (s32[8,18,1]{0,1,2:T(8,128)S(1)}, s32[8,18,1]{0,1,2:T(8,128)}, u32[]{:S(2)}) copy-start(s32[8,18,1]{0,1,2:T(8,128)} %get-tuple-element.174) | copy-start | bytes 1732
  840.8 21.1 %copy-start.50 = (s32[64,2]{0,1:T(2,128)S(1)}, s32[64,2]{0,1:T(2,128)}, u32[]{:S(2)}) copy-start(s32[64,2]{0,1:T(2,128)} %get-tuple-element.184) | copy-start | bytes 1540
  856.9 26.7 %all-to-all-start.10 = ((f32[8,18,2048]{2,1,0:T(8,128)}), f32[8,18,2048]{2,1,0:T(8,128)}, u32[]{:S(2)}, u32[]{:S(2)}) async-start(f32[8,18,2048]{2,1,0:T(8,128)} %reshape.671), calls=%async_computation.10 | async-start | bytes 3145728 | tf_op jit(solution)/shard_map/all_to_all | solution.py:236
  861.2 140.6 %all-gather.21.cloned.1.call-start = ((), (), s32[]{:S(2)}) async-start(), calls=%async_computation.24 | async-start | bytes 10027008 | tf_op jit(solution)/shard_map/all_gather | solution.py:223
  918.8 83.0 %copy-start.29 = (bf16[128,2048]{1,0:T(8,128)(2,1)S(1)}, bf16[128,2048]{1,0:T(8,128)(2,1)}, u32[]{:S(2)}) copy-start(bf16[128,2048]{1,0:T(8,128)(2,1)} %param.26) | copy-start | bytes 1572868
  1011.1 13.8 %copy-start.36 = (f32[2304]{0:T(1024)S(1)}, f32[2304]{0:T(1024)}, u32[]{:S(2)}) copy-start(f32[2304]{0:T(1024)} %copy-done.35) | copy-start | bytes 27652
  1011.1 13.8 %copy-start.47 = (f32[64]{0:T(128)S(1)}, f32[64]{0:T(128)}, u32[]{:S(2)}) copy-start(f32[64]{0:T(128)} %copy-done.46) | copy-start | bytes 772
  1036.3 15.3 %all-to-all-start.12 = ((bf16[16,144,128]{2,1,0:T(8,128)(2,1)}), bf16[16,144,128]{2,1,0:T(8,128)(2,1)}, u32[]{:S(2)}, u32[]{:S(2)}) async-start(bf16[16,144,128]{2,1,0:T(8,128)(2,1)} %copy.527), calls=%async_computation.12 | async-start | bytes 1179648 | tf_op jit(solution)/shard_map/all_to_all | solution.py:239
  1051.6 64.1 %all-to-all-start.14 = ((bf16[8,1024,256]{2,1,0:T(8,128)(2,1)}), bf16[8,1024,256]{2,1,0:T(8,128)(2,1)}, u32[]{:S(2)}, u32[]{:S(2)}) async-start(bf16[8,1024,256]{2,1,0:T(8,128)(2,1)} %pad_maximum_fusion), calls=%async_computation.14 | async-start | bytes 8388608 | tf_op jit(solution)/shard_map/all_to_all | solution.py:484
  1115.7 27.6 %all-to-all-start.13 = ((f32[8,18,2048]{2,1,0:T(8,128)}), f32[8,18,2048]{2,1,0:T(8,128)}, u32[]{:S(2)}, u32[]{:S(2)}) async-start(f32[8,18,2048]{2,1,0:T(8,128)} %fusion), calls=%async_computation.13 | async-start | bytes 3145728 | tf_op jit(solution)/shard_map/all_to_all | solution.py:249
  1143.3 6.4 copy-start.3
  1143.3 55.9 %all-to-all-start.15 = ((bf16[16,64,2048]{2,1,0:T(8,128)(2,1)}), bf16[16,64,2048]{2,1,0:T(8,128)(2,1)}, u32[]{:S(2)}, u32[]{:S(2)}) async-start(bf16[16,64,2048]{2,1,0:T(8,128)(2,1)} %bitcast.131), calls=%async_computation.15 | async-start | bytes 8388608 | tf_op jit(solution)/shard_map/all_to_all | solution.py:506
  1149.3 124.3 %reduce-scatter.2.cloned.1.call-start = ((), (), s32[]{:S(2)}) async-start(), calls=%async_computation.26 | async-start | bytes 3538944 | tf_op jit(solution)/shard_map/reduce_scatter | solution.py:540
  1161.5 40.6 %copy-start.19 = (bf16[128,2048]{1,0:T(8,128)(2,1)S(1)}, bf16[128,2048]{1,0:T(8,128)(2,1)}, u32[]{:S(2)}) copy-start(bf16[128,2048]{1,0:T(8,128)(2,1)} %param.21) | copy-start | bytes 1572868
  1161.5 40.6 %copy-start.33 = (f32[2048]{0:T(1024)S(1)}, f32[2048]{0:T(1024)}, u32[]{:S(2)}) copy-start(f32[2048]{0:T(1024)} %copy-done.32) | copy-start | bytes 24580
  1161.5 40.6 %copy-start.49 = (f32[64]{0:T(128)S(1)}, f32[64]{0:T(128)}, u32[]{:S(2)}) copy-start(f32[64]{0:T(128)} %copy-done.48) | copy-start | bytes 772
  1207.2 96.3 %all-gather.23.cloned.1.call-start = ((), (), s32[]{:S(2)}) async-start(), calls=%async_computation.25 | async-start | bytes 1572864 | tf_op jit(solution)/shard_map/all_gather | solution.py:556
  1208.6 9.7 copy-start.21
  1208.7 18.6 %slice-start = ((s8[9437184]{0:T(1024)(128)(4,1)}), s8[4194304]{0:T(1024)(128)(4,1)S(1)}, s32[]{:S(2)}) async-start(s8[9437184]{0:T(1024)(128)(4,1)} %bitcast.170), calls=%async_computation.27 | async-start | bytes 8388608
  1208.7 18.6 %slice-start.1 = ((s8[9437184]{0:T(1024)(128)(4,1)}), s8[4194304]{0:T(1024)(128)(4,1)S(1)}, s32[]{:S(2)}) async-start(s8[9437184]{0:T(1024)(128)(4,1)} %bitcast.170), calls=%async_computation.28 | async-start | bytes 8388608
  1218.3 9.0 copy-start.16
  1218.3 9.0 slice-start.2
  1235.4 6.2 copy-start.28
  1275.5 30.5 %all-to-all-start.16 = ((f32[16,16,384]{2,1,0:T(8,128)}), f32[16,16,384]{2,1,0:T(8,128)S(1)}, u32[]{:S(2)}, u32[]{:S(2)}) async-start(f32[16,16,384]{2,1,0:T(8,128)} %bitcast.45), calls=%async_computation.17 | async-start | bytes 786432 | tf_op jit(solution)/shard_map/all_to_all | solution.py:541
  (32 other events, 82.4 us)
Sparse Core Ops, SparseCore 0:
  68.5 59.6 all-gather.10
  131.2 114.9 all-gather.8
  248.7 77.1 all-gather.12
  400.5 76.4 all-gather.14
  479.9 75.2 all-gather.18
  586.7 232.7 all-gather.16
  921.1 80.5 all-gather.20
  1207.4 66.1 reduce-scatter.1
  1275.8 27.7 all-gather.22

commit v11 on v10

--- a/solution.py
+++ b/solution.py
@@ -235,6 +235,18 @@
         summed = jnp.sum(parts.astype(jnp.float32), axis=0).reshape(groups, slot_cap, width)
         return lax.all_to_all(summed, "grp", split_axis=0, concat_axis=0, tiled=True)
 
+    def combine_scattered(partial_value):
+        summed = lax.psum_scatter(
+            partial_value.astype(jnp.bfloat16), GROUP_AXES, scatter_dimension=0, tiled=True
+        )
+        return lax.all_to_all(
+            summed.astype(jnp.float32).reshape(groups, slot_cap, width),
+            "grp",
+            split_axis=0,
+            concat_axis=0,
+            tiled=True,
+        )
+
     def to_rows(per_head):
         parts = lax.all_to_all(
             per_head.reshape(group_size, groups * slot_cap, head_cols),
@@ -411,7 +423,7 @@
     activated = jax.nn.silu(gate_pre)
     inner_rows = (activated * up_pre).astype(jnp.bfloat16)
     mlp_partial = jnp.dot(inner_rows, down_weight, preferred_element_type=jnp.float32)
-    mlp_slots = combine(mlp_partial)
+    mlp_slots = combine_scattered(mlp_partial)
     query_stack = lax.all_gather(query_weight, GROUP_AXES, axis=1, tiled=True)
     mlp_slots, query_stack = lax.optimization_barrier((mlp_slots, query_stack))
     mlp_picked = mlp_slots.reshape(EXPERTS * slot_cap, width)[mlp_index]

time: 1330 us -> 1270 us (0.955)
  waiting for transfers between devices: 815 us -> 621 us
  blocking collectives: 63.5 us -> 201 us
  local copies, waits for them, and re-layouts: 115 us -> 130 us
    all_to_all x2 -> x1, waiting for transfers between devices: 210 us -> 0.01 us  [combine_scattered(): lax.all_to_all(summed.astype(jnp.float32).reshape(groups, slot_cap, width...]
    all_to_all x0 -> x1, blocking collectives: none -> 136 us  [combine(): lax.all_to_all(partial_value.astype(jnp.bfloat16).reshape(group_size, gro...]
    all_gather x1, waiting for transfers between devices: 0.01 us -> 48.8 us  [shards(): query_stack = lax.all_gather(query_weight, GROUP_AXES, axis=1, tiled=True)]
    all_to_all x2 -> x1, waiting for transfers between devices: 31.2 us -> 19.3 us  [combine(): lax.all_to_all(summed, 'grp', split_axis=0, concat_axis=0, tiled=True)]
  transfers between devices with their start and end apart: 22 -> 21, of which waited for: 20 -> 19; matrix products, arithmetic and copies ran while one was open for 16% -> 17% of each run, Pallas kernels for 1% -> 1%
where the time goes in v11:
time: 1270 us
  waiting for transfers between devices  621 us (49%)
  blocking collectives  201 us (16%)
  matrix products  143 us (11%)
  local copies, waits for them, and re-layouts  130 us (10%)
  other arithmetic  74 us (6%)
  starting transfers between devices  54.9 us (4%)
  Pallas kernels  24.6 us (2%)
  between operations  15.9 us (1%)
    all_to_all x1, blocking collectives, combine(): lax.all_to_all(partial_value.astype(jnp.bfloat16).reshape(group_size, gro...  136 us
    all_gather x2, waiting for transfers between devices, dispatch(): lax.all_gather(by_group.reshape(groups * slot_cap, width), GROUP_AXES, ax...  113 us
    all_gather x1, waiting for transfers between devices, shards(): lax.all_gather(mlp_by_group[:, :slot_cap].reshape(groups * slot_cap, widt...  73.8 us
    all_gather x1, waiting for transfers between devices, shards(): lax.all_gather(mlp_by_group[:, slot_cap:].reshape(groups * slot_cap, widt...  68.9 us
    all_to_all x1, waiting for transfers between devices, shards(): lax.all_to_all(jnp.concatenate([seq_key_grad, seq_value_grad], axis=2).as...  50.5 us
    all_gather x1, waiting for transfers between devices, shards(): query_stack = lax.all_gather(query_weight, GROUP_AXES, axis=1, tiled=True)  48.8 us
    all_to_all x1, waiting for transfers between devices, shards(): lax.all_to_all(jnp.einsum('rc,dc->rd', kv_col_grad, head_kv, preferred_el...  37.5 us
    all_to_all x1, waiting for transfers between devices, shards(): lax.all_to_all(jnp.broadcast_to(seq_pair[None], (groups,) + seq_pair.shap...  37.4 us
  transfers between devices with their start and end apart: 21, of which 19 were waited for; matrix products, arithmetic and copies ran while one was open for 17% of the time, Pallas kernels for 1%

profile of v11, /device:TPU:1, one launch (start us, length us, event | category | flops | bytes accessed | tf_op | source)
XLA Modules:
  0.0 1265.1 jit_solution(562347584210450217)
XLA Ops:
  17.2 17.5 %all_to_all.80 = bf16[16,16,384]{2,1,0:T(8,128)(2,1)S(1)} all-to-all(bf16[16,16,384]{2,1,0:T(8,128)(2,1)S(1)} %pad_maximum_fusion.10), channel_id=1, replica_groups=mesh['grp'=8,'sub'=8,'expert'=2] {'sub','expert'}, dimensions={0} | all-to-all | bytes 393216 | tf_op jit(solution)/shard_map/all_to_all | solution.py:301
  40.8 23.2 %all-to-all-done.1 = bf16[8,256,384]{1,2,0:T(8,128)(2,1)} async-done(((bf16[8,256,384]{1,2,0:T(8,128)(2,1)}), bf16[8,256,384]{1,2,0:T(8,128)(2,1)}, u32[]{:S(2)}, u32[]{:S(2)}) %all-to-all-start.1) | async-done | bytes 1572896 | tf_op jit(solution)/shard_map/all_to_all | solution.py:314
  75.7 13.9 %all_to_all.81 = bf16[8,18,2048]{2,1,0:T(8,128)(2,1)} all-to-all(bf16[8,18,2048]{2,1,0:T(8,128)(2,1)S(1)} %broadcast_select_fusion.1), channel_id=1, replica_groups=mesh['grp'=8,'sub'=8,'expert'=2] {'grp'}, dimensions={0} | all-to-all | bytes 1179648 | tf_op jit(solution)/shard_map/all_to_all | solution.py:222
  92.6 36.3 %all-gather.11.cloned.1.call-done = bf16[1024,2048]{1,0:T(8,128)(2,1)} async-done(((bf16[64,2048]{1,0:T(8,128)(2,1)}), bf16[1024,2048]{1,0:T(8,128)(2,1)}) %all-gather.11.cloned.1.call-update) | async-done | bytes 4194320 | tf_op jit(solution)/shard_map/all_gather | solution.py:334
  139.7 4.8 all-to-all-start.3
  155.0 5.6 multiply_reduce_fusion
  166.6 37.4 %all-to-all-done.3 = bf16[8,1024,256]{2,1,0:T(8,128)(2,1)} async-done(((bf16[8,1024,256]{2,1,0:T(8,128)(2,1)}), bf16[8,1024,256]{2,1,0:T(8,128)(2,1)}, u32[]{:S(2)}, u32[]{:S(2)}) %all-to-all-start.3) | async-done | bytes 4194336 | tf_op jit(solution)/shard_map/all_to_all | solution.py:346
  208.7 36.4 %all-gather.9.cloned.1.call-done = bf16[2304,2048]{1,0:T(8,128)(2,1)} async-done(((bf16[144,2048]{1,0:T(8,128)(2,1)}), bf16[2304,2048]{1,0:T(8,128)(2,1)}) %all-gather.9.cloned.1.call-update) | async-done | bytes 9437200 | tf_op jit(solution)/shard_map/all_gather | solution.py:223
  245.1 7.4 fusion.86
  256.5 5.4 fusion.14
  263.0 10.8 shard_map.238
  283.1 14.8 %all-to-all-done.4 = bf16[16,144,128]{2,1,0:T(8,128)(2,1)S(1)} async-done(((bf16[16,144,128]{2,1,0:T(8,128)(2,1)}), bf16[16,144,128]{2,1,0:T(8,128)(2,1)S(1)}, u32[]{:S(2)}, u32[]{:S(2)}) %all-to-all-start.4) | async-done | bytes 589856 | tf_op jit(solution)/shard_map/all_to_all | solution.py:251
  300.2 24.5 %all-gather.13.cloned.1.call-done = bf16[2048,2048]{1,0:T(8,128)(2,1)} async-done(((bf16[128,2048]{1,0:T(8,128)(2,1)}), bf16[2048,2048]{1,0:T(8,128)(2,1)}) %all-gather.13.cloned.1.call-update) | async-done | bytes 8388624 | tf_op jit(solution)/shard_map/all_gather | solution.py:382
  324.7 6.4 fusion.2
  346.0 13.3 %all-to-all-done.5 = f32[8,18,2048]{2,1,0:T(8,128)} async-done(((f32[8,18,2048]{2,1,0:T(8,128)}), f32[8,18,2048]{2,1,0:T(8,128)}, u32[]{:S(2)}, u32[]{:S(2)}) %all-to-all-start.5) | async-done | bytes 1179680 | tf_op jit(solution)/shard_map/all_to_all | solution.py:261
  383.1 19.2 %all_to_all.82 = bf16[8,36,2048]{2,1,0:T(8,128)(2,1)S(1)} all-to-all(bf16[8,36,2048]{2,1,0:T(8,128)(2,1)S(1)} %pad_maximum_fusion.2), channel_id=1, replica_groups=mesh['grp'=8,'sub'=8,'expert'=2] {'grp'}, dimensions={0} | all-to-all | bytes 2359296 | tf_op jit(solution)/shard_map/all_to_all | solution.py:402
  408.2 73.8 %all-gather.15.cloned.1.call-done = bf16[2304,2048]{1,0:T(8,128)(2,1)} async-done(((bf16[144,2048]{1,0:T(8,128)(2,1)}), bf16[2304,2048]{1,0:T(8,128)(2,1)}) %all-gather.15.cloned.1.call-update) | async-done | bytes 9437200 | tf_op jit(solution)/shard_map/all_gather | solution.py:409
  482.0 9.3 fusion.87
  491.3 68.9 %all-gather.19.cloned.1.call-done = bf16[2304,2048]{1,0:T(8,128)(2,1)} async-done(((bf16[144,2048]{1,0:T(8,128)(2,1)}), bf16[2304,2048]{1,0:T(8,128)(2,1)}) %all-gather.19.cloned.1.call-update) | async-done | bytes 9437200 | tf_op jit(solution)/shard_map/all_gather | solution.py:415
  560.2 7.1 fusion.88
  568.0 8.6 multiply_convert_fusion.2
  577.8 7.5 convolution_convert_fusion
  586.0 12.2 fusion.89
  598.3 11.1 add_convert_fusion
  609.3 136.2 %all_to_all.83 = bf16[16,144,2048]{2,1,0:T(8,128)(2,1)} all-to-all(bf16[16,144,2048]{2,1,0:T(8,128)(2,1)S(1)} %bitcast.129), channel_id=1, replica_groups=mesh['grp'=8,'sub'=8,'expert'=2] {'sub','expert'}, dimensions={0} | all-to-all | bytes 18874368 | tf_op jit(solution)/shard_map/all_to_all | solution.py:228
  745.5 5.9 convert_reduce_fusion
  761.3 19.3 %all-to-all-done.9 = f32[8,18,2048]{2,1,0:T(8,128)} async-done(((f32[8,18,2048]{2,1,0:T(8,128)}), f32[8,18,2048]{2,1,0:T(8,128)}, u32[]{:S(2)}, u32[]{:S(2)}) %all-to-all-start.9) | async-done | bytes 1179680 | tf_op jit(solution)/shard_map/all_to_all | solution.py:236
  793.6 48.8 %all-gather.17.cloned.1.call-done = bf16[2048,2048]{1,0:T(8,128)(2,1)} async-done(((bf16[2048,128]{1,0:T(8,128)(2,1)}), bf16[2048,2048]{1,0:T(8,128)(2,1)}) %all-gather.17.cloned.1.call-update) | async-done | bytes 8388624 | tf_op jit(solution)/shard_map/all_gather | solution.py:427
  862.9 14.7 %all_to_all.84 = bf16[8,18,2048]{2,1,0:T(8,128)(2,1)S(1)} all-to-all(bf16[8,18,2048]{2,1,0:T(8,128)(2,1)S(1)} %multiply_convert_fusion.3), channel_id=1, replica_groups=mesh['grp'=8,'sub'=8,'expert'=2] {'grp'}, dimensions={0} | all-to-all | bytes 1179648 | tf_op jit(solution)/shard_map/all_to_all | solution.py:222
  878.6 76.2 %all-gather.21.cloned.1.call-done = bf16[2304,2048]{1,0:T(8,128)(2,1)} async-done(((bf16[144,2048]{1,0:T(8,128)(2,1)}), bf16[2304,2048]{1,0:T(8,128)(2,1)}) %all-gather.21.cloned.1.call-update) | async-done | bytes 9437200 | tf_op jit(solution)/shard_map/all_gather | solution.py:223
  954.8 6.3 convolution_convert_fusion.2
  962.3 13.8 %shard_map.239 = (f32[8,288,128]{2,1,0:T(8,128)}, f32[8,1024,128]{2,1,0:T(8,128)}, f32[8,1024,128]{2,1,0:T(8,128)}) custom-call(bf16[8,288,128]{2,1,0:T(8,128)(2,1)} %pad_maximum_fusion.3.q_ref, bf16[8,1024,128]{2,1,0:T(8,128)(2,1)} %bitcast.142, bf16[8,1024,128]{2,1,0:T(8,128)(2,1)} %bitcast.140, s32[8,288,1]{2,1,0:T(8,128)} %add_select_fusion.qb_ref, ...), custom_call_target="tpu_custom_call" | custom-call | flops 3019898880 | bytes 25100288 | tf_op jit(solution)/shard_map/pallas_call | solution.py:76
  976.1 7.9 fusion.18
  995.4 4.7 all-to-all-done.11
  1006.1 7.6 fusion
  1013.7 50.5 %all-to-all-done.13 = bf16[8,1024,256]{2,1,0:T(8,128)(2,1)} async-done(((bf16[8,1024,256]{2,1,0:T(8,128)(2,1)}), bf16[8,1024,256]{2,1,0:T(8,128)(2,1)}, u32[]{:S(2)}, u32[]{:S(2)}) %all-to-all-start.13) | async-done | bytes 4194336 | tf_op jit(solution)/shard_map/all_to_all | solution.py:496
  1084.3 7.6 all-to-all-done.12
  1091.8 6.0 all-to-all-start.14
  1105.4 4.9 fusion.53
  1110.2 37.5 %all-to-all-done.14 = bf16[16,64,2048]{2,1,0:T(8,128)(2,1)} async-done(((bf16[16,64,2048]{2,1,0:T(8,128)(2,1)}), bf16[16,64,2048]{2,1,0:T(8,128)(2,1)}, u32[]{:S(2)}, u32[]{:S(2)}) %all-to-all-start.14) | async-done | bytes 4194336 | tf_op jit(solution)/shard_map/all_to_all | solution.py:518
  1157.3 9.6 fusion.94
  1166.9 9.0 fusion.95
  1175.9 5.1 fusion.96
  1183.9 6.2 fusion.93
  1190.2 7.4 fusion.92
  1197.5 24.6 %reduce-scatter.5.cloned.1.call-done = f32[256,384]{0,1:T(8,128)} async-done(((f32[2048,384]{0,1:T(8,128)}), f32[256,384]{0,1:T(8,128)}) %reduce-scatter.5.cloned.1.call-update) | async-done | bytes 393232 | tf_op jit(solution)/shard_map/reduce_scatter | solution.py:552
  1224.1 8.1 all-to-all-start.15
  1232.2 20.0 %all-gather.23.cloned.1.call-done = bf16[128,4096]{1,0:T(8,128)(2,1)} async-done(((bf16[64,4096]{1,0:T(8,128)(2,1)}), bf16[128,4096]{1,0:T(8,128)(2,1)}) %all-gather.23.cloned.1.call-update) | async-done | bytes 1048592 | tf_op jit(solution)/shard_map/all_gather | solution.py:568
  (381 shorter events, 236.1 us)
Async XLA Ops:
  7.2 560.1 %copy-start = (bf16[2048,352]{0,1:T(8,128)(2,1)S(1)}, bf16[2048,352]{0,1:T(8,128)(2,1)}, u32[]{:S(2)}) copy-start(bf16[2048,352]{0,1:T(8,128)(2,1)} %param.30) | copy-start | bytes 4325380
  36.1 27.9 %all-to-all-start.1 = ((bf16[8,256,384]{1,2,0:T(8,128)(2,1)}), bf16[8,256,384]{1,2,0:T(8,128)(2,1)}, u32[]{:S(2)}, u32[]{:S(2)}) async-start(bf16[8,256,384]{1,2,0:T(8,128)(2,1)} %broadcast_in_dim.57), calls=%async_computation.1 | async-start | bytes 3145728 | tf_op jit(solution)/shard_map/all_to_all | solution.py:314
  40.6 88.3 %all-gather.11.cloned.1.call-start = ((), (), s32[]{:S(2)}) async-start(), calls=%async_computation.19 | async-start | bytes 4456448 | tf_op jit(solution)/shard_map/all_gather | solution.py:334
  40.8 25.6 %copy-start.45 = (f32[64]{0:T(128)}, f32[64]{0:T(128)S(1)}, u32[]{:S(2)}) copy-start(f32[64]{0:T(128)S(1)} %add_rsqrt_fusion.1) | copy-start | bytes 772
  65.9 80.2 %copy-start.3 = (bf16[8,256,384]{2,1,0:T(8,128)(2,1)}, bf16[8,256,384]{2,1,0:T(8,128)(2,1)S(1)}, u32[]{:S(2)}) copy-start(bf16[8,256,384]{2,1,0:T(8,128)(2,1)S(1)} %copy.482) | copy-start | bytes 4718596
  68.9 176.2 %all-gather.9.cloned.1.call-start = ((), (), s32[]{:S(2)}) async-start(), calls=%async_computation.18 | async-start | bytes 10027008 | tf_op jit(solution)/shard_map/all_gather | solution.py:223
  91.8 232.9 %all-gather.13.cloned.1.call-start = ((), (), s32[]{:S(2)}) async-start(), calls=%async_computation.20 | async-start | bytes 8912896 | tf_op jit(solution)/shard_map/all_gather | solution.py:382
  92.5 164.0 %copy-start.43 = (f32[64]{0:T(128)}, f32[64]{0:T(128)S(1)}, u32[]{:S(2)}) copy-start(f32[64]{0:T(128)S(1)} %multiply_exponential_fusion) | copy-start | bytes 772
  92.6 39.9 %copy-start.36 = (f32[1024]{0:T(1024)}, f32[1024]{0:T(1024)S(1)}, u32[]{:S(2)}) copy-start(f32[1024]{0:T(1024)S(1)} %iota_convert_fusion) | copy-start | bytes 12292
  139.7 64.2 %all-to-all-start.3 = ((bf16[8,1024,256]{2,1,0:T(8,128)(2,1)}), bf16[8,1024,256]{2,1,0:T(8,128)(2,1)}, u32[]{:S(2)}, u32[]{:S(2)}) async-start(bf16[8,1024,256]{2,1,0:T(8,128)(2,1)} %broadcast_in_dim.66), calls=%async_computation.3 | async-start | bytes 8388608 | tf_op jit(solution)/shard_map/all_to_all | solution.py:346
  155.0 8.2 copy-start.8
  163.2 93.3 %copy-start.29 = (f32[2304]{0:T(1024)}, f32[2304]{0:T(1024)S(1)}, u32[]{:S(2)}) copy-start(f32[2304]{0:T(1024)S(1)} %fusion.66) | copy-start | bytes 27652
  204.0 41.1 %copy-start.23 = (bf16[2048,128]{1,0:T(8,128)(2,1)S(1)}, bf16[2048,128]{1,0:T(8,128)(2,1)}, u32[]{:S(2)}) copy-start(bf16[2048,128]{1,0:T(8,128)(2,1)} %param.25) | copy-start | bytes 1572868
  277.1 20.8 %all-to-all-start.4 = ((bf16[16,144,128]{2,1,0:T(8,128)(2,1)}), bf16[16,144,128]{2,1,0:T(8,128)(2,1)S(1)}, u32[]{:S(2)}, u32[]{:S(2)}) async-start(bf16[16,144,128]{2,1,0:T(8,128)(2,1)} %copy.493), calls=%async_computation.4 | async-start | bytes 1179648 | tf_op jit(solution)/shard_map/all_to_all | solution.py:251
  331.0 28.3 %all-to-all-start.5 = ((f32[8,18,2048]{2,1,0:T(8,128)}), f32[8,18,2048]{2,1,0:T(8,128)}, u32[]{:S(2)}, u32[]{:S(2)}) async-start(f32[8,18,2048]{2,1,0:T(8,128)} %fusion.2), calls=%async_computation.5 | async-start | bytes 3145728 | tf_op jit(solution)/shard_map/all_to_all | solution.py:261
  335.3 146.7 %all-gather.15.cloned.1.call-start = ((), (), s32[]{:S(2)}) async-start(), calls=%async_computation.21 | async-start | bytes 10027008 | tf_op jit(solution)/shard_map/all_gather | solution.py:409
  345.9 511.4 %copy-start.41 = (f32[64,2]{0,1:T(2,128)}, f32[64,2]{0,1:T(2,128)S(1)}, u32[]{:S(2)}) copy-start(f32[64,2]{0,1:T(2,128)S(1)} %get-tuple-element.152) | copy-start | bytes 1540
  405.8 154.4 %all-gather.19.cloned.1.call-start = ((), (), s32[]{:S(2)}) async-start(), calls=%async_computation.24 | async-start | bytes 10027008 | tf_op jit(solution)/shard_map/all_gather | solution.py:415
  408.0 350.9 %reduce-scatter.3.cloned.1.call-start = ((), (), s32[]{:S(2)}) async-start(), calls=%async_computation.22 | async-start | bytes 10027008 | tf_op jit(solution)/shard_map/reduce_scatter | solution.py:239
  560.2 7.1 copy-start.48
  560.2 7.8 copy-start.50
  568.0 9.8 copy-start.49
  585.3 257.1 %all-gather.17.cloned.1.call-start = ((), (), s32[]{:S(2)}) async-start(), calls=%async_computation.23 | async-start | bytes 8912896 | tf_op jit(solution)/shard_map/all_gather | solution.py:427
  586.0 12.2 copy-start.10
  752.7 27.8 %all-to-all-start.9 = ((f32[8,18,2048]{2,1,0:T(8,128)}), f32[8,18,2048]{2,1,0:T(8,128)}, u32[]{:S(2)}, u32[]{:S(2)}) async-start(f32[8,18,2048]{2,1,0:T(8,128)} %reshape.671), calls=%async_computation.10 | async-start | bytes 3145728 | tf_op jit(solution)/shard_map/all_to_all | solution.py:236
  761.3 24.0 %copy-start.35 = (s32[8,18,1]{0,1,2:T(8,128)S(1)}, s32[8,18,1]{0,1,2:T(8,128)}, u32[]{:S(2)}) copy-start(s32[8,18,1]{0,1,2:T(8,128)} %get-tuple-element.174) | copy-start | bytes 1732
  761.3 24.2 %copy-start.47 = (s32[64,2]{0,1:T(2,128)S(1)}, s32[64,2]{0,1:T(2,128)}, u32[]{:S(2)}) copy-start(s32[64,2]{0,1:T(2,128)} %get-tuple-element.184) | copy-start | bytes 1540
  780.6 61.8 %all-to-all-start.7 = ((f32[8,18,2048]{2,1,0:T(8,128)}), f32[8,18,2048]{2,1,0:T(8,128)}, u32[]{:S(2)}, u32[]{:S(2)}) async-start(f32[8,18,2048]{2,1,0:T(8,128)} %reshape.724), calls=%async_computation.8 | async-start | bytes 3145728 | tf_op jit(solution)/shard_map/all_to_all | solution.py:242
  784.8 170.0 %all-gather.21.cloned.1.call-start = ((), (), s32[]{:S(2)}) async-start(), calls=%async_computation.25 | async-start | bytes 10027008 | tf_op jit(solution)/shard_map/all_gather | solution.py:223
  862.9 91.9 %copy-start.24 = (bf16[128,2048]{1,0:T(8,128)(2,1)S(1)}, bf16[128,2048]{1,0:T(8,128)(2,1)}, u32[]{:S(2)}) copy-start(bf16[128,2048]{1,0:T(8,128)(2,1)} %param.26) | copy-start | bytes 1572868
  962.3 13.8 %copy-start.30 = (f32[2304]{0:T(1024)S(1)}, f32[2304]{0:T(1024)}, u32[]{:S(2)}) copy-start(f32[2304]{0:T(1024)} %copy-done.29) | copy-start | bytes 27652
  962.3 13.8 %copy-start.44 = (f32[64]{0:T(128)S(1)}, f32[64]{0:T(128)}, u32[]{:S(2)}) copy-start(f32[64]{0:T(128)} %copy-done.43) | copy-start | bytes 772
  985.6 14.6 %all-to-all-start.11 = ((bf16[16,144,128]{2,1,0:T(8,128)(2,1)}), bf16[16,144,128]{2,1,0:T(8,128)(2,1)S(1)}, u32[]{:S(2)}, u32[]{:S(2)}) async-start(bf16[16,144,128]{2,1,0:T(8,128)(2,1)} %copy.527), calls=%async_computation.12 | async-start | bytes 1179648 | tf_op jit(solution)/shard_map/all_to_all | solution.py:251
  1000.1 64.1 %all-to-all-start.13 = ((bf16[8,1024,256]{2,1,0:T(8,128)(2,1)}), bf16[8,1024,256]{2,1,0:T(8,128)(2,1)}, u32[]{:S(2)}, u32[]{:S(2)}) async-start(bf16[8,1024,256]{2,1,0:T(8,128)(2,1)} %pad_maximum_fusion), calls=%async_computation.14 | async-start | bytes 8388608 | tf_op jit(solution)/shard_map/all_to_all | solution.py:496
  1064.3 27.6 %all-to-all-start.12 = ((f32[8,18,2048]{2,1,0:T(8,128)}), f32[8,18,2048]{2,1,0:T(8,128)}, u32[]{:S(2)}, u32[]{:S(2)}) async-start(f32[8,18,2048]{2,1,0:T(8,128)} %fusion), calls=%async_computation.13 | async-start | bytes 3145728 | tf_op jit(solution)/shard_map/all_to_all | solution.py:261
  1073.2 6.8 copy-start.4
  1091.8 55.9 %all-to-all-start.14 = ((bf16[16,64,2048]{2,1,0:T(8,128)(2,1)}), bf16[16,64,2048]{2,1,0:T(8,128)(2,1)}, u32[]{:S(2)}, u32[]{:S(2)}) async-start(bf16[16,64,2048]{2,1,0:T(8,128)(2,1)} %bitcast.130), calls=%async_computation.15 | async-start | bytes 8388608 | tf_op jit(solution)/shard_map/all_to_all | solution.py:518
  1097.9 124.3 %reduce-scatter.5.cloned.1.call-start = ((), (), s32[]{:S(2)}) async-start(), calls=%async_computation.27 | async-start | bytes 3538944 | tf_op jit(solution)/shard_map/reduce_scatter | solution.py:552
  1110.2 40.5 %copy-start.14 = (bf16[128,2048]{1,0:T(8,128)(2,1)S(1)}, bf16[128,2048]{1,0:T(8,128)(2,1)}, u32[]{:S(2)}) copy-start(bf16[128,2048]{1,0:T(8,128)(2,1)} %param.21) | copy-start | bytes 1572868
  1110.2 40.5 %copy-start.27 = (f32[2048]{0:T(1024)S(1)}, f32[2048]{0:T(1024)}, u32[]{:S(2)}) copy-start(f32[2048]{0:T(1024)} %copy-done.26) | copy-start | bytes 24580
  1110.2 40.5 %copy-start.46 = (f32[64]{0:T(128)S(1)}, f32[64]{0:T(128)}, u32[]{:S(2)}) copy-start(f32[64]{0:T(128)} %copy-done.45) | copy-start | bytes 772
  1155.8 96.3 %all-gather.23.cloned.1.call-start = ((), (), s32[]{:S(2)}) async-start(), calls=%async_computation.26 | async-start | bytes 1572864 | tf_op jit(solution)/shard_map/all_gather | solution.py:568
  1157.2 9.7 copy-start.16
  1157.2 18.6 %slice-start = ((s8[9437184]{0:T(1024)(128)(4,1)}), s8[4194304]{0:T(1024)(128)(4,1)S(1)}, s32[]{:S(2)}) async-start(s8[9437184]{0:T(1024)(128)(4,1)} %bitcast.169), calls=%async_computation.28 | async-start | bytes 8388608
  1157.3 18.6 %slice-start.1 = ((s8[9437184]{0:T(1024)(128)(4,1)}), s8[4194304]{0:T(1024)(128)(4,1)S(1)}, s32[]{:S(2)}) async-start(s8[9437184]{0:T(1024)(128)(4,1)} %bitcast.169), calls=%async_computation.29 | async-start | bytes 8388608
  1166.9 9.0 copy-start.11
  1166.9 9.0 slice-start.2
  1224.1 30.5 %all-to-all-start.15 = ((f32[16,16,384]{2,1,0:T(8,128)}), f32[16,16,384]{2,1,0:T(8,128)S(1)}, u32[]{:S(2)}, u32[]{:S(2)}) async-start(f32[16,16,384]{2,1,0:T(8,128)} %bitcast.44), calls=%async_computation.17 | async-start | bytes 786432 | tf_op jit(solution)/shard_map/all_to_all | solution.py:553
  (28 other events, 74.6 us)
Sparse Core Ops, SparseCore 0:
  69.0 59.7 all-gather.10
  131.9 113.1 all-gather.8
  247.5 77.1 all-gather.12
  405.9 76.0 all-gather.14
  484.9 75.2 all-gather.18
  585.4 173.4 reduce-scatter.2
  761.4 80.8 all-gather.16
  878.7 76.0 all-gather.20
  1155.9 66.1 reduce-scatter.4
  1224.3 27.7 all-gather.22

commit v12 on v11

--- a/solution.py
+++ b/solution.py
@@ -392,6 +392,8 @@
     inverse_two = lax.rsqrt(jnp.mean(hidden_state * hidden_state, axis=-1, keepdims=True) + epsilon)
     normed_two = hidden_state * inverse_two
     mlp_input = (normed_two * gain_two.astype(jnp.float32)).astype(jnp.bfloat16)
+    query_stack = lax.all_gather(query_weight, GROUP_AXES, axis=1, tiled=True)
+    mlp_input, query_stack = lax.optimization_barrier((mlp_input, query_stack))
     mlp_logits = jnp.dot(mlp_input, router_two, preferred_element_type=jnp.float32)
     mlp_gates = pair_gates(mlp_logits, own_mlp)
     mlp_index, mlp_pair_kept = pair_index(own_mlp, mlp_places, mlp_kept, slot_cap)
@@ -424,8 +426,6 @@
     inner_rows = (activated * up_pre).astype(jnp.bfloat16)
     mlp_partial = jnp.dot(inner_rows, down_weight, preferred_element_type=jnp.float32)
     mlp_slots = combine_scattered(mlp_partial)
-    query_stack = lax.all_gather(query_weight, GROUP_AXES, axis=1, tiled=True)
-    mlp_slots, query_stack = lax.optimization_barrier((mlp_slots, query_stack))
     mlp_picked = mlp_slots.reshape(EXPERTS * slot_cap, width)[mlp_index]
     own_output = hidden_state + jnp.sum(
         mlp_picked * (mlp_gates * mlp_pair_kept)[:, :, None], axis=1

time: 1270 us -> 1290 us (1.016)
  waiting for transfers between devices: 621 us -> 641 us
    all_to_all x1, waiting for transfers between devices: 0.01 us -> 13.7 us  [combine_scattered(): lax.all_to_all(summed.astype(jnp.float32).reshape(groups, slot_cap, width...]
  transfers between devices with their start and end apart: 21 -> 21, of which waited for: 19 -> 20; matrix products, arithmetic and copies ran while one was open for 17% -> 18% of each run, Pallas kernels for 1% -> 1%
where the time goes in v12:
time: 1290 us; the launch traced here: 1280 us
  waiting for transfers between devices  641 us (50%)
  blocking collectives  201 us (16%)
  matrix products  143 us (11%)
  local copies, waits for them, and re-layouts  127 us (10%)
  other arithmetic  74.7 us (6%)
  starting transfers between devices  54 us (4%)
  Pallas kernels  24.6 us (2%)
  between operations  16.1 us (1%)
    all_to_all x1, blocking collectives, combine(): lax.all_to_all(partial_value.astype(jnp.bfloat16).reshape(group_size, gro...  136 us
    all_gather x2, waiting for transfers between devices, dispatch(): lax.all_gather(by_group.reshape(groups * slot_cap, width), GROUP_AXES, ax...  120 us
    all_gather x1, waiting for transfers between devices, shards(): lax.all_gather(mlp_by_group[:, :slot_cap].reshape(groups * slot_cap, widt...  73.8 us
    all_gather x1, waiting for transfers between devices, shards(): lax.all_gather(mlp_by_group[:, slot_cap:].reshape(groups * slot_cap, widt...  68.9 us
    all_to_all x1, waiting for transfers between devices, shards(): lax.all_to_all(jnp.concatenate([seq_key_grad, seq_value_grad], axis=2).as...  51.7 us
    all_gather x1, waiting for transfers between devices, shards(): query_stack = lax.all_gather(query_weight, GROUP_AXES, axis=1, tiled=True)  46.3 us
    all_to_all x1, waiting for transfers between devices, shards(): lax.all_to_all(jnp.broadcast_to(seq_pair[None], (groups,) + seq_pair.shap...  37.4 us
    all_gather x1, waiting for transfers between devices, shards(): seq_input = lax.all_gather(attn_input, GROUP_AXES, axis=0, tiled=True)  35.8 us
  transfers between devices with their start and end apart: 21, of which 20 were waited for; matrix products, arithmetic and copies ran while one was open for 18% of the time, Pallas kernels for 1%

profile of v12, /device:TPU:1, one launch (start us, length us, event | category | flops | bytes accessed | tf_op | source)
XLA Modules:
  0.0 1281.1 jit_solution(4271811277957469946)
XLA Ops:
  17.3 17.5 %all_to_all.80 = bf16[16,16,384]{2,1,0:T(8,128)(2,1)S(1)} all-to-all(bf16[16,16,384]{2,1,0:T(8,128)(2,1)S(1)} %pad_maximum_fusion.10), channel_id=1, replica_groups=mesh['grp'=8,'sub'=8,'expert'=2] {'sub','expert'}, dimensions={0} | all-to-all | bytes 393216 | tf_op jit(solution)/shard_map/all_to_all | solution.py:301
  40.9 23.2 %all-to-all-done.1 = bf16[8,256,384]{1,2,0:T(8,128)(2,1)} async-done(((bf16[8,256,384]{1,2,0:T(8,128)(2,1)}), bf16[8,256,384]{1,2,0:T(8,128)(2,1)}, u32[]{:S(2)}, u32[]{:S(2)}) %all-to-all-start.1) | async-done | bytes 1572896 | tf_op jit(solution)/shard_map/all_to_all | solution.py:314
  75.8 13.9 %all_to_all.81 = bf16[8,18,2048]{2,1,0:T(8,128)(2,1)} all-to-all(bf16[8,18,2048]{2,1,0:T(8,128)(2,1)S(1)} %broadcast_select_fusion.1), channel_id=1, replica_groups=mesh['grp'=8,'sub'=8,'expert'=2] {'grp'}, dimensions={0} | all-to-all | bytes 1179648 | tf_op jit(solution)/shard_map/all_to_all | solution.py:222
  93.1 35.8 %all-gather.11.cloned.1.call-done = bf16[1024,2048]{1,0:T(8,128)(2,1)} async-done(((bf16[64,2048]{1,0:T(8,128)(2,1)}), bf16[1024,2048]{1,0:T(8,128)(2,1)}) %all-gather.11.cloned.1.call-update) | async-done | bytes 4194320 | tf_op jit(solution)/shard_map/all_gather | solution.py:334
  139.8 4.8 all-to-all-start.3
  155.1 5.6 multiply_reduce_fusion
  166.7 37.4 %all-to-all-done.3 = bf16[8,1024,256]{2,1,0:T(8,128)(2,1)} async-done(((bf16[8,1024,256]{2,1,0:T(8,128)(2,1)}), bf16[8,1024,256]{2,1,0:T(8,128)(2,1)}, u32[]{:S(2)}, u32[]{:S(2)}) %all-to-all-start.3) | async-done | bytes 4194336 | tf_op jit(solution)/shard_map/all_to_all | solution.py:346
  208.8 36.4 %all-gather.9.cloned.1.call-done = bf16[2304,2048]{1,0:T(8,128)(2,1)} async-done(((bf16[144,2048]{1,0:T(8,128)(2,1)}), bf16[2304,2048]{1,0:T(8,128)(2,1)}) %all-gather.9.cloned.1.call-update) | async-done | bytes 9437200 | tf_op jit(solution)/shard_map/all_gather | solution.py:223
  245.2 7.4 fusion.86
  256.7 5.4 fusion.14
  263.2 10.8 shard_map.238
  283.3 14.8 %all-to-all-done.4 = bf16[16,144,128]{2,1,0:T(8,128)(2,1)S(1)} async-done(((bf16[16,144,128]{2,1,0:T(8,128)(2,1)}), bf16[16,144,128]{2,1,0:T(8,128)(2,1)S(1)}, u32[]{:S(2)}, u32[]{:S(2)}) %all-to-all-start.4) | async-done | bytes 589856 | tf_op jit(solution)/shard_map/all_to_all | solution.py:251
  300.5 24.4 %all-gather.13.cloned.1.call-done = bf16[2048,2048]{1,0:T(8,128)(2,1)} async-done(((bf16[128,2048]{1,0:T(8,128)(2,1)}), bf16[2048,2048]{1,0:T(8,128)(2,1)}) %all-gather.13.cloned.1.call-update) | async-done | bytes 8388624 | tf_op jit(solution)/shard_map/all_gather | solution.py:382
  324.9 6.4 fusion.2
  346.3 13.4 %all-to-all-done.5 = f32[8,18,2048]{2,1,0:T(8,128)} async-done(((f32[8,18,2048]{2,1,0:T(8,128)}), f32[8,18,2048]{2,1,0:T(8,128)}, u32[]{:S(2)}, u32[]{:S(2)}) %all-to-all-start.5) | async-done | bytes 1179680 | tf_op jit(solution)/shard_map/all_to_all | solution.py:261
  371.9 46.3 %all-gather.15.cloned.1.call-done = bf16[2048,2048]{1,0:T(8,128)(2,1)} async-done(((bf16[2048,128]{1,0:T(8,128)(2,1)}), bf16[2048,2048]{1,0:T(8,128)(2,1)}) %all-gather.15.cloned.1.call-update) | async-done | bytes 8388624 | tf_op jit(solution)/shard_map/all_gather | solution.py:395
  429.7 21.0 %all_to_all.82 = bf16[8,36,2048]{2,1,0:T(8,128)(2,1)S(1)} all-to-all(bf16[8,36,2048]{2,1,0:T(8,128)(2,1)S(1)} %pad_maximum_fusion.2), channel_id=1, replica_groups=mesh['grp'=8,'sub'=8,'expert'=2] {'grp'}, dimensions={0} | all-to-all | bytes 2359296 | tf_op jit(solution)/shard_map/all_to_all | solution.py:404
  456.6 73.8 %all-gather.17.cloned.1.call-done = bf16[2304,2048]{1,0:T(8,128)(2,1)} async-done(((bf16[144,2048]{1,0:T(8,128)(2,1)}), bf16[2304,2048]{1,0:T(8,128)(2,1)}) %all-gather.17.cloned.1.call-update) | async-done | bytes 9437200 | tf_op jit(solution)/shard_map/all_gather | solution.py:411
  530.4 9.3 fusion.87
  539.7 68.9 %all-gather.19.cloned.1.call-done = bf16[2304,2048]{1,0:T(8,128)(2,1)} async-done(((bf16[144,2048]{1,0:T(8,128)(2,1)}), bf16[2304,2048]{1,0:T(8,128)(2,1)}) %all-gather.19.cloned.1.call-update) | async-done | bytes 9437200 | tf_op jit(solution)/shard_map/all_gather | solution.py:417
  608.6 7.1 fusion.88
  616.3 8.6 multiply_convert_fusion.2
  626.2 7.5 convolution_convert_fusion
  633.7 12.3 fusion.89
  646.0 11.0 add_convert_fusion
  657.1 136.1 %all_to_all.83 = bf16[16,144,2048]{2,1,0:T(8,128)(2,1)} all-to-all(bf16[16,144,2048]{2,1,0:T(8,128)(2,1)S(1)} %bitcast.129), channel_id=1, replica_groups=mesh['grp'=8,'sub'=8,'expert'=2] {'sub','expert'}, dimensions={0} | all-to-all | bytes 18874368 | tf_op jit(solution)/shard_map/all_to_all | solution.py:228
  793.2 5.9 convert_reduce_fusion
  809.3 18.3 %all-to-all-done.9 = f32[8,18,2048]{2,1,0:T(8,128)} async-done(((f32[8,18,2048]{2,1,0:T(8,128)}), f32[8,18,2048]{2,1,0:T(8,128)}, u32[]{:S(2)}, u32[]{:S(2)}) %all-to-all-start.9) | async-done | bytes 1179680 | tf_op jit(solution)/shard_map/all_to_all | solution.py:236
  840.2 13.7 %all-to-all-done.7 = f32[8,18,2048]{2,1,0:T(8,128)} async-done(((f32[8,18,2048]{2,1,0:T(8,128)}), f32[8,18,2048]{2,1,0:T(8,128)}, u32[]{:S(2)}, u32[]{:S(2)}) %all-to-all-start.7) | async-done | bytes 1179680 | tf_op jit(solution)/shard_map/all_to_all | solution.py:242
  874.6 12.6 all_to_all.84
  888.2 83.1 %all-gather.21.cloned.1.call-done = bf16[2304,2048]{1,0:T(8,128)(2,1)} async-done(((bf16[144,2048]{1,0:T(8,128)(2,1)}), bf16[2304,2048]{1,0:T(8,128)(2,1)}) %all-gather.21.cloned.1.call-update) | async-done | bytes 9437200 | tf_op jit(solution)/shard_map/all_gather | solution.py:223
  971.3 6.3 convolution_convert_fusion.2
  978.8 13.8 %shard_map.239 = (f32[8,288,128]{2,1,0:T(8,128)}, f32[8,1024,128]{2,1,0:T(8,128)}, f32[8,1024,128]{2,1,0:T(8,128)}) custom-call(bf16[8,288,128]{2,1,0:T(8,128)(2,1)} %pad_maximum_fusion.3.q_ref, bf16[8,1024,128]{2,1,0:T(8,128)(2,1)} %bitcast.142, bf16[8,1024,128]{2,1,0:T(8,128)(2,1)} %bitcast.140, s32[8,288,1]{2,1,0:T(8,128)} %add_select_fusion.qb_ref, ...), custom_call_target="tpu_custom_call" | custom-call | flops 3019898880 | bytes 25100288 | tf_op jit(solution)/shard_map/pallas_call | solution.py:76
  992.6 8.0 fusion.18
  1021.7 7.4 fusion
  1029.1 51.7 %all-to-all-done.13 = bf16[8,1024,256]{2,1,0:T(8,128)(2,1)} async-done(((bf16[8,1024,256]{2,1,0:T(8,128)(2,1)}), bf16[8,1024,256]{2,1,0:T(8,128)(2,1)}, u32[]{:S(2)}, u32[]{:S(2)}) %all-to-all-start.13) | async-done | bytes 4194336 | tf_op jit(solution)/shard_map/all_to_all | solution.py:496
  1095.8 12.5 all-to-all-done.12
  1108.3 6.0 all-to-all-start.14
  1124.5 4.9 fusion.53
  1129.3 34.9 %all-to-all-done.14 = bf16[16,64,2048]{2,1,0:T(8,128)(2,1)} async-done(((bf16[16,64,2048]{2,1,0:T(8,128)(2,1)}), bf16[16,64,2048]{2,1,0:T(8,128)(2,1)}, u32[]{:S(2)}, u32[]{:S(2)}) %all-to-all-start.14) | async-done | bytes 4194336 | tf_op jit(solution)/shard_map/all_to_all | solution.py:518
  1173.2 9.6 fusion.94
  1182.8 9.0 fusion.95
  1191.8 5.1 fusion.96
  1200.6 6.1 fusion.93
  1206.7 7.4 fusion.92
  1214.1 23.9 %reduce-scatter.5.cloned.1.call-done = f32[256,384]{0,1:T(8,128)} async-done(((f32[2048,384]{0,1:T(8,128)}), f32[256,384]{0,1:T(8,128)}) %reduce-scatter.5.cloned.1.call-update) | async-done | bytes 393232 | tf_op jit(solution)/shard_map/reduce_scatter | solution.py:552
  1240.0 8.1 all-to-all-start.15
  1248.1 20.0 %all-gather.23.cloned.1.call-done = bf16[128,4096]{1,0:T(8,128)(2,1)} async-done(((bf16[64,4096]{1,0:T(8,128)(2,1)}), bf16[128,4096]{1,0:T(8,128)(2,1)}) %all-gather.23.cloned.1.call-update) | async-done | bytes 1048592 | tf_op jit(solution)/shard_map/all_gather | solution.py:568
  (399 shorter events, 237.8 us)
Async XLA Ops:
  7.2 608.5 %copy-start = (bf16[2048,352]{0,1:T(8,128)(2,1)S(1)}, bf16[2048,352]{0,1:T(8,128)(2,1)}, u32[]{:S(2)}) copy-start(bf16[2048,352]{0,1:T(8,128)(2,1)} %param.30) | copy-start | bytes 4325380
  36.2 27.9 %all-to-all-start.1 = ((bf16[8,256,384]{1,2,0:T(8,128)(2,1)}), bf16[8,256,384]{1,2,0:T(8,128)(2,1)}, u32[]{:S(2)}, u32[]{:S(2)}) async-start(bf16[8,256,384]{1,2,0:T(8,128)(2,1)} %broadcast_in_dim.57), calls=%async_computation.1 | async-start | bytes 3145728 | tf_op jit(solution)/shard_map/all_to_all | solution.py:314
  40.6 88.3 %all-gather.11.cloned.1.call-start = ((), (), s32[]{:S(2)}) async-start(), calls=%async_computation.19 | async-start | bytes 4456448 | tf_op jit(solution)/shard_map/all_gather | solution.py:334
  40.9 25.6 %copy-start.52 = (f32[64]{0:T(128)}, f32[64]{0:T(128)S(1)}, u32[]{:S(2)}) copy-start(f32[64]{0:T(128)S(1)} %add_rsqrt_fusion.1) | copy-start | bytes 772
  65.9 80.2 %copy-start.3 = (bf16[8,256,384]{2,1,0:T(8,128)(2,1)}, bf16[8,256,384]{2,1,0:T(8,128)(2,1)S(1)}, u32[]{:S(2)}) copy-start(bf16[8,256,384]{2,1,0:T(8,128)(2,1)S(1)} %copy.482) | copy-start | bytes 4718596
  68.9 176.3 %all-gather.9.cloned.1.call-start = ((), (), s32[]{:S(2)}) async-start(), calls=%async_computation.18 | async-start | bytes 10027008 | tf_op jit(solution)/shard_map/all_gather | solution.py:223
  91.8 233.1 %all-gather.13.cloned.1.call-start = ((), (), s32[]{:S(2)}) async-start(), calls=%async_computation.20 | async-start | bytes 8912896 | tf_op jit(solution)/shard_map/all_gather | solution.py:382
  92.5 325.6 %all-gather.15.cloned.1.call-start = ((), (), s32[]{:S(2)}) async-start(), calls=%async_computation.21 | async-start | bytes 8912896 | tf_op jit(solution)/shard_map/all_gather | solution.py:395
  93.1 163.5 %copy-start.50 = (f32[64]{0:T(128)}, f32[64]{0:T(128)S(1)}, u32[]{:S(2)}) copy-start(f32[64]{0:T(128)S(1)} %multiply_exponential_fusion) | copy-start | bytes 772
  93.1 39.4 %copy-start.43 = (f32[1024]{0:T(1024)}, f32[1024]{0:T(1024)S(1)}, u32[]{:S(2)}) copy-start(f32[1024]{0:T(1024)S(1)} %iota_convert_fusion) | copy-start | bytes 12292
  139.8 64.2 %all-to-all-start.3 = ((bf16[8,1024,256]{2,1,0:T(8,128)(2,1)}), bf16[8,1024,256]{2,1,0:T(8,128)(2,1)}, u32[]{:S(2)}, u32[]{:S(2)}) async-start(bf16[8,1024,256]{2,1,0:T(8,128)(2,1)} %broadcast_in_dim.66), calls=%async_computation.3 | async-start | bytes 8388608 | tf_op jit(solution)/shard_map/all_to_all | solution.py:346
  155.1 8.2 copy-start.10
  163.3 93.4 %copy-start.36 = (f32[2304]{0:T(1024)}, f32[2304]{0:T(1024)S(1)}, u32[]{:S(2)}) copy-start(f32[2304]{0:T(1024)S(1)} %fusion.66) | copy-start | bytes 27652
  204.1 41.1 %copy-start.27 = (bf16[2048,128]{1,0:T(8,128)(2,1)S(1)}, bf16[2048,128]{1,0:T(8,128)(2,1)}, u32[]{:S(2)}) copy-start(bf16[2048,128]{1,0:T(8,128)(2,1)} %param.25) | copy-start | bytes 1572868
  277.3 20.9 %all-to-all-start.4 = ((bf16[16,144,128]{2,1,0:T(8,128)(2,1)}), bf16[16,144,128]{2,1,0:T(8,128)(2,1)S(1)}, u32[]{:S(2)}, u32[]{:S(2)}) async-start(bf16[16,144,128]{2,1,0:T(8,128)(2,1)} %copy.493), calls=%async_computation.4 | async-start | bytes 1179648 | tf_op jit(solution)/shard_map/all_to_all | solution.py:251
  331.2 28.4 %all-to-all-start.5 = ((f32[8,18,2048]{2,1,0:T(8,128)}), f32[8,18,2048]{2,1,0:T(8,128)}, u32[]{:S(2)}, u32[]{:S(2)}) async-start(f32[8,18,2048]{2,1,0:T(8,128)} %fusion.2), calls=%async_computation.5 | async-start | bytes 3145728 | tf_op jit(solution)/shard_map/all_to_all | solution.py:261
  335.5 194.8 %all-gather.17.cloned.1.call-start = ((), (), s32[]{:S(2)}) async-start(), calls=%async_computation.22 | async-start | bytes 10027008 | tf_op jit(solution)/shard_map/all_gather | solution.py:411
  346.2 522.7 %copy-start.48 = (f32[64,2]{0,1:T(2,128)}, f32[64,2]{0,1:T(2,128)S(1)}, u32[]{:S(2)}) copy-start(f32[64,2]{0,1:T(2,128)S(1)} %get-tuple-element.152) | copy-start | bytes 1540
  454.2 154.4 %all-gather.19.cloned.1.call-start = ((), (), s32[]{:S(2)}) async-start(), calls=%async_computation.24 | async-start | bytes 10027008 | tf_op jit(solution)/shard_map/all_gather | solution.py:417
  456.4 350.5 %reduce-scatter.3.cloned.1.call-start = ((), (), s32[]{:S(2)}) async-start(), calls=%async_computation.23 | async-start | bytes 10027008 | tf_op jit(solution)/shard_map/reduce_scatter | solution.py:239
  608.6 7.1 copy-start.57
  608.6 7.8 copy-start.59
  616.3 9.8 copy-start.58
  633.7 12.4 copy-start.12
  800.4 27.2 %all-to-all-start.9 = ((f32[8,18,2048]{2,1,0:T(8,128)}), f32[8,18,2048]{2,1,0:T(8,128)}, u32[]{:S(2)}, u32[]{:S(2)}) async-start(f32[8,18,2048]{2,1,0:T(8,128)} %reshape.671), calls=%async_computation.10 | async-start | bytes 3145728 | tf_op jit(solution)/shard_map/all_to_all | solution.py:236
  809.2 22.7 %copy-start.42 = (s32[8,18,1]{0,1,2:T(8,128)S(1)}, s32[8,18,1]{0,1,2:T(8,128)}, u32[]{:S(2)}) copy-start(s32[8,18,1]{0,1,2:T(8,128)} %get-tuple-element.174) | copy-start | bytes 1732
  809.2 22.9 %copy-start.55 = (s32[64,2]{0,1:T(2,128)S(1)}, s32[64,2]{0,1:T(2,128)}, u32[]{:S(2)}) copy-start(s32[64,2]{0,1:T(2,128)} %get-tuple-element.184) | copy-start | bytes 1540
  827.6 26.3 %all-to-all-start.7 = ((f32[8,18,2048]{2,1,0:T(8,128)}), f32[8,18,2048]{2,1,0:T(8,128)}, u32[]{:S(2)}, u32[]{:S(2)}) async-start(f32[8,18,2048]{2,1,0:T(8,128)} %reshape.724), calls=%async_computation.8 | async-start | bytes 3145728 | tf_op jit(solution)/shard_map/all_to_all | solution.py:242
  831.9 139.4 %all-gather.21.cloned.1.call-start = ((), (), s32[]{:S(2)}) async-start(), calls=%async_computation.25 | async-start | bytes 10027008 | tf_op jit(solution)/shard_map/all_gather | solution.py:223
  874.6 96.7 %copy-start.28 = (bf16[128,2048]{1,0:T(8,128)(2,1)S(1)}, bf16[128,2048]{1,0:T(8,128)(2,1)}, u32[]{:S(2)}) copy-start(bf16[128,2048]{1,0:T(8,128)(2,1)} %param.26) | copy-start | bytes 1572868
  978.8 13.8 %copy-start.37 = (f32[2304]{0:T(1024)S(1)}, f32[2304]{0:T(1024)}, u32[]{:S(2)}) copy-start(f32[2304]{0:T(1024)} %copy-done.36) | copy-start | bytes 27652
  978.8 13.8 %copy-start.51 = (f32[64]{0:T(128)S(1)}, f32[64]{0:T(128)}, u32[]{:S(2)}) copy-start(f32[64]{0:T(128)} %copy-done.50) | copy-start | bytes 772
  1002.1 14.5 %all-to-all-start.11 = ((bf16[16,144,128]{2,1,0:T(8,128)(2,1)}), bf16[16,144,128]{2,1,0:T(8,128)(2,1)S(1)}, u32[]{:S(2)}, u32[]{:S(2)}) async-start(bf16[16,144,128]{2,1,0:T(8,128)(2,1)} %copy.527), calls=%async_computation.12 | async-start | bytes 1179648 | tf_op jit(solution)/shard_map/all_to_all | solution.py:251
  1016.6 64.1 %all-to-all-start.13 = ((bf16[8,1024,256]{2,1,0:T(8,128)(2,1)}), bf16[8,1024,256]{2,1,0:T(8,128)(2,1)}, u32[]{:S(2)}, u32[]{:S(2)}) async-start(bf16[8,1024,256]{2,1,0:T(8,128)(2,1)} %pad_maximum_fusion), calls=%async_computation.14 | async-start | bytes 8388608 | tf_op jit(solution)/shard_map/all_to_all | solution.py:496
  1080.7 27.6 %all-to-all-start.12 = ((f32[8,18,2048]{2,1,0:T(8,128)}), f32[8,18,2048]{2,1,0:T(8,128)}, u32[]{:S(2)}, u32[]{:S(2)}) async-start(f32[8,18,2048]{2,1,0:T(8,128)} %fusion), calls=%async_computation.13 | async-start | bytes 3145728 | tf_op jit(solution)/shard_map/all_to_all | solution.py:261
  1108.3 55.9 %all-to-all-start.14 = ((bf16[16,64,2048]{2,1,0:T(8,128)(2,1)}), bf16[16,64,2048]{2,1,0:T(8,128)(2,1)}, u32[]{:S(2)}, u32[]{:S(2)}) async-start(bf16[16,64,2048]{2,1,0:T(8,128)(2,1)} %bitcast.130), calls=%async_computation.15 | async-start | bytes 8388608 | tf_op jit(solution)/shard_map/all_to_all | solution.py:518
  1114.3 123.7 %reduce-scatter.5.cloned.1.call-start = ((), (), s32[]{:S(2)}) async-start(), calls=%async_computation.27 | async-start | bytes 3538944 | tf_op jit(solution)/shard_map/reduce_scatter | solution.py:552
  1129.3 37.9 %copy-start.16 = (bf16[128,2048]{1,0:T(8,128)(2,1)S(1)}, bf16[128,2048]{1,0:T(8,128)(2,1)}, u32[]{:S(2)}) copy-start(bf16[128,2048]{1,0:T(8,128)(2,1)} %param.21) | copy-start | bytes 1572868
  1129.3 37.9 %copy-start.22 = (f32[64,2048]{1,0:T(8,128)S(1)}, f32[64,2048]{1,0:T(8,128)}, u32[]{:S(2)}) copy-start(f32[64,2048]{1,0:T(8,128)} %multiply_reduce_fusion.3) | copy-start | bytes 1572868
  1129.3 37.9 %copy-start.33 = (f32[2048]{0:T(1024)S(1)}, f32[2048]{0:T(1024)}, u32[]{:S(2)}) copy-start(f32[2048]{0:T(1024)} %copy-done.32) | copy-start | bytes 24580
  1129.3 37.9 %copy-start.53 = (f32[64]{0:T(128)S(1)}, f32[64]{0:T(128)}, u32[]{:S(2)}) copy-start(f32[64]{0:T(128)} %copy-done.52) | copy-start | bytes 772
  1171.7 96.3 %all-gather.23.cloned.1.call-start = ((), (), s32[]{:S(2)}) async-start(), calls=%async_computation.26 | async-start | bytes 1572864 | tf_op jit(solution)/shard_map/all_gather | solution.py:568
  1173.1 9.7 copy-start.19
  1173.1 18.6 %slice-start = ((s8[9437184]{0:T(1024)(128)(4,1)}), s8[4194304]{0:T(1024)(128)(4,1)S(1)}, s32[]{:S(2)}) async-start(s8[9437184]{0:T(1024)(128)(4,1)} %bitcast.169), calls=%async_computation.28 | async-start | bytes 8388608
  1173.1 18.6 %slice-start.1 = ((s8[9437184]{0:T(1024)(128)(4,1)}), s8[4194304]{0:T(1024)(128)(4,1)S(1)}, s32[]{:S(2)}) async-start(s8[9437184]{0:T(1024)(128)(4,1)} %bitcast.169), calls=%async_computation.29 | async-start | bytes 8388608
  1182.8 9.0 copy-start.13
  1182.8 9.0 slice-start.2
  1240.0 30.5 %all-to-all-start.15 = ((f32[16,16,384]{2,1,0:T(8,128)}), f32[16,16,384]{2,1,0:T(8,128)S(1)}, u32[]{:S(2)}, u32[]{:S(2)}) async-start(f32[16,16,384]{2,1,0:T(8,128)} %bitcast.44), calls=%async_computation.17 | async-start | bytes 786432 | tf_op jit(solution)/shard_map/all_to_all | solution.py:553
  (37 other events, 101.1 us)
Sparse Core Ops, SparseCore 0:
  69.0 59.8 all-gather.10
  132.0 113.1 all-gather.8
  247.7 77.1 all-gather.12
  327.0 91.1 all-gather.14
  454.3 76.0 all-gather.16
  533.3 75.2 all-gather.18
  633.8 173.0 reduce-scatter.2
  888.3 82.9 all-gather.20
  1171.8 66.1 reduce-scatter.4
  1240.2 27.7 all-gather.22

commit v13 on v11

--- a/solution.py
+++ b/solution.py
@@ -331,7 +331,13 @@
     normed_one = own_input * inverse_one
     attn_input = (normed_one * gain_one.astype(jnp.float32)).astype(jnp.bfloat16)
     attn_logits = jnp.dot(attn_input, router_one, preferred_element_type=jnp.float32)
-    seq_input = lax.all_gather(attn_input, GROUP_AXES, axis=0, tiled=True)
+    seq_input = lax.all_to_all(
+        jnp.broadcast_to(attn_input[None], (group_size,) + attn_input.shape),
+        GROUP_AXES,
+        split_axis=0,
+        concat_axis=0,
+        tiled=True,
+    ).reshape(group_size * own_rows, width)
     seq_kv = jnp.dot(seq_input, head_kv, preferred_element_type=jnp.float32)
     seq_cos, seq_sin = rope_tables(jnp.arange(seq_length, dtype=jnp.int32), HEAD)
     seq_pair = jnp.concatenate(
@@ -430,6 +436,7 @@
     own_output = hidden_state + jnp.sum(
         mlp_picked * (mlp_gates * mlp_pair_kept)[:, :, None], axis=1
     )
+    mixed_full = lax.all_gather(own_output.astype(jnp.bfloat16), "expert", axis=0, tiled=True)
     mlp_gate_grad = jnp.sum(mlp_picked * own_cotangent[:, None, :], axis=-1) * mlp_pair_kept
     mlp_logit_grad = gates_back(mlp_gates, mlp_gate_grad, own_mlp)
     inner_grad = jnp.einsum("rd,fd->rf", down_rows, down_weight, preferred_element_type=jnp.float32)
@@ -565,15 +572,7 @@
     gain_two_grad = extra_grad[:, 1]
     attn_router_grad = extra_grad[:, 2 : 2 + EXPERTS]
     mlp_router_grad = extra_grad[:, 2 + EXPERTS : 2 + 2 * EXPERTS]
-    both_full = lax.all_gather(
-        jnp.concatenate(
-            [own_output.astype(jnp.bfloat16), input_grad.astype(jnp.bfloat16)], axis=1
-        ),
-        "expert",
-        axis=0,
-        tiled=True,
-    )
-    mixed_full, input_full = both_full[:, :width], both_full[:, width:]
+    input_full = lax.all_gather(input_grad.astype(jnp.bfloat16), "expert", axis=0, tiled=True)
     return (
         mixed_full,
         input_full,

time: 1270 us -> 1280 us (level)
  waiting for transfers between devices: 621 us -> 581 us
  blocking collectives: 201 us -> 237 us
    all_to_all x0 -> x1, waiting for transfers between devices: none -> 57.4 us  [shards(): lax.all_to_all(jnp.broadcast_to(attn_input[None], (group_size,) + attn_in...]
    all_gather x2 -> x0, waiting for transfers between devices: 56.2 us -> none  [the longest x1 36.3 us: shards(): seq_input = lax.all_gather(attn_input, GROUP_AXES, axis=0, tiled=True)]
    all_gather x0 -> x2, blocking collectives: none -> 34.8 us  [the longest x1 21.3 us: shards(): lax.all_gather(own_output.astype(jnp.bfloat16), 'expert', axis=0, tiled=T...]
    all_gather x2, waiting for transfers between devices: 113 us -> 88.9 us  [dispatch(): lax.all_gather(by_group.reshape(groups * slot_cap, width), GROUP_AXES, ax...]
    reduce_scatter x1, waiting for transfers between devices: 24.6 us -> 11.3 us  [shards(): lax.psum_scatter(packed_grad, 'grp', scatter_dimension=0, tiled=True)]
  transfers between devices with their start and end apart: 21 -> 20, of which waited for: 19 -> 17; matrix products, arithmetic and copies ran while one was open for 17% -> 17% of each run, Pallas kernels for 1% -> 1%
where the time goes in v13:
time: 1280 us; the launch traced here: 1270 us
  waiting for transfers between devices  581 us (45%)
  blocking collectives  237 us (19%)
  matrix products  145 us (11%)
  local copies, waits for them, and re-layouts  126 us (10%)
  other arithmetic  74.8 us (6%)
  starting transfers between devices  62.4 us (5%)
  Pallas kernels  24.6 us (2%)
  between operations  16 us (1%)
    all_to_all x1, blocking collectives, combine(): lax.all_to_all(partial_value.astype(jnp.bfloat16).reshape(group_size, gro...  138 us
    all_gather x2, waiting for transfers between devices, dispatch(): lax.all_gather(by_group.reshape(groups * slot_cap, width), GROUP_AXES, ax...  88.9 us
    all_gather x1, waiting for transfers between devices, shards(): lax.all_gather(mlp_by_group[:, :slot_cap].reshape(groups * slot_cap, widt...  73.8 us
    all_gather x1, waiting for transfers between devices, shards(): lax.all_gather(mlp_by_group[:, slot_cap:].reshape(groups * slot_cap, widt...  63.6 us
    all_to_all x1, waiting for transfers between devices, shards(): lax.all_to_all(jnp.broadcast_to(attn_input[None], (group_size,) + attn_in...  57.4 us
    all_to_all x1, waiting for transfers between devices, shards(): lax.all_to_all(jnp.concatenate([seq_key_grad, seq_value_grad], axis=2).as...  51.7 us
    all_gather x1, waiting for transfers between devices, shards(): query_stack = lax.all_gather(query_weight, GROUP_AXES, axis=1, tiled=True)  48.4 us
    all_to_all x1, waiting for transfers between devices, shards(): lax.all_to_all(jnp.broadcast_to(seq_pair[None], (groups,) + seq_pair.shap...  37.8 us
  transfers between devices with their start and end apart: 20, of which 17 were waited for; matrix products, arithmetic and copies ran while one was open for 17% of the time, Pallas kernels for 1%

profile of v13, /device:TPU:1, one launch (start us, length us, event | category | flops | bytes accessed | tf_op | source)
XLA Modules:
  0.0 1267.2 jit_solution(10640642797139231545)
XLA Ops:
  17.3 17.5 %all_to_all.85 = bf16[16,16,384]{2,1,0:T(8,128)(2,1)S(1)} all-to-all(bf16[16,16,384]{2,1,0:T(8,128)(2,1)S(1)} %pad_maximum_fusion.9), channel_id=1, replica_groups=mesh['grp'=8,'sub'=8,'expert'=2] {'sub','expert'}, dimensions={0} | all-to-all | bytes 393216 | tf_op jit(solution)/shard_map/all_to_all | solution.py:301
  42.5 21.6 %all-to-all-done.1 = bf16[8,256,384]{1,2,0:T(8,128)(2,1)} async-done(((bf16[8,256,384]{1,2,0:T(8,128)(2,1)}), bf16[8,256,384]{1,2,0:T(8,128)(2,1)}, u32[]{:S(2)}, u32[]{:S(2)}) %all-to-all-start.1) | async-done | bytes 1572896 | tf_op jit(solution)/shard_map/all_to_all | solution.py:314
  73.4 13.9 %all_to_all.86 = bf16[8,18,2048]{2,1,0:T(8,128)(2,1)} all-to-all(bf16[8,18,2048]{2,1,0:T(8,128)(2,1)S(1)} %broadcast_select_fusion.1), channel_id=1, replica_groups=mesh['grp'=8,'sub'=8,'expert'=2] {'grp'}, dimensions={0} | all-to-all | bytes 1179648 | tf_op jit(solution)/shard_map/all_to_all | solution.py:222
  92.7 7.0 all-to-all-start.3
  99.7 57.4 %all-to-all-done.3 = bf16[16,64,2048]{2,1,0:T(8,128)(2,1)} async-done(((bf16[16,64,2048]{2,1,0:T(8,128)(2,1)}), bf16[16,64,2048]{2,1,0:T(8,128)(2,1)}, u32[]{:S(2)}, u32[]{:S(2)}) %all-to-all-start.3) | async-done | bytes 4194336 | tf_op jit(solution)/shard_map/all_to_all | solution.py:334
  183.4 5.6 multiply_reduce_fusion
  195.0 37.8 %all-to-all-done.4 = bf16[8,1024,256]{2,1,0:T(8,128)(2,1)} async-done(((bf16[8,1024,256]{2,1,0:T(8,128)(2,1)}), bf16[8,1024,256]{2,1,0:T(8,128)(2,1)}, u32[]{:S(2)}, u32[]{:S(2)}) %all-to-all-start.4) | async-done | bytes 4194336 | tf_op jit(solution)/shard_map/all_to_all | solution.py:352
  237.4 12.3 all-gather.7.cloned.1.call-done
  249.7 7.4 fusion.85
  261.1 5.4 fusion.14
  267.6 10.8 shard_map.238
  287.7 14.8 %all-to-all-done.5 = bf16[16,144,128]{2,1,0:T(8,128)(2,1)S(1)} async-done(((bf16[16,144,128]{2,1,0:T(8,128)(2,1)}), bf16[16,144,128]{2,1,0:T(8,128)(2,1)S(1)}, u32[]{:S(2)}, u32[]{:S(2)}) %all-to-all-start.5) | async-done | bytes 589856 | tf_op jit(solution)/shard_map/all_to_all | solution.py:251
  304.8 24.5 %all-gather.9.cloned.1.call-done = bf16[2048,2048]{1,0:T(8,128)(2,1)} async-done(((bf16[128,2048]{1,0:T(8,128)(2,1)}), bf16[2048,2048]{1,0:T(8,128)(2,1)}) %all-gather.9.cloned.1.call-update) | async-done | bytes 8388624 | tf_op jit(solution)/shard_map/all_gather | solution.py:388
  329.3 6.4 fusion.2
  350.6 13.3 %all-to-all-done.6 = f32[8,18,2048]{2,1,0:T(8,128)} async-done(((f32[8,18,2048]{2,1,0:T(8,128)}), f32[8,18,2048]{2,1,0:T(8,128)}, u32[]{:S(2)}, u32[]{:S(2)}) %all-to-all-start.6) | async-done | bytes 1179680 | tf_op jit(solution)/shard_map/all_to_all | solution.py:261
  387.7 19.2 %all_to_all.87 = bf16[8,36,2048]{2,1,0:T(8,128)(2,1)S(1)} all-to-all(bf16[8,36,2048]{2,1,0:T(8,128)(2,1)S(1)} %pad_maximum_fusion.2), channel_id=1, replica_groups=mesh['grp'=8,'sub'=8,'expert'=2] {'grp'}, dimensions={0} | all-to-all | bytes 2359296 | tf_op jit(solution)/shard_map/all_to_all | solution.py:408
  412.8 73.8 %all-gather.11.cloned.1.call-done = bf16[2304,2048]{1,0:T(8,128)(2,1)} async-done(((bf16[144,2048]{1,0:T(8,128)(2,1)}), bf16[2304,2048]{1,0:T(8,128)(2,1)}) %all-gather.11.cloned.1.call-update) | async-done | bytes 9437200 | tf_op jit(solution)/shard_map/all_gather | solution.py:415
  486.6 9.4 fusion.87
  496.0 5.2 fusion.86
  501.2 63.6 %all-gather.15.cloned.1.call-done = bf16[2304,2048]{1,0:T(8,128)(2,1)} async-done(((bf16[144,2048]{1,0:T(8,128)(2,1)}), bf16[2304,2048]{1,0:T(8,128)(2,1)}) %all-gather.15.cloned.1.call-update) | async-done | bytes 9437200 | tf_op jit(solution)/shard_map/all_gather | solution.py:421
  564.8 13.1 %multiply_convert_fusion = (bf16[2304,352]{0,1:T(8,128)(2,1)}, bf16[2304,352]{0,1:T(8,128)(2,1)}, bf16[2304,352]{0,1:T(8,128)(2,1)S(1)}) fusion(f32[2304,352]{0,1:T(8,128)} %fusion.86, f32[2304,352]{0,1:T(8,128)} %fusion.87, bf16[2304,2048]{1,0:T(8,128)(2,1)} %all-gather.15.cloned.1.call-done, bf16[352,2048]{1,0:T(8,128)(2,1)S(1)} %copy-done), kind=kOutput, calls=%fused_computation.31 | convolution fusion | flops 3334053888 | bytes 22233088 | tf_op jit(solution)/shard_map/rd,fd->rf/dot_general | solution.py:442
  579.1 7.4 convolution_convert_fusion
  587.9 12.0 fusion.88
  600.0 11.6 add_convert_fusion
  611.6 137.5 %all_to_all.88 = bf16[16,144,2048]{2,1,0:T(8,128)(2,1)} all-to-all(bf16[16,144,2048]{2,1,0:T(8,128)(2,1)S(1)} %bitcast.130), channel_id=1, replica_groups=mesh['grp'=8,'sub'=8,'expert'=2] {'sub','expert'}, dimensions={0} | all-to-all | bytes 18874368 | tf_op jit(solution)/shard_map/all_to_all | solution.py:228
  749.1 5.9 convert_reduce_fusion
  756.3 5.2 all-to-all-start.10
  763.9 21.0 %all-to-all-done.10 = f32[8,18,2048]{2,1,0:T(8,128)} async-done(((f32[8,18,2048]{2,1,0:T(8,128)}), f32[8,18,2048]{2,1,0:T(8,128)}, u32[]{:S(2)}, u32[]{:S(2)}) %all-to-all-start.10) | async-done | bytes 1179680 | tf_op jit(solution)/shard_map/all_to_all | solution.py:236
  798.0 48.4 %all-gather.13.cloned.1.call-done = bf16[2048,2048]{1,0:T(8,128)(2,1)} async-done(((bf16[2048,128]{1,0:T(8,128)(2,1)}), bf16[2048,2048]{1,0:T(8,128)(2,1)}) %all-gather.13.cloned.1.call-update) | async-done | bytes 8388624 | tf_op jit(solution)/shard_map/all_gather | solution.py:433
  866.8 14.5 %all_to_all.89 = bf16[8,18,2048]{2,1,0:T(8,128)(2,1)S(1)} all-to-all(bf16[8,18,2048]{2,1,0:T(8,128)(2,1)S(1)} %multiply_convert_fusion.3), channel_id=1, replica_groups=mesh['grp'=8,'sub'=8,'expert'=2] {'grp'}, dimensions={0} | all-to-all | bytes 1179648 | tf_op jit(solution)/shard_map/all_to_all | solution.py:222
  882.3 76.6 %all-gather.17.cloned.1.call-done = bf16[2304,2048]{1,0:T(8,128)(2,1)} async-done(((bf16[144,2048]{1,0:T(8,128)(2,1)}), bf16[2304,2048]{1,0:T(8,128)(2,1)}) %all-gather.17.cloned.1.call-update) | async-done | bytes 9437200 | tf_op jit(solution)/shard_map/all_gather | solution.py:223
  958.9 6.3 convolution_convert_fusion.2
  966.4 13.8 %shard_map.239 = (f32[8,288,128]{2,1,0:T(8,128)}, f32[8,1024,128]{2,1,0:T(8,128)}, f32[8,1024,128]{2,1,0:T(8,128)}) custom-call(bf16[8,288,128]{2,1,0:T(8,128)(2,1)} %pad_maximum_fusion.3.q_ref, bf16[8,1024,128]{2,1,0:T(8,128)(2,1)} %bitcast.143, bf16[8,1024,128]{2,1,0:T(8,128)(2,1)} %bitcast.141, s32[8,288,1]{2,1,0:T(8,128)} %add_select_fusion.qb_ref, ...), custom_call_target="tpu_custom_call" | custom-call | flops 3019898880 | bytes 25100288 | tf_op jit(solution)/shard_map/pallas_call | solution.py:76
  980.2 7.9 fusion.18
  1009.3 7.4 fusion
  1016.7 51.7 %all-to-all-done.14 = bf16[8,1024,256]{2,1,0:T(8,128)(2,1)} async-done(((bf16[8,1024,256]{2,1,0:T(8,128)(2,1)}), bf16[8,1024,256]{2,1,0:T(8,128)(2,1)}, u32[]{:S(2)}, u32[]{:S(2)}) %all-to-all-start.14) | async-done | bytes 4194336 | tf_op jit(solution)/shard_map/all_to_all | solution.py:503
  1083.2 12.5 all-to-all-done.13
  1095.7 6.0 all-to-all-start.15
  1117.0 34.7 %all-to-all-done.15 = bf16[16,64,2048]{2,1,0:T(8,128)(2,1)} async-done(((bf16[16,64,2048]{2,1,0:T(8,128)(2,1)}), bf16[16,64,2048]{2,1,0:T(8,128)(2,1)}, u32[]{:S(2)}, u32[]{:S(2)}) %all-to-all-start.15) | async-done | bytes 4194336 | tf_op jit(solution)/shard_map/all_to_all | solution.py:525
  1160.6 9.6 fusion.93
  1170.2 9.0 fusion.95
  1179.2 5.4 fusion.94
  1184.6 21.3 %all_gather.28 = bf16[128,2048]{1,0:T(8,128)(2,1)} all-gather(bf16[64,2048]{1,0:T(8,128)(2,1)S(1)} %copy-done.29), channel_id=1, replica_groups=mesh['grp'=8,'sub'=8,'expert'=2] {'expert'}, dimensions={0}, use_global_device_ids=true | all-gather | bytes 786432 | tf_op jit(solution)/shard_map/all_gather | solution.py:439
  1206.2 6.1 fusion.92
  1212.4 7.4 fusion.91
  1219.8 11.3 reduce-scatter.5.cloned.1.call-done
  1233.0 8.3 all-to-all-start.16
  1241.5 13.5 %all_gather.31 = bf16[128,2048]{1,0:T(8,128)(2,1)S(1)} all-gather(bf16[64,2048]{1,0:T(8,128)(2,1)S(1)} %fusion.36), channel_id=1, replica_groups=mesh['grp'=8,'sub'=8,'expert'=2] {'expert'}, dimensions={0}, use_global_device_ids=true | all-gather | bytes 786432 | tf_op jit(solution)/shard_map/all_gather | solution.py:575
  (398 shorter events, 239.0 us)
Async XLA Ops:
  7.2 557.6 %copy-start = (bf16[352,2048]{1,0:T(8,128)(2,1)S(1)}, bf16[352,2048]{1,0:T(8,128)(2,1)}, u32[]{:S(2)}) copy-start(bf16[352,2048]{1,0:T(8,128)(2,1)} %param.31) | copy-start | bytes 4325380
  36.2 27.9 %all-to-all-start.1 = ((bf16[8,256,384]{1,2,0:T(8,128)(2,1)}), bf16[8,256,384]{1,2,0:T(8,128)(2,1)}, u32[]{:S(2)}, u32[]{:S(2)}) async-start(bf16[8,256,384]{1,2,0:T(8,128)(2,1)} %broadcast_in_dim.59), calls=%async_computation.1 | async-start | bytes 3145728 | tf_op jit(solution)/shard_map/all_to_all | solution.py:314
  40.7 209.0 %all-gather.7.cloned.1.call-start = ((), (), s32[]{:S(2)}) async-start(), calls=%async_computation.19 | async-start | bytes 10027008 | tf_op jit(solution)/shard_map/all_gather | solution.py:223
  41.4 24.6 %copy-start.40 = (s32[8,18]{0,1:T(8,128)}, s32[8,18]{0,1:T(8,128)S(1)}, u32[]{:S(2)}) copy-start(s32[8,18]{0,1:T(8,128)S(1)} %get-tuple-element.136) | copy-start | bytes 1732
  41.4 24.6 %copy-start.42 = (s32[8,18]{0,1:T(8,128)}, s32[8,18]{0,1:T(8,128)S(1)}, u32[]{:S(2)}) copy-start(s32[8,18]{0,1:T(8,128)S(1)} %get-tuple-element.137) | copy-start | bytes 1732
  42.4 25.8 %copy-start.47 = (s32[1024]{0:T(1024)}, s32[1024]{0:T(1024)S(1)}, u32[]{:S(2)}) copy-start(s32[1024]{0:T(1024)S(1)} %pad_clamp_fusion.3) | copy-start | bytes 12292
  42.5 24.1 %copy-start.54 = (f32[64]{0:T(128)}, f32[64]{0:T(128)S(1)}, u32[]{:S(2)}) copy-start(f32[64]{0:T(128)S(1)} %add_rsqrt_fusion.1) | copy-start | bytes 772
  66.0 108.5 %copy-start.2 = (bf16[8,256,384]{2,1,0:T(8,128)(2,1)}, bf16[8,256,384]{2,1,0:T(8,128)(2,1)S(1)}, u32[]{:S(2)}) copy-start(bf16[8,256,384]{2,1,0:T(8,128)(2,1)S(1)} %copy.482) | copy-start | bytes 4718596
  89.4 239.9 %all-gather.9.cloned.1.call-start = ((), (), s32[]{:S(2)}) async-start(), calls=%async_computation.20 | async-start | bytes 8912896 | tf_op jit(solution)/shard_map/all_gather | solution.py:388
  92.7 64.5 %all-to-all-start.3 = ((bf16[16,64,2048]{2,1,0:T(8,128)(2,1)}), bf16[16,64,2048]{2,1,0:T(8,128)(2,1)}, u32[]{:S(2)}, u32[]{:S(2)}) async-start(bf16[16,64,2048]{2,1,0:T(8,128)(2,1)} %broadcast_in_dim.68), calls=%async_computation.3 | async-start | bytes 8388608 | tf_op jit(solution)/shard_map/all_to_all | solution.py:334
  99.7 161.4 %copy-start.52 = (f32[64]{0:T(128)}, f32[64]{0:T(128)S(1)}, u32[]{:S(2)}) copy-start(f32[64]{0:T(128)S(1)} %multiply_exponential_fusion) | copy-start | bytes 772
  99.7 61.0 %copy-start.45 = (f32[1024]{0:T(1024)}, f32[1024]{0:T(1024)S(1)}, u32[]{:S(2)}) copy-start(f32[1024]{0:T(1024)S(1)} %iota_convert_fusion) | copy-start | bytes 12292
  168.2 64.6 %all-to-all-start.4 = ((bf16[8,1024,256]{2,1,0:T(8,128)(2,1)}), bf16[8,1024,256]{2,1,0:T(8,128)(2,1)}, u32[]{:S(2)}, u32[]{:S(2)}) async-start(bf16[8,1024,256]{2,1,0:T(8,128)(2,1)} %broadcast_in_dim.69), calls=%async_computation.4 | async-start | bytes 8388608 | tf_op jit(solution)/shard_map/all_to_all | solution.py:352
  191.6 69.5 %copy-start.38 = (f32[2304]{0:T(1024)}, f32[2304]{0:T(1024)S(1)}, u32[]{:S(2)}) copy-start(f32[2304]{0:T(1024)S(1)} %fusion.66) | copy-start | bytes 27652
  232.8 16.8 %copy-start.30 = (bf16[2048,128]{1,0:T(8,128)(2,1)S(1)}, bf16[2048,128]{1,0:T(8,128)(2,1)}, u32[]{:S(2)}) copy-start(bf16[2048,128]{1,0:T(8,128)(2,1)} %param.25) | copy-start | bytes 1572868
  281.7 20.8 %all-to-all-start.5 = ((bf16[16,144,128]{2,1,0:T(8,128)(2,1)}), bf16[16,144,128]{2,1,0:T(8,128)(2,1)S(1)}, u32[]{:S(2)}, u32[]{:S(2)}) async-start(bf16[16,144,128]{2,1,0:T(8,128)(2,1)} %copy.493), calls=%async_computation.5 | async-start | bytes 1179648 | tf_op jit(solution)/shard_map/all_to_all | solution.py:251
  335.6 28.3 %all-to-all-start.6 = ((f32[8,18,2048]{2,1,0:T(8,128)}), f32[8,18,2048]{2,1,0:T(8,128)}, u32[]{:S(2)}, u32[]{:S(2)}) async-start(f32[8,18,2048]{2,1,0:T(8,128)} %fusion.2), calls=%async_computation.6 | async-start | bytes 3145728 | tf_op jit(solution)/shard_map/all_to_all | solution.py:261
  339.9 146.7 %all-gather.11.cloned.1.call-start = ((), (), s32[]{:S(2)}) async-start(), calls=%async_computation.21 | async-start | bytes 10027008 | tf_op jit(solution)/shard_map/all_gather | solution.py:415
  350.5 510.7 %copy-start.50 = (f32[64,2]{0,1:T(2,128)}, f32[64,2]{0,1:T(2,128)S(1)}, u32[]{:S(2)}) copy-start(f32[64,2]{0,1:T(2,128)S(1)} %get-tuple-element.152) | copy-start | bytes 1540
  410.4 154.4 %all-gather.15.cloned.1.call-start = ((), (), s32[]{:S(2)}) async-start(), calls=%async_computation.24 | async-start | bytes 10027008 | tf_op jit(solution)/shard_map/all_gather | solution.py:421
  412.6 348.9 %reduce-scatter.3.cloned.1.call-start = ((), (), s32[]{:S(2)}) async-start(), calls=%async_computation.22 | async-start | bytes 10027008 | tf_op jit(solution)/shard_map/reduce_scatter | solution.py:239
  586.6 259.8 %all-gather.13.cloned.1.call-start = ((), (), s32[]{:S(2)}) async-start(), calls=%async_computation.23 | async-start | bytes 8912896 | tf_op jit(solution)/shard_map/all_gather | solution.py:433
  587.9 12.1 copy-start.11
  756.3 28.6 %all-to-all-start.10 = ((f32[8,18,2048]{2,1,0:T(8,128)}), f32[8,18,2048]{2,1,0:T(8,128)}, u32[]{:S(2)}, u32[]{:S(2)}) async-start(f32[8,18,2048]{2,1,0:T(8,128)} %reshape.676), calls=%async_computation.11 | async-start | bytes 3145728 | tf_op jit(solution)/shard_map/all_to_all | solution.py:236
  763.9 25.8 %copy-start.44 = (s32[8,18,1]{0,1,2:T(8,128)S(1)}, s32[8,18,1]{0,1,2:T(8,128)}, u32[]{:S(2)}) copy-start(s32[8,18,1]{0,1,2:T(8,128)} %get-tuple-element.173) | copy-start | bytes 1732
  763.9 25.9 %copy-start.57 = (s32[64,2]{0,1:T(2,128)S(1)}, s32[64,2]{0,1:T(2,128)}, u32[]{:S(2)}) copy-start(s32[64,2]{0,1:T(2,128)} %get-tuple-element.183) | copy-start | bytes 1540
  784.9 61.4 %all-to-all-start.8 = ((f32[8,18,2048]{2,1,0:T(8,128)}), f32[8,18,2048]{2,1,0:T(8,128)}, u32[]{:S(2)}, u32[]{:S(2)}) async-start(f32[8,18,2048]{2,1,0:T(8,128)} %reshape.729), calls=%async_computation.9 | async-start | bytes 3145728 | tf_op jit(solution)/shard_map/all_to_all | solution.py:242
  789.2 169.7 %all-gather.17.cloned.1.call-start = ((), (), s32[]{:S(2)}) async-start(), calls=%async_computation.25 | async-start | bytes 10027008 | tf_op jit(solution)/shard_map/all_gather | solution.py:223
  866.8 92.1 %copy-start.31 = (bf16[128,2048]{1,0:T(8,128)(2,1)S(1)}, bf16[128,2048]{1,0:T(8,128)(2,1)}, u32[]{:S(2)}) copy-start(bf16[128,2048]{1,0:T(8,128)(2,1)} %param.26) | copy-start | bytes 1572868
  966.4 13.8 %copy-start.39 = (f32[2304]{0:T(1024)S(1)}, f32[2304]{0:T(1024)}, u32[]{:S(2)}) copy-start(f32[2304]{0:T(1024)} %copy-done.38) | copy-start | bytes 27652
  966.4 13.8 %copy-start.53 = (f32[64]{0:T(128)S(1)}, f32[64]{0:T(128)}, u32[]{:S(2)}) copy-start(f32[64]{0:T(128)} %copy-done.52) | copy-start | bytes 772
  989.7 14.6 %all-to-all-start.12 = ((bf16[16,144,128]{2,1,0:T(8,128)(2,1)}), bf16[16,144,128]{2,1,0:T(8,128)(2,1)S(1)}, u32[]{:S(2)}, u32[]{:S(2)}) async-start(bf16[16,144,128]{2,1,0:T(8,128)(2,1)} %copy.527), calls=%async_computation.13 | async-start | bytes 1179648 | tf_op jit(solution)/shard_map/all_to_all | solution.py:251
  1004.3 64.1 %all-to-all-start.14 = ((bf16[8,1024,256]{2,1,0:T(8,128)(2,1)}), bf16[8,1024,256]{2,1,0:T(8,128)(2,1)}, u32[]{:S(2)}, u32[]{:S(2)}) async-start(bf16[8,1024,256]{2,1,0:T(8,128)(2,1)} %pad_maximum_fusion), calls=%async_computation.15 | async-start | bytes 8388608 | tf_op jit(solution)/shard_map/all_to_all | solution.py:503
  1068.4 27.4 %all-to-all-start.13 = ((f32[8,18,2048]{2,1,0:T(8,128)}), f32[8,18,2048]{2,1,0:T(8,128)}, u32[]{:S(2)}, u32[]{:S(2)}) async-start(f32[8,18,2048]{2,1,0:T(8,128)} %fusion), calls=%async_computation.14 | async-start | bytes 3145728 | tf_op jit(solution)/shard_map/all_to_all | solution.py:261
  1095.7 55.9 %all-to-all-start.15 = ((bf16[16,64,2048]{2,1,0:T(8,128)(2,1)}), bf16[16,64,2048]{2,1,0:T(8,128)(2,1)}, u32[]{:S(2)}, u32[]{:S(2)}) async-start(bf16[16,64,2048]{2,1,0:T(8,128)(2,1)} %bitcast.131), calls=%async_computation.16 | async-start | bytes 8388608 | tf_op jit(solution)/shard_map/all_to_all | solution.py:525
  1101.8 129.3 %reduce-scatter.5.cloned.1.call-start = ((), (), s32[]{:S(2)}) async-start(), calls=%async_computation.26 | async-start | bytes 3538944 | tf_op jit(solution)/shard_map/reduce_scatter | solution.py:559
  1117.0 37.7 %copy-start.15 = (bf16[128,2048]{1,0:T(8,128)(2,1)S(1)}, bf16[128,2048]{1,0:T(8,128)(2,1)}, u32[]{:S(2)}) copy-start(bf16[128,2048]{1,0:T(8,128)(2,1)} %param.21) | copy-start | bytes 1572868
  1117.0 37.7 %copy-start.21 = (f32[64,2048]{1,0:T(8,128)S(1)}, f32[64,2048]{1,0:T(8,128)}, u32[]{:S(2)}) copy-start(f32[64,2048]{1,0:T(8,128)} %multiply_reduce_fusion.3) | copy-start | bytes 1572868
  1117.0 37.7 %copy-start.35 = (f32[2048]{0:T(1024)S(1)}, f32[2048]{0:T(1024)}, u32[]{:S(2)}) copy-start(f32[2048]{0:T(1024)} %copy-done.34) | copy-start | bytes 24580
  1117.0 37.7 %copy-start.55 = (f32[64]{0:T(128)S(1)}, f32[64]{0:T(128)}, u32[]{:S(2)}) copy-start(f32[64]{0:T(128)} %copy-done.54) | copy-start | bytes 772
  1160.6 18.6 %slice-start = ((s8[9437184]{0:T(1024)(128)(4,1)}), s8[4194304]{0:T(1024)(128)(4,1)S(1)}, s32[]{:S(2)}) async-start(s8[9437184]{0:T(1024)(128)(4,1)} %bitcast.170), calls=%async_computation.27 | async-start | bytes 8388608
  1160.6 18.6 %slice-start.1 = ((s8[9437184]{0:T(1024)(128)(4,1)}), s8[4194304]{0:T(1024)(128)(4,1)S(1)}, s32[]{:S(2)}) async-start(s8[9437184]{0:T(1024)(128)(4,1)} %bitcast.170), calls=%async_computation.28 | async-start | bytes 8388608
  1179.2 26.7 %copy-start.6 = (bf16[8,16,18,128]{3,2,1,0:T(8,128)(2,1)S(1)}, bf16[8,16,18,128]{3,2,1,0:T(8,128)(2,1)}, u32[]{:S(2)}) copy-start(bf16[8,16,18,128]{3,2,1,0:T(8,128)(2,1)} %copy-done.5) | copy-start | bytes 1769476
  1212.4 28.9 %copy-start.56 = (f32[64]{0:T(128)S(1)}, f32[64]{0:T(128)}, u32[]{:S(2)}) copy-start(f32[64]{0:T(128)} %copy-done.54) | copy-start | bytes 772
  1219.8 21.5 %copy-start.16 = (bf16[128,2048]{1,0:T(8,128)(2,1)S(1)}, bf16[128,2048]{1,0:T(8,128)(2,1)}, u32[]{:S(2)}) copy-start(bf16[128,2048]{1,0:T(8,128)(2,1)} %param.21) | copy-start | bytes 1572868
  1219.8 21.5 %copy-start.20 = (f32[64,2048]{1,0:T(8,128)S(1)}, f32[64,2048]{1,0:T(8,128)}, u32[]{:S(2)}) copy-start(f32[64,2048]{1,0:T(8,128)} %get-tuple-element.182) | copy-start | bytes 1572868
  1233.0 22.0 %all-to-all-start.16 = ((f32[16,16,384]{2,1,0:T(8,128)}), f32[16,16,384]{2,1,0:T(8,128)S(1)}, u32[]{:S(2)}, u32[]{:S(2)}) async-start(f32[16,16,384]{2,1,0:T(8,128)} %bitcast.45), calls=%async_computation.18 | async-start | bytes 786432 | tf_op jit(solution)/shard_map/all_to_all | solution.py:560
  1241.5 16.8 %copy-start.22 = (bf16[128,2048]{1,0:T(8,128)(2,1)S(1)}, bf16[128,2048]{1,0:T(8,128)(2,1)}, u32[]{:S(2)}) copy-start(bf16[128,2048]{1,0:T(8,128)(2,1)} %all_gather.28) | copy-start | bytes 1572868
  (36 other events, 144.0 us)
Sparse Core Ops, SparseCore 0:
  89.6 160.0 all-gather.6
  252.1 77.1 all-gather.8
  410.5 76.0 all-gather.10
  489.5 75.2 all-gather.14
  586.7 174.2 reduce-scatter.2
  763.4 82.8 all-gather.12
  882.4 76.4 all-gather.16
  1159.3 71.7 reduce-scatter.4

commit v14 on v11

--- a/solution.py
+++ b/solution.py
@@ -515,6 +515,17 @@
     kv_col_weight = jnp.einsum(
         "rd,rc->dc", seq_input, kv_col_grad, preferred_element_type=jnp.float32
     )
+    kv_sum = lax.psum_scatter(kv_col_weight, "grp", scatter_dimension=0, tiled=True)
+    kv_dealt = lax.all_to_all(
+        kv_sum.reshape(group_size, kv_rows, pair_cols),
+        GROUP_AXES,
+        split_axis=0,
+        concat_axis=0,
+        tiled=True,
+    )
+    kv_grad = jnp.transpose(
+        kv_dealt.reshape(group_size, kv_rows, 2, head_cols), (1, 2, 0, 3)
+    ).reshape(kv_rows, kv_width)
     kv_input_parts = lax.all_to_all(
         jnp.einsum("rc,dc->rd", kv_col_grad, head_kv, preferred_element_type=jnp.float32)
         .astype(jnp.bfloat16)
@@ -542,25 +553,22 @@
     grad_extras = jnp.concatenate(
         [gain_one_own[:, None], gain_two_own[:, None], attn_router_own, mlp_router_own], axis=1
     )
-    packed_grad = jnp.concatenate(
-        [
-            kv_col_weight,
-            jnp.pad(grad_extras, ((0, 0), (0, extra_pad - grad_extras.shape[1]))),
-        ],
-        axis=1,
-    )
-    group_sum = lax.psum_scatter(packed_grad, "grp", scatter_dimension=0, tiled=True)
-    dealt = lax.all_to_all(
-        group_sum.reshape(group_size, kv_rows, pair_cols + extra_pad),
-        GROUP_AXES,
-        split_axis=0,
-        concat_axis=0,
-        tiled=True,
-    )
-    kv_grad = jnp.transpose(
-        dealt[:, :, :pair_cols].reshape(group_size, kv_rows, 2, head_cols), (1, 2, 0, 3)
-    ).reshape(kv_rows, kv_width)
-    extra_grad = jnp.sum(dealt[:, :, pair_cols:], axis=0)
+    extra_sum = lax.psum_scatter(
+        jnp.pad(grad_extras, ((0, 0), (0, extra_pad - grad_extras.shape[1]))),
+        "grp",
+        scatter_dimension=0,
+        tiled=True,
+    )
+    extra_grad = jnp.sum(
+        lax.all_to_all(
+            extra_sum.reshape(group_size, kv_rows, extra_pad),
+            GROUP_AXES,
+            split_axis=0,
+            concat_axis=0,
+            tiled=True,
+        ),
+        axis=0,
+    )
     gain_one_grad = extra_grad[:, 0]
     gain_two_grad = extra_grad[:, 1]
     attn_router_grad = extra_grad[:, 2 : 2 + EXPERTS]

time: 1270 us -> 1270 us (level)
  local copies, waits for them, and re-layouts: 130 us -> 113 us
  waiting for transfers between devices: 621 us -> 637 us
    reduce_scatter x1 -> x2, waiting for transfers between devices: 24.6 us -> 0.01 us  [the longest x1 0.01 us: shards(): lax.psum_scatter(kv_col_weight, 'grp', scatter_dimension=0, tiled=True)]
    all_to_all x1, waiting for transfers between devices: 37.5 us -> 56.3 us  [shards(): lax.all_to_all(jnp.einsum('rc,dc->rd', kv_col_grad, head_kv, preferred_el...]
  transfers between devices with their start and end apart: 21 -> 23, of which waited for: 19 -> 19; matrix products, arithmetic and copies ran while one was open for 17% -> 17% of each run, Pallas kernels for 1% -> 1%
where the time goes in v14:
time: 1270 us
  waiting for transfers between devices  637 us (50%)
  blocking collectives  201 us (16%)
  matrix products  143 us (11%)
  local copies, waits for them, and re-layouts  113 us (9%)
  other arithmetic  72.1 us (6%)
  starting transfers between devices  57.6 us (5%)
  Pallas kernels  24.6 us (2%)
  between operations  15.8 us (1%)
    all_to_all x1, blocking collectives, combine(): lax.all_to_all(partial_value.astype(jnp.bfloat16).reshape(group_size, gro...  136 us
    all_gather x2, waiting for transfers between devices, dispatch(): lax.all_gather(by_group.reshape(groups * slot_cap, width), GROUP_AXES, ax...  118 us
    all_gather x1, waiting for transfers between devices, shards(): lax.all_gather(mlp_by_group[:, :slot_cap].reshape(groups * slot_cap, widt...  73.6 us
    all_gather x1, waiting for transfers between devices, shards(): lax.all_gather(mlp_by_group[:, slot_cap:].reshape(groups * slot_cap, widt...  68.9 us
    all_to_all x1, waiting for transfers between devices, shards(): lax.all_to_all(jnp.einsum('rc,dc->rd', kv_col_grad, head_kv, preferred_el...  56.3 us
    all_to_all x1, waiting for transfers between devices, shards(): lax.all_to_all(jnp.concatenate([seq_key_grad, seq_value_grad], axis=2).as...  51.7 us
    all_gather x1, waiting for transfers between devices, shards(): query_stack = lax.all_gather(query_weight, GROUP_AXES, axis=1, tiled=True)  48.8 us
    all_gather x1, waiting for transfers between devices, shards(): seq_input = lax.all_gather(attn_input, GROUP_AXES, axis=0, tiled=True)  39.5 us
  transfers between devices with their start and end apart: 23, of which 19 were waited for; matrix products, arithmetic and copies ran while one was open for 17% of the time, Pallas kernels for 1%

profile of v14, /device:TPU:1, one launch (start us, length us, event | category | flops | bytes accessed | tf_op | source)
XLA Modules:
  0.0 1265.1 jit_solution(9489915246559118646)
XLA Ops:
  17.2 17.5 %all_to_all.85 = bf16[16,16,384]{2,1,0:T(8,128)(2,1)S(1)} all-to-all(bf16[16,16,384]{2,1,0:T(8,128)(2,1)S(1)} %pad_maximum_fusion.9), channel_id=1, replica_groups=mesh['grp'=8,'sub'=8,'expert'=2] {'sub','expert'}, dimensions={0} | all-to-all | bytes 393216 | tf_op jit(solution)/shard_map/all_to_all | solution.py:301
  40.8 23.2 %all-to-all-done.1 = bf16[8,256,384]{1,2,0:T(8,128)(2,1)} async-done(((bf16[8,256,384]{1,2,0:T(8,128)(2,1)}), bf16[8,256,384]{1,2,0:T(8,128)(2,1)}, u32[]{:S(2)}, u32[]{:S(2)}) %all-to-all-start.1) | async-done | bytes 1572896 | tf_op jit(solution)/shard_map/all_to_all | solution.py:314
  73.3 13.5 %all_to_all.86 = bf16[8,18,2048]{2,1,0:T(8,128)(2,1)S(1)} all-to-all(bf16[8,18,2048]{2,1,0:T(8,128)(2,1)S(1)} %broadcast_select_fusion.1), channel_id=1, replica_groups=mesh['grp'=8,'sub'=8,'expert'=2] {'grp'}, dimensions={0} | all-to-all | bytes 1179648 | tf_op jit(solution)/shard_map/all_to_all | solution.py:222
  88.5 39.5 %all-gather.11.cloned.1.call-done = bf16[1024,2048]{1,0:T(8,128)(2,1)} async-done(((bf16[64,2048]{1,0:T(8,128)(2,1)}), bf16[1024,2048]{1,0:T(8,128)(2,1)}) %all-gather.11.cloned.1.call-update) | async-done | bytes 4194320 | tf_op jit(solution)/shard_map/all_gather | solution.py:334
  135.6 4.8 all-to-all-start.3
  150.9 5.6 multiply_reduce_fusion
  162.5 37.4 %all-to-all-done.3 = bf16[8,1024,256]{2,1,0:T(8,128)(2,1)} async-done(((bf16[8,1024,256]{2,1,0:T(8,128)(2,1)}), bf16[8,1024,256]{2,1,0:T(8,128)(2,1)}, u32[]{:S(2)}, u32[]{:S(2)}) %all-to-all-start.3) | async-done | bytes 4194336 | tf_op jit(solution)/shard_map/all_to_all | solution.py:346
  204.4 41.8 %all-gather.9.cloned.1.call-done = bf16[2304,2048]{1,0:T(8,128)(2,1)} async-done(((bf16[144,2048]{1,0:T(8,128)(2,1)}), bf16[2304,2048]{1,0:T(8,128)(2,1)}) %all-gather.9.cloned.1.call-update) | async-done | bytes 9437200 | tf_op jit(solution)/shard_map/all_gather | solution.py:223
  246.1 5.3 fusion.86
  256.9 5.4 fusion.14
  263.5 10.8 shard_map.238
  282.5 15.5 %all-to-all-done.4 = bf16[16,144,128]{2,1,0:T(8,128)(2,1)S(1)} async-done(((bf16[16,144,128]{2,1,0:T(8,128)(2,1)}), bf16[16,144,128]{2,1,0:T(8,128)(2,1)S(1)}, u32[]{:S(2)}, u32[]{:S(2)}) %all-to-all-start.4) | async-done | bytes 589856 | tf_op jit(solution)/shard_map/all_to_all | solution.py:251
  300.4 25.3 %all-gather.13.cloned.1.call-done = bf16[2048,2048]{1,0:T(8,128)(2,1)} async-done(((bf16[128,2048]{1,0:T(8,128)(2,1)}), bf16[2048,2048]{1,0:T(8,128)(2,1)}) %all-gather.13.cloned.1.call-update) | async-done | bytes 8388624 | tf_op jit(solution)/shard_map/all_gather | solution.py:382
  325.8 6.4 fusion.2
  344.8 15.6 %all-to-all-done.5 = f32[8,18,2048]{2,1,0:T(8,128)} async-done(((f32[8,18,2048]{2,1,0:T(8,128)}), f32[8,18,2048]{2,1,0:T(8,128)}, u32[]{:S(2)}, u32[]{:S(2)}) %all-to-all-start.5) | async-done | bytes 1179680 | tf_op jit(solution)/shard_map/all_to_all | solution.py:261
  380.1 19.2 %all_to_all.87 = bf16[8,36,2048]{2,1,0:T(8,128)(2,1)S(1)} all-to-all(bf16[8,36,2048]{2,1,0:T(8,128)(2,1)S(1)} %pad_maximum_fusion.1), channel_id=1, replica_groups=mesh['grp'=8,'sub'=8,'expert'=2] {'grp'}, dimensions={0} | all-to-all | bytes 2359296 | tf_op jit(solution)/shard_map/all_to_all | solution.py:402
  405.3 73.6 %all-gather.15.cloned.1.call-done = bf16[2304,2048]{1,0:T(8,128)(2,1)} async-done(((bf16[144,2048]{1,0:T(8,128)(2,1)}), bf16[2304,2048]{1,0:T(8,128)(2,1)}) %all-gather.15.cloned.1.call-update) | async-done | bytes 9437200 | tf_op jit(solution)/shard_map/all_gather | solution.py:409
  478.9 9.2 fusion.87
  488.1 68.9 %all-gather.19.cloned.1.call-done = bf16[2304,2048]{1,0:T(8,128)(2,1)} async-done(((bf16[144,2048]{1,0:T(8,128)(2,1)}), bf16[2304,2048]{1,0:T(8,128)(2,1)}) %all-gather.19.cloned.1.call-update) | async-done | bytes 9437200 | tf_op jit(solution)/shard_map/all_gather | solution.py:415
  557.1 7.1 fusion.88
  564.9 8.6 multiply_convert_fusion.2
  574.7 7.5 convolution_convert_fusion
  582.9 12.2 fusion.89
  595.1 11.1 add_convert_fusion
  606.2 136.2 %all_to_all.88 = bf16[16,144,2048]{2,1,0:T(8,128)(2,1)} all-to-all(bf16[16,144,2048]{2,1,0:T(8,128)(2,1)S(1)} %bitcast.130), channel_id=1, replica_groups=mesh['grp'=8,'sub'=8,'expert'=2] {'sub','expert'}, dimensions={0} | all-to-all | bytes 18874368 | tf_op jit(solution)/shard_map/all_to_all | solution.py:228
  742.4 5.9 convert_reduce_fusion
  758.2 19.3 %all-to-all-done.9 = f32[8,18,2048]{2,1,0:T(8,128)} async-done(((f32[8,18,2048]{2,1,0:T(8,128)}), f32[8,18,2048]{2,1,0:T(8,128)}, u32[]{:S(2)}, u32[]{:S(2)}) %all-to-all-start.9) | async-done | bytes 1179680 | tf_op jit(solution)/shard_map/all_to_all | solution.py:236
  790.5 48.8 %all-gather.17.cloned.1.call-done = bf16[2048,2048]{1,0:T(8,128)(2,1)} async-done(((bf16[2048,128]{1,0:T(8,128)(2,1)}), bf16[2048,2048]{1,0:T(8,128)(2,1)}) %all-gather.17.cloned.1.call-update) | async-done | bytes 8388624 | tf_op jit(solution)/shard_map/all_gather | solution.py:427
  861.0 14.7 %all_to_all.89 = bf16[8,18,2048]{2,1,0:T(8,128)(2,1)S(1)} all-to-all(bf16[8,18,2048]{2,1,0:T(8,128)(2,1)S(1)} %multiply_convert_fusion.3), channel_id=1, replica_groups=mesh['grp'=8,'sub'=8,'expert'=2] {'grp'}, dimensions={0} | all-to-all | bytes 1179648 | tf_op jit(solution)/shard_map/all_to_all | solution.py:222
  876.7 76.2 %all-gather.21.cloned.1.call-done = bf16[2304,2048]{1,0:T(8,128)(2,1)} async-done(((bf16[144,2048]{1,0:T(8,128)(2,1)}), bf16[2304,2048]{1,0:T(8,128)(2,1)}) %all-gather.21.cloned.1.call-update) | async-done | bytes 9437200 | tf_op jit(solution)/shard_map/all_gather | solution.py:223
  952.9 6.3 convolution_convert_fusion.2
  960.4 13.8 %shard_map.239 = (f32[8,288,128]{2,1,0:T(8,128)}, f32[8,1024,128]{2,1,0:T(8,128)}, f32[8,1024,128]{2,1,0:T(8,128)}) custom-call(bf16[8,288,128]{2,1,0:T(8,128)(2,1)} %pad_maximum_fusion.2.q_ref, bf16[8,1024,128]{2,1,0:T(8,128)(2,1)} %bitcast.143, bf16[8,1024,128]{2,1,0:T(8,128)(2,1)} %bitcast.141, s32[8,288,1]{2,1,0:T(8,128)} %add_select_fusion.qb_ref, ...), custom_call_target="tpu_custom_call" | custom-call | flops 3019898880 | bytes 25100288 | tf_op jit(solution)/shard_map/pallas_call | solution.py:76
  974.2 7.9 fusion.18
  1003.3 7.4 fusion
  1010.6 51.7 %all-to-all-done.13 = bf16[8,1024,256]{2,1,0:T(8,128)(2,1)} async-done(((bf16[8,1024,256]{2,1,0:T(8,128)(2,1)}), bf16[8,1024,256]{2,1,0:T(8,128)(2,1)}, u32[]{:S(2)}, u32[]{:S(2)}) %all-to-all-start.13) | async-done | bytes 4194336 | tf_op jit(solution)/shard_map/all_to_all | solution.py:496
  1075.5 14.4 %all-to-all-done.12 = f32[8,18,2048]{2,1,0:T(8,128)} async-done(((f32[8,18,2048]{2,1,0:T(8,128)}), f32[8,18,2048]{2,1,0:T(8,128)}, u32[]{:S(2)}, u32[]{:S(2)}) %all-to-all-start.12) | async-done | bytes 1179680 | tf_op jit(solution)/shard_map/all_to_all | solution.py:261
  1089.9 5.9 all-to-all-start.14
  1095.8 4.8 fusion.53
  1102.1 9.4 fusion.94
  1111.5 8.9 fusion.95
  1127.7 56.3 %all-to-all-done.14 = bf16[16,64,2048]{2,1,0:T(8,128)(2,1)} async-done(((bf16[16,64,2048]{2,1,0:T(8,128)(2,1)}), bf16[16,64,2048]{2,1,0:T(8,128)(2,1)}, u32[]{:S(2)}, u32[]{:S(2)}) %all-to-all-start.14) | async-done | bytes 4194336 | tf_op jit(solution)/shard_map/all_to_all | solution.py:529
  1190.6 9.3 fusion.96
  1204.0 7.5 fusion.92
  1211.5 5.2 all-to-all-start.16
  1216.7 6.1 fusion.93
  1222.8 4.7 all-to-all-done.16
  1230.4 5.7 all-to-all-start.15
  1236.1 17.6 %all-gather.23.cloned.1.call-done = bf16[128,4096]{1,0:T(8,128)(2,1)} async-done(((bf16[64,4096]{1,0:T(8,128)(2,1)}), bf16[128,4096]{1,0:T(8,128)(2,1)}) %all-gather.23.cloned.1.call-update) | async-done | bytes 1048592 | tf_op jit(solution)/shard_map/all_gather | solution.py:576
  (377 shorter events, 220.2 us)
Async XLA Ops:
  7.2 557.0 %copy-start = (bf16[2048,352]{0,1:T(8,128)(2,1)S(1)}, bf16[2048,352]{0,1:T(8,128)(2,1)}, u32[]{:S(2)}) copy-start(bf16[2048,352]{0,1:T(8,128)(2,1)} %param.30) | copy-start | bytes 4325380
  36.1 27.9 %all-to-all-start.1 = ((bf16[8,256,384]{1,2,0:T(8,128)(2,1)}), bf16[8,256,384]{1,2,0:T(8,128)(2,1)}, u32[]{:S(2)}, u32[]{:S(2)}) async-start(bf16[8,256,384]{1,2,0:T(8,128)(2,1)} %broadcast_in_dim.57), calls=%async_computation.1 | async-start | bytes 3145728 | tf_op jit(solution)/shard_map/all_to_all | solution.py:314
  40.6 87.5 %all-gather.11.cloned.1.call-start = ((), (), s32[]{:S(2)}) async-start(), calls=%async_computation.21 | async-start | bytes 4456448 | tf_op jit(solution)/shard_map/all_gather | solution.py:334
  40.8 25.6 %copy-start.45 = (f32[64]{0:T(128)}, f32[64]{0:T(128)S(1)}, u32[]{:S(2)}) copy-start(f32[64]{0:T(128)S(1)} %add_rsqrt_fusion.1) | copy-start | bytes 772
  66.4 4.5 copy-start.28
  68.3 177.8 %all-gather.9.cloned.1.call-start = ((), (), s32[]{:S(2)}) async-start(), calls=%async_computation.20 | async-start | bytes 10027008 | tf_op jit(solution)/shard_map/all_gather | solution.py:223
  87.7 238.0 %all-gather.13.cloned.1.call-start = ((), (), s32[]{:S(2)}) async-start(), calls=%async_computation.22 | async-start | bytes 8912896 | tf_op jit(solution)/shard_map/all_gather | solution.py:382
  88.5 168.4 %copy-start.43 = (f32[64]{0:T(128)}, f32[64]{0:T(128)S(1)}, u32[]{:S(2)}) copy-start(f32[64]{0:T(128)S(1)} %multiply_exponential_fusion) | copy-start | bytes 772
  88.5 43.4 %copy-start.38 = (f32[1024]{0:T(1024)}, f32[1024]{0:T(1024)S(1)}, u32[]{:S(2)}) copy-start(f32[1024]{0:T(1024)S(1)} %iota_convert_fusion) | copy-start | bytes 12292
  135.6 64.3 %all-to-all-start.3 = ((bf16[8,1024,256]{2,1,0:T(8,128)(2,1)}), bf16[8,1024,256]{2,1,0:T(8,128)(2,1)}, u32[]{:S(2)}, u32[]{:S(2)}) async-start(bf16[8,1024,256]{2,1,0:T(8,128)(2,1)} %broadcast_in_dim.66), calls=%async_computation.3 | async-start | bytes 8388608 | tf_op jit(solution)/shard_map/all_to_all | solution.py:346
  159.1 97.8 %copy-start.31 = (f32[2304]{0:T(1024)}, f32[2304]{0:T(1024)S(1)}, u32[]{:S(2)}) copy-start(f32[2304]{0:T(1024)S(1)} %fusion.66) | copy-start | bytes 27652
  276.4 6.1 copy-start.26
  277.5 20.5 %all-to-all-start.4 = ((bf16[16,144,128]{2,1,0:T(8,128)(2,1)}), bf16[16,144,128]{2,1,0:T(8,128)(2,1)S(1)}, u32[]{:S(2)}, u32[]{:S(2)}) async-start(bf16[16,144,128]{2,1,0:T(8,128)(2,1)} %copy.493), calls=%async_computation.4 | async-start | bytes 1179648 | tf_op jit(solution)/shard_map/all_to_all | solution.py:251
  332.1 28.3 %all-to-all-start.5 = ((f32[8,18,2048]{2,1,0:T(8,128)}), f32[8,18,2048]{2,1,0:T(8,128)}, u32[]{:S(2)}, u32[]{:S(2)}) async-start(f32[8,18,2048]{2,1,0:T(8,128)} %fusion.2), calls=%async_computation.5 | async-start | bytes 3145728 | tf_op jit(solution)/shard_map/all_to_all | solution.py:261
  336.4 142.5 %all-gather.15.cloned.1.call-start = ((), (), s32[]{:S(2)}) async-start(), calls=%async_computation.23 | async-start | bytes 10027008 | tf_op jit(solution)/shard_map/all_gather | solution.py:409
  341.8 20.2 %copy-start.22 = (s32[1024]{0:T(1024)}, s32[1024]{0:T(1024)S(1)}, u32[]{:S(2)}) copy-start(s32[1024]{0:T(1024)S(1)} %pad_clamp_fusion.2) | copy-start | bytes 12292
  402.8 154.2 %all-gather.19.cloned.1.call-start = ((), (), s32[]{:S(2)}) async-start(), calls=%async_computation.26 | async-start | bytes 10027008 | tf_op jit(solution)/shard_map/all_gather | solution.py:415
  405.0 350.8 %reduce-scatter.4.cloned.1.call-start = ((), (), s32[]{:S(2)}) async-start(), calls=%async_computation.24 | async-start | bytes 10027008 | tf_op jit(solution)/shard_map/reduce_scatter | solution.py:239
  557.1 7.1 copy-start.48
  557.1 7.8 copy-start.50
  564.9 9.8 copy-start.49
  582.1 257.2 %all-gather.17.cloned.1.call-start = ((), (), s32[]{:S(2)}) async-start(), calls=%async_computation.25 | async-start | bytes 8912896 | tf_op jit(solution)/shard_map/all_gather | solution.py:427
  582.9 12.2 copy-start.15
  749.7 27.8 %all-to-all-start.9 = ((f32[8,18,2048]{2,1,0:T(8,128)}), f32[8,18,2048]{2,1,0:T(8,128)}, u32[]{:S(2)}, u32[]{:S(2)}) async-start(f32[8,18,2048]{2,1,0:T(8,128)} %reshape.674), calls=%async_computation.10 | async-start | bytes 3145728 | tf_op jit(solution)/shard_map/all_to_all | solution.py:236
  758.1 24.1 %copy-start.37 = (s32[8,18,1]{0,1,2:T(8,128)S(1)}, s32[8,18,1]{0,1,2:T(8,128)}, u32[]{:S(2)}) copy-start(s32[8,18,1]{0,1,2:T(8,128)} %get-tuple-element.174) | copy-start | bytes 1732
  758.2 24.3 %copy-start.47 = (s32[64,2]{0,1:T(2,128)S(1)}, s32[64,2]{0,1:T(2,128)}, u32[]{:S(2)}) copy-start(s32[64,2]{0,1:T(2,128)} %get-tuple-element.184) | copy-start | bytes 1540
  777.5 61.8 %all-to-all-start.7 = ((f32[8,18,2048]{2,1,0:T(8,128)}), f32[8,18,2048]{2,1,0:T(8,128)}, u32[]{:S(2)}, u32[]{:S(2)}) async-start(f32[8,18,2048]{2,1,0:T(8,128)} %reshape.728), calls=%async_computation.8 | async-start | bytes 3145728 | tf_op jit(solution)/shard_map/all_to_all | solution.py:242
  781.8 171.1 %all-gather.21.cloned.1.call-start = ((), (), s32[]{:S(2)}) async-start(), calls=%async_computation.27 | async-start | bytes 10027008 | tf_op jit(solution)/shard_map/all_gather | solution.py:223
  861.0 91.9 %copy-start.25 = (bf16[128,2048]{1,0:T(8,128)(2,1)S(1)}, bf16[128,2048]{1,0:T(8,128)(2,1)}, u32[]{:S(2)}) copy-start(bf16[128,2048]{1,0:T(8,128)(2,1)} %param.26) | copy-start | bytes 1572868
  960.4 13.8 %copy-start.32 = (f32[2304]{0:T(1024)S(1)}, f32[2304]{0:T(1024)}, u32[]{:S(2)}) copy-start(f32[2304]{0:T(1024)} %copy-done.31) | copy-start | bytes 27652
  960.4 13.8 %copy-start.44 = (f32[64]{0:T(128)S(1)}, f32[64]{0:T(128)}, u32[]{:S(2)}) copy-start(f32[64]{0:T(128)} %copy-done.43) | copy-start | bytes 772
  983.7 14.5 %all-to-all-start.11 = ((bf16[16,144,128]{2,1,0:T(8,128)(2,1)}), bf16[16,144,128]{2,1,0:T(8,128)(2,1)S(1)}, u32[]{:S(2)}, u32[]{:S(2)}) async-start(bf16[16,144,128]{2,1,0:T(8,128)(2,1)} %copy.527), calls=%async_computation.12 | async-start | bytes 1179648 | tf_op jit(solution)/shard_map/all_to_all | solution.py:251
  998.2 64.1 %all-to-all-start.13 = ((bf16[8,1024,256]{2,1,0:T(8,128)(2,1)}), bf16[8,1024,256]{2,1,0:T(8,128)(2,1)}, u32[]{:S(2)}, u32[]{:S(2)}) async-start(bf16[8,1024,256]{2,1,0:T(8,128)(2,1)} %pad_maximum_fusion), calls=%async_computation.14 | async-start | bytes 8388608 | tf_op jit(solution)/shard_map/all_to_all | solution.py:496
  1062.3 27.6 %all-to-all-start.12 = ((f32[8,18,2048]{2,1,0:T(8,128)}), f32[8,18,2048]{2,1,0:T(8,128)}, u32[]{:S(2)}, u32[]{:S(2)}) async-start(f32[8,18,2048]{2,1,0:T(8,128)} %fusion), calls=%async_computation.13 | async-start | bytes 3145728 | tf_op jit(solution)/shard_map/all_to_all | solution.py:261
  1089.9 94.1 %all-to-all-start.14 = ((bf16[16,64,2048]{2,1,0:T(8,128)(2,1)}), bf16[16,64,2048]{2,1,0:T(8,128)(2,1)}, u32[]{:S(2)}, u32[]{:S(2)}) async-start(bf16[16,64,2048]{2,1,0:T(8,128)(2,1)} %bitcast.131), calls=%async_computation.15 | async-start | bytes 8388608 | tf_op jit(solution)/shard_map/all_to_all | solution.py:529
  1095.8 115.7 %reduce-scatter.8.cloned.1.call-start = ((), (), s32[]{:S(2)}) async-start(), calls=%async_computation.30 | async-start | bytes 2359296 | tf_op jit(solution)/shard_map/reduce_scatter | solution.py:518
  1100.7 128.0 %reduce-scatter.6.cloned.1.call-start = ((), (), s32[]{:S(2)}) async-start(), calls=%async_computation.29 | async-start | bytes 1179648 | tf_op jit(solution)/shard_map/reduce_scatter | solution.py:556
  1102.1 9.4 copy-start.20
  1111.5 8.9 copy-start.5
  1111.5 9.1 copy-start.3
  1127.7 59.3 %copy-start.18 = (bf16[128,2048]{1,0:T(8,128)(2,1)S(1)}, bf16[128,2048]{1,0:T(8,128)(2,1)}, u32[]{:S(2)}) copy-start(bf16[128,2048]{1,0:T(8,128)(2,1)} %param.21) | copy-start | bytes 1572868
  1127.7 59.3 %copy-start.29 = (f32[2048]{0:T(1024)S(1)}, f32[2048]{0:T(1024)}, u32[]{:S(2)}) copy-start(f32[2048]{0:T(1024)} %copy-done.28) | copy-start | bytes 24580
  1127.7 59.3 %copy-start.46 = (f32[64]{0:T(128)S(1)}, f32[64]{0:T(128)}, u32[]{:S(2)}) copy-start(f32[64]{0:T(128)} %copy-done.45) | copy-start | bytes 772
  1190.3 9.6 copy-start.11
  1190.3 63.5 %all-gather.23.cloned.1.call-start = ((), (), s32[]{:S(2)}) async-start(), calls=%async_computation.28 | async-start | bytes 1572864 | tf_op jit(solution)/shard_map/all_gather | solution.py:576
  1211.5 16.1 %all-to-all-start.16 = ((f32[16,16,256]{2,1,0:T(8,128)}), f32[16,16,256]{2,1,0:T(8,128)S(1)}, u32[]{:S(2)}, u32[]{:S(2)}) async-start(f32[16,16,256]{2,1,0:T(8,128)} %bitcast.163), calls=%async_computation.19 | async-start | bytes 524288 | tf_op jit(solution)/shard_map/all_to_all | solution.py:519
  1227.9 30.3 %copy-start.1 = (bf16[2048,352]{0,1:T(8,128)(2,1)S(1)}, bf16[2048,352]{0,1:T(8,128)(2,1)}, u32[]{:S(2)}) copy-start(bf16[2048,352]{0,1:T(8,128)(2,1)} %param.30) | copy-start | bytes 4325380
  1230.4 25.6 %all-to-all-start.15 = ((f32[16,16,128]{2,1,0:T(8,128)}), f32[16,16,128]{2,1,0:T(8,128)S(1)}, u32[]{:S(2)}, u32[]{:S(2)}) async-start(f32[16,16,128]{2,1,0:T(8,128)} %bitcast.44), calls=%async_computation.17 | async-start | bytes 262144 | tf_op jit(solution)/shard_map/all_to_all | solution.py:563
  (27 other events, 57.9 us)
Sparse Core Ops, SparseCore 0:
  68.4 59.6 all-gather.10
  131.1 114.9 all-gather.8
  248.6 77.1 all-gather.12
  403.0 75.9 all-gather.14
  481.8 75.2 all-gather.18
  582.3 173.4 reduce-scatter.3
  758.3 80.9 all-gather.16
  876.8 76.0 all-gather.20
  1100.8 69.3 reduce-scatter.7
  1190.4 32.1 reduce-scatter.5
  1224.9 28.7 all-gather.22

commit v15 on v11

--- a/solution.py
+++ b/solution.py
@@ -233,19 +233,17 @@
             tiled=True,
         )
         summed = jnp.sum(parts.astype(jnp.float32), axis=0).reshape(groups, slot_cap, width)
-        return lax.all_to_all(summed, "grp", split_axis=0, concat_axis=0, tiled=True)
+        return lax.all_to_all(
+            summed.astype(jnp.bfloat16), "grp", split_axis=0, concat_axis=0, tiled=True
+        ).astype(jnp.float32)
 
     def combine_scattered(partial_value):
         summed = lax.psum_scatter(
             partial_value.astype(jnp.bfloat16), GROUP_AXES, scatter_dimension=0, tiled=True
         )
         return lax.all_to_all(
-            summed.astype(jnp.float32).reshape(groups, slot_cap, width),
-            "grp",
-            split_axis=0,
-            concat_axis=0,
-            tiled=True,
-        )
+            summed.reshape(groups, slot_cap, width), "grp", split_axis=0, concat_axis=0, tiled=True
+        ).astype(jnp.float32)
 
     def to_rows(per_head):
         parts = lax.all_to_all(
@@ -259,8 +257,12 @@
 
     def to_owners(row_values):
         return lax.all_to_all(
-            row_values.reshape(groups, slot_cap, width), "grp", split_axis=0, concat_axis=0, tiled=True
-        )
+            row_values.astype(jnp.bfloat16).reshape(groups, slot_cap, width),
+            "grp",
+            split_axis=0,
+            concat_axis=0,
+            tiled=True,
+        ).astype(jnp.float32)
 
     def to_gj(rows):
         shaped = rows.reshape((group_size, groups, slot_cap) + rows.shape[1:])

time: 1270 us -> 1270 us (level)
    all_to_all x4, waiting for transfers between devices: 40.1 us -> 20.9 us  [the longest x2 9.03 us: to_owners(): lax.all_to_all(row_values.astype(jnp.bfloat16).reshape(groups, slot_cap,...]
    all_to_all x2, waiting for transfers between devices: 19.5 us -> 4.74 us  [to_rows(): lax.all_to_all(per_head.reshape(group_size, groups * slot_cap, head_cols)...]
    all_gather x1, waiting for transfers between devices: 24.5 us -> 38.7 us  [shards(): output_stack = lax.all_gather(output_weight, GROUP_AXES, axis=0, tiled=True)]
  transfers between devices with their start and end apart: 21 -> 21, of which waited for: 19 -> 18; matrix products, arithmetic and copies ran while one was open for 17% -> 17% of each run, Pallas kernels for 1% -> 1%
where the time goes in v15:
time: 1270 us; the launch traced here: 1260 us
  waiting for transfers between devices  614 us (48%)
  blocking collectives  203 us (16%)
  matrix products  141 us (11%)
  local copies, waits for them, and re-layouts  129 us (10%)
  other arithmetic  78 us (6%)
  starting transfers between devices  53.8 us (4%)
  Pallas kernels  25 us (2%)
  between operations  15.9 us (1%)
    all_to_all x1, blocking collectives, combine(): lax.all_to_all(partial_value.astype(jnp.bfloat16).reshape(group_size, gro...  136 us
    all_gather x2, waiting for transfers between devices, dispatch(): lax.all_gather(by_group.reshape(groups * slot_cap, width), GROUP_AXES, ax...  113 us
    all_gather x1, waiting for transfers between devices, shards(): lax.all_gather(mlp_by_group[:, :slot_cap].reshape(groups * slot_cap, widt...  74.6 us
    all_gather x1, waiting for transfers between devices, shards(): lax.all_gather(mlp_by_group[:, slot_cap:].reshape(groups * slot_cap, widt...  68.9 us
    all_gather x1, waiting for transfers between devices, shards(): query_stack = lax.all_gather(query_weight, GROUP_AXES, axis=1, tiled=True)  58.9 us
    all_to_all x1, waiting for transfers between devices, shards(): lax.all_to_all(jnp.concatenate([seq_key_grad, seq_value_grad], axis=2).as...  52.2 us
    all_gather x1, waiting for transfers between devices, shards(): output_stack = lax.all_gather(output_weight, GROUP_AXES, axis=0, tiled=True)  38.7 us
    all_to_all x1, waiting for transfers between devices, shards(): lax.all_to_all(jnp.einsum('rc,dc->rd', kv_col_grad, head_kv, preferred_el...  37.8 us
  transfers between devices with their start and end apart: 21, of which 18 were waited for; matrix products, arithmetic and copies ran while one was open for 17% of the time, Pallas kernels for 1%

profile of v15, /device:TPU:1, one launch (start us, length us, event | category | flops | bytes accessed | tf_op | source)
XLA Modules:
  0.0 1258.8 jit_solution(342726608622120382)
XLA Ops:
  17.3 17.5 %all_to_all.80 = bf16[16,16,384]{2,1,0:T(8,128)(2,1)S(1)} all-to-all(bf16[16,16,384]{2,1,0:T(8,128)(2,1)S(1)} %pad_maximum_fusion.10), channel_id=1, replica_groups=mesh['grp'=8,'sub'=8,'expert'=2] {'sub','expert'}, dimensions={0} | all-to-all | bytes 393216 | tf_op jit(solution)/shard_map/all_to_all | solution.py:303
  40.9 23.2 %all-to-all-done.1 = bf16[8,256,384]{1,2,0:T(8,128)(2,1)} async-done(((bf16[8,256,384]{1,2,0:T(8,128)(2,1)}), bf16[8,256,384]{1,2,0:T(8,128)(2,1)}, u32[]{:S(2)}, u32[]{:S(2)}) %all-to-all-start.1) | async-done | bytes 1572896 | tf_op jit(solution)/shard_map/all_to_all | solution.py:316
  75.8 13.9 %all_to_all.81 = bf16[8,18,2048]{2,1,0:T(8,128)(2,1)} all-to-all(bf16[8,18,2048]{2,1,0:T(8,128)(2,1)S(1)} %broadcast_select_fusion.1), channel_id=1, replica_groups=mesh['grp'=8,'sub'=8,'expert'=2] {'grp'}, dimensions={0} | all-to-all | bytes 1179648 | tf_op jit(solution)/shard_map/all_to_all | solution.py:222
  92.6 36.4 %all-gather.11.cloned.1.call-done = bf16[1024,2048]{1,0:T(8,128)(2,1)} async-done(((bf16[64,2048]{1,0:T(8,128)(2,1)}), bf16[1024,2048]{1,0:T(8,128)(2,1)}) %all-gather.11.cloned.1.call-update) | async-done | bytes 4194320 | tf_op jit(solution)/shard_map/all_gather | solution.py:336
  139.8 4.8 all-to-all-start.3
  158.9 5.6 multiply_reduce_fusion
  170.5 33.6 %all-to-all-done.3 = bf16[8,1024,256]{2,1,0:T(8,128)(2,1)} async-done(((bf16[8,1024,256]{2,1,0:T(8,128)(2,1)}), bf16[8,1024,256]{2,1,0:T(8,128)(2,1)}, u32[]{:S(2)}, u32[]{:S(2)}) %all-to-all-start.3) | async-done | bytes 4194336 | tf_op jit(solution)/shard_map/all_to_all | solution.py:348
  204.1 4.7 fusion.82
  208.8 36.4 %all-gather.9.cloned.1.call-done = bf16[2304,2048]{1,0:T(8,128)(2,1)} async-done(((bf16[144,2048]{1,0:T(8,128)(2,1)}), bf16[2304,2048]{1,0:T(8,128)(2,1)}) %all-gather.9.cloned.1.call-update) | async-done | bytes 9437200 | tf_op jit(solution)/shard_map/all_gather | solution.py:223
  245.2 7.4 fusion.86
  256.6 5.4 fusion.10
  263.1 11.2 shard_map.238
  286.1 38.7 %all-gather.13.cloned.1.call-done = bf16[2048,2048]{1,0:T(8,128)(2,1)} async-done(((bf16[128,2048]{1,0:T(8,128)(2,1)}), bf16[2048,2048]{1,0:T(8,128)(2,1)}) %all-gather.13.cloned.1.call-update) | async-done | bytes 8388624 | tf_op jit(solution)/shard_map/all_gather | solution.py:384
  324.8 5.7 convolution_convert_fusion.4
  339.7 9.0 all-to-all-done.5
  371.1 19.3 %all_to_all.82 = bf16[8,36,2048]{2,1,0:T(8,128)(2,1)S(1)} all-to-all(bf16[8,36,2048]{2,1,0:T(8,128)(2,1)S(1)} %pad_maximum_fusion.2), channel_id=1, replica_groups=mesh['grp'=8,'sub'=8,'expert'=2] {'grp'}, dimensions={0} | all-to-all | bytes 2359296 | tf_op jit(solution)/shard_map/all_to_all | solution.py:404
  396.4 74.6 %all-gather.15.cloned.1.call-done = bf16[2304,2048]{1,0:T(8,128)(2,1)} async-done(((bf16[144,2048]{1,0:T(8,128)(2,1)}), bf16[2304,2048]{1,0:T(8,128)(2,1)}) %all-gather.15.cloned.1.call-update) | async-done | bytes 9437200 | tf_op jit(solution)/shard_map/all_gather | solution.py:411
  471.0 9.2 fusion.87
  480.3 68.9 %all-gather.19.cloned.1.call-done = bf16[2304,2048]{1,0:T(8,128)(2,1)} async-done(((bf16[144,2048]{1,0:T(8,128)(2,1)}), bf16[2304,2048]{1,0:T(8,128)(2,1)}) %all-gather.19.cloned.1.call-update) | async-done | bytes 9437200 | tf_op jit(solution)/shard_map/all_gather | solution.py:417
  549.2 7.1 fusion.88
  557.0 8.6 multiply_convert_fusion.2
  566.8 7.5 convolution_convert_fusion
  575.1 12.2 fusion.89
  587.3 11.1 add_convert_fusion
  598.3 136.2 %all_to_all.83 = bf16[16,144,2048]{2,1,0:T(8,128)(2,1)} all-to-all(bf16[16,144,2048]{2,1,0:T(8,128)(2,1)S(1)} %bitcast.137), channel_id=1, replica_groups=mesh['grp'=8,'sub'=8,'expert'=2] {'sub','expert'}, dimensions={0} | all-to-all | bytes 18874368 | tf_op jit(solution)/shard_map/all_to_all | solution.py:228
  734.6 5.9 reduce_sum.342
  741.5 4.6 all-to-all-start.9
  750.1 7.6 all-to-all-done.9
  777.1 58.9 %all-gather.17.cloned.1.call-done = bf16[2048,2048]{1,0:T(8,128)(2,1)} async-done(((bf16[2048,128]{1,0:T(8,128)(2,1)}), bf16[2048,2048]{1,0:T(8,128)(2,1)}) %all-gather.17.cloned.1.call-update) | async-done | bytes 8388624 | tf_op jit(solution)/shard_map/all_gather | solution.py:429
  856.5 15.7 %all_to_all.84 = bf16[8,18,2048]{2,1,0:T(8,128)(2,1)S(1)} all-to-all(bf16[8,18,2048]{2,1,0:T(8,128)(2,1)S(1)} %multiply_convert_fusion.3), channel_id=1, replica_groups=mesh['grp'=8,'sub'=8,'expert'=2] {'grp'}, dimensions={0} | all-to-all | bytes 1179648 | tf_op jit(solution)/shard_map/all_to_all | solution.py:222
  873.2 76.2 %all-gather.21.cloned.1.call-done = bf16[2304,2048]{1,0:T(8,128)(2,1)} async-done(((bf16[144,2048]{1,0:T(8,128)(2,1)}), bf16[2304,2048]{1,0:T(8,128)(2,1)}) %all-gather.21.cloned.1.call-update) | async-done | bytes 9437200 | tf_op jit(solution)/shard_map/all_gather | solution.py:223
  949.4 6.3 convolution_convert_fusion.2
  956.9 13.8 %shard_map.239 = (f32[8,288,128]{2,1,0:T(8,128)}, f32[8,1024,128]{2,1,0:T(8,128)}, f32[8,1024,128]{2,1,0:T(8,128)}) custom-call(bf16[8,288,128]{2,1,0:T(8,128)(2,1)} %pad_maximum_fusion.3.q_ref, bf16[8,1024,128]{2,1,0:T(8,128)(2,1)} %bitcast.150, bf16[8,1024,128]{2,1,0:T(8,128)(2,1)} %bitcast.148, s32[8,288,1]{2,1,0:T(8,128)} %add_select_fusion.qb_ref, ...), custom_call_target="tpu_custom_call" | custom-call | flops 3019898880 | bytes 25100288 | tf_op jit(solution)/shard_map/pallas_call | solution.py:76
  970.7 7.9 fusion.14
  989.9 4.7 all-to-all-done.11
  999.2 6.3 convolution_convert_fusion.3
  1006.6 52.2 %all-to-all-done.13 = bf16[8,1024,256]{2,1,0:T(8,128)(2,1)} async-done(((bf16[8,1024,256]{2,1,0:T(8,128)(2,1)}), bf16[8,1024,256]{2,1,0:T(8,128)(2,1)}, u32[]{:S(2)}, u32[]{:S(2)}) %all-to-all-start.13) | async-done | bytes 4194336 | tf_op jit(solution)/shard_map/all_to_all | solution.py:498
  1082.2 5.7 all-to-all-start.14
  1095.1 4.9 fusion.53
  1100.0 37.8 %all-to-all-done.14 = bf16[16,64,2048]{2,1,0:T(8,128)(2,1)} async-done(((bf16[16,64,2048]{2,1,0:T(8,128)(2,1)}), bf16[16,64,2048]{2,1,0:T(8,128)(2,1)}, u32[]{:S(2)}, u32[]{:S(2)}) %all-to-all-start.14) | async-done | bytes 4194336 | tf_op jit(solution)/shard_map/all_to_all | solution.py:520
  1147.3 9.4 fusion.94
  1156.7 8.9 fusion.95
  1165.6 5.1 fusion.96
  1173.7 6.2 fusion.93
  1179.9 7.4 fusion.92
  1187.3 28.4 %reduce-scatter.5.cloned.1.call-done = f32[256,384]{0,1:T(8,128)} async-done(((f32[2048,384]{0,1:T(8,128)}), f32[256,384]{0,1:T(8,128)}) %reduce-scatter.5.cloned.1.call-update) | async-done | bytes 393232 | tf_op jit(solution)/shard_map/reduce_scatter | solution.py:554
  1217.6 8.3 all-to-all-start.15
  1225.9 20.0 %all-gather.23.cloned.1.call-done = bf16[128,4096]{1,0:T(8,128)(2,1)} async-done(((bf16[64,4096]{1,0:T(8,128)(2,1)}), bf16[128,4096]{1,0:T(8,128)(2,1)}) %all-gather.23.cloned.1.call-update) | async-done | bytes 1048592 | tf_op jit(solution)/shard_map/all_gather | solution.py:570
  (378 shorter events, 232.6 us)
Async XLA Ops:
  7.2 549.1 %copy-start = (bf16[2048,352]{0,1:T(8,128)(2,1)S(1)}, bf16[2048,352]{0,1:T(8,128)(2,1)}, u32[]{:S(2)}) copy-start(bf16[2048,352]{0,1:T(8,128)(2,1)} %param.30) | copy-start | bytes 4325380
  36.2 27.9 %all-to-all-start.1 = ((bf16[8,256,384]{1,2,0:T(8,128)(2,1)}), bf16[8,256,384]{1,2,0:T(8,128)(2,1)}, u32[]{:S(2)}, u32[]{:S(2)}) async-start(bf16[8,256,384]{1,2,0:T(8,128)(2,1)} %broadcast_in_dim.57), calls=%async_computation.1 | async-start | bytes 3145728 | tf_op jit(solution)/shard_map/all_to_all | solution.py:316
  40.6 88.3 %all-gather.11.cloned.1.call-start = ((), (), s32[]{:S(2)}) async-start(), calls=%async_computation.19 | async-start | bytes 4456448 | tf_op jit(solution)/shard_map/all_gather | solution.py:336
  40.9 25.6 %copy-start.44 = (f32[64]{0:T(128)}, f32[64]{0:T(128)S(1)}, u32[]{:S(2)}) copy-start(f32[64]{0:T(128)S(1)} %add_rsqrt_fusion.1) | copy-start | bytes 772
  65.9 84.1 %copy-start.3 = (bf16[8,256,384]{2,1,0:T(8,128)(2,1)}, bf16[8,256,384]{2,1,0:T(8,128)(2,1)S(1)}, u32[]{:S(2)}) copy-start(bf16[8,256,384]{2,1,0:T(8,128)(2,1)S(1)} %copy.448) | copy-start | bytes 4718596
  68.9 176.3 %all-gather.9.cloned.1.call-start = ((), (), s32[]{:S(2)}) async-start(), calls=%async_computation.18 | async-start | bytes 10027008 | tf_op jit(solution)/shard_map/all_gather | solution.py:223
  91.8 233.0 %all-gather.13.cloned.1.call-start = ((), (), s32[]{:S(2)}) async-start(), calls=%async_computation.20 | async-start | bytes 8912896 | tf_op jit(solution)/shard_map/all_gather | solution.py:384
  92.5 878.1 %copy-start.43 = (f32[64]{0:T(128)}, f32[64]{0:T(128)S(1)}, u32[]{:S(2)}) copy-start(f32[64]{0:T(128)S(1)} %multiply_exponential_fusion) | copy-start | bytes 772
  92.6 40.0 %copy-start.36 = (f32[1024]{0:T(1024)}, f32[1024]{0:T(1024)S(1)}, u32[]{:S(2)}) copy-start(f32[1024]{0:T(1024)S(1)} %iota_convert_fusion) | copy-start | bytes 12292
  139.8 64.2 %all-to-all-start.3 = ((bf16[8,1024,256]{2,1,0:T(8,128)(2,1)}), bf16[8,1024,256]{2,1,0:T(8,128)(2,1)}, u32[]{:S(2)}, u32[]{:S(2)}) async-start(bf16[8,1024,256]{2,1,0:T(8,128)(2,1)} %broadcast_in_dim.66), calls=%async_computation.3 | async-start | bytes 8388608 | tf_op jit(solution)/shard_map/all_to_all | solution.py:348
  158.9 8.2 copy-start.8
  204.1 41.1 %copy-start.25 = (bf16[2048,128]{1,0:T(8,128)(2,1)S(1)}, bf16[2048,128]{1,0:T(8,128)(2,1)}, u32[]{:S(2)}) copy-start(bf16[2048,128]{1,0:T(8,128)(2,1)} %param.25) | copy-start | bytes 1572868
  276.8 48.1 %all-to-all-start.4 = ((bf16[16,144,128]{2,1,0:T(8,128)(2,1)}), bf16[16,144,128]{2,1,0:T(8,128)(2,1)S(1)}, u32[]{:S(2)}, u32[]{:S(2)}) async-start(bf16[16,144,128]{2,1,0:T(8,128)(2,1)} %copy.459), calls=%async_computation.4 | async-start | bytes 1179648 | tf_op jit(solution)/shard_map/all_to_all | solution.py:249
  332.6 16.1 %all-to-all-start.5 = ((bf16[8,18,2048]{2,1,0:T(8,128)(2,1)}), bf16[8,18,2048]{2,1,0:T(8,128)(2,1)S(1)}, u32[]{:S(2)}, u32[]{:S(2)}) async-start(bf16[8,18,2048]{2,1,0:T(8,128)(2,1)} %reshape.674), calls=%async_computation.5 | async-start | bytes 1572864 | tf_op jit(solution)/shard_map/all_to_all | solution.py:259
  336.6 134.4 %all-gather.15.cloned.1.call-start = ((), (), s32[]{:S(2)}) async-start(), calls=%async_computation.21 | async-start | bytes 10027008 | tf_op jit(solution)/shard_map/all_gather | solution.py:411
  339.6 511.4 %copy-start.41 = (f32[64,2]{0,1:T(2,128)}, f32[64,2]{0,1:T(2,128)S(1)}, u32[]{:S(2)}) copy-start(f32[64,2]{0,1:T(2,128)S(1)} %get-tuple-element.152) | copy-start | bytes 1540
  394.0 155.2 %all-gather.19.cloned.1.call-start = ((), (), s32[]{:S(2)}) async-start(), calls=%async_computation.24 | async-start | bytes 10027008 | tf_op jit(solution)/shard_map/all_gather | solution.py:417
  396.2 351.8 %reduce-scatter.3.cloned.1.call-start = ((), (), s32[]{:S(2)}) async-start(), calls=%async_computation.22 | async-start | bytes 10027008 | tf_op jit(solution)/shard_map/reduce_scatter | solution.py:241
  549.2 7.1 copy-start.47
  549.2 7.8 copy-start.49
  557.0 9.8 copy-start.48
  574.3 261.7 %all-gather.17.cloned.1.call-start = ((), (), s32[]{:S(2)}) async-start(), calls=%async_computation.23 | async-start | bytes 8912896 | tf_op jit(solution)/shard_map/all_gather | solution.py:429
  575.1 12.2 copy-start.10
  741.5 16.2 %all-to-all-start.9 = ((bf16[8,18,2048]{2,1,0:T(8,128)(2,1)}), bf16[8,18,2048]{2,1,0:T(8,128)(2,1)S(1)}, u32[]{:S(2)}, u32[]{:S(2)}) async-start(bf16[8,18,2048]{2,1,0:T(8,128)(2,1)} %convert_element_type.231), calls=%async_computation.10 | async-start | bytes 1572864 | tf_op jit(solution)/shard_map/all_to_all | solution.py:236
  746.1 16.3 %copy-start.35 = (s32[8,18,1]{0,1,2:T(8,128)S(1)}, s32[8,18,1]{0,1,2:T(8,128)}, u32[]{:S(2)}) copy-start(s32[8,18,1]{0,1,2:T(8,128)} %get-tuple-element.174) | copy-start | bytes 1732
  746.1 16.5 %copy-start.46 = (s32[64,2]{0,1:T(2,128)S(1)}, s32[64,2]{0,1:T(2,128)}, u32[]{:S(2)}) copy-start(s32[64,2]{0,1:T(2,128)} %get-tuple-element.184) | copy-start | bytes 1540
  757.7 16.9 %all-to-all-start.7 = ((bf16[8,18,2048]{2,1,0:T(8,128)(2,1)}), bf16[8,18,2048]{2,1,0:T(8,128)(2,1)}, u32[]{:S(2)}, u32[]{:S(2)}) async-start(bf16[8,18,2048]{2,1,0:T(8,128)(2,1)} %reshape.678), calls=%async_computation.8 | async-start | bytes 1572864 | tf_op jit(solution)/shard_map/all_to_all | solution.py:244
  761.9 187.5 %all-gather.21.cloned.1.call-start = ((), (), s32[]{:S(2)}) async-start(), calls=%async_computation.25 | async-start | bytes 10027008 | tf_op jit(solution)/shard_map/all_gather | solution.py:223
  856.5 92.9 %copy-start.26 = (bf16[128,2048]{1,0:T(8,128)(2,1)S(1)}, bf16[128,2048]{1,0:T(8,128)(2,1)}, u32[]{:S(2)}) copy-start(bf16[128,2048]{1,0:T(8,128)(2,1)} %param.26) | copy-start | bytes 1572868
  980.1 14.5 %all-to-all-start.11 = ((bf16[16,144,128]{2,1,0:T(8,128)(2,1)}), bf16[16,144,128]{2,1,0:T(8,128)(2,1)S(1)}, u32[]{:S(2)}, u32[]{:S(2)}) async-start(bf16[16,144,128]{2,1,0:T(8,128)(2,1)} %copy.493), calls=%async_computation.12 | async-start | bytes 1179648 | tf_op jit(solution)/shard_map/all_to_all | solution.py:249
  994.7 64.1 %all-to-all-start.13 = ((bf16[8,1024,256]{2,1,0:T(8,128)(2,1)}), bf16[8,1024,256]{2,1,0:T(8,128)(2,1)}, u32[]{:S(2)}, u32[]{:S(2)}) async-start(bf16[8,1024,256]{2,1,0:T(8,128)(2,1)} %pad_maximum_fusion), calls=%async_computation.14 | async-start | bytes 8388608 | tf_op jit(solution)/shard_map/all_to_all | solution.py:498
  1058.8 23.4 %all-to-all-start.12 = ((bf16[8,18,2048]{2,1,0:T(8,128)(2,1)}), bf16[8,18,2048]{2,1,0:T(8,128)(2,1)}, u32[]{:S(2)}, u32[]{:S(2)}) async-start(bf16[8,18,2048]{2,1,0:T(8,128)(2,1)} %reshape.688), calls=%async_computation.13 | async-start | bytes 1572864 | tf_op jit(solution)/shard_map/all_to_all | solution.py:259
  1067.9 10.1 copy-start.4
  1082.2 5.8 copy-start.42
  1082.2 55.6 %all-to-all-start.14 = ((bf16[16,64,2048]{2,1,0:T(8,128)(2,1)}), bf16[16,64,2048]{2,1,0:T(8,128)(2,1)}, u32[]{:S(2)}, u32[]{:S(2)}) async-start(bf16[16,64,2048]{2,1,0:T(8,128)(2,1)} %bitcast.138), calls=%async_computation.15 | async-start | bytes 8388608 | tf_op jit(solution)/shard_map/all_to_all | solution.py:520
  1087.9 127.8 %reduce-scatter.5.cloned.1.call-start = ((), (), s32[]{:S(2)}) async-start(), calls=%async_computation.27 | async-start | bytes 3538944 | tf_op jit(solution)/shard_map/reduce_scatter | solution.py:554
  1100.0 40.8 %copy-start.14 = (bf16[128,2048]{1,0:T(8,128)(2,1)S(1)}, bf16[128,2048]{1,0:T(8,128)(2,1)}, u32[]{:S(2)}) copy-start(bf16[128,2048]{1,0:T(8,128)(2,1)} %param.21) | copy-start | bytes 1572868
  1100.0 40.8 %copy-start.29 = (f32[2048]{0:T(1024)S(1)}, f32[2048]{0:T(1024)}, u32[]{:S(2)}) copy-start(f32[2048]{0:T(1024)} %copy-done.28) | copy-start | bytes 24580
  1100.0 40.8 %copy-start.45 = (f32[64]{0:T(128)S(1)}, f32[64]{0:T(128)}, u32[]{:S(2)}) copy-start(f32[64]{0:T(128)} %copy-done.44) | copy-start | bytes 772
  1145.8 100.0 %all-gather.23.cloned.1.call-start = ((), (), s32[]{:S(2)}) async-start(), calls=%async_computation.26 | async-start | bytes 1572864 | tf_op jit(solution)/shard_map/all_gather | solution.py:570
  1147.3 9.4 copy-start.18
  1147.3 18.4 %slice-start = ((s8[9437184]{0:T(1024)(128)(4,1)}), s8[4194304]{0:T(1024)(128)(4,1)S(1)}, s32[]{:S(2)}) async-start(s8[9437184]{0:T(1024)(128)(4,1)} %bitcast.175), calls=%async_computation.28 | async-start | bytes 8388608
  1147.3 18.3 %slice-start.1 = ((s8[9437184]{0:T(1024)(128)(4,1)}), s8[4194304]{0:T(1024)(128)(4,1)S(1)}, s32[]{:S(2)}) async-start(s8[9437184]{0:T(1024)(128)(4,1)} %bitcast.175), calls=%async_computation.29 | async-start | bytes 8388608
  1156.7 8.9 copy-start.11
  1156.7 8.9 slice-start.2
  1173.7 6.2 copy-start.24
  1217.6 30.7 %all-to-all-start.15 = ((f32[16,16,384]{2,1,0:T(8,128)}), f32[16,16,384]{2,1,0:T(8,128)S(1)}, u32[]{:S(2)}, u32[]{:S(2)}) async-start(f32[16,16,384]{2,1,0:T(8,128)} %bitcast.42), calls=%async_computation.17 | async-start | bytes 786432 | tf_op jit(solution)/shard_map/all_to_all | solution.py:555
  1245.9 5.7 copy-start.1
  (27 other events, 60.6 us)
Sparse Core Ops, SparseCore 0:
  69.0 59.8 all-gather.10
  132.0 113.1 all-gather.8
  247.7 77.1 all-gather.12
  394.1 76.9 all-gather.14
  473.9 75.2 all-gather.18
  574.4 173.4 reduce-scatter.2
  750.5 85.5 all-gather.16
  873.3 76.0 all-gather.20
  1146.0 69.6 reduce-scatter.4
  1217.8 27.9 all-gather.22

commit v16 on v15

--- a/solution.py
+++ b/solution.py
@@ -394,6 +394,8 @@
     inverse_two = lax.rsqrt(jnp.mean(hidden_state * hidden_state, axis=-1, keepdims=True) + epsilon)
     normed_two = hidden_state * inverse_two
     mlp_input = (normed_two * gain_two.astype(jnp.float32)).astype(jnp.bfloat16)
+    query_high = lax.all_gather(query_weight[: width // 2], GROUP_AXES, axis=1, tiled=True)
+    mlp_input, query_high = lax.optimization_barrier((mlp_input, query_high))
     mlp_logits = jnp.dot(mlp_input, router_two, preferred_element_type=jnp.float32)
     mlp_gates = pair_gates(mlp_logits, own_mlp)
     mlp_index, mlp_pair_kept = pair_index(own_mlp, mlp_places, mlp_kept, slot_cap)
@@ -426,8 +428,8 @@
     inner_rows = (activated * up_pre).astype(jnp.bfloat16)
     mlp_partial = jnp.dot(inner_rows, down_weight, preferred_element_type=jnp.float32)
     mlp_slots = combine_scattered(mlp_partial)
-    query_stack = lax.all_gather(query_weight, GROUP_AXES, axis=1, tiled=True)
-    mlp_slots, query_stack = lax.optimization_barrier((mlp_slots, query_stack))
+    query_low = lax.all_gather(query_weight[width // 2 :], GROUP_AXES, axis=1, tiled=True)
+    mlp_slots, query_low = lax.optimization_barrier((mlp_slots, query_low))
     mlp_picked = mlp_slots.reshape(EXPERTS * slot_cap, width)[mlp_index]
     own_output = hidden_state + jnp.sum(
         mlp_picked * (mlp_gates * mlp_pair_kept)[:, :, None], axis=1
@@ -490,9 +492,14 @@
     query_grad = jnp.einsum(
         "rd,rw->dw", attn_rows, query_rot_grad, preferred_element_type=jnp.float32
     )
+    query_rows = to_rows(query_rot_grad)
     attn_row_grad = to_owners(
-        jnp.einsum(
-            "rw,dw->rd", to_rows(query_rot_grad), query_stack, preferred_element_type=jnp.float32
+        jnp.concatenate(
+            [
+                jnp.einsum("rw,dw->rd", query_rows, query_high, preferred_element_type=jnp.float32),
+                jnp.einsum("rw,dw->rd", query_rows, query_low, preferred_element_type=jnp.float32),
+            ],
+            axis=1,
         )
     )
     pair_back = lax.all_to_all(

time: 1270 us -> 1290 us (1.016)
  waiting for transfers between devices: 614 us -> 767 us
  blocking collectives: 203 us -> 67.7 us
    all_to_all x1 -> x0, blocking collectives: 136 us -> none  [combine(): lax.all_to_all(partial_value.astype(jnp.bfloat16).reshape(group_size, gro...]
    all_to_all x0 -> x1, waiting for transfers between devices: none -> 127 us  [combine(): lax.all_to_all(partial_value.astype(jnp.bfloat16).reshape(group_size, gro...]
    reduce_scatter x1, waiting for transfers between devices: 1.82 us -> 27.4 us  [combine_scattered(): lax.psum_scatter(partial_value.astype(jnp.bfloat16), GROUP_AXES, scatter_...]
    all_gather x1 -> x2, waiting for transfers between devices: 58.9 us -> 72.3 us  [the longest x1 41.7 us: shards(): lax.all_gather(query_weight[width // 2:], GROUP_AXES, axis=1, tiled=True)]
  transfers between devices with their start and end apart: 21 -> 23, of which waited for: 18 -> 19; matrix products, arithmetic and copies ran while one was open for 17% -> 19% of each run, Pallas kernels for 1% -> 1%
where the time goes in v16:
time: 1290 us; the launch traced here: 1280 us
  waiting for transfers between devices  767 us (59%)
  matrix products  143 us (11%)
  local copies, waits for them, and re-layouts  127 us (10%)
  other arithmetic  82.4 us (6%)
  blocking collectives  67.7 us (5%)
  starting transfers between devices  57.9 us (4%)
  Pallas kernels  24.6 us (2%)
  between operations  15.4 us (1%)
    all_to_all x1, waiting for transfers between devices, combine(): lax.all_to_all(partial_value.astype(jnp.bfloat16).reshape(group_size, gro...  127 us
    all_gather x2, waiting for transfers between devices, dispatch(): lax.all_gather(by_group.reshape(groups * slot_cap, width), GROUP_AXES, ax...  118 us
    all_gather x1, waiting for transfers between devices, shards(): lax.all_gather(mlp_by_group[:, :slot_cap].reshape(groups * slot_cap, widt...  74.1 us
    all_gather x1, waiting for transfers between devices, shards(): lax.all_gather(mlp_by_group[:, slot_cap:].reshape(groups * slot_cap, widt...  68.9 us
    all_to_all x1, waiting for transfers between devices, shards(): lax.all_to_all(jnp.concatenate([seq_key_grad, seq_value_grad], axis=2).as...  51.6 us
    all_gather x1, waiting for transfers between devices, shards(): lax.all_gather(query_weight[width // 2:], GROUP_AXES, axis=1, tiled=True)  41.7 us
    all_gather x1, waiting for transfers between devices, shards(): seq_input = lax.all_gather(attn_input, GROUP_AXES, axis=0, tiled=True)  40 us
    all_to_all x1, waiting for transfers between devices, shards(): lax.all_to_all(jnp.einsum('rc,dc->rd', kv_col_grad, head_kv, preferred_el...  37.1 us
  transfers between devices with their start and end apart: 23, of which 19 were waited for; matrix products, arithmetic and copies ran while one was open for 19% of the time, Pallas kernels for 1%

profile of v16, /device:TPU:1, one launch (start us, length us, event | category | flops | bytes accessed | tf_op | source)
XLA Modules:
  0.0 1284.7 jit_solution(16075063236767260581)
XLA Ops:
  17.3 17.5 %all_to_all.80 = bf16[16,16,384]{2,1,0:T(8,128)(2,1)S(1)} all-to-all(bf16[16,16,384]{2,1,0:T(8,128)(2,1)S(1)} %pad_maximum_fusion.11), channel_id=1, replica_groups=mesh['grp'=8,'sub'=8,'expert'=2] {'sub','expert'}, dimensions={0} | all-to-all | bytes 393216 | tf_op jit(solution)/shard_map/all_to_all | solution.py:303
  40.9 23.2 %all-to-all-done.1 = bf16[8,256,384]{1,2,0:T(8,128)(2,1)} async-done(((bf16[8,256,384]{1,2,0:T(8,128)(2,1)}), bf16[8,256,384]{1,2,0:T(8,128)(2,1)}, u32[]{:S(2)}, u32[]{:S(2)}) %all-to-all-start.1) | async-done | bytes 1572896 | tf_op jit(solution)/shard_map/all_to_all | solution.py:316
  72.3 13.5 %all_to_all.81 = bf16[8,18,2048]{2,1,0:T(8,128)(2,1)S(1)} all-to-all(bf16[8,18,2048]{2,1,0:T(8,128)(2,1)S(1)} %broadcast_select_fusion.1), channel_id=1, replica_groups=mesh['grp'=8,'sub'=8,'expert'=2] {'grp'}, dimensions={0} | all-to-all | bytes 1179648 | tf_op jit(solution)/shard_map/all_to_all | solution.py:222
  87.6 40.0 %all-gather.12.cloned.1.call-done = bf16[1024,2048]{1,0:T(8,128)(2,1)} async-done(((bf16[64,2048]{1,0:T(8,128)(2,1)}), bf16[1024,2048]{1,0:T(8,128)(2,1)}) %all-gather.12.cloned.1.call-update) | async-done | bytes 4194320 | tf_op jit(solution)/shard_map/all_gather | solution.py:336
  135.1 4.8 all-to-all-start.3
  156.3 5.6 multiply_reduce_fusion
  168.3 31.0 %all-to-all-done.3 = bf16[8,1024,256]{2,1,0:T(8,128)(2,1)} async-done(((bf16[8,1024,256]{2,1,0:T(8,128)(2,1)}), bf16[8,1024,256]{2,1,0:T(8,128)(2,1)}, u32[]{:S(2)}, u32[]{:S(2)}) %all-to-all-start.3) | async-done | bytes 4194336 | tf_op jit(solution)/shard_map/all_to_all | solution.py:348
  203.8 41.8 %all-gather.10.cloned.1.call-done = bf16[2304,2048]{1,0:T(8,128)(2,1)} async-done(((bf16[144,2048]{1,0:T(8,128)(2,1)}), bf16[2304,2048]{1,0:T(8,128)(2,1)}) %all-gather.10.cloned.1.call-update) | async-done | bytes 9437200 | tf_op jit(solution)/shard_map/all_gather | solution.py:223
  245.7 7.4 fusion.95
  260.6 7.9 fusion.20
  269.7 10.8 shard_map.238
  292.9 32.4 %all-gather.14.cloned.1.call-done = bf16[2048,2048]{1,0:T(8,128)(2,1)} async-done(((bf16[128,2048]{1,0:T(8,128)(2,1)}), bf16[2048,2048]{1,0:T(8,128)(2,1)}) %all-gather.14.cloned.1.call-update) | async-done | bytes 8388624 | tf_op jit(solution)/shard_map/all_gather | solution.py:384
  325.3 5.7 convolution_convert_fusion.3
  340.1 9.2 all-to-all-done.5
  360.2 30.6 %all-gather.16.cloned.1.call-done = bf16[1024,2048]{1,0:T(8,128)(2,1)} async-done(((bf16[1024,128]{1,0:T(8,128)(2,1)}), bf16[1024,2048]{1,0:T(8,128)(2,1)}) %all-gather.16.cloned.1.call-update) | async-done | bytes 4194320 | tf_op jit(solution)/shard_map/all_gather | solution.py:397
  402.4 21.0 %all_to_all.82 = bf16[8,36,2048]{2,1,0:T(8,128)(2,1)S(1)} all-to-all(bf16[8,36,2048]{2,1,0:T(8,128)(2,1)S(1)} %pad_maximum_fusion.2), channel_id=1, replica_groups=mesh['grp'=8,'sub'=8,'expert'=2] {'grp'}, dimensions={0} | all-to-all | bytes 2359296 | tf_op jit(solution)/shard_map/all_to_all | solution.py:406
  429.1 74.1 %all-gather.18.cloned.1.call-done = bf16[2304,2048]{1,0:T(8,128)(2,1)} async-done(((bf16[144,2048]{1,0:T(8,128)(2,1)}), bf16[2304,2048]{1,0:T(8,128)(2,1)}) %all-gather.18.cloned.1.call-update) | async-done | bytes 9437200 | tf_op jit(solution)/shard_map/all_gather | solution.py:413
  503.3 9.3 fusion.96
  512.5 68.9 %all-gather.22.cloned.1.call-done = bf16[2304,2048]{1,0:T(8,128)(2,1)} async-done(((bf16[144,2048]{1,0:T(8,128)(2,1)}), bf16[2304,2048]{1,0:T(8,128)(2,1)}) %all-gather.22.cloned.1.call-update) | async-done | bytes 9437200 | tf_op jit(solution)/shard_map/all_gather | solution.py:419
  581.4 7.2 fusion.97
  589.2 8.6 multiply_convert_fusion.2
  599.0 7.5 convolution_convert_fusion
  606.5 12.4 fusion.98
  618.8 13.2 %add_convert_fusion = bf16[2304,2048]{1,0:T(8,128)(2,1)} fusion(f32[2304,2048]{1,0:T(8,128)} %fusion.98, bf16[2304,352]{0,1:T(8,128)(2,1)S(1)} %copy-done.7, bf16[2048,352]{0,1:T(8,128)(2,1)S(1)} %copy-done), kind=kOutput, calls=%fused_computation.16 | convolution fusion | flops 3331325952 | bytes 31375360 | tf_op jit(solution)/shard_map/rf,df->rd/dot_general | solution.py:450
  632.0 4.8 all-to-all-start.8
  637.5 127.2 %all-to-all-done.8 = bf16[16,144,2048]{2,1,0:T(8,128)(2,1)} async-done(((bf16[16,144,2048]{2,1,0:T(8,128)(2,1)}), bf16[16,144,2048]{2,1,0:T(8,128)(2,1)}, u32[]{:S(2)}, u32[]{:S(2)}) %all-to-all-start.8) | async-done | bytes 9437216 | tf_op jit(solution)/shard_map/all_to_all | solution.py:228
  764.8 5.8 reduce_sum.342
  775.7 27.4 %reduce-scatter.3.cloned.1.call-done = bf16[144,2048]{1,0:T(8,128)(2,1)} async-done(((bf16[2304,2048]{1,0:T(8,128)(2,1)}), bf16[144,2048]{1,0:T(8,128)(2,1)}) %reduce-scatter.3.cloned.1.call-update) | async-done | bytes 589840 | tf_op jit(solution)/shard_map/reduce_scatter | solution.py:241
  823.7 41.7 %all-gather.20.cloned.1.call-done = bf16[1024,2048]{1,0:T(8,128)(2,1)} async-done(((bf16[1024,128]{1,0:T(8,128)(2,1)}), bf16[1024,2048]{1,0:T(8,128)(2,1)}) %all-gather.20.cloned.1.call-update) | async-done | bytes 4194320 | tf_op jit(solution)/shard_map/all_gather | solution.py:431
  885.5 15.8 %all_to_all.83 = bf16[8,18,2048]{2,1,0:T(8,128)(2,1)S(1)} all-to-all(bf16[8,18,2048]{2,1,0:T(8,128)(2,1)S(1)} %multiply_convert_fusion.3), channel_id=1, replica_groups=mesh['grp'=8,'sub'=8,'expert'=2] {'grp'}, dimensions={0} | all-to-all | bytes 1179648 | tf_op jit(solution)/shard_map/all_to_all | solution.py:222
  902.3 76.4 %all-gather.24.cloned.1.call-done = bf16[2304,2048]{1,0:T(8,128)(2,1)} async-done(((bf16[144,2048]{1,0:T(8,128)(2,1)}), bf16[2304,2048]{1,0:T(8,128)(2,1)}) %all-gather.24.cloned.1.call-update) | async-done | bytes 9437200 | tf_op jit(solution)/shard_map/all_gather | solution.py:223
  978.7 6.3 convolution_convert_fusion.2
  986.2 13.7 %shard_map.239 = (f32[8,288,128]{2,1,0:T(8,128)}, f32[8,1024,128]{2,1,0:T(8,128)}, f32[8,1024,128]{2,1,0:T(8,128)}) custom-call(bf16[8,288,128]{2,1,0:T(8,128)(2,1)} %pad_maximum_fusion.4.q_ref, bf16[8,1024,128]{2,1,0:T(8,128)(2,1)} %bitcast.154, bf16[8,1024,128]{2,1,0:T(8,128)(2,1)} %bitcast.152, s32[8,288,1]{2,1,0:T(8,128)} %add_select_fusion.qb_ref, ...), custom_call_target="tpu_custom_call" | custom-call | flops 3019898880 | bytes 25100288 | tf_op jit(solution)/shard_map/pallas_call | solution.py:76
  999.9 7.9 fusion.24
  1021.1 4.7 all-to-all-done.11
  1038.3 51.6 %all-to-all-done.13 = bf16[8,1024,256]{2,1,0:T(8,128)(2,1)} async-done(((bf16[8,1024,256]{2,1,0:T(8,128)(2,1)}), bf16[8,1024,256]{2,1,0:T(8,128)(2,1)}, u32[]{:S(2)}, u32[]{:S(2)}) %all-to-all-start.13) | async-done | bytes 4194336 | tf_op jit(solution)/shard_map/all_to_all | solution.py:505
  1104.0 4.6 convolution_convert_fusion.1
  1108.6 5.6 all-to-all-start.14
  1122.2 4.8 fusion.61
  1127.0 37.1 %all-to-all-done.14 = bf16[16,64,2048]{2,1,0:T(8,128)(2,1)} async-done(((bf16[16,64,2048]{2,1,0:T(8,128)(2,1)}), bf16[16,64,2048]{2,1,0:T(8,128)(2,1)}, u32[]{:S(2)}, u32[]{:S(2)}) %all-to-all-start.14) | async-done | bytes 4194336 | tf_op jit(solution)/shard_map/all_to_all | solution.py:527
  1175.6 9.4 fusion.103
  1185.0 9.1 fusion.104
  1194.1 5.1 fusion.105
  1203.7 6.2 fusion.102
  1209.9 7.4 fusion.101
  1217.3 24.7 %reduce-scatter.5.cloned.1.call-done = f32[256,384]{0,1:T(8,128)} async-done(((f32[2048,384]{0,1:T(8,128)}), f32[256,384]{0,1:T(8,128)}) %reduce-scatter.5.cloned.1.call-update) | async-done | bytes 393232 | tf_op jit(solution)/shard_map/reduce_scatter | solution.py:561
  1243.9 8.3 all-to-all-start.15
  1252.2 20.0 %all-gather.26.cloned.1.call-done = bf16[128,4096]{1,0:T(8,128)(2,1)} async-done(((bf16[64,4096]{1,0:T(8,128)(2,1)}), bf16[128,4096]{1,0:T(8,128)(2,1)}) %all-gather.26.cloned.1.call-update) | async-done | bytes 1048592 | tf_op jit(solution)/shard_map/all_gather | solution.py:577
  (374 shorter events, 240.1 us)
Async XLA Ops:
  7.2 581.5 %copy-start = (bf16[2048,352]{0,1:T(8,128)(2,1)S(1)}, bf16[2048,352]{0,1:T(8,128)(2,1)}, u32[]{:S(2)}) copy-start(bf16[2048,352]{0,1:T(8,128)(2,1)} %param.30) | copy-start | bytes 4325380
  36.2 4.5 copy-start.9
  36.2 27.9 %all-to-all-start.1 = ((bf16[8,256,384]{1,2,0:T(8,128)(2,1)}), bf16[8,256,384]{1,2,0:T(8,128)(2,1)}, u32[]{:S(2)}, u32[]{:S(2)}) async-start(bf16[8,256,384]{1,2,0:T(8,128)(2,1)} %broadcast_in_dim.57), calls=%async_computation.1 | async-start | bytes 3145728 | tf_op jit(solution)/shard_map/all_to_all | solution.py:316
  40.6 86.9 %all-gather.12.cloned.1.call-start = ((), (), s32[]{:S(2)}) async-start(), calls=%async_computation.19 | async-start | bytes 4456448 | tf_op jit(solution)/shard_map/all_gather | solution.py:336
  40.9 27.6 %copy-start.37 = (f32[64]{0:T(128)}, f32[64]{0:T(128)S(1)}, u32[]{:S(2)}) copy-start(f32[64]{0:T(128)S(1)} %add_rsqrt_fusion.1) | copy-start | bytes 772
  69.3 176.3 %all-gather.10.cloned.1.call-start = ((), (), s32[]{:S(2)}) async-start(), calls=%async_computation.18 | async-start | bytes 10027008 | tf_op jit(solution)/shard_map/all_gather | solution.py:223
  86.8 238.5 %all-gather.14.cloned.1.call-start = ((), (), s32[]{:S(2)}) async-start(), calls=%async_computation.20 | async-start | bytes 8912896 | tf_op jit(solution)/shard_map/all_gather | solution.py:384
  87.6 43.9 %copy-start.33 = (f32[1024]{0:T(1024)}, f32[1024]{0:T(1024)S(1)}, u32[]{:S(2)}) copy-start(f32[1024]{0:T(1024)S(1)} %iota_convert_fusion) | copy-start | bytes 12292
  135.1 4.8 copy-start.23
  135.1 64.2 %all-to-all-start.3 = ((bf16[8,1024,256]{2,1,0:T(8,128)(2,1)}), bf16[8,1024,256]{2,1,0:T(8,128)(2,1)}, u32[]{:S(2)}, u32[]{:S(2)}) async-start(bf16[8,1024,256]{2,1,0:T(8,128)(2,1)} %broadcast_in_dim.66), calls=%async_computation.3 | async-start | bytes 8388608 | tf_op jit(solution)/shard_map/all_to_all | solution.py:348
  139.9 250.9 %all-gather.16.cloned.1.call-start = ((), (), s32[]{:S(2)}) async-start(), calls=%async_computation.21 | async-start | bytes 4456448 | tf_op jit(solution)/shard_map/all_gather | solution.py:397
  283.1 42.2 %all-to-all-start.4 = ((bf16[16,144,128]{2,1,0:T(8,128)(2,1)}), bf16[16,144,128]{2,1,0:T(8,128)(2,1)S(1)}, u32[]{:S(2)}, u32[]{:S(2)}) async-start(bf16[16,144,128]{2,1,0:T(8,128)(2,1)} %copy.493), calls=%async_computation.4 | async-start | bytes 1179648 | tf_op jit(solution)/shard_map/all_to_all | solution.py:249
  333.1 16.2 %all-to-all-start.5 = ((bf16[8,18,2048]{2,1,0:T(8,128)(2,1)}), bf16[8,18,2048]{2,1,0:T(8,128)(2,1)S(1)}, u32[]{:S(2)}, u32[]{:S(2)}) async-start(bf16[8,18,2048]{2,1,0:T(8,128)(2,1)} %reshape.676), calls=%async_computation.5 | async-start | bytes 1572864 | tf_op jit(solution)/shard_map/all_to_all | solution.py:259
  337.1 166.2 %all-gather.18.cloned.1.call-start = ((), (), s32[]{:S(2)}) async-start(), calls=%async_computation.22 | async-start | bytes 10027008 | tf_op jit(solution)/shard_map/all_gather | solution.py:413
  426.9 154.6 %all-gather.22.cloned.1.call-start = ((), (), s32[]{:S(2)}) async-start(), calls=%async_computation.25 | async-start | bytes 10027008 | tf_op jit(solution)/shard_map/all_gather | solution.py:419
  429.1 374.0 %reduce-scatter.3.cloned.1.call-start = ((), (), s32[]{:S(2)}) async-start(), calls=%async_computation.23 | async-start | bytes 10027008 | tf_op jit(solution)/shard_map/reduce_scatter | solution.py:241
  581.4 7.3 copy-start.40
  581.4 7.8 copy-start.43
  589.2 9.7 copy-start.42
  606.5 12.4 copy-start.7
  632.0 132.7 %all-to-all-start.8 = ((bf16[16,144,2048]{2,1,0:T(8,128)(2,1)}), bf16[16,144,2048]{2,1,0:T(8,128)(2,1)}, u32[]{:S(2)}, u32[]{:S(2)}) async-start(bf16[16,144,2048]{2,1,0:T(8,128)(2,1)} %bitcast.141), calls=%async_computation.9 | async-start | bytes 18874368 | tf_op jit(solution)/shard_map/all_to_all | solution.py:228
  636.8 228.6 %all-gather.20.cloned.1.call-start = ((), (), s32[]{:S(2)}) async-start(), calls=%async_computation.24 | async-start | bytes 4456448 | tf_op jit(solution)/shard_map/all_gather | solution.py:431
  771.6 33.6 %all-to-all-start.9 = ((bf16[8,18,2048]{2,1,0:T(8,128)(2,1)}), bf16[8,18,2048]{2,1,0:T(8,128)(2,1)S(1)}, u32[]{:S(2)}, u32[]{:S(2)}) async-start(bf16[8,18,2048]{2,1,0:T(8,128)(2,1)} %convert_element_type.230), calls=%async_computation.10 | async-start | bytes 1572864 | tf_op jit(solution)/shard_map/all_to_all | solution.py:236
  775.7 34.2 %copy-start.32 = (s32[8,18,1]{0,1,2:T(8,128)S(1)}, s32[8,18,1]{0,1,2:T(8,128)}, u32[]{:S(2)}) copy-start(s32[8,18,1]{0,1,2:T(8,128)} %get-tuple-element.180) | copy-start | bytes 1732
  775.7 34.4 %copy-start.39 = (s32[64,2]{0,1:T(2,128)S(1)}, s32[64,2]{0,1:T(2,128)}, u32[]{:S(2)}) copy-start(s32[64,2]{0,1:T(2,128)} %get-tuple-element.190) | copy-start | bytes 1540
  805.3 5.1 copy-start.12
  805.3 16.0 %all-to-all-start.7 = ((bf16[8,18,2048]{2,1,0:T(8,128)(2,1)}), bf16[8,18,2048]{2,1,0:T(8,128)(2,1)}, u32[]{:S(2)}, u32[]{:S(2)}) async-start(bf16[8,18,2048]{2,1,0:T(8,128)(2,1)} %reshape.680), calls=%async_computation.8 | async-start | bytes 1572864 | tf_op jit(solution)/shard_map/all_to_all | solution.py:244
  809.8 168.9 %all-gather.24.cloned.1.call-start = ((), (), s32[]{:S(2)}) async-start(), calls=%async_computation.26 | async-start | bytes 10027008 | tf_op jit(solution)/shard_map/all_gather | solution.py:223
  901.3 77.4 %copy-start.24 = (bf16[128,2048]{1,0:T(8,128)(2,1)S(1)}, bf16[128,2048]{1,0:T(8,128)(2,1)}, u32[]{:S(2)}) copy-start(bf16[128,2048]{1,0:T(8,128)(2,1)} %param.26) | copy-start | bytes 1572868
  1011.3 14.5 %all-to-all-start.11 = ((bf16[16,144,128]{2,1,0:T(8,128)(2,1)}), bf16[16,144,128]{2,1,0:T(8,128)(2,1)S(1)}, u32[]{:S(2)}, u32[]{:S(2)}) async-start(bf16[16,144,128]{2,1,0:T(8,128)(2,1)} %copy.527), calls=%async_computation.12 | async-start | bytes 1179648 | tf_op jit(solution)/shard_map/all_to_all | solution.py:249
  1025.8 64.1 %all-to-all-start.13 = ((bf16[8,1024,256]{2,1,0:T(8,128)(2,1)}), bf16[8,1024,256]{2,1,0:T(8,128)(2,1)}, u32[]{:S(2)}, u32[]{:S(2)}) async-start(bf16[8,1024,256]{2,1,0:T(8,128)(2,1)} %pad_maximum_fusion), calls=%async_computation.14 | async-start | bytes 8388608 | tf_op jit(solution)/shard_map/all_to_all | solution.py:505
  1089.9 18.7 %all-to-all-start.12 = ((bf16[8,18,2048]{2,1,0:T(8,128)(2,1)}), bf16[8,18,2048]{2,1,0:T(8,128)(2,1)}, u32[]{:S(2)}, u32[]{:S(2)}) async-start(bf16[8,18,2048]{2,1,0:T(8,128)(2,1)} %pad_maximum_fusion.3), calls=%async_computation.13 | async-start | bytes 1572864 | tf_op jit(solution)/shard_map/all_to_all | solution.py:259
  1104.0 4.6 copy-start.18
  1108.6 55.4 %all-to-all-start.14 = ((bf16[16,64,2048]{2,1,0:T(8,128)(2,1)}), bf16[16,64,2048]{2,1,0:T(8,128)(2,1)}, u32[]{:S(2)}, u32[]{:S(2)}) async-start(bf16[16,64,2048]{2,1,0:T(8,128)(2,1)} %bitcast.142), calls=%async_computation.15 | async-start | bytes 8388608 | tf_op jit(solution)/shard_map/all_to_all | solution.py:527
  1114.2 127.8 %reduce-scatter.5.cloned.1.call-start = ((), (), s32[]{:S(2)}) async-start(), calls=%async_computation.28 | async-start | bytes 3538944 | tf_op jit(solution)/shard_map/reduce_scatter | solution.py:561
  1126.9 40.1 %copy-start.11 = (bf16[128,2048]{1,0:T(8,128)(2,1)S(1)}, bf16[128,2048]{1,0:T(8,128)(2,1)}, u32[]{:S(2)}) copy-start(bf16[128,2048]{1,0:T(8,128)(2,1)} %param.21) | copy-start | bytes 1572868
  1126.9 40.1 %copy-start.17 = (f32[64,2048]{1,0:T(8,128)S(1)}, f32[64,2048]{1,0:T(8,128)}, u32[]{:S(2)}) copy-start(f32[64,2048]{1,0:T(8,128)} %multiply_reduce_fusion.3) | copy-start | bytes 1572868
  1126.9 40.1 %copy-start.26 = (f32[2048]{0:T(1024)S(1)}, f32[2048]{0:T(1024)}, u32[]{:S(2)}) copy-start(f32[2048]{0:T(1024)} %copy-done.25) | copy-start | bytes 24580
  1126.9 40.1 %copy-start.38 = (f32[64]{0:T(128)S(1)}, f32[64]{0:T(128)}, u32[]{:S(2)}) copy-start(f32[64]{0:T(128)} %copy-done.37) | copy-start | bytes 772
  1172.2 100.0 %all-gather.26.cloned.1.call-start = ((), (), s32[]{:S(2)}) async-start(), calls=%async_computation.27 | async-start | bytes 1572864 | tf_op jit(solution)/shard_map/all_gather | solution.py:577
  1175.6 9.4 copy-start.14
  1175.6 18.5 %slice-start = ((s8[9437184]{0:T(1024)(128)(4,1)}), s8[4194304]{0:T(1024)(128)(4,1)S(1)}, s32[]{:S(2)}) async-start(s8[9437184]{0:T(1024)(128)(4,1)} %bitcast.180), calls=%async_computation.29 | async-start | bytes 8388608
  1175.6 18.5 %slice-start.1 = ((s8[9437184]{0:T(1024)(128)(4,1)}), s8[4194304]{0:T(1024)(128)(4,1)S(1)}, s32[]{:S(2)}) async-start(s8[9437184]{0:T(1024)(128)(4,1)} %bitcast.180), calls=%async_computation.30 | async-start | bytes 8388608
  1185.0 9.1 copy-start.8
  1185.0 9.1 slice-start.2
  1203.7 6.2 copy-start.22
  1243.9 30.7 %all-to-all-start.15 = ((f32[16,16,384]{2,1,0:T(8,128)}), f32[16,16,384]{2,1,0:T(8,128)S(1)}, u32[]{:S(2)}, u32[]{:S(2)}) async-start(f32[16,16,384]{2,1,0:T(8,128)} %bitcast.44), calls=%async_computation.17 | async-start | bytes 786432 | tf_op jit(solution)/shard_map/all_to_all | solution.py:562
  1272.2 5.7 copy-start.1
  (23 other events, 55.0 us)
Sparse Core Ops, SparseCore 0:
  69.4 58.0 all-gather.11
  130.6 114.9 all-gather.9
  248.1 77.1 all-gather.13
  328.0 62.7 all-gather.15
  427.0 76.2 all-gather.17
  506.2 75.2 all-gather.21
  606.6 196.4 reduce-scatter.2
  806.2 59.1 all-gather.19
  902.4 76.2 all-gather.23
  1172.3 69.6 reduce-scatter.4
  1244.3 27.7 all-gather.25

commit v17 on v15

--- a/solution.py
+++ b/solution.py
@@ -37,16 +37,17 @@
                          preferred_element_type=jnp.float32).astype(o_ref.dtype)
     lse_ref[...] = largest + jnp.log(totals)
 
-def _bwd_kernel(scale, q_ref, k_ref, v_ref, qb_ref, lse_ref, do_ref, dq_ref, dk_ref, dv_ref):
+def _bwd_kernel(scale, q_ref, k_ref, v_ref, qb_ref, lse_ref, do_ref, dq_ref, dkv_ref):
     q = q_ref[...]; k = k_ref[...]; v = v_ref[...]; do = do_ref[...]
     probs = jnp.exp(_scores(q, k, qb_ref[...], scale) - lse_ref[...])
     dp = lax.dot_general(do, v, (((1,), (1,)), ((), ())), preferred_element_type=jnp.float32)
     inner = jnp.sum(probs * dp, axis=-1, keepdims=True)
     ds = (probs * (dp - inner)).astype(jnp.bfloat16)
-    dv_ref[...] = lax.dot_general(probs.astype(jnp.bfloat16), do, (((0,), (0,)), ((), ())),
-                                  preferred_element_type=jnp.float32)
-    dk_ref[...] = lax.dot_general(ds, q, (((0,), (0,)), ((), ())),
-                                  preferred_element_type=jnp.float32) * scale
+    d = q.shape[1]
+    dkv_ref[:, d:] = lax.dot_general(probs.astype(jnp.bfloat16), do, (((0,), (0,)), ((), ())),
+                                     preferred_element_type=jnp.float32).astype(dkv_ref.dtype)
+    dkv_ref[:, :d] = (lax.dot_general(ds, q, (((0,), (0,)), ((), ())),
+                                      preferred_element_type=jnp.float32) * scale).astype(dkv_ref.dtype)
     dq_ref[...] = jnp.dot(ds, k, preferred_element_type=jnp.float32) * scale
 
 def attn_fwd(q, k, v, qb):
@@ -77,10 +78,9 @@
         functools.partial(_bwd_kernel, scale),
         grid=(n,),
         in_specs=[rspec, kspec, kspec, cspec, cspec, rspec],
-        out_specs=[rspec, kspec, kspec],
+        out_specs=[rspec, pl.BlockSpec((None, keys, 2 * d), lambda i: (i, 0, 0))],
         out_shape=[jax.ShapeDtypeStruct((n, rows, d), jnp.float32),
-                   jax.ShapeDtypeStruct((n, keys, d), jnp.float32),
-                   jax.ShapeDtypeStruct((n, keys, d), jnp.float32)],
+                   jax.ShapeDtypeStruct((n, keys, 2 * d), jnp.bfloat16)],
         cost_estimate=pl.CostEstimate(flops=10 * n * rows * keys * d,
                                       transcendentals=n * rows * keys,
                                       bytes_accessed=2 * n * (3 * rows * d + 2 * keys * d) + 8 * n * (rows * d + 2 * keys * d)),
@@ -474,7 +474,7 @@
     ).astype(jnp.bfloat16)
     seq_mixed_grad = to_gj(mixed_grad).reshape(sequences, seq_rows, local_heads, HEAD)
 
-    seq_query_grad, seq_key_grad, seq_value_grad = attn_bwd(
+    seq_query_grad, seq_pair_back = attn_bwd(
         seq_queries.reshape(sequences, seq_rows, HEAD),
         seq_keys.reshape(sequences, seq_length, HEAD),
         seq_values.reshape(sequences, seq_length, HEAD),
@@ -496,7 +496,7 @@
         )
     )
     pair_back = lax.all_to_all(
-        jnp.concatenate([seq_key_grad, seq_value_grad], axis=2).astype(jnp.bfloat16),
+        seq_pair_back,
         "grp",
         split_axis=0,
         concat_axis=0,

time: 1270 us -> 1270 us (level)
  blocking collectives: 203 us -> 218 us
    all_to_all x0 -> x1, blocking collectives: none -> 15.6 us  [to_rows(): lax.all_to_all(per_head.reshape(group_size, groups * slot_cap, head_cols)...]
  transfers between devices with their start and end apart: 21 -> 20, of which waited for: 18 -> 17; matrix products, arithmetic and copies ran while one was open for 17% -> 17% of each run, Pallas kernels for 1% -> 1%
where the time goes in v17:
time: 1270 us; the launch traced here: 1260 us
  waiting for transfers between devices  606 us (48%)
  blocking collectives  218 us (17%)
  matrix products  142 us (11%)
  local copies, waits for them, and re-layouts  129 us (10%)
  other arithmetic  73.5 us (6%)
  starting transfers between devices  50 us (4%)
  Pallas kernels  24.1 us (2%)
  between operations  16 us (1%)
    all_to_all x1, blocking collectives, combine(): lax.all_to_all(partial_value.astype(jnp.bfloat16).reshape(group_size, gro...  136 us
    all_gather x2, waiting for transfers between devices, dispatch(): lax.all_gather(by_group.reshape(groups * slot_cap, width), GROUP_AXES, ax...  113 us
    all_gather x1, waiting for transfers between devices, shards(): lax.all_gather(mlp_by_group[:, :slot_cap].reshape(groups * slot_cap, widt...  74.7 us
    all_gather x1, waiting for transfers between devices, shards(): lax.all_gather(mlp_by_group[:, slot_cap:].reshape(groups * slot_cap, widt...  68.9 us
    all_gather x1, waiting for transfers between devices, shards(): query_stack = lax.all_gather(query_weight, GROUP_AXES, axis=1, tiled=True)  58.9 us
    all_to_all x1, waiting for transfers between devices, shards(): lax.all_to_all(seq_pair_back, 'grp', split_axis=0, concat_axis=0, tiled=T...  51.7 us
    all_gather x1, waiting for transfers between devices, shards(): output_stack = lax.all_gather(output_weight, GROUP_AXES, axis=0, tiled=True)  38.7 us
    all_gather x1, waiting for transfers between devices, shards(): seq_input = lax.all_gather(attn_input, GROUP_AXES, axis=0, tiled=True)  36.3 us
  transfers between devices with their start and end apart: 20, of which 17 were waited for; matrix products, arithmetic and copies ran while one was open for 17% of the time, Pallas kernels for 1%

profile of v17, /device:TPU:1, one launch (start us, length us, event | category | flops | bytes accessed | tf_op | source)
XLA Modules:
  0.0 1258.2 jit_solution(9408474715993202786)
XLA Ops:
  17.3 17.5 %all_to_all.80 = bf16[16,16,384]{2,1,0:T(8,128)(2,1)S(1)} all-to-all(bf16[16,16,384]{2,1,0:T(8,128)(2,1)S(1)} %pad_maximum_fusion.9), channel_id=1, replica_groups=mesh['grp'=8,'sub'=8,'expert'=2] {'sub','expert'}, dimensions={0} | all-to-all | bytes 393216 | tf_op jit(solution)/shard_map/all_to_all | solution.py:303
  40.9 23.2 %all-to-all-done.1 = bf16[8,256,384]{1,2,0:T(8,128)(2,1)} async-done(((bf16[8,256,384]{1,2,0:T(8,128)(2,1)}), bf16[8,256,384]{1,2,0:T(8,128)(2,1)}, u32[]{:S(2)}, u32[]{:S(2)}) %all-to-all-start.1) | async-done | bytes 1572896 | tf_op jit(solution)/shard_map/all_to_all | solution.py:316
  75.8 13.9 %all_to_all.81 = bf16[8,18,2048]{2,1,0:T(8,128)(2,1)} all-to-all(bf16[8,18,2048]{2,1,0:T(8,128)(2,1)S(1)} %broadcast_select_fusion.1), channel_id=1, replica_groups=mesh['grp'=8,'sub'=8,'expert'=2] {'grp'}, dimensions={0} | all-to-all | bytes 1179648 | tf_op jit(solution)/shard_map/all_to_all | solution.py:222
  92.6 36.3 %all-gather.11.cloned.1.call-done = bf16[1024,2048]{1,0:T(8,128)(2,1)} async-done(((bf16[64,2048]{1,0:T(8,128)(2,1)}), bf16[1024,2048]{1,0:T(8,128)(2,1)}) %all-gather.11.cloned.1.call-update) | async-done | bytes 4194320 | tf_op jit(solution)/shard_map/all_gather | solution.py:336
  139.8 4.8 all-to-all-start.3
  158.9 5.6 multiply_reduce_fusion
  170.5 33.5 %all-to-all-done.3 = bf16[8,1024,256]{2,1,0:T(8,128)(2,1)} async-done(((bf16[8,1024,256]{2,1,0:T(8,128)(2,1)}), bf16[8,1024,256]{2,1,0:T(8,128)(2,1)}, u32[]{:S(2)}, u32[]{:S(2)}) %all-to-all-start.3) | async-done | bytes 4194336 | tf_op jit(solution)/shard_map/all_to_all | solution.py:348
  204.1 4.7 fusion.82
  208.8 36.4 %all-gather.9.cloned.1.call-done = bf16[2304,2048]{1,0:T(8,128)(2,1)} async-done(((bf16[144,2048]{1,0:T(8,128)(2,1)}), bf16[2304,2048]{1,0:T(8,128)(2,1)}) %all-gather.9.cloned.1.call-update) | async-done | bytes 9437200 | tf_op jit(solution)/shard_map/all_gather | solution.py:223
  245.2 7.4 fusion.86
  256.6 5.4 fusion.10
  263.2 11.2 shard_map.238
  286.1 38.7 %all-gather.13.cloned.1.call-done = bf16[2048,2048]{1,0:T(8,128)(2,1)} async-done(((bf16[128,2048]{1,0:T(8,128)(2,1)}), bf16[2048,2048]{1,0:T(8,128)(2,1)}) %all-gather.13.cloned.1.call-update) | async-done | bytes 8388624 | tf_op jit(solution)/shard_map/all_gather | solution.py:384
  324.9 5.7 convolution_convert_fusion.4
  339.7 9.0 all-to-all-done.5
  371.1 19.3 %all_to_all.82 = bf16[8,36,2048]{2,1,0:T(8,128)(2,1)S(1)} all-to-all(bf16[8,36,2048]{2,1,0:T(8,128)(2,1)S(1)} %pad_maximum_fusion.1), channel_id=1, replica_groups=mesh['grp'=8,'sub'=8,'expert'=2] {'grp'}, dimensions={0} | all-to-all | bytes 2359296 | tf_op jit(solution)/shard_map/all_to_all | solution.py:404
  396.3 74.7 %all-gather.15.cloned.1.call-done = bf16[2304,2048]{1,0:T(8,128)(2,1)} async-done(((bf16[144,2048]{1,0:T(8,128)(2,1)}), bf16[2304,2048]{1,0:T(8,128)(2,1)}) %all-gather.15.cloned.1.call-update) | async-done | bytes 9437200 | tf_op jit(solution)/shard_map/all_gather | solution.py:411
  471.0 9.2 fusion.87
  480.3 68.9 %all-gather.19.cloned.1.call-done = bf16[2304,2048]{1,0:T(8,128)(2,1)} async-done(((bf16[144,2048]{1,0:T(8,128)(2,1)}), bf16[2304,2048]{1,0:T(8,128)(2,1)}) %all-gather.19.cloned.1.call-update) | async-done | bytes 9437200 | tf_op jit(solution)/shard_map/all_gather | solution.py:417
  549.2 7.1 fusion.88
  557.0 8.6 multiply_convert_fusion.2
  566.8 7.5 convolution_convert_fusion
  575.0 12.2 fusion.89
  587.3 11.1 add_convert_fusion
  598.3 136.2 %all_to_all.83 = bf16[16,144,2048]{2,1,0:T(8,128)(2,1)} all-to-all(bf16[16,144,2048]{2,1,0:T(8,128)(2,1)S(1)} %bitcast.137), channel_id=1, replica_groups=mesh['grp'=8,'sub'=8,'expert'=2] {'sub','expert'}, dimensions={0} | all-to-all | bytes 18874368 | tf_op jit(solution)/shard_map/all_to_all | solution.py:228
  734.5 5.9 reduce_sum.342
  750.1 7.6 all-to-all-done.9
  777.1 58.9 %all-gather.17.cloned.1.call-done = bf16[2048,2048]{1,0:T(8,128)(2,1)} async-done(((bf16[2048,128]{1,0:T(8,128)(2,1)}), bf16[2048,2048]{1,0:T(8,128)(2,1)}) %all-gather.17.cloned.1.call-update) | async-done | bytes 8388624 | tf_op jit(solution)/shard_map/all_gather | solution.py:429
  856.6 15.7 %all_to_all.84 = bf16[8,18,2048]{2,1,0:T(8,128)(2,1)S(1)} all-to-all(bf16[8,18,2048]{2,1,0:T(8,128)(2,1)S(1)} %multiply_convert_fusion.3), channel_id=1, replica_groups=mesh['grp'=8,'sub'=8,'expert'=2] {'grp'}, dimensions={0} | all-to-all | bytes 1179648 | tf_op jit(solution)/shard_map/all_to_all | solution.py:222
  873.2 76.2 %all-gather.21.cloned.1.call-done = bf16[2304,2048]{1,0:T(8,128)(2,1)} async-done(((bf16[144,2048]{1,0:T(8,128)(2,1)}), bf16[2304,2048]{1,0:T(8,128)(2,1)}) %all-gather.21.cloned.1.call-update) | async-done | bytes 9437200 | tf_op jit(solution)/shard_map/all_gather | solution.py:223
  949.4 6.3 convolution_convert_fusion.2
  956.9 12.9 %shard_map.239 = (f32[8,288,128]{2,1,0:T(8,128)}, bf16[8,1024,256]{2,1,0:T(8,128)(2,1)}) custom-call(bf16[8,288,128]{2,1,0:T(8,128)(2,1)} %pad_maximum_fusion.2.q_ref, bf16[8,1024,128]{2,1,0:T(8,128)(2,1)} %bitcast.150, bf16[8,1024,128]{2,1,0:T(8,128)(2,1)} %bitcast.148, s32[8,288,1]{2,1,0:T(8,128)} %add_select_fusion.qb_ref, ...), custom_call_target="tpu_custom_call" | custom-call | flops 3019898880 | bytes 25100288 | tf_op jit(solution)/shard_map/pallas_call | solution.py:77
  969.8 7.9 fusion.14
  978.5 15.6 %all_to_all.85 = bf16[16,144,128]{2,1,0:T(8,128)(2,1)S(1)} all-to-all(bf16[16,144,128]{2,1,0:T(8,128)(2,1)S(1)} %copy.493), channel_id=1, replica_groups=mesh['grp'=8,'sub'=8,'expert'=2] {'sub','expert'}, dimensions={0} | all-to-all | bytes 1179648 | tf_op jit(solution)/shard_map/all_to_all | solution.py:249
  994.1 4.9 all-to-all-start.13
  999.0 6.3 convolution_convert_fusion.3
  1006.4 51.7 %all-to-all-done.13 = bf16[8,1024,256]{2,1,0:T(8,128)(2,1)} async-done(((bf16[8,1024,256]{2,1,0:T(8,128)(2,1)}), bf16[8,1024,256]{2,1,0:T(8,128)(2,1)}, u32[]{:S(2)}, u32[]{:S(2)}) %all-to-all-start.13) | async-done | bytes 4194336 | tf_op jit(solution)/shard_map/all_to_all | solution.py:498
  1081.5 5.9 all-to-all-start.14
  1097.5 4.9 fusion.53
  1102.4 34.9 %all-to-all-done.14 = bf16[16,64,2048]{2,1,0:T(8,128)(2,1)} async-done(((bf16[16,64,2048]{2,1,0:T(8,128)(2,1)}), bf16[16,64,2048]{2,1,0:T(8,128)(2,1)}, u32[]{:S(2)}, u32[]{:S(2)}) %all-to-all-start.14) | async-done | bytes 4194336 | tf_op jit(solution)/shard_map/all_to_all | solution.py:520
  1146.2 9.4 fusion.94
  1155.6 8.9 fusion.95
  1164.6 5.1 fusion.96
  1173.4 6.1 fusion.93
  1179.6 7.4 fusion.92
  1186.9 28.1 %reduce-scatter.5.cloned.1.call-done = f32[256,384]{0,1:T(8,128)} async-done(((f32[2048,384]{0,1:T(8,128)}), f32[256,384]{0,1:T(8,128)}) %reduce-scatter.5.cloned.1.call-update) | async-done | bytes 393232 | tf_op jit(solution)/shard_map/reduce_scatter | solution.py:554
  1216.9 8.3 all-to-all-start.15
  1225.2 20.0 %all-gather.23.cloned.1.call-done = bf16[128,4096]{1,0:T(8,128)(2,1)} async-done(((bf16[64,4096]{1,0:T(8,128)(2,1)}), bf16[128,4096]{1,0:T(8,128)(2,1)}) %all-gather.23.cloned.1.call-update) | async-done | bytes 1048592 | tf_op jit(solution)/shard_map/all_gather | solution.py:570
  (390 shorter events, 225.2 us)
Async XLA Ops:
  7.2 549.1 %copy-start = (bf16[2048,352]{0,1:T(8,128)(2,1)S(1)}, bf16[2048,352]{0,1:T(8,128)(2,1)}, u32[]{:S(2)}) copy-start(bf16[2048,352]{0,1:T(8,128)(2,1)} %param.30) | copy-start | bytes 4325380
  36.2 27.9 %all-to-all-start.1 = ((bf16[8,256,384]{1,2,0:T(8,128)(2,1)}), bf16[8,256,384]{1,2,0:T(8,128)(2,1)}, u32[]{:S(2)}, u32[]{:S(2)}) async-start(bf16[8,256,384]{1,2,0:T(8,128)(2,1)} %broadcast_in_dim.57), calls=%async_computation.1 | async-start | bytes 3145728 | tf_op jit(solution)/shard_map/all_to_all | solution.py:316
  40.7 88.3 %all-gather.11.cloned.1.call-start = ((), (), s32[]{:S(2)}) async-start(), calls=%async_computation.19 | async-start | bytes 4456448 | tf_op jit(solution)/shard_map/all_gather | solution.py:336
  40.9 25.6 %copy-start.50 = (f32[64]{0:T(128)}, f32[64]{0:T(128)S(1)}, u32[]{:S(2)}) copy-start(f32[64]{0:T(128)S(1)} %add_rsqrt_fusion.1) | copy-start | bytes 772
  66.0 84.0 %copy-start.3 = (bf16[8,256,384]{2,1,0:T(8,128)(2,1)}, bf16[8,256,384]{2,1,0:T(8,128)(2,1)S(1)}, u32[]{:S(2)}) copy-start(bf16[8,256,384]{2,1,0:T(8,128)(2,1)S(1)} %copy.448) | copy-start | bytes 4718596
  68.9 176.3 %all-gather.9.cloned.1.call-start = ((), (), s32[]{:S(2)}) async-start(), calls=%async_computation.18 | async-start | bytes 10027008 | tf_op jit(solution)/shard_map/all_gather | solution.py:223
  91.8 233.0 %all-gather.13.cloned.1.call-start = ((), (), s32[]{:S(2)}) async-start(), calls=%async_computation.20 | async-start | bytes 8912896 | tf_op jit(solution)/shard_map/all_gather | solution.py:384
  92.6 877.3 %copy-start.49 = (f32[64]{0:T(128)}, f32[64]{0:T(128)S(1)}, u32[]{:S(2)}) copy-start(f32[64]{0:T(128)S(1)} %multiply_exponential_fusion) | copy-start | bytes 772
  92.6 39.9 %copy-start.42 = (f32[1024]{0:T(1024)}, f32[1024]{0:T(1024)S(1)}, u32[]{:S(2)}) copy-start(f32[1024]{0:T(1024)S(1)} %iota_convert_fusion) | copy-start | bytes 12292
  139.8 64.2 %all-to-all-start.3 = ((bf16[8,1024,256]{2,1,0:T(8,128)(2,1)}), bf16[8,1024,256]{2,1,0:T(8,128)(2,1)}, u32[]{:S(2)}, u32[]{:S(2)}) async-start(bf16[8,1024,256]{2,1,0:T(8,128)(2,1)} %broadcast_in_dim.66), calls=%async_computation.3 | async-start | bytes 8388608 | tf_op jit(solution)/shard_map/all_to_all | solution.py:348
  158.9 8.2 copy-start.10
  204.1 41.1 %copy-start.28 = (bf16[2048,128]{1,0:T(8,128)(2,1)S(1)}, bf16[2048,128]{1,0:T(8,128)(2,1)}, u32[]{:S(2)}) copy-start(bf16[2048,128]{1,0:T(8,128)(2,1)} %param.25) | copy-start | bytes 1572868
  276.8 48.0 %all-to-all-start.4 = ((bf16[16,144,128]{2,1,0:T(8,128)(2,1)}), bf16[16,144,128]{2,1,0:T(8,128)(2,1)S(1)}, u32[]{:S(2)}, u32[]{:S(2)}) async-start(bf16[16,144,128]{2,1,0:T(8,128)(2,1)} %copy.459), calls=%async_computation.4 | async-start | bytes 1179648 | tf_op jit(solution)/shard_map/all_to_all | solution.py:249
  332.7 16.1 %all-to-all-start.5 = ((bf16[8,18,2048]{2,1,0:T(8,128)(2,1)}), bf16[8,18,2048]{2,1,0:T(8,128)(2,1)S(1)}, u32[]{:S(2)}, u32[]{:S(2)}) async-start(bf16[8,18,2048]{2,1,0:T(8,128)(2,1)} %reshape.674), calls=%async_computation.5 | async-start | bytes 1572864 | tf_op jit(solution)/shard_map/all_to_all | solution.py:259
  336.7 134.3 %all-gather.15.cloned.1.call-start = ((), (), s32[]{:S(2)}) async-start(), calls=%async_computation.21 | async-start | bytes 10027008 | tf_op jit(solution)/shard_map/all_gather | solution.py:411
  339.6 511.3 %copy-start.47 = (f32[64,2]{0,1:T(2,128)}, f32[64,2]{0,1:T(2,128)S(1)}, u32[]{:S(2)}) copy-start(f32[64,2]{0,1:T(2,128)S(1)} %get-tuple-element.150) | copy-start | bytes 1540
  393.9 155.2 %all-gather.19.cloned.1.call-start = ((), (), s32[]{:S(2)}) async-start(), calls=%async_computation.24 | async-start | bytes 10027008 | tf_op jit(solution)/shard_map/all_gather | solution.py:417
  396.1 351.8 %reduce-scatter.3.cloned.1.call-start = ((), (), s32[]{:S(2)}) async-start(), calls=%async_computation.22 | async-start | bytes 10027008 | tf_op jit(solution)/shard_map/reduce_scatter | solution.py:241
  549.2 7.1 copy-start.55
  549.2 7.8 copy-start.57
  557.0 9.8 copy-start.56
  574.3 261.7 %all-gather.17.cloned.1.call-start = ((), (), s32[]{:S(2)}) async-start(), calls=%async_computation.23 | async-start | bytes 8912896 | tf_op jit(solution)/shard_map/all_gather | solution.py:429
  575.0 12.2 copy-start.11
  741.5 16.2 %all-to-all-start.9 = ((bf16[8,18,2048]{2,1,0:T(8,128)(2,1)}), bf16[8,18,2048]{2,1,0:T(8,128)(2,1)S(1)}, u32[]{:S(2)}, u32[]{:S(2)}) async-start(bf16[8,18,2048]{2,1,0:T(8,128)(2,1)} %convert_element_type.230), calls=%async_computation.10 | async-start | bytes 1572864 | tf_op jit(solution)/shard_map/all_to_all | solution.py:236
  746.1 16.3 %copy-start.41 = (s32[8,18,1]{0,1,2:T(8,128)S(1)}, s32[8,18,1]{0,1,2:T(8,128)}, u32[]{:S(2)}) copy-start(s32[8,18,1]{0,1,2:T(8,128)} %get-tuple-element.172) | copy-start | bytes 1732
  746.1 16.5 %copy-start.53 = (s32[64,2]{0,1:T(2,128)S(1)}, s32[64,2]{0,1:T(2,128)}, u32[]{:S(2)}) copy-start(s32[64,2]{0,1:T(2,128)} %get-tuple-element.182) | copy-start | bytes 1540
  757.7 16.9 %all-to-all-start.7 = ((bf16[8,18,2048]{2,1,0:T(8,128)(2,1)}), bf16[8,18,2048]{2,1,0:T(8,128)(2,1)}, u32[]{:S(2)}, u32[]{:S(2)}) async-start(bf16[8,18,2048]{2,1,0:T(8,128)(2,1)} %reshape.678), calls=%async_computation.8 | async-start | bytes 1572864 | tf_op jit(solution)/shard_map/all_to_all | solution.py:244
  761.9 187.5 %all-gather.21.cloned.1.call-start = ((), (), s32[]{:S(2)}) async-start(), calls=%async_computation.25 | async-start | bytes 10027008 | tf_op jit(solution)/shard_map/all_gather | solution.py:223
  856.5 92.9 %copy-start.29 = (bf16[128,2048]{1,0:T(8,128)(2,1)S(1)}, bf16[128,2048]{1,0:T(8,128)(2,1)}, u32[]{:S(2)}) copy-start(bf16[128,2048]{1,0:T(8,128)(2,1)} %param.26) | copy-start | bytes 1572868
  978.3 15.9 %copy-start.6 = (bf16[8,16,18,128]{3,2,1,0:T(8,128)(2,1)}, bf16[8,16,18,128]{3,2,1,0:T(8,128)(2,1)S(1)}, u32[]{:S(2)}) copy-start(bf16[8,16,18,128]{3,2,1,0:T(8,128)(2,1)S(1)} %convert_element_type.234) | copy-start | bytes 1769476
  994.1 64.0 %all-to-all-start.13 = ((bf16[8,1024,256]{2,1,0:T(8,128)(2,1)}), bf16[8,1024,256]{2,1,0:T(8,128)(2,1)}, u32[]{:S(2)}, u32[]{:S(2)}) async-start(bf16[8,1024,256]{2,1,0:T(8,128)(2,1)} %get-tuple-element.26), calls=%async_computation.14 | async-start | bytes 8388608 | tf_op jit(solution)/shard_map/all_to_all | solution.py:498
  1058.1 22.6 %all-to-all-start.12 = ((bf16[8,18,2048]{2,1,0:T(8,128)(2,1)}), bf16[8,18,2048]{2,1,0:T(8,128)(2,1)S(1)}, u32[]{:S(2)}, u32[]{:S(2)}) async-start(bf16[8,18,2048]{2,1,0:T(8,128)(2,1)} %reshape.688), calls=%async_computation.13 | async-start | bytes 1572864 | tf_op jit(solution)/shard_map/all_to_all | solution.py:259
  1066.3 10.1 copy-start.4
  1080.7 7.0 copy-start.48
  1081.5 55.8 %all-to-all-start.14 = ((bf16[16,64,2048]{2,1,0:T(8,128)(2,1)}), bf16[16,64,2048]{2,1,0:T(8,128)(2,1)}, u32[]{:S(2)}, u32[]{:S(2)}) async-start(bf16[16,64,2048]{2,1,0:T(8,128)(2,1)} %bitcast.138), calls=%async_computation.15 | async-start | bytes 8388608 | tf_op jit(solution)/shard_map/all_to_all | solution.py:520
  1087.4 127.6 %reduce-scatter.5.cloned.1.call-start = ((), (), s32[]{:S(2)}) async-start(), calls=%async_computation.27 | async-start | bytes 3538944 | tf_op jit(solution)/shard_map/reduce_scatter | solution.py:554
  1102.4 37.9 %copy-start.15 = (bf16[128,2048]{1,0:T(8,128)(2,1)S(1)}, bf16[128,2048]{1,0:T(8,128)(2,1)}, u32[]{:S(2)}) copy-start(bf16[128,2048]{1,0:T(8,128)(2,1)} %param.21) | copy-start | bytes 1572868
  1102.4 37.9 %copy-start.24 = (f32[64,2048]{1,0:T(8,128)S(1)}, f32[64,2048]{1,0:T(8,128)}, u32[]{:S(2)}) copy-start(f32[64,2048]{1,0:T(8,128)} %multiply_reduce_fusion.3) | copy-start | bytes 1572868
  1102.4 38.0 %copy-start.34 = (f32[2048]{0:T(1024)S(1)}, f32[2048]{0:T(1024)}, u32[]{:S(2)}) copy-start(f32[2048]{0:T(1024)} %copy-done.33) | copy-start | bytes 24580
  1102.4 38.0 %copy-start.51 = (f32[64]{0:T(128)S(1)}, f32[64]{0:T(128)}, u32[]{:S(2)}) copy-start(f32[64]{0:T(128)} %copy-done.50) | copy-start | bytes 772
  1144.8 100.4 %all-gather.23.cloned.1.call-start = ((), (), s32[]{:S(2)}) async-start(), calls=%async_computation.26 | async-start | bytes 1572864 | tf_op jit(solution)/shard_map/all_gather | solution.py:570
  1146.2 9.4 copy-start.21
  1146.2 18.4 %slice-start = ((s8[9437184]{0:T(1024)(128)(4,1)}), s8[4194304]{0:T(1024)(128)(4,1)S(1)}, s32[]{:S(2)}) async-start(s8[9437184]{0:T(1024)(128)(4,1)} %bitcast.175), calls=%async_computation.28 | async-start | bytes 8388608
  1146.2 18.3 %slice-start.1 = ((s8[9437184]{0:T(1024)(128)(4,1)}), s8[4194304]{0:T(1024)(128)(4,1)S(1)}, s32[]{:S(2)}) async-start(s8[9437184]{0:T(1024)(128)(4,1)} %bitcast.175), calls=%async_computation.29 | async-start | bytes 8388608
  1155.6 8.9 copy-start.12
  1155.6 8.9 slice-start.2
  1216.9 30.7 %all-to-all-start.15 = ((f32[16,16,384]{2,1,0:T(8,128)}), f32[16,16,384]{2,1,0:T(8,128)S(1)}, u32[]{:S(2)}, u32[]{:S(2)}) async-start(f32[16,16,384]{2,1,0:T(8,128)} %bitcast.42), calls=%async_computation.17 | async-start | bytes 786432 | tf_op jit(solution)/shard_map/all_to_all | solution.py:555
  1245.2 5.7 copy-start.1
  (34 other events, 79.7 us)
Sparse Core Ops, SparseCore 0:
  69.1 59.8 all-gather.10
  132.0 113.1 all-gather.8
  247.7 77.1 all-gather.12
  394.0 76.9 all-gather.14
  473.9 75.2 all-gather.18
  574.4 173.4 reduce-scatter.2
  750.4 85.5 all-gather.16
  873.3 76.0 all-gather.20
  1144.9 70.0 reduce-scatter.4
  1217.2 27.9 all-gather.22

commit v18 on v15

--- a/solution.py
+++ b/solution.py
@@ -567,14 +567,16 @@
     gain_two_grad = extra_grad[:, 1]
     attn_router_grad = extra_grad[:, 2 : 2 + EXPERTS]
     mlp_router_grad = extra_grad[:, 2 + EXPERTS : 2 + 2 * EXPERTS]
-    both_full = lax.all_gather(
-        jnp.concatenate(
-            [own_output.astype(jnp.bfloat16), input_grad.astype(jnp.bfloat16)], axis=1
-        ),
+    both_own = jnp.concatenate(
+        [own_output.astype(jnp.bfloat16), input_grad.astype(jnp.bfloat16)], axis=1
+    )
+    both_full = lax.all_to_all(
+        jnp.broadcast_to(both_own[None], (halves,) + both_own.shape),
         "expert",
-        axis=0,
-        tiled=True,
-    )
+        split_axis=0,
+        concat_axis=0,
+        tiled=True,
+    ).reshape(halves * own_rows, 2 * width)
     mixed_full, input_full = both_full[:, :width], both_full[:, width:]
     return (
         mixed_full,

time: 1270 us -> 1270 us (level)
    all_gather x1 -> x0, waiting for transfers between devices: 20 us -> none  [shards(): lax.all_gather(jnp.concatenate([own_output.astype(jnp.bfloat16), input_gr...]
  transfers between devices with their start and end apart: 21 -> 21, of which waited for: 18 -> 18; matrix products, arithmetic and copies ran while one was open for 17% -> 18% of each run, Pallas kernels for 1% -> 1%
where the time goes in v18:
time: 1270 us; the launch traced here: 1260 us
  waiting for transfers between devices  606 us (48%)
  blocking collectives  203 us (16%)
  matrix products  141 us (11%)
  local copies, waits for them, and re-layouts  131 us (10%)
  other arithmetic  78 us (6%)
  starting transfers between devices  56.2 us (4%)
  Pallas kernels  25 us (2%)
  between operations  15.6 us (1%)
    all_to_all x1, blocking collectives, combine(): lax.all_to_all(partial_value.astype(jnp.bfloat16).reshape(group_size, gro...  136 us
    all_gather x2, waiting for transfers between devices, dispatch(): lax.all_gather(by_group.reshape(groups * slot_cap, width), GROUP_AXES, ax...  113 us
    all_gather x1, waiting for transfers between devices, shards(): lax.all_gather(mlp_by_group[:, :slot_cap].reshape(groups * slot_cap, widt...  74.6 us
    all_gather x1, waiting for transfers between devices, shards(): lax.all_gather(mlp_by_group[:, slot_cap:].reshape(groups * slot_cap, widt...  68.9 us
    all_gather x1, waiting for transfers between devices, shards(): query_stack = lax.all_gather(query_weight, GROUP_AXES, axis=1, tiled=True)  58.9 us
    all_to_all x1, waiting for transfers between devices, shards(): lax.all_to_all(jnp.concatenate([seq_key_grad, seq_value_grad], axis=2).as...  52.2 us
    all_gather x1, waiting for transfers between devices, shards(): output_stack = lax.all_gather(output_weight, GROUP_AXES, axis=0, tiled=True)  38.7 us
    all_to_all x1, waiting for transfers between devices, shards(): lax.all_to_all(jnp.einsum('rc,dc->rd', kv_col_grad, head_kv, preferred_el...  36.4 us
  transfers between devices with their start and end apart: 21, of which 18 were waited for; matrix products, arithmetic and copies ran while one was open for 18% of the time, Pallas kernels for 1%

profile of v18, /device:TPU:1, one launch (start us, length us, event | category | flops | bytes accessed | tf_op | source)
XLA Modules:
  0.0 1256.4 jit_solution(1131092285651727333)
XLA Ops:
  17.3 17.5 %all_to_all.85 = bf16[16,16,384]{2,1,0:T(8,128)(2,1)S(1)} all-to-all(bf16[16,16,384]{2,1,0:T(8,128)(2,1)S(1)} %pad_maximum_fusion.10), channel_id=1, replica_groups=mesh['grp'=8,'sub'=8,'expert'=2] {'sub','expert'}, dimensions={0} | all-to-all | bytes 393216 | tf_op jit(solution)/shard_map/all_to_all | solution.py:303
  40.9 23.2 %all-to-all-done.1 = bf16[8,256,384]{1,2,0:T(8,128)(2,1)} async-done(((bf16[8,256,384]{1,2,0:T(8,128)(2,1)}), bf16[8,256,384]{1,2,0:T(8,128)(2,1)}, u32[]{:S(2)}, u32[]{:S(2)}) %all-to-all-start.1) | async-done | bytes 1572896 | tf_op jit(solution)/shard_map/all_to_all | solution.py:316
  75.8 13.9 %all_to_all.86 = bf16[8,18,2048]{2,1,0:T(8,128)(2,1)} all-to-all(bf16[8,18,2048]{2,1,0:T(8,128)(2,1)S(1)} %broadcast_select_fusion.1), channel_id=1, replica_groups=mesh['grp'=8,'sub'=8,'expert'=2] {'grp'}, dimensions={0} | all-to-all | bytes 1179648 | tf_op jit(solution)/shard_map/all_to_all | solution.py:222
  92.6 36.4 %all-gather.10.cloned.1.call-done = bf16[1024,2048]{1,0:T(8,128)(2,1)} async-done(((bf16[64,2048]{1,0:T(8,128)(2,1)}), bf16[1024,2048]{1,0:T(8,128)(2,1)}) %all-gather.10.cloned.1.call-update) | async-done | bytes 4194320 | tf_op jit(solution)/shard_map/all_gather | solution.py:336
  139.8 4.8 all-to-all-start.3
  158.9 5.6 multiply_reduce_fusion
  170.5 33.6 %all-to-all-done.3 = bf16[8,1024,256]{2,1,0:T(8,128)(2,1)} async-done(((bf16[8,1024,256]{2,1,0:T(8,128)(2,1)}), bf16[8,1024,256]{2,1,0:T(8,128)(2,1)}, u32[]{:S(2)}, u32[]{:S(2)}) %all-to-all-start.3) | async-done | bytes 4194336 | tf_op jit(solution)/shard_map/all_to_all | solution.py:348
  204.1 4.7 fusion.82
  208.8 36.4 %all-gather.8.cloned.1.call-done = bf16[2304,2048]{1,0:T(8,128)(2,1)} async-done(((bf16[144,2048]{1,0:T(8,128)(2,1)}), bf16[2304,2048]{1,0:T(8,128)(2,1)}) %all-gather.8.cloned.1.call-update) | async-done | bytes 9437200 | tf_op jit(solution)/shard_map/all_gather | solution.py:223
  245.2 7.4 fusion.86
  256.6 5.4 fusion.10
  263.1 11.2 shard_map.238
  286.1 38.7 %all-gather.12.cloned.1.call-done = bf16[2048,2048]{1,0:T(8,128)(2,1)} async-done(((bf16[128,2048]{1,0:T(8,128)(2,1)}), bf16[2048,2048]{1,0:T(8,128)(2,1)}) %all-gather.12.cloned.1.call-update) | async-done | bytes 8388624 | tf_op jit(solution)/shard_map/all_gather | solution.py:384
  324.8 5.7 convolution_convert_fusion.4
  339.7 9.0 all-to-all-done.5
  371.1 19.3 %all_to_all.87 = bf16[8,36,2048]{2,1,0:T(8,128)(2,1)S(1)} all-to-all(bf16[8,36,2048]{2,1,0:T(8,128)(2,1)S(1)} %pad_maximum_fusion.2), channel_id=1, replica_groups=mesh['grp'=8,'sub'=8,'expert'=2] {'grp'}, dimensions={0} | all-to-all | bytes 2359296 | tf_op jit(solution)/shard_map/all_to_all | solution.py:404
  396.4 74.6 %all-gather.14.cloned.1.call-done = bf16[2304,2048]{1,0:T(8,128)(2,1)} async-done(((bf16[144,2048]{1,0:T(8,128)(2,1)}), bf16[2304,2048]{1,0:T(8,128)(2,1)}) %all-gather.14.cloned.1.call-update) | async-done | bytes 9437200 | tf_op jit(solution)/shard_map/all_gather | solution.py:411
  471.0 9.2 fusion.87
  480.3 68.9 %all-gather.18.cloned.1.call-done = bf16[2304,2048]{1,0:T(8,128)(2,1)} async-done(((bf16[144,2048]{1,0:T(8,128)(2,1)}), bf16[2304,2048]{1,0:T(8,128)(2,1)}) %all-gather.18.cloned.1.call-update) | async-done | bytes 9437200 | tf_op jit(solution)/shard_map/all_gather | solution.py:417
  549.2 7.1 fusion.88
  557.0 8.6 multiply_convert_fusion.2
  566.8 7.5 convolution_convert_fusion
  575.1 12.2 fusion.89
  587.3 11.1 add_convert_fusion
  598.3 136.2 %all_to_all.88 = bf16[16,144,2048]{2,1,0:T(8,128)(2,1)} all-to-all(bf16[16,144,2048]{2,1,0:T(8,128)(2,1)S(1)} %bitcast.138), channel_id=1, replica_groups=mesh['grp'=8,'sub'=8,'expert'=2] {'sub','expert'}, dimensions={0} | all-to-all | bytes 18874368 | tf_op jit(solution)/shard_map/all_to_all | solution.py:228
  734.6 5.9 reduce_sum.342
  741.5 4.6 all-to-all-start.9
  750.1 7.6 all-to-all-done.9
  777.1 58.9 %all-gather.16.cloned.1.call-done = bf16[2048,2048]{1,0:T(8,128)(2,1)} async-done(((bf16[2048,128]{1,0:T(8,128)(2,1)}), bf16[2048,2048]{1,0:T(8,128)(2,1)}) %all-gather.16.cloned.1.call-update) | async-done | bytes 8388624 | tf_op jit(solution)/shard_map/all_gather | solution.py:429
  856.5 15.7 %all_to_all.89 = bf16[8,18,2048]{2,1,0:T(8,128)(2,1)S(1)} all-to-all(bf16[8,18,2048]{2,1,0:T(8,128)(2,1)S(1)} %multiply_convert_fusion.3), channel_id=1, replica_groups=mesh['grp'=8,'sub'=8,'expert'=2] {'grp'}, dimensions={0} | all-to-all | bytes 1179648 | tf_op jit(solution)/shard_map/all_to_all | solution.py:222
  873.2 76.2 %all-gather.20.cloned.1.call-done = bf16[2304,2048]{1,0:T(8,128)(2,1)} async-done(((bf16[144,2048]{1,0:T(8,128)(2,1)}), bf16[2304,2048]{1,0:T(8,128)(2,1)}) %all-gather.20.cloned.1.call-update) | async-done | bytes 9437200 | tf_op jit(solution)/shard_map/all_gather | solution.py:223
  949.4 6.3 convolution_convert_fusion.2
  956.9 13.8 %shard_map.239 = (f32[8,288,128]{2,1,0:T(8,128)}, f32[8,1024,128]{2,1,0:T(8,128)}, f32[8,1024,128]{2,1,0:T(8,128)}) custom-call(bf16[8,288,128]{2,1,0:T(8,128)(2,1)} %pad_maximum_fusion.3.q_ref, bf16[8,1024,128]{2,1,0:T(8,128)(2,1)} %bitcast.151, bf16[8,1024,128]{2,1,0:T(8,128)(2,1)} %bitcast.149, s32[8,288,1]{2,1,0:T(8,128)} %add_select_fusion.qb_ref, ...), custom_call_target="tpu_custom_call" | custom-call | flops 3019898880 | bytes 25100288 | tf_op jit(solution)/shard_map/pallas_call | solution.py:76
  970.7 7.9 fusion.14
  989.9 4.7 all-to-all-done.11
  999.2 6.3 convolution_convert_fusion.3
  1006.6 52.2 %all-to-all-done.13 = bf16[8,1024,256]{2,1,0:T(8,128)(2,1)} async-done(((bf16[8,1024,256]{2,1,0:T(8,128)(2,1)}), bf16[8,1024,256]{2,1,0:T(8,128)(2,1)}, u32[]{:S(2)}, u32[]{:S(2)}) %all-to-all-start.13) | async-done | bytes 4194336 | tf_op jit(solution)/shard_map/all_to_all | solution.py:498
  1082.2 5.7 all-to-all-start.14
  1096.5 4.8 fusion.53
  1101.3 36.4 %all-to-all-done.14 = bf16[16,64,2048]{2,1,0:T(8,128)(2,1)} async-done(((bf16[16,64,2048]{2,1,0:T(8,128)(2,1)}), bf16[16,64,2048]{2,1,0:T(8,128)(2,1)}, u32[]{:S(2)}, u32[]{:S(2)}) %all-to-all-start.14) | async-done | bytes 4194336 | tf_op jit(solution)/shard_map/all_to_all | solution.py:520
  1149.5 9.4 fusion.94
  1158.9 9.0 fusion.95
  1167.9 5.1 fusion.96
  1174.2 7.5 fusion.92
  1187.7 6.1 fusion.93
  1193.9 33.7 %reduce-scatter.5.cloned.1.call-done = f32[256,384]{0,1:T(8,128)} async-done(((f32[2048,384]{0,1:T(8,128)}), f32[256,384]{0,1:T(8,128)}) %reduce-scatter.5.cloned.1.call-update) | async-done | bytes 393232 | tf_op jit(solution)/shard_map/reduce_scatter | solution.py:554
  1229.4 7.1 all-to-all-start.16
  1237.6 8.5 all-to-all-done.16
  (380 shorter events, 239.1 us)
Async XLA Ops:
  7.2 549.1 %copy-start = (bf16[2048,352]{0,1:T(8,128)(2,1)S(1)}, bf16[2048,352]{0,1:T(8,128)(2,1)}, u32[]{:S(2)}) copy-start(bf16[2048,352]{0,1:T(8,128)(2,1)} %param.30) | copy-start | bytes 4325380
  36.2 27.9 %all-to-all-start.1 = ((bf16[8,256,384]{1,2,0:T(8,128)(2,1)}), bf16[8,256,384]{1,2,0:T(8,128)(2,1)}, u32[]{:S(2)}, u32[]{:S(2)}) async-start(bf16[8,256,384]{1,2,0:T(8,128)(2,1)} %broadcast_in_dim.59), calls=%async_computation.1 | async-start | bytes 3145728 | tf_op jit(solution)/shard_map/all_to_all | solution.py:316
  40.6 88.3 %all-gather.10.cloned.1.call-start = ((), (), s32[]{:S(2)}) async-start(), calls=%async_computation.20 | async-start | bytes 4456448 | tf_op jit(solution)/shard_map/all_gather | solution.py:336
  40.9 25.6 %copy-start.45 = (f32[64]{0:T(128)}, f32[64]{0:T(128)S(1)}, u32[]{:S(2)}) copy-start(f32[64]{0:T(128)S(1)} %add_rsqrt_fusion.1) | copy-start | bytes 772
  65.9 84.1 %copy-start.3 = (bf16[8,256,384]{2,1,0:T(8,128)(2,1)}, bf16[8,256,384]{2,1,0:T(8,128)(2,1)S(1)}, u32[]{:S(2)}) copy-start(bf16[8,256,384]{2,1,0:T(8,128)(2,1)S(1)} %copy.448) | copy-start | bytes 4718596
  68.9 176.3 %all-gather.8.cloned.1.call-start = ((), (), s32[]{:S(2)}) async-start(), calls=%async_computation.19 | async-start | bytes 10027008 | tf_op jit(solution)/shard_map/all_gather | solution.py:223
  91.8 233.0 %all-gather.12.cloned.1.call-start = ((), (), s32[]{:S(2)}) async-start(), calls=%async_computation.21 | async-start | bytes 8912896 | tf_op jit(solution)/shard_map/all_gather | solution.py:384
  92.5 878.1 %copy-start.44 = (f32[64]{0:T(128)}, f32[64]{0:T(128)S(1)}, u32[]{:S(2)}) copy-start(f32[64]{0:T(128)S(1)} %multiply_exponential_fusion) | copy-start | bytes 772
  92.6 40.0 %copy-start.37 = (f32[1024]{0:T(1024)}, f32[1024]{0:T(1024)S(1)}, u32[]{:S(2)}) copy-start(f32[1024]{0:T(1024)S(1)} %iota_convert_fusion) | copy-start | bytes 12292
  139.8 64.2 %all-to-all-start.3 = ((bf16[8,1024,256]{2,1,0:T(8,128)(2,1)}), bf16[8,1024,256]{2,1,0:T(8,128)(2,1)}, u32[]{:S(2)}, u32[]{:S(2)}) async-start(bf16[8,1024,256]{2,1,0:T(8,128)(2,1)} %broadcast_in_dim.68), calls=%async_computation.3 | async-start | bytes 8388608 | tf_op jit(solution)/shard_map/all_to_all | solution.py:348
  158.9 8.2 copy-start.8
  204.1 41.1 %copy-start.26 = (bf16[2048,128]{1,0:T(8,128)(2,1)S(1)}, bf16[2048,128]{1,0:T(8,128)(2,1)}, u32[]{:S(2)}) copy-start(bf16[2048,128]{1,0:T(8,128)(2,1)} %param.25) | copy-start | bytes 1572868
  276.8 48.1 %all-to-all-start.4 = ((bf16[16,144,128]{2,1,0:T(8,128)(2,1)}), bf16[16,144,128]{2,1,0:T(8,128)(2,1)S(1)}, u32[]{:S(2)}, u32[]{:S(2)}) async-start(bf16[16,144,128]{2,1,0:T(8,128)(2,1)} %copy.459), calls=%async_computation.4 | async-start | bytes 1179648 | tf_op jit(solution)/shard_map/all_to_all | solution.py:249
  332.6 16.1 %all-to-all-start.5 = ((bf16[8,18,2048]{2,1,0:T(8,128)(2,1)}), bf16[8,18,2048]{2,1,0:T(8,128)(2,1)S(1)}, u32[]{:S(2)}, u32[]{:S(2)}) async-start(bf16[8,18,2048]{2,1,0:T(8,128)(2,1)} %reshape.678), calls=%async_computation.5 | async-start | bytes 1572864 | tf_op jit(solution)/shard_map/all_to_all | solution.py:259
  336.6 134.4 %all-gather.14.cloned.1.call-start = ((), (), s32[]{:S(2)}) async-start(), calls=%async_computation.22 | async-start | bytes 10027008 | tf_op jit(solution)/shard_map/all_gather | solution.py:411
  339.6 511.4 %copy-start.42 = (f32[64,2]{0,1:T(2,128)}, f32[64,2]{0,1:T(2,128)S(1)}, u32[]{:S(2)}) copy-start(f32[64,2]{0,1:T(2,128)S(1)} %get-tuple-element.152) | copy-start | bytes 1540
  394.0 155.2 %all-gather.18.cloned.1.call-start = ((), (), s32[]{:S(2)}) async-start(), calls=%async_computation.25 | async-start | bytes 10027008 | tf_op jit(solution)/shard_map/all_gather | solution.py:417
  396.2 351.8 %reduce-scatter.3.cloned.1.call-start = ((), (), s32[]{:S(2)}) async-start(), calls=%async_computation.23 | async-start | bytes 10027008 | tf_op jit(solution)/shard_map/reduce_scatter | solution.py:241
  549.2 7.1 copy-start.48
  549.2 7.8 copy-start.50
  557.0 9.8 copy-start.49
  574.3 261.7 %all-gather.16.cloned.1.call-start = ((), (), s32[]{:S(2)}) async-start(), calls=%async_computation.24 | async-start | bytes 8912896 | tf_op jit(solution)/shard_map/all_gather | solution.py:429
  575.1 12.2 copy-start.10
  741.5 16.2 %all-to-all-start.9 = ((bf16[8,18,2048]{2,1,0:T(8,128)(2,1)}), bf16[8,18,2048]{2,1,0:T(8,128)(2,1)S(1)}, u32[]{:S(2)}, u32[]{:S(2)}) async-start(bf16[8,18,2048]{2,1,0:T(8,128)(2,1)} %convert_element_type.231), calls=%async_computation.10 | async-start | bytes 1572864 | tf_op jit(solution)/shard_map/all_to_all | solution.py:236
  746.1 16.3 %copy-start.36 = (s32[8,18,1]{0,1,2:T(8,128)S(1)}, s32[8,18,1]{0,1,2:T(8,128)}, u32[]{:S(2)}) copy-start(s32[8,18,1]{0,1,2:T(8,128)} %get-tuple-element.174) | copy-start | bytes 1732
  746.1 16.5 %copy-start.47 = (s32[64,2]{0,1:T(2,128)S(1)}, s32[64,2]{0,1:T(2,128)}, u32[]{:S(2)}) copy-start(s32[64,2]{0,1:T(2,128)} %get-tuple-element.184) | copy-start | bytes 1540
  757.7 16.9 %all-to-all-start.7 = ((bf16[8,18,2048]{2,1,0:T(8,128)(2,1)}), bf16[8,18,2048]{2,1,0:T(8,128)(2,1)}, u32[]{:S(2)}, u32[]{:S(2)}) async-start(bf16[8,18,2048]{2,1,0:T(8,128)(2,1)} %reshape.682), calls=%async_computation.8 | async-start | bytes 1572864 | tf_op jit(solution)/shard_map/all_to_all | solution.py:244
  761.9 187.5 %all-gather.20.cloned.1.call-start = ((), (), s32[]{:S(2)}) async-start(), calls=%async_computation.26 | async-start | bytes 10027008 | tf_op jit(solution)/shard_map/all_gather | solution.py:223
  856.5 92.9 %copy-start.27 = (bf16[128,2048]{1,0:T(8,128)(2,1)S(1)}, bf16[128,2048]{1,0:T(8,128)(2,1)}, u32[]{:S(2)}) copy-start(bf16[128,2048]{1,0:T(8,128)(2,1)} %param.26) | copy-start | bytes 1572868
  980.1 14.5 %all-to-all-start.11 = ((bf16[16,144,128]{2,1,0:T(8,128)(2,1)}), bf16[16,144,128]{2,1,0:T(8,128)(2,1)S(1)}, u32[]{:S(2)}, u32[]{:S(2)}) async-start(bf16[16,144,128]{2,1,0:T(8,128)(2,1)} %copy.493), calls=%async_computation.12 | async-start | bytes 1179648 | tf_op jit(solution)/shard_map/all_to_all | solution.py:249
  994.7 64.1 %all-to-all-start.13 = ((bf16[8,1024,256]{2,1,0:T(8,128)(2,1)}), bf16[8,1024,256]{2,1,0:T(8,128)(2,1)}, u32[]{:S(2)}, u32[]{:S(2)}) async-start(bf16[8,1024,256]{2,1,0:T(8,128)(2,1)} %pad_maximum_fusion), calls=%async_computation.14 | async-start | bytes 8388608 | tf_op jit(solution)/shard_map/all_to_all | solution.py:498
  1058.8 23.4 %all-to-all-start.12 = ((bf16[8,18,2048]{2,1,0:T(8,128)(2,1)}), bf16[8,18,2048]{2,1,0:T(8,128)(2,1)}, u32[]{:S(2)}, u32[]{:S(2)}) async-start(bf16[8,18,2048]{2,1,0:T(8,128)(2,1)} %reshape.692), calls=%async_computation.13 | async-start | bytes 1572864 | tf_op jit(solution)/shard_map/all_to_all | solution.py:259
  1067.9 10.1 copy-start.4
  1082.2 55.6 %all-to-all-start.14 = ((bf16[16,64,2048]{2,1,0:T(8,128)(2,1)}), bf16[16,64,2048]{2,1,0:T(8,128)(2,1)}, u32[]{:S(2)}, u32[]{:S(2)}) async-start(bf16[16,64,2048]{2,1,0:T(8,128)(2,1)} %bitcast.139), calls=%async_computation.15 | async-start | bytes 8388608 | tf_op jit(solution)/shard_map/all_to_all | solution.py:520
  1087.9 139.6 %reduce-scatter.5.cloned.1.call-start = ((), (), s32[]{:S(2)}) async-start(), calls=%async_computation.27 | async-start | bytes 3538944 | tf_op jit(solution)/shard_map/reduce_scatter | solution.py:554
  1101.3 39.4 %copy-start.14 = (bf16[128,2048]{1,0:T(8,128)(2,1)S(1)}, bf16[128,2048]{1,0:T(8,128)(2,1)}, u32[]{:S(2)}) copy-start(bf16[128,2048]{1,0:T(8,128)(2,1)} %param.21) | copy-start | bytes 1572868
  1101.3 39.5 %copy-start.30 = (f32[2048]{0:T(1024)S(1)}, f32[2048]{0:T(1024)}, u32[]{:S(2)}) copy-start(f32[2048]{0:T(1024)} %copy-done.29) | copy-start | bytes 24580
  1101.3 39.5 %copy-start.46 = (f32[64]{0:T(128)S(1)}, f32[64]{0:T(128)}, u32[]{:S(2)}) copy-start(f32[64]{0:T(128)} %copy-done.45) | copy-start | bytes 772
  1149.5 9.4 copy-start.19
  1149.5 18.4 %slice-start = ((s8[9437184]{0:T(1024)(128)(4,1)}), s8[4194304]{0:T(1024)(128)(4,1)S(1)}, s32[]{:S(2)}) async-start(s8[9437184]{0:T(1024)(128)(4,1)} %bitcast.177), calls=%async_computation.28 | async-start | bytes 8388608
  1149.5 18.4 %slice-start.1 = ((s8[9437184]{0:T(1024)(128)(4,1)}), s8[4194304]{0:T(1024)(128)(4,1)S(1)}, s32[]{:S(2)}) async-start(s8[9437184]{0:T(1024)(128)(4,1)} %bitcast.177), calls=%async_computation.29 | async-start | bytes 8388608
  1158.9 9.0 copy-start.11
  1158.9 9.0 slice-start.2
  1174.2 7.5 copy-start.15
  1174.2 7.5 copy-start.21
  1183.8 45.6 %all-to-all-start.15 = ((bf16[2,64,4096]{2,1,0:T(8,128)(2,1)}), bf16[2,64,4096]{2,1,0:T(8,128)(2,1)S(1)}, u32[]{:S(2)}, u32[]{:S(2)}) async-start(bf16[2,64,4096]{2,1,0:T(8,128)(2,1)} %broadcast_in_dim.73), calls=%async_computation.16 | async-start | bytes 2097152 | tf_op jit(solution)/shard_map/all_to_all | solution.py:573
  1229.4 16.7 %all-to-all-start.16 = ((f32[16,16,384]{2,1,0:T(8,128)}), f32[16,16,384]{2,1,0:T(8,128)S(1)}, u32[]{:S(2)}, u32[]{:S(2)}) async-start(f32[16,16,384]{2,1,0:T(8,128)} %bitcast.43), calls=%async_computation.18 | async-start | bytes 786432 | tf_op jit(solution)/shard_map/all_to_all | solution.py:555
  1236.5 12.9 %copy-start.1 = (bf16[2048,352]{0,1:T(8,128)(2,1)S(1)}, bf16[2048,352]{0,1:T(8,128)(2,1)}, u32[]{:S(2)}) copy-start(bf16[2048,352]{0,1:T(8,128)(2,1)} %param.30) | copy-start | bytes 4325380
  (28 other events, 70.3 us)
Sparse Core Ops, SparseCore 0:
  69.0 59.8 all-gather.9
  132.0 113.1 all-gather.7
  247.7 77.1 all-gather.11
  394.1 76.9 all-gather.13
  473.9 75.2 all-gather.17
  574.4 173.4 reduce-scatter.2
  750.5 85.5 all-gather.15
  873.3 76.0 all-gather.19
  1146.0 81.5 reduce-scatter.4

commit v19 on v17

--- a/solution.py
+++ b/solution.py
@@ -567,14 +567,16 @@
     gain_two_grad = extra_grad[:, 1]
     attn_router_grad = extra_grad[:, 2 : 2 + EXPERTS]
     mlp_router_grad = extra_grad[:, 2 + EXPERTS : 2 + 2 * EXPERTS]
-    both_full = lax.all_gather(
-        jnp.concatenate(
-            [own_output.astype(jnp.bfloat16), input_grad.astype(jnp.bfloat16)], axis=1
-        ),
+    both_own = jnp.concatenate(
+        [own_output.astype(jnp.bfloat16), input_grad.astype(jnp.bfloat16)], axis=1
+    )
+    both_full = lax.all_to_all(
+        jnp.broadcast_to(both_own[None], (halves,) + both_own.shape),
         "expert",
-        axis=0,
-        tiled=True,
-    )
+        split_axis=0,
+        concat_axis=0,
+        tiled=True,
+    ).reshape(halves * own_rows, 2 * width)
     mixed_full, input_full = both_full[:, :width], both_full[:, width:]
     return (
         mixed_full,

time: 1270 us -> 1270 us (level)
    all_gather x1 -> x0, waiting for transfers between devices: 20 us -> none  [shards(): lax.all_gather(jnp.concatenate([own_output.astype(jnp.bfloat16), input_gr...]
where the time goes in v19:
time: 1270 us; the launch traced here: 1260 us
  waiting for transfers between devices  602 us (47%)
  blocking collectives  218 us (17%)
  matrix products  142 us (11%)
  local copies, waits for them, and re-layouts  129 us (10%)
  other arithmetic  72.7 us (6%)
  starting transfers between devices  53.6 us (4%)
  Pallas kernels  24.1 us (2%)
  between operations  15.6 us (1%)
    all_to_all x1, blocking collectives, combine(): lax.all_to_all(partial_value.astype(jnp.bfloat16).reshape(group_size, gro...  136 us
    all_gather x2, waiting for transfers between devices, dispatch(): lax.all_gather(by_group.reshape(groups * slot_cap, width), GROUP_AXES, ax...  113 us
    all_gather x1, waiting for transfers between devices, shards(): lax.all_gather(mlp_by_group[:, :slot_cap].reshape(groups * slot_cap, widt...  74.6 us
    all_gather x1, waiting for transfers between devices, shards(): lax.all_gather(mlp_by_group[:, slot_cap:].reshape(groups * slot_cap, widt...  68.9 us
    all_gather x1, waiting for transfers between devices, shards(): query_stack = lax.all_gather(query_weight, GROUP_AXES, axis=1, tiled=True)  58.9 us
    all_to_all x1, waiting for transfers between devices, shards(): lax.all_to_all(seq_pair_back, 'grp', split_axis=0, concat_axis=0, tiled=T...  51.7 us
    all_gather x1, waiting for transfers between devices, shards(): output_stack = lax.all_gather(output_weight, GROUP_AXES, axis=0, tiled=True)  38.7 us
    all_gather x1, waiting for transfers between devices, shards(): seq_input = lax.all_gather(attn_input, GROUP_AXES, axis=0, tiled=True)  36.3 us
  transfers between devices with their start and end apart: 20, of which 17 were waited for; matrix products, arithmetic and copies ran while one was open for 17% of the time, Pallas kernels for 1%

profile of v19, /device:TPU:1, one launch (start us, length us, event | category | flops | bytes accessed | tf_op | source)
XLA Modules:
  0.0 1256.5 jit_solution(3435426328139533835)
XLA Ops:
  17.3 17.5 %all_to_all.85 = bf16[16,16,384]{2,1,0:T(8,128)(2,1)S(1)} all-to-all(bf16[16,16,384]{2,1,0:T(8,128)(2,1)S(1)} %pad_maximum_fusion.9), channel_id=1, replica_groups=mesh['grp'=8,'sub'=8,'expert'=2] {'sub','expert'}, dimensions={0} | all-to-all | bytes 393216 | tf_op jit(solution)/shard_map/all_to_all | solution.py:303
  40.9 23.2 %all-to-all-done.1 = bf16[8,256,384]{1,2,0:T(8,128)(2,1)} async-done(((bf16[8,256,384]{1,2,0:T(8,128)(2,1)}), bf16[8,256,384]{1,2,0:T(8,128)(2,1)}, u32[]{:S(2)}, u32[]{:S(2)}) %all-to-all-start.1) | async-done | bytes 1572896 | tf_op jit(solution)/shard_map/all_to_all | solution.py:316
  75.8 13.9 %all_to_all.86 = bf16[8,18,2048]{2,1,0:T(8,128)(2,1)} all-to-all(bf16[8,18,2048]{2,1,0:T(8,128)(2,1)S(1)} %broadcast_select_fusion.1), channel_id=1, replica_groups=mesh['grp'=8,'sub'=8,'expert'=2] {'grp'}, dimensions={0} | all-to-all | bytes 1179648 | tf_op jit(solution)/shard_map/all_to_all | solution.py:222
  92.6 36.3 %all-gather.10.cloned.1.call-done = bf16[1024,2048]{1,0:T(8,128)(2,1)} async-done(((bf16[64,2048]{1,0:T(8,128)(2,1)}), bf16[1024,2048]{1,0:T(8,128)(2,1)}) %all-gather.10.cloned.1.call-update) | async-done | bytes 4194320 | tf_op jit(solution)/shard_map/all_gather | solution.py:336
  139.8 4.8 all-to-all-start.3
  158.9 5.6 multiply_reduce_fusion
  170.5 33.6 %all-to-all-done.3 = bf16[8,1024,256]{2,1,0:T(8,128)(2,1)} async-done(((bf16[8,1024,256]{2,1,0:T(8,128)(2,1)}), bf16[8,1024,256]{2,1,0:T(8,128)(2,1)}, u32[]{:S(2)}, u32[]{:S(2)}) %all-to-all-start.3) | async-done | bytes 4194336 | tf_op jit(solution)/shard_map/all_to_all | solution.py:348
  204.1 4.7 fusion.82
  208.7 36.4 %all-gather.8.cloned.1.call-done = bf16[2304,2048]{1,0:T(8,128)(2,1)} async-done(((bf16[144,2048]{1,0:T(8,128)(2,1)}), bf16[2304,2048]{1,0:T(8,128)(2,1)}) %all-gather.8.cloned.1.call-update) | async-done | bytes 9437200 | tf_op jit(solution)/shard_map/all_gather | solution.py:223
  245.1 7.4 fusion.86
  256.6 5.4 fusion.10
  263.1 11.2 shard_map.238
  286.1 38.7 %all-gather.12.cloned.1.call-done = bf16[2048,2048]{1,0:T(8,128)(2,1)} async-done(((bf16[128,2048]{1,0:T(8,128)(2,1)}), bf16[2048,2048]{1,0:T(8,128)(2,1)}) %all-gather.12.cloned.1.call-update) | async-done | bytes 8388624 | tf_op jit(solution)/shard_map/all_gather | solution.py:384
  324.8 5.7 convolution_convert_fusion.4
  339.7 9.0 all-to-all-done.5
  371.0 19.3 %all_to_all.87 = bf16[8,36,2048]{2,1,0:T(8,128)(2,1)S(1)} all-to-all(bf16[8,36,2048]{2,1,0:T(8,128)(2,1)S(1)} %pad_maximum_fusion.1), channel_id=1, replica_groups=mesh['grp'=8,'sub'=8,'expert'=2] {'grp'}, dimensions={0} | all-to-all | bytes 2359296 | tf_op jit(solution)/shard_map/all_to_all | solution.py:404
  396.3 74.6 %all-gather.14.cloned.1.call-done = bf16[2304,2048]{1,0:T(8,128)(2,1)} async-done(((bf16[144,2048]{1,0:T(8,128)(2,1)}), bf16[2304,2048]{1,0:T(8,128)(2,1)}) %all-gather.14.cloned.1.call-update) | async-done | bytes 9437200 | tf_op jit(solution)/shard_map/all_gather | solution.py:411
  470.9 9.3 fusion.87
  480.2 68.9 %all-gather.18.cloned.1.call-done = bf16[2304,2048]{1,0:T(8,128)(2,1)} async-done(((bf16[144,2048]{1,0:T(8,128)(2,1)}), bf16[2304,2048]{1,0:T(8,128)(2,1)}) %all-gather.18.cloned.1.call-update) | async-done | bytes 9437200 | tf_op jit(solution)/shard_map/all_gather | solution.py:417
  549.1 7.1 fusion.88
  556.9 8.6 multiply_convert_fusion.2
  566.7 7.5 convolution_convert_fusion
  575.0 12.2 fusion.89
  587.2 11.1 add_convert_fusion
  598.3 136.2 %all_to_all.88 = bf16[16,144,2048]{2,1,0:T(8,128)(2,1)} all-to-all(bf16[16,144,2048]{2,1,0:T(8,128)(2,1)S(1)} %bitcast.138), channel_id=1, replica_groups=mesh['grp'=8,'sub'=8,'expert'=2] {'sub','expert'}, dimensions={0} | all-to-all | bytes 18874368 | tf_op jit(solution)/shard_map/all_to_all | solution.py:228
  734.5 5.9 reduce_sum.342
  750.0 7.6 all-to-all-done.9
  777.0 58.9 %all-gather.16.cloned.1.call-done = bf16[2048,2048]{1,0:T(8,128)(2,1)} async-done(((bf16[2048,128]{1,0:T(8,128)(2,1)}), bf16[2048,2048]{1,0:T(8,128)(2,1)}) %all-gather.16.cloned.1.call-update) | async-done | bytes 8388624 | tf_op jit(solution)/shard_map/all_gather | solution.py:429
  856.4 15.7 %all_to_all.89 = bf16[8,18,2048]{2,1,0:T(8,128)(2,1)S(1)} all-to-all(bf16[8,18,2048]{2,1,0:T(8,128)(2,1)S(1)} %multiply_convert_fusion.3), channel_id=1, replica_groups=mesh['grp'=8,'sub'=8,'expert'=2] {'grp'}, dimensions={0} | all-to-all | bytes 1179648 | tf_op jit(solution)/shard_map/all_to_all | solution.py:222
  873.1 76.2 %all-gather.20.cloned.1.call-done = bf16[2304,2048]{1,0:T(8,128)(2,1)} async-done(((bf16[144,2048]{1,0:T(8,128)(2,1)}), bf16[2304,2048]{1,0:T(8,128)(2,1)}) %all-gather.20.cloned.1.call-update) | async-done | bytes 9437200 | tf_op jit(solution)/shard_map/all_gather | solution.py:223
  949.3 6.3 convolution_convert_fusion.2
  956.8 12.9 %shard_map.239 = (f32[8,288,128]{2,1,0:T(8,128)}, bf16[8,1024,256]{2,1,0:T(8,128)(2,1)}) custom-call(bf16[8,288,128]{2,1,0:T(8,128)(2,1)} %pad_maximum_fusion.2.q_ref, bf16[8,1024,128]{2,1,0:T(8,128)(2,1)} %bitcast.151, bf16[8,1024,128]{2,1,0:T(8,128)(2,1)} %bitcast.149, s32[8,288,1]{2,1,0:T(8,128)} %add_select_fusion.qb_ref, ...), custom_call_target="tpu_custom_call" | custom-call | flops 3019898880 | bytes 25100288 | tf_op jit(solution)/shard_map/pallas_call | solution.py:77
  969.7 7.9 fusion.14
  978.4 15.6 %all_to_all.90 = bf16[16,144,128]{2,1,0:T(8,128)(2,1)S(1)} all-to-all(bf16[16,144,128]{2,1,0:T(8,128)(2,1)S(1)} %copy.493), channel_id=1, replica_groups=mesh['grp'=8,'sub'=8,'expert'=2] {'sub','expert'}, dimensions={0} | all-to-all | bytes 1179648 | tf_op jit(solution)/shard_map/all_to_all | solution.py:249
  994.0 4.8 all-to-all-start.13
  998.9 6.3 convolution_convert_fusion.3
  1006.3 51.7 %all-to-all-done.13 = bf16[8,1024,256]{2,1,0:T(8,128)(2,1)} async-done(((bf16[8,1024,256]{2,1,0:T(8,128)(2,1)}), bf16[8,1024,256]{2,1,0:T(8,128)(2,1)}, u32[]{:S(2)}, u32[]{:S(2)}) %all-to-all-start.13) | async-done | bytes 4194336 | tf_op jit(solution)/shard_map/all_to_all | solution.py:498
  1081.4 5.9 all-to-all-start.14
  1097.4 4.9 fusion.53
  1102.2 34.9 %all-to-all-done.14 = bf16[16,64,2048]{2,1,0:T(8,128)(2,1)} async-done(((bf16[16,64,2048]{2,1,0:T(8,128)(2,1)}), bf16[16,64,2048]{2,1,0:T(8,128)(2,1)}, u32[]{:S(2)}, u32[]{:S(2)}) %all-to-all-start.14) | async-done | bytes 4194336 | tf_op jit(solution)/shard_map/all_to_all | solution.py:520
  1146.1 9.4 fusion.94
  1155.5 8.9 fusion.95
  1164.5 5.4 fusion.96
  1171.0 7.6 fusion.92
  1184.3 6.1 fusion.93
  1190.4 35.7 %reduce-scatter.5.cloned.1.call-done = f32[256,384]{0,1:T(8,128)} async-done(((f32[2048,384]{0,1:T(8,128)}), f32[256,384]{0,1:T(8,128)}) %reduce-scatter.5.cloned.1.call-update) | async-done | bytes 393232 | tf_op jit(solution)/shard_map/reduce_scatter | solution.py:554
  1228.0 8.7 all-to-all-start.16
  1237.7 8.5 all-to-all-done.16
  (390 shorter events, 227.0 us)
Async XLA Ops:
  7.2 549.0 %copy-start = (bf16[2048,352]{0,1:T(8,128)(2,1)S(1)}, bf16[2048,352]{0,1:T(8,128)(2,1)}, u32[]{:S(2)}) copy-start(bf16[2048,352]{0,1:T(8,128)(2,1)} %param.30) | copy-start | bytes 4325380
  36.2 27.9 %all-to-all-start.1 = ((bf16[8,256,384]{1,2,0:T(8,128)(2,1)}), bf16[8,256,384]{1,2,0:T(8,128)(2,1)}, u32[]{:S(2)}, u32[]{:S(2)}) async-start(bf16[8,256,384]{1,2,0:T(8,128)(2,1)} %broadcast_in_dim.59), calls=%async_computation.1 | async-start | bytes 3145728 | tf_op jit(solution)/shard_map/all_to_all | solution.py:316
  40.6 88.3 %all-gather.10.cloned.1.call-start = ((), (), s32[]{:S(2)}) async-start(), calls=%async_computation.20 | async-start | bytes 4456448 | tf_op jit(solution)/shard_map/all_gather | solution.py:336
  40.9 25.7 %copy-start.50 = (f32[64]{0:T(128)}, f32[64]{0:T(128)S(1)}, u32[]{:S(2)}) copy-start(f32[64]{0:T(128)S(1)} %add_rsqrt_fusion.1) | copy-start | bytes 772
  66.0 84.0 %copy-start.3 = (bf16[8,256,384]{2,1,0:T(8,128)(2,1)}, bf16[8,256,384]{2,1,0:T(8,128)(2,1)S(1)}, u32[]{:S(2)}) copy-start(bf16[8,256,384]{2,1,0:T(8,128)(2,1)S(1)} %copy.448) | copy-start | bytes 4718596
  68.9 176.2 %all-gather.8.cloned.1.call-start = ((), (), s32[]{:S(2)}) async-start(), calls=%async_computation.19 | async-start | bytes 10027008 | tf_op jit(solution)/shard_map/all_gather | solution.py:223
  91.8 233.0 %all-gather.12.cloned.1.call-start = ((), (), s32[]{:S(2)}) async-start(), calls=%async_computation.21 | async-start | bytes 8912896 | tf_op jit(solution)/shard_map/all_gather | solution.py:384
  92.5 877.2 %copy-start.49 = (f32[64]{0:T(128)}, f32[64]{0:T(128)S(1)}, u32[]{:S(2)}) copy-start(f32[64]{0:T(128)S(1)} %multiply_exponential_fusion) | copy-start | bytes 772
  92.6 39.9 %copy-start.42 = (f32[1024]{0:T(1024)}, f32[1024]{0:T(1024)S(1)}, u32[]{:S(2)}) copy-start(f32[1024]{0:T(1024)S(1)} %iota_convert_fusion) | copy-start | bytes 12292
  139.8 64.2 %all-to-all-start.3 = ((bf16[8,1024,256]{2,1,0:T(8,128)(2,1)}), bf16[8,1024,256]{2,1,0:T(8,128)(2,1)}, u32[]{:S(2)}, u32[]{:S(2)}) async-start(bf16[8,1024,256]{2,1,0:T(8,128)(2,1)} %broadcast_in_dim.68), calls=%async_computation.3 | async-start | bytes 8388608 | tf_op jit(solution)/shard_map/all_to_all | solution.py:348
  158.9 8.2 copy-start.10
  204.1 41.1 %copy-start.28 = (bf16[2048,128]{1,0:T(8,128)(2,1)S(1)}, bf16[2048,128]{1,0:T(8,128)(2,1)}, u32[]{:S(2)}) copy-start(bf16[2048,128]{1,0:T(8,128)(2,1)} %param.25) | copy-start | bytes 1572868
  276.7 48.1 %all-to-all-start.4 = ((bf16[16,144,128]{2,1,0:T(8,128)(2,1)}), bf16[16,144,128]{2,1,0:T(8,128)(2,1)S(1)}, u32[]{:S(2)}, u32[]{:S(2)}) async-start(bf16[16,144,128]{2,1,0:T(8,128)(2,1)} %copy.459), calls=%async_computation.4 | async-start | bytes 1179648 | tf_op jit(solution)/shard_map/all_to_all | solution.py:249
  332.6 16.1 %all-to-all-start.5 = ((bf16[8,18,2048]{2,1,0:T(8,128)(2,1)}), bf16[8,18,2048]{2,1,0:T(8,128)(2,1)S(1)}, u32[]{:S(2)}, u32[]{:S(2)}) async-start(bf16[8,18,2048]{2,1,0:T(8,128)(2,1)} %reshape.678), calls=%async_computation.5 | async-start | bytes 1572864 | tf_op jit(solution)/shard_map/all_to_all | solution.py:259
  336.6 134.3 %all-gather.14.cloned.1.call-start = ((), (), s32[]{:S(2)}) async-start(), calls=%async_computation.22 | async-start | bytes 10027008 | tf_op jit(solution)/shard_map/all_gather | solution.py:411
  339.6 511.3 %copy-start.47 = (f32[64,2]{0,1:T(2,128)}, f32[64,2]{0,1:T(2,128)S(1)}, u32[]{:S(2)}) copy-start(f32[64,2]{0,1:T(2,128)S(1)} %get-tuple-element.150) | copy-start | bytes 1540
  393.9 155.2 %all-gather.18.cloned.1.call-start = ((), (), s32[]{:S(2)}) async-start(), calls=%async_computation.25 | async-start | bytes 10027008 | tf_op jit(solution)/shard_map/all_gather | solution.py:417
  396.1 351.8 %reduce-scatter.3.cloned.1.call-start = ((), (), s32[]{:S(2)}) async-start(), calls=%async_computation.23 | async-start | bytes 10027008 | tf_op jit(solution)/shard_map/reduce_scatter | solution.py:241
  549.1 7.8 copy-start.57
  556.9 9.8 copy-start.56
  574.2 261.7 %all-gather.16.cloned.1.call-start = ((), (), s32[]{:S(2)}) async-start(), calls=%async_computation.24 | async-start | bytes 8912896 | tf_op jit(solution)/shard_map/all_gather | solution.py:429
  575.0 12.2 copy-start.11
  741.4 16.2 %all-to-all-start.9 = ((bf16[8,18,2048]{2,1,0:T(8,128)(2,1)}), bf16[8,18,2048]{2,1,0:T(8,128)(2,1)S(1)}, u32[]{:S(2)}, u32[]{:S(2)}) async-start(bf16[8,18,2048]{2,1,0:T(8,128)(2,1)} %convert_element_type.230), calls=%async_computation.10 | async-start | bytes 1572864 | tf_op jit(solution)/shard_map/all_to_all | solution.py:236
  746.1 16.3 %copy-start.41 = (s32[8,18,1]{0,1,2:T(8,128)S(1)}, s32[8,18,1]{0,1,2:T(8,128)}, u32[]{:S(2)}) copy-start(s32[8,18,1]{0,1,2:T(8,128)} %get-tuple-element.172) | copy-start | bytes 1732
  746.1 16.5 %copy-start.53 = (s32[64,2]{0,1:T(2,128)S(1)}, s32[64,2]{0,1:T(2,128)}, u32[]{:S(2)}) copy-start(s32[64,2]{0,1:T(2,128)} %get-tuple-element.182) | copy-start | bytes 1540
  757.7 16.9 %all-to-all-start.7 = ((bf16[8,18,2048]{2,1,0:T(8,128)(2,1)}), bf16[8,18,2048]{2,1,0:T(8,128)(2,1)}, u32[]{:S(2)}, u32[]{:S(2)}) async-start(bf16[8,18,2048]{2,1,0:T(8,128)(2,1)} %reshape.682), calls=%async_computation.8 | async-start | bytes 1572864 | tf_op jit(solution)/shard_map/all_to_all | solution.py:244
  761.9 187.4 %all-gather.20.cloned.1.call-start = ((), (), s32[]{:S(2)}) async-start(), calls=%async_computation.26 | async-start | bytes 10027008 | tf_op jit(solution)/shard_map/all_gather | solution.py:223
  856.4 92.9 %copy-start.29 = (bf16[128,2048]{1,0:T(8,128)(2,1)S(1)}, bf16[128,2048]{1,0:T(8,128)(2,1)}, u32[]{:S(2)}) copy-start(bf16[128,2048]{1,0:T(8,128)(2,1)} %param.26) | copy-start | bytes 1572868
  978.2 15.9 %copy-start.6 = (bf16[8,16,18,128]{3,2,1,0:T(8,128)(2,1)}, bf16[8,16,18,128]{3,2,1,0:T(8,128)(2,1)S(1)}, u32[]{:S(2)}) copy-start(bf16[8,16,18,128]{3,2,1,0:T(8,128)(2,1)S(1)} %convert_element_type.234) | copy-start | bytes 1769476
  994.0 63.9 %all-to-all-start.13 = ((bf16[8,1024,256]{2,1,0:T(8,128)(2,1)}), bf16[8,1024,256]{2,1,0:T(8,128)(2,1)}, u32[]{:S(2)}, u32[]{:S(2)}) async-start(bf16[8,1024,256]{2,1,0:T(8,128)(2,1)} %get-tuple-element.26), calls=%async_computation.14 | async-start | bytes 8388608 | tf_op jit(solution)/shard_map/all_to_all | solution.py:498
  1058.0 22.6 %all-to-all-start.12 = ((bf16[8,18,2048]{2,1,0:T(8,128)(2,1)}), bf16[8,18,2048]{2,1,0:T(8,128)(2,1)S(1)}, u32[]{:S(2)}, u32[]{:S(2)}) async-start(bf16[8,18,2048]{2,1,0:T(8,128)(2,1)} %reshape.692), calls=%async_computation.13 | async-start | bytes 1572864 | tf_op jit(solution)/shard_map/all_to_all | solution.py:259
  1066.2 10.1 copy-start.4
  1081.4 55.7 %all-to-all-start.14 = ((bf16[16,64,2048]{2,1,0:T(8,128)(2,1)}), bf16[16,64,2048]{2,1,0:T(8,128)(2,1)}, u32[]{:S(2)}, u32[]{:S(2)}) async-start(bf16[16,64,2048]{2,1,0:T(8,128)(2,1)} %bitcast.139), calls=%async_computation.15 | async-start | bytes 8388608 | tf_op jit(solution)/shard_map/all_to_all | solution.py:520
  1087.3 138.8 %reduce-scatter.5.cloned.1.call-start = ((), (), s32[]{:S(2)}) async-start(), calls=%async_computation.27 | async-start | bytes 3538944 | tf_op jit(solution)/shard_map/reduce_scatter | solution.py:554
  1102.2 37.9 %copy-start.15 = (bf16[128,2048]{1,0:T(8,128)(2,1)S(1)}, bf16[128,2048]{1,0:T(8,128)(2,1)}, u32[]{:S(2)}) copy-start(bf16[128,2048]{1,0:T(8,128)(2,1)} %param.21) | copy-start | bytes 1572868
  1102.2 37.9 %copy-start.24 = (f32[64,2048]{1,0:T(8,128)S(1)}, f32[64,2048]{1,0:T(8,128)}, u32[]{:S(2)}) copy-start(f32[64,2048]{1,0:T(8,128)} %multiply_reduce_fusion.3) | copy-start | bytes 1572868
  1102.2 38.0 %copy-start.34 = (f32[2048]{0:T(1024)S(1)}, f32[2048]{0:T(1024)}, u32[]{:S(2)}) copy-start(f32[2048]{0:T(1024)} %copy-done.33) | copy-start | bytes 24580
  1102.2 38.0 %copy-start.51 = (f32[64]{0:T(128)S(1)}, f32[64]{0:T(128)}, u32[]{:S(2)}) copy-start(f32[64]{0:T(128)} %copy-done.50) | copy-start | bytes 772
  1146.1 9.4 copy-start.21
  1146.1 18.4 %slice-start = ((s8[9437184]{0:T(1024)(128)(4,1)}), s8[4194304]{0:T(1024)(128)(4,1)S(1)}, s32[]{:S(2)}) async-start(s8[9437184]{0:T(1024)(128)(4,1)} %bitcast.177), calls=%async_computation.28 | async-start | bytes 8388608
  1146.1 18.3 %slice-start.1 = ((s8[9437184]{0:T(1024)(128)(4,1)}), s8[4194304]{0:T(1024)(128)(4,1)S(1)}, s32[]{:S(2)}) async-start(s8[9437184]{0:T(1024)(128)(4,1)} %bitcast.177), calls=%async_computation.29 | async-start | bytes 8388608
  1155.5 8.9 copy-start.12
  1155.5 8.9 slice-start.2
  1171.0 7.6 copy-start.23
  1171.0 7.6 copy-start.52
  1180.7 47.4 %all-to-all-start.15 = ((bf16[2,64,4096]{2,1,0:T(8,128)(2,1)}), bf16[2,64,4096]{2,1,0:T(8,128)(2,1)S(1)}, u32[]{:S(2)}, u32[]{:S(2)}) async-start(bf16[2,64,4096]{2,1,0:T(8,128)(2,1)} %broadcast_in_dim.73), calls=%async_computation.16 | async-start | bytes 2097152 | tf_op jit(solution)/shard_map/all_to_all | solution.py:573
  1228.0 18.2 %all-to-all-start.16 = ((f32[16,16,384]{2,1,0:T(8,128)}), f32[16,16,384]{2,1,0:T(8,128)S(1)}, u32[]{:S(2)}, u32[]{:S(2)}) async-start(f32[16,16,384]{2,1,0:T(8,128)} %bitcast.43), calls=%async_computation.18 | async-start | bytes 786432 | tf_op jit(solution)/shard_map/all_to_all | solution.py:555
  1236.7 12.9 %copy-start.1 = (bf16[2048,352]{0,1:T(8,128)(2,1)S(1)}, bf16[2048,352]{0,1:T(8,128)(2,1)}, u32[]{:S(2)}) copy-start(bf16[2048,352]{0,1:T(8,128)(2,1)} %param.30) | copy-start | bytes 4325380
  (34 other events, 97.8 us)
Sparse Core Ops, SparseCore 0:
  69.0 59.8 all-gather.9
  132.0 113.1 all-gather.7
  247.6 77.1 all-gather.11
  394.0 76.9 all-gather.13
  473.9 75.2 all-gather.17
  574.3 173.4 reduce-scatter.2
  750.4 85.4 all-gather.15
  873.2 76.0 all-gather.19
  1144.8 81.3 reduce-scatter.4
